TPU v7x, 128 devices: a whole 4x4x4 slice. The times are simulated.
128 devices in a mesh: gx: 32 (over y, z, core), gy: 4 (over x).
Axes of the slice: x: 4, y: 4, z: 4, core: 2. Of those that a mesh axis runs over, the one named last changes fastest.
Arguments:
- initial_heat_state: float32 [1, 2048, 8192], P(None, 'gx', 'gy'), may hold values from -6 to 6
- thermal_coefficient: float32 [1, 2048, 8192], P(None, 'gx', 'gy'), may hold values from 0.5 to 4
Outputs:
- updated: float32 [1, 2048, 8192], P(None, 'gx', 'gy')
All inputs are finite; a program needn't handle non-finite values.
Results may differ from a plain program's by a relative error of at most 0.0025.
Values sent between devices are 32-bit elements; how exact they have to be, the bound alone decides.
No kernel may reach another device: no remote copies, remote signals or barrier semaphores. Data moves between devices by JAX's collectives and lax.ppermute only.
A program may use at most 128 MiB of HBM per device.

v0:
```python
import jax
import jax.numpy as jnp
from jax import lax
from jax.experimental import pallas as pl
from jax.experimental.pallas import tpu as pltpu
from jax.sharding import PartitionSpec as P

ROWS, COLS = 64, 2048
BANDS, TILES = ROWS // 8, COLS // 128
SEGMENTS = 4
Y_STEPS = 128
X_LEVELS, Y_LEVELS = 2, 6
F32 = jnp.float32
VMEM = pl.BlockSpec(memory_space=pltpu.VMEM)


def struct(*shape):
    return jax.ShapeDtypeStruct(shape, F32)


def whole(outs, args):
    return dict(in_specs=[VMEM] * len(args), out_specs=jax.tree.map(lambda _: VMEM, outs))


def call(kernel, outs, scratch=(), flops=2_000_000, name=None, **windows):
    def run(*args):
        return pl.pallas_call(
            kernel,
            out_shape=outs,
            **(windows or whole(outs, args)),
            scratch_shapes=list(scratch),
            compiler_params=pltpu.CompilerParams(vmem_limit_bytes=32 << 20),
            cost_estimate=pl.CostEstimate(flops=flops, bytes_accessed=1 << 20, transcendentals=0),
            name=name,
        )(*args)

    return run


def moved(chain, by, shift):
    out = []
    for s in range(SEGMENTS):
        runs, at = divmod(s + by, SEGMENTS)
        out.append(shift(chain[at], runs) if runs else chain[at])
    return out


def factor(link, n, levels, shift, along, back, gain, sep):
    m = n // SEGMENTS
    near = [link(s * m) for s in range(SEGMENTS)]
    ground = [jnp.ones_like(near[0])] * SEGMENTS
    held = [jnp.ones_like(near[0])] * SEGMENTS
    for step in range(1, m):
        for s in range(SEGMENTS):
            l = s * m + step
            v = link(l)
            r = 1.0 / (near[s] + ground[s] + v)
            t = v * r
            c = near[s] * r
            along[l], back[l], gain[l] = t, c, r
            held[s] = held[s] + ground[s] * c
            near[s] = near[s] * t
            ground[s] = ground[s] * t
            if step < m - 1:
                ground[s] = ground[s] + 1.0
    before = moved(ground, -1, shift)
    own = [held[s] + before[s] for s in range(SEGMENTS)]
    up = near
    down = moved(near, -1, shift)
    for level in range(levels):
        stride = 1 << level
        r = [1.0 / (own[s] + up[s] + down[s]) for s in range(SEGMENTS)]
        r_down, r_up = moved(r, -stride, shift), moved(r, stride, shift)
        own_down, own_up = moved(own, -stride, shift), moved(own, stride, shift)
        down_down, up_up = moved(down, -stride, shift), moved(up, stride, shift)
        for s in range(SEGMENTS):
            a, b = down[s] * r_down[s], up[s] * r_up[s]
            sep[(level * 2) * SEGMENTS + s] = a
            sep[(level * 2 + 1) * SEGMENTS + s] = b
            own[s] = own[s] + a * own_down[s] + b * own_up[s]
            down[s], up[s] = a * down_down[s], b * up_up[s]
    for s in range(SEGMENTS):
        sep[levels * 2 * SEGMENTS + s] = 1.0 / own[s]


def plus(a, b):
    return b if a is None else a if b is None else a + b


def times(a, b):
    return None if a is None else a * b


def solve(source, n, levels, shift, along, back, gain, sep, part, store):
    m = n // SEGMENTS
    total = [source(s * m) for s in range(SEGMENTS)]
    z = [source(s * m + 1) for s in range(SEGMENTS)]
    zero = [[False] * SEGMENTS for _ in range(m)]
    for step in range(1, m):
        for s in range(SEGMENTS):
            l = s * m + step
            zero[step][s] = z[s] is None
            if z[s] is not None:
                part[l] = z[s] * gain[l]
                total[s] = plus(total[s], z[s] * back[l])
                z[s] = z[s] * along[l]
            if step < m - 1:
                z[s] = plus(source(l + 1), z[s])
    shape = jnp.zeros(along.shape[1:], F32)
    z = [shape if v is None else v for v in z]
    before = moved(z, -1, shift)
    total = [plus(total[s], before[s]) for s in range(SEGMENTS)]
    for level in range(levels):
        stride = 1 << level
        lo, hi = moved(total, -stride, shift), moved(total, stride, shift)
        total = [
            total[s]
            + sep[(level * 2) * SEGMENTS + s] * lo[s]
            + sep[(level * 2 + 1) * SEGMENTS + s] * hi[s]
            for s in range(SEGMENTS)
        ]
    value = [total[s] * sep[levels * 2 * SEGMENTS + s] for s in range(SEGMENTS)]
    after = moved(value, 1, shift)
    for s in range(SEGMENTS):
        store(s * m, value[s])
    for step in reversed(range(1, m)):
        for s in range(SEGMENTS):
            l = s * m + step
            known = back[l] * value[s]
            if not zero[step][s]:
                known = known + part[l]
            after[s] = known + along[l] * after[s]
            store(l, after[s])


def x_shift(value, runs):
    return value


def y_shift(value, runs):
    if runs % 2 == 0:
        return pltpu.roll(value, (-(runs // 2)) % 8, 0)
    swapped = pltpu.roll(value, 64, 1)
    late = lax.broadcasted_iota(jnp.int32, value.shape, 1) >= 64
    if runs == 1:
        return jnp.where(late, pltpu.roll(swapped, 7, 0), swapped)
    return jnp.where(late, swapped, pltpu.roll(swapped, 1, 0))


def tile(ref, band, column):
    return ref[8 * band : 8 * band + 8, 128 * column : 128 * column + 128]


def row(ref, i):
    return ref[pl.ds((i // 8) * (8 * TILES) + i % 8, TILES, stride=8), :]


def edges_kernel(t_lo, k_lo, t_hi, k_hi, lo, hi):
    lo[...] = jnp.zeros_like(lo)
    hi[...] = jnp.zeros_like(hi)
    lo[0:1, 0:ROWS] = t_lo[...].T[0:1, :]
    lo[1:2, 0:ROWS] = k_lo[...].T[0:1, :]
    hi[0:1, 0:ROWS] = t_hi[...].T[127:128, :]
    hi[1:2, 0:ROWS] = k_hi[...].T[127:128, :]


def x_matrix_kernel(t, k, e, along, back, gain, sep, lo, hi, ends, flat):
    lane = lax.broadcasted_iota(jnp.int32, (8, 128), 1)
    for band in range(BANDS):
        ks = [tile(k, band, c) for c in range(TILES)]
        ts = [tile(t, band, c) for c in range(TILES)]
        k_left = [pltpu.roll(v, 127, 1) for v in ks]
        t_left = [pltpu.roll(v, 127, 1) for v in ts]
        flow = []
        for c in range(TILES):
            at = pl.ds((band * TILES + c) * 8, 8)
            flat[at, :] = ks[c]
            n = min(c + 1, TILES - 1)
            k_next = jnp.where(lane == 127, k_left[n], k_left[c])
            t_next = jnp.where(lane == 127, t_left[n], t_left[c])
            f = 8000.0 * (ks[c] + k_next) * (t_next - ts[c])
            if c == TILES - 1:
                f = jnp.where(lane == 127, 0.0, f)
            flow.append(f)
        turned = [pltpu.roll(v, 1, 1) for v in flow]
        for c in range(TILES):
            at = pl.ds((band * TILES + c) * 8, 8)
            first = turned[c - 1] if c else jnp.zeros_like(turned[0])
            f_before = jnp.where(lane == 0, first, turned[c])
            e[at, :] = 2.0 * ts[c] + (flow[c] - f_before)

    def link(l):
        if l == ROWS - 1:
            return jnp.zeros((TILES, 128), F32)
        return 1000.0 * (row(flat, l) + row(flat, l + 1))

    factor(link, ROWS, X_LEVELS, x_shift, along, back, gain, sep)
    one = jnp.ones((TILES, 128), F32)

    def at_start(l):
        return one if l == 0 else None

    def at_end(l):
        return one if l == ROWS - 1 else None

    def to(ref):
        def store(l, value):
            ref[l] = value

        return store

    args = (ROWS, X_LEVELS, x_shift, along, back, gain, sep)
    solve(at_start, *args, lo, to(lo))
    solve(at_end, *args, hi, to(hi))
    ends[0] = lo[0]
    ends[1] = lo[ROWS - 1]
    ends[2] = hi[ROWS - 1]
    ends[3] = row(flat, 0)
    ends[4] = row(flat, ROWS - 1)


def x_source_kernel(
    e, along, back, gain, sep, ends, own_lo, own_hi, below, above, u, port, flat, side
):
    side[...] = jnp.zeros_like(side)
    t_lo, k_lo = own_lo[0:1, :], own_lo[1:2, :]
    t_hi, k_hi = own_hi[0:1, :], own_hi[1:2, :]
    side[0:1, :] = -8000.0 * (k_lo + below[1:2, :]) * (t_lo - below[0:1, :])
    side[127:128, :] = 8000.0 * (k_hi + above[1:2, :]) * (above[0:1, :] - t_hi)
    edge = side[...].T
    lane = lax.broadcasted_iota(jnp.int32, (8, 128), 1)
    flat[...] = e[...]
    for band in range(BANDS):
        part = edge[8 * band : 8 * band + 8, :]
        at = pl.ds(band * TILES * 8, 8)
        flat[at, :] = flat[at, :] + jnp.where(lane == 0, part, 0.0)
        at = pl.ds((band * TILES + TILES - 1) * 8, 8)
        flat[at, :] = flat[at, :] + jnp.where(lane == 127, part, 0.0)

    def store(l, value):
        u[l] = value

    def source(l):
        return row(flat, l)

    solve(source, ROWS, X_LEVELS, x_shift, along, back, gain, sep, u, store)
    port[0] = u[0]
    port[1] = u[ROWS - 1]
    for n in range(5):
        port[2 + n] = ends[n]


def take(ref):
    return tuple(ref[n] for n in range(7))


def join(one, two, scale):
    a1, b1, al1, be1, ga1, kf1, kl1 = one
    a2, b2, al2, be2, ga2, kf2, kl2 = two
    rho = 1.0 / (1.0 / (scale * (kl1 + kf2)) + al2 + ga1)
    delta = (a2 - b1) * rho
    return (
        a1 + be1 * delta,
        b2 - be2 * delta,
        al1 - be1 * be1 * rho,
        be1 * be2 * rho,
        ga2 - be2 * be2 * rho,
        kf1,
        kl2,
    )


def past_up(state, port, scale):
    p, q, k = state
    a, b, al, be, ga, kf, kl = port
    w = be / (1.0 / (scale * (k + kf)) + al + q)
    return (b - w * (a - p), ga - w * be, kl)


def past_down(state, port, scale):
    p, q, k = state
    a, b, al, be, ga, kf, kl = port
    w = be / (1.0 / (scale * (k + kl)) + ga + q)
    return (a + w * (p - b), al - w * be, kf)


def choose(condition, new, old):
    return tuple(jnp.where(condition, x, y) for x, y in zip(new, old))


def reach(index, ports, lo, hi, scale):
    count = len(ports)
    for n in range(count - 1):
        lo = choose(n < index, past_up(lo, ports[n], scale), lo)
    for n in reversed(range(1, count)):
        hi = choose(n > index, past_down(hi, ports[n], scale), hi)
    return lo, hi


def flows(port, lo, hi, scale):
    a, b, al, be, ga, kf, kl = port
    d_lo = 1.0 / (scale * (lo[2] + kf)) + al + lo[1]
    d_hi = 1.0 / (scale * (hi[2] + kl)) + ga + hi[1]
    c_lo, c_hi = a - lo[0], hi[0] - b
    inverse = 1.0 / (d_lo * d_hi - be * be)
    return (d_hi * c_lo + be * c_hi) * inverse, (d_lo * c_hi + be * c_lo) * inverse


def place(index, own, received, table):
    table[index] = own[...]
    for s in (1, 2, 3):
        table[lax.rem(index + 4 - s, 4)] = received[s - 1][...]


def pair_kernel(own, other, out):
    core = lax.rem(lax.axis_index("gx"), 2)
    mine, theirs = take(own), take(other)
    first = choose(core == 0, mine, theirs)
    second = choose(core == 0, theirs, mine)
    for n, value in enumerate(join(first, second, 1000.0)):
        out[n] = value


def four_kernel(own, r1, r2, r3, out, table):
    z = lax.rem(lax.div(lax.axis_index("gx"), 2), 4)
    place(z, own, (r1, r2, r3), table)
    ports = [take(table.at[j]) for j in range(4)]
    joined = join(join(ports[0], ports[1], 1000.0), join(ports[2], ports[3], 1000.0), 1000.0)
    for n, value in enumerate(joined):
        out[n] = value


def to_runs(blocks, out):
    for p in range(TILES // 2):
        stack = [blocks(band, 2 * p + half) for half in range(2) for band in range(BANDS)]
        out[128 * p : 128 * p + 128, :] = jnp.concatenate(stack, axis=0).T


def cell(ref, l):
    return ref[pl.ds(l, 8, stride=128), :]


def y_matrix_kernel(k, along, back, gain, sep, lo, hi, ends, turned):
    to_runs(lambda band, column: tile(k, band, column), turned)
    lane = lax.broadcasted_iota(jnp.int32, (8, 128), 1)
    sublane = lax.broadcasted_iota(jnp.int32, (8, 128), 0)
    very_last = (lane >= 64) & (sublane == 7)
    very_first = (lane < 64) & (sublane == 0)

    def link(l):
        if l == Y_STEPS - 1:
            both = 4000.0 * (cell(turned, l) + y_shift(cell(turned, 0), 1))
            return jnp.where(very_last, 0.0, both)
        return 4000.0 * (cell(turned, l) + cell(turned, l + 1))

    factor(link, Y_STEPS, Y_LEVELS, y_shift, along, back, gain, sep)

    def at_start(l):
        return jnp.where(very_first, 1.0, 0.0) if l == 0 else None

    def at_end(l):
        return jnp.where(very_last, 1.0, 0.0) if l == Y_STEPS - 1 else None

    def to(ref):
        def store(l, value):
            ref[l] = value

        return store

    args = (Y_STEPS, Y_LEVELS, y_shift, along, back, gain, sep)
    solve(at_start, *args, lo, to(lo))
    solve(at_end, *args, hi, to(hi))
    last = Y_STEPS - 1
    ends[...] = jnp.zeros_like(ends)
    ends[0:1, :] = lo[0, 0:1, :]
    ends[1:2, :] = pltpu.roll(lo[last], 64, 1)[7:8, :]
    ends[2:3, :] = pltpu.roll(hi[last], 64, 1)[7:8, :]
    ends[3:4, :] = cell(turned, 0)[0:1, :]
    ends[4:5, :] = pltpu.roll(cell(turned, last), 64, 1)[7:8, :]


def y_source_kernel(
    own_y, y1, y2, y3, own_z, z1, z2, z3, own, other, u, x_lo, x_hi, t,
    along, back, gain, sep, ends, d, port, table_y, table_z, flat, turned,
):
    index = lax.axis_index("gx")
    core, z, y = lax.rem(index, 2), lax.rem(lax.div(index, 2), 4), lax.div(index, 8)
    place(y, own_y, (y1, y2, y3), table_y)
    place(z, own_z, (z1, z2, z3), table_z)
    nothing = (jnp.zeros((TILES, 128), F32),) * 3
    scale = 1000.0
    lo, hi = reach(y, [take(table_y.at[j]) for j in range(4)], nothing, nothing, scale)
    lo, hi = reach(z, [take(table_z.at[j]) for j in range(4)], lo, hi, scale)
    mine, theirs = take(own), take(other)
    lo = choose(core == 1, past_up(lo, theirs, scale), lo)
    hi = choose(core == 0, past_down(hi, theirs, scale), hi)
    f_lo, f_hi = flows(mine, lo, hi, scale)
    for i in range(ROWS):
        at = pl.ds((i // 8) * (8 * TILES) + i % 8, TILES, stride=8)
        flat[at, :] = u[i] - f_lo * x_lo[i] + f_hi * x_hi[i]

    def block(band, column):
        at = (band * TILES + column) * 8
        return flat[at : at + 8, :] - 2.0 * tile(t, band, column)

    to_runs(block, turned)

    def store(l, value):
        d[l] = value

    def source(l):
        return cell(turned, l)

    solve(source, Y_STEPS, Y_LEVELS, y_shift, along, back, gain, sep, d, store)
    port[...] = jnp.zeros_like(port)
    port[0:1, :] = d[0, 0:1, :]
    port[1:2, :] = pltpu.roll(d[Y_STEPS - 1], 64, 1)[7:8, :]
    port[2:7, :] = ends[0:5, :]


def finish_kernel(own, r1, r2, r3, d, y_lo, y_hi, t, out, table, turned):
    index = lax.axis_index("gy")
    place(index, own, (r1, r2, r3), table)
    lane = lax.broadcasted_iota(jnp.int32, (1, 128), 1)

    def port_of(ref):
        return tuple(jnp.where(lane < ROWS, ref[n : n + 1, :], 1.0) for n in range(7))

    nothing = (jnp.zeros((1, 128), F32),) * 3
    scale = 4000.0
    lo, hi = reach(index, [port_of(table.at[j]) for j in range(4)], nothing, nothing, scale)
    f_lo, f_hi = flows(port_of(own), lo, hi, scale)

    def doubled(f):
        f = jnp.broadcast_to(jnp.where(lane < ROWS, f, 0.0), (8, 128))
        return f + pltpu.roll(f, 64, 1)

    f_lo, f_hi = doubled(f_lo), doubled(f_hi)
    for l in range(Y_STEPS):
        turned[pl.ds(l, 8, stride=128), :] = d[l] - f_lo * y_lo[l] + f_hi * y_hi[l]
    for p in range(TILES // 2):
        block = turned[128 * p : 128 * p + 128, :].T
        for half in range(2):
            column = 2 * p + half
            for band in range(BANDS):
                at = 64 * half + 8 * band
                out[8 * band : 8 * band + 8, 128 * column : 128 * column + 128] = (
                    tile(t, band, column) + block[at : at + 8, :]
                )


def around(value, axis, size, stride, step):
    pairs = []
    for i in range(size):
        digit = (i // stride) % 4
        pairs.append((i, i + ((digit + step) % 4 - digit) * stride))
    return lax.ppermute(value, axis, pairs)


def per_device(initial_heat_state, thermal_coefficient):
    t, k = initial_heat_state[0], thermal_coefficient[0]
    first = pl.BlockSpec((ROWS, 128), lambda n: (0, 0))
    last = pl.BlockSpec((ROWS, 128), lambda n: (0, TILES - 1))
    own_lo, own_hi = call(
        edges_kernel,
        [struct(8, 128)] * 2,
        name="edges",
        grid=(1,),
        in_specs=[first, first, last, last],
        out_specs=[pl.BlockSpec((8, 128), lambda n: (0, 0))] * 2,
    )(t, k, t, k)
    below = lax.ppermute(own_hi, "gy", [(i, i + 1) for i in range(3)])
    above = lax.ppermute(own_lo, "gy", [(i + 1, i) for i in range(3)])
    flat = pltpu.VMEM((BANDS * TILES * 8, 128), F32)
    runs = pltpu.VMEM((TILES // 2 * 128, 128), F32)
    x_field, y_field = struct(ROWS, TILES, 128), struct(Y_STEPS, 8, 128)
    e, *x_coefficients, x_lo, x_hi, x_ends = call(
        x_matrix_kernel,
        [
            struct(BANDS * TILES * 8, 128),
            x_field,
            x_field,
            x_field,
            struct((2 * X_LEVELS + 1) * SEGMENTS, TILES, 128),
            x_field,
            x_field,
            struct(5, TILES, 128),
        ],
        [flat],
        name="x_matrix",
    )(t, k)
    x_port = struct(7, TILES, 128)
    u, own = call(
        x_source_kernel,
        [x_field, x_port],
        [flat, pltpu.VMEM((128, 128), F32)],
        name="x_source",
    )(e, *x_coefficients, x_ends, own_lo, own_hi, below, above)
    other = lax.ppermute(own, "gx", [(i, i ^ 1) for i in range(32)])
    own_z = call(pair_kernel, x_port, name="pair")(own, other)
    k_y, own_z = lax.optimization_barrier((k, own_z))
    from_z = [around(own_z, "gx", 32, 2, s) for s in (1, 2, 3)]
    *y_coefficients, y_lo, y_hi, y_ends = call(
        y_matrix_kernel,
        [
            y_field,
            y_field,
            y_field,
            struct((2 * Y_LEVELS + 1) * SEGMENTS, 8, 128),
            y_field,
            y_field,
            struct(8, 128),
        ],
        [runs],
        name="y_matrix",
    )(k_y)
    table = pltpu.VMEM((4, 7, TILES, 128), F32)
    own_y = call(four_kernel, x_port, [table], name="four")(own_z, *from_z)
    from_y = [around(own_y, "gx", 32, 8, s) for s in (1, 2, 3)]
    d, port = call(
        y_source_kernel,
        [y_field, struct(8, 128)],
        [table, table, flat, runs],
        name="y_source",
    )(own_y, *from_y, own_z, *from_z, own, other, u, x_lo, x_hi, t, *y_coefficients, y_ends)
    from_gy = [around(port, "gy", 4, 1, s) for s in (1, 2, 3)]
    updated = call(
        finish_kernel,
        struct(ROWS, COLS),
        [pltpu.VMEM((4, 8, 128), F32), runs],
        name="finish",
    )(port, *from_gy, d, y_lo, y_hi, t)
    return updated[None]


def solution(mesh):
    placed = (P(None, "gx", "gy"), P(None, "gx", "gy"))
    return jax.shard_map(
        per_device, mesh=mesh, in_specs=placed, out_specs=P(None, "gx", "gy"), check_vma=False
    )
```

profile of v0, /device:TPU:0, one launch (start us, length us, event | category | flops | bytes accessed | tf_op | source)
XLA Modules:
  0.0 42.8 jit_solution(3928043571007403078)
XLA Ops:
  0.0 0.0 copy-start
  0.0 1.0 %copy-done = f32[1,64,2048]{2,1,0:T(8,128)S(1)} copy-done((f32[1,64,2048]{2,1,0:T(8,128)S(1)}, f32[1,64,2048]{2,1,0:T(8,128)}, u32[]{:S(2)}) %copy-start) | copy-done | bytes 524312
  1.0 0.0 copy-start.2
  1.0 1.0 %copy-done.2 = f32[1,64,2048]{2,1,0:T(8,128)S(1)} copy-done((f32[1,64,2048]{2,1,0:T(8,128)S(1)}, f32[1,64,2048]{2,1,0:T(8,128)}, u32[]{:S(2)}) %copy-start.2) | copy-done | bytes 524312
  2.1 0.1 edges.1
  2.2 1.3 %collective-permute-start.1 = (f32[8,128]{1,0:T(8,128)S(1)}, f32[8,128]{1,0:T(8,128)S(1)}, u32[]{:S(2)}, u32[]{:S(2)}) collective-permute-start(f32[8,128]{1,0:T(8,128)S(1)} %get-tuple-element.34.own_lo), channel_id=1, source_target_pairs={{1,0},{2,1},{3,2},{5,4},{6,5},{7,6},{9,8},{10,9},{11,10},{13,12},{... | collective-permute-start | bytes 12296 | tf_op jit(solution)/shard_map/ppermute | solution.py:473
  3.5 4.5 %collective-permute-start = (f32[8,128]{1,0:T(8,128)S(1)}, f32[8,128]{1,0:T(8,128)S(1)}, u32[]{:S(2)}, u32[]{:S(2)}) collective-permute-start(f32[8,128]{1,0:T(8,128)S(1)} %get-tuple-element.35.own_hi), channel_id=1, source_target_pairs={{0,1},{1,2},{2,3},{4,5},{5,6},{6,7},{8,9},{9,10},{10,11},{12,13},{... | collective-permute-start | bytes 12296 | tf_op jit(solution)/shard_map/ppermute | solution.py:472
  8.0 1.0 %x_matrix.1 = (f32[1024,128]{1,0:T(8,128)S(1)}, f32[64,16,128]{2,1,0:T(8,128)S(1)}, f32[64,16,128]{2,1,0:T(8,128)S(1)}, f32[64,16,128]{2,1,0:T(8,128)S(1)}, f32[...) custom-call(f32[64,2048]{1,0:T(8,128)S(1)} %bitcast.5, ...), custom_call_target="tpu_custom_call" | custom-call | flops 2000000 | bytes 1048576 | tf_op jit(solution)/shard_map/x_matrix/pallas_call | solution.py:27
  9.1 0.0 collective-permute-done.1.above
  9.1 0.3 collective-permute-done.below
  9.4 0.0 copy-start.3
  9.4 0.4 x_source.1
  9.7 0.0 copy-start.1
  9.7 0.1 collective-permute-start.2
  9.8 1.2 %collective-permute-done.2.other = f32[7,16,128]{2,1,0:T(8,128)S(1)} collective-permute-done((f32[7,16,128]{2,1,0:T(8,128)S(1)}, f32[7,16,128]{2,1,0:T(8,128)S(1)}, u32[]{:S(2)}, u32[]{:S(2)}) %collective-permute-start.2) | collective-permute-done | bytes 57376 | tf_op jit(solution)/shard_map/ppermute | solution.py:499
  11.1 4.2 %collective-permute-start.5 = (f32[7,16,128]{2,1,0:T(8,128)S(1)}, f32[7,16,128]{2,1,0:T(8,128)S(1)}, u32[]{:S(2)}, u32[]{:S(2)}) collective-permute-start(f32[7,16,128]{2,1,0:T(8,128)S(1)} %pair.1.own.own_z), channel_id=1, source_target_pairs={{0,24},{4,28},{8,0},{12,4},{16,8},{20,12},{24,16},{28,20},{32,56},... | collective-permute-start | bytes 172040 | tf_op jit(solution)/shard_map/ppermute | solution.py:457
  15.3 0.0 collective-permute-start.4
  15.3 1.3 %collective-permute-start.3 = (f32[7,16,128]{2,1,0:T(8,128)S(1)}, f32[7,16,128]{2,1,0:T(8,128)S(1)}, u32[]{:S(2)}, u32[]{:S(2)}) collective-permute-start(f32[7,16,128]{2,1,0:T(8,128)S(1)} %pair.1.own.own_z), channel_id=1, source_target_pairs={{0,8},{4,12},{8,16},{12,20},{16,24},{20,28},{24,0},{28,4},{32,40},... | collective-permute-start | bytes 172040 | tf_op jit(solution)/shard_map/ppermute | solution.py:457
  16.5 1.5 %collective-permute-done.5.r3.z3 = f32[7,16,128]{2,1,0:T(8,128)S(1)} collective-permute-done((f32[7,16,128]{2,1,0:T(8,128)S(1)}, f32[7,16,128]{2,1,0:T(8,128)S(1)}, u32[]{:S(2)}, u32[]{:S(2)}) %collective-permute-start.5) | collective-permute-done | bytes 57376 | tf_op jit(solution)/shard_map/ppermute | solution.py:457
  18.0 3.1 %collective-permute-done.4.r2.z2 = f32[7,16,128]{2,1,0:T(8,128)S(1)} collective-permute-done((f32[7,16,128]{2,1,0:T(8,128)S(1)}, f32[7,16,128]{2,1,0:T(8,128)S(1)}, u32[]{:S(2)}, u32[]{:S(2)}) %collective-permute-start.4) | collective-permute-done | bytes 57376 | tf_op jit(solution)/shard_map/ppermute | solution.py:457
  21.1 0.3 collective-permute-done.3.r1.z1
  21.4 0.1 four.1.own_y
  21.5 3.1 %collective-permute-start.8 = (f32[7,16,128]{2,1,0:T(8,128)S(1)}, f32[7,16,128]{2,1,0:T(8,128)S(1)}, u32[]{:S(2)}, u32[]{:S(2)}) collective-permute-start(f32[7,16,128]{2,1,0:T(8,128)S(1)} %four.1.own_y), channel_id=1, source_target_pairs={{0,96},{4,100},{8,104},{12,108},{16,112},{20,116},{24,120},{28,124... | collective-permute-start | bytes 172040 | tf_op jit(solution)/shard_map/ppermute | solution.py:457
  24.6 0.6 %collective-permute-start.7 = (f32[7,16,128]{2,1,0:T(8,128)S(1)}, f32[7,16,128]{2,1,0:T(8,128)S(1)}, u32[]{:S(2)}, u32[]{:S(2)}) collective-permute-start(f32[7,16,128]{2,1,0:T(8,128)S(1)} %four.1.own_y), channel_id=1, source_target_pairs={{0,64},{4,68},{8,72},{12,76},{16,80},{20,84},{24,88},{28,92},{32,9... | collective-permute-start | bytes 172040 | tf_op jit(solution)/shard_map/ppermute | solution.py:457
  25.2 1.0 %collective-permute-start.6 = (f32[7,16,128]{2,1,0:T(8,128)S(1)}, f32[7,16,128]{2,1,0:T(8,128)S(1)}, u32[]{:S(2)}, u32[]{:S(2)}) collective-permute-start(f32[7,16,128]{2,1,0:T(8,128)S(1)} %four.1.own_y), channel_id=1, source_target_pairs={{0,32},{4,36},{8,40},{12,44},{16,48},{20,52},{24,56},{28,60},{32,6... | collective-permute-start | bytes 172040 | tf_op jit(solution)/shard_map/ppermute | solution.py:457
  26.2 0.0 copy-done.3
  26.2 1.2 %y_matrix.1 = (f32[128,8,128]{2,1,0:T(8,128)S(1)}, f32[128,8,128]{2,1,0:T(8,128)S(1)}, f32[128,8,128]{2,1,0:T(8,128)S(1)}, f32[52,8,128]{2,1,0:T(8,128)S(1)}, f3...) custom-call(f32[64,2048]{1,0:T(8,128)S(1)} %bitcast.11), custom_call_target="tpu_custom_call" | custom-call | flops 2000000 | bytes 1048576 | tf_op jit(solution)/shard_map/y_matrix/pallas_call | solution.py:27
  27.4 0.0 collective-permute-done.8.y3
  27.4 2.9 %collective-permute-done.7.y2 = f32[7,16,128]{2,1,0:T(8,128)S(1)} collective-permute-done((f32[7,16,128]{2,1,0:T(8,128)S(1)}, f32[7,16,128]{2,1,0:T(8,128)S(1)}, u32[]{:S(2)}, u32[]{:S(2)}) %collective-permute-start.7) | collective-permute-done | bytes 57376 | tf_op jit(solution)/shard_map/ppermute | solution.py:457
  30.3 0.6 %collective-permute-done.6.y1 = f32[7,16,128]{2,1,0:T(8,128)S(1)} collective-permute-done((f32[7,16,128]{2,1,0:T(8,128)S(1)}, f32[7,16,128]{2,1,0:T(8,128)S(1)}, u32[]{:S(2)}, u32[]{:S(2)}) %collective-permute-start.6) | collective-permute-done | bytes 57376 | tf_op jit(solution)/shard_map/ppermute | solution.py:457
  30.9 0.0 copy-done.1
  30.9 1.2 %y_source.1 = (f32[128,8,128]{2,1,0:T(8,128)S(1)}, f32[8,128]{1,0:T(8,128)S(1)}) custom-call(f32[7,16,128]{2,1,0:T(8,128)S(1)} %four.1.own_y, f32[7,16,128]{2,1,0:T(8,128)S(1)} %collective-permute-done.6.y1, f32[7,16,128]{2,1,0:T(8,128)S(1)} %collective-permute-done.7.y2, f32[7,16,128]{2,1,0:T(8,128)S(1)} %collective-permute-done.8.y3, ...), custom_call_target="tpu_custom_call" | custom-call | flops 2000000 | bytes 1048576 | tf_op jit(solution)/shard_map/y_source/pallas_call | solution.py:27
  32.0 3.9 %collective-permute-start.11 = (f32[8,128]{1,0:T(8,128)S(1)}, f32[8,128]{1,0:T(8,128)S(1)}, u32[]{:S(2)}, u32[]{:S(2)}) collective-permute-start(f32[8,128]{1,0:T(8,128)S(1)} %get-tuple-element.47.own), channel_id=1, source_target_pairs={{0,3},{1,0},{2,1},{3,2},{4,7},{5,4},{6,5},{7,6},{8,11},{9,8},{10,9... | collective-permute-start | bytes 12296 | tf_op jit(solution)/shard_map/ppermute | solution.py:457
  35.9 0.5 %collective-permute-start.10 = (f32[8,128]{1,0:T(8,128)S(1)}, f32[8,128]{1,0:T(8,128)S(1)}, u32[]{:S(2)}, u32[]{:S(2)}) collective-permute-start(f32[8,128]{1,0:T(8,128)S(1)} %get-tuple-element.47.own), channel_id=1, source_target_pairs={{0,2},{1,3},{2,0},{3,1},{4,6},{5,7},{6,4},{7,5},{8,10},{9,11},{10,... | collective-permute-start | bytes 12296 | tf_op jit(solution)/shard_map/ppermute | solution.py:457
  36.5 0.9 %collective-permute-start.9 = (f32[8,128]{1,0:T(8,128)S(1)}, f32[8,128]{1,0:T(8,128)S(1)}, u32[]{:S(2)}, u32[]{:S(2)}) collective-permute-start(f32[8,128]{1,0:T(8,128)S(1)} %get-tuple-element.47.own), channel_id=1, source_target_pairs={{0,1},{1,2},{2,3},{3,0},{4,5},{5,6},{6,7},{7,4},{8,9},{9,10},{10,1... | collective-permute-start | bytes 12296 | tf_op jit(solution)/shard_map/ppermute | solution.py:457
  37.3 0.0 collective-permute-done.11.r3
  37.3 3.7 %collective-permute-done.10.r2 = f32[8,128]{1,0:T(8,128)S(1)} collective-permute-done((f32[8,128]{1,0:T(8,128)S(1)}, f32[8,128]{1,0:T(8,128)S(1)}, u32[]{:S(2)}, u32[]{:S(2)}) %collective-permute-start.10) | collective-permute-done | bytes 4128 | tf_op jit(solution)/shard_map/ppermute | solution.py:457
  41.1 0.2 collective-permute-done.9.r1
  41.3 1.5 %finish.1 = f32[64,2048]{1,0:T(8,128)} custom-call(f32[8,128]{1,0:T(8,128)S(1)} %get-tuple-element.47.own, f32[8,128]{1,0:T(8,128)S(1)} %collective-permute-done.9.r1, f32[8,128]{1,0:T(8,128)S(1)} %collective-permute-done.10.r2, f32[8,128]{1,0:T(8,128)S(1)} %collective-permute-done.11.r3, f32[128,8,128]{2,1,0:T(8,128)S(1)} %get-tuple-element.48.d, ...), custom_call_target="tpu_custom_call" | custom-call | flops 2000000 | bytes 1048576 | tf_op jit(solution)/shard_map/finish/pallas_call | solution.py:27
  (1 shorter events, 0.0 us)
Async XLA Ops:
  0.0 1.0 %copy-start = (f32[1,64,2048]{2,1,0:T(8,128)S(1)}, f32[1,64,2048]{2,1,0:T(8,128)}, u32[]{:S(2)}) copy-start(f32[1,64,2048]{2,1,0:T(8,128)} %param.2) | copy-start | bytes 1572868
  1.0 1.0 %copy-start.2 = (f32[1,64,2048]{2,1,0:T(8,128)S(1)}, f32[1,64,2048]{2,1,0:T(8,128)}, u32[]{:S(2)}) copy-start(f32[1,64,2048]{2,1,0:T(8,128)} %param.3) | copy-start | bytes 1572868
  2.2 6.9 %collective-permute-start.1 = (f32[8,128]{1,0:T(8,128)S(1)}, f32[8,128]{1,0:T(8,128)S(1)}, u32[]{:S(2)}, u32[]{:S(2)}) collective-permute-start(f32[8,128]{1,0:T(8,128)S(1)} %get-tuple-element.34.own_lo), channel_id=1, source_target_pairs={{1,0},{2,1},{3,2},{5,4},{6,5},{7,6},{9,8},{10,9},{11,10},{13,12},{... | collective-permute-start | bytes 12296 | tf_op jit(solution)/shard_map/ppermute | solution.py:473
  3.5 5.9 %collective-permute-start = (f32[8,128]{1,0:T(8,128)S(1)}, f32[8,128]{1,0:T(8,128)S(1)}, u32[]{:S(2)}, u32[]{:S(2)}) collective-permute-start(f32[8,128]{1,0:T(8,128)S(1)} %get-tuple-element.35.own_hi), channel_id=1, source_target_pairs={{0,1},{1,2},{2,3},{4,5},{5,6},{6,7},{8,9},{9,10},{10,11},{12,13},{... | collective-permute-start | bytes 12296 | tf_op jit(solution)/shard_map/ppermute | solution.py:472
  9.4 16.8 %copy-start.3 = (f32[1,64,2048]{2,1,0:T(8,128)S(1)}, f32[1,64,2048]{2,1,0:T(8,128)}, u32[]{:S(2)}) copy-start(f32[1,64,2048]{2,1,0:T(8,128)} %param.3) | copy-start | bytes 1572868
  9.7 21.1 %copy-start.1 = (f32[1,64,2048]{2,1,0:T(8,128)S(1)}, f32[1,64,2048]{2,1,0:T(8,128)}, u32[]{:S(2)}) copy-start(f32[1,64,2048]{2,1,0:T(8,128)} %param.2) | copy-start | bytes 1572868
  9.7 1.3 %collective-permute-start.2 = (f32[7,16,128]{2,1,0:T(8,128)S(1)}, f32[7,16,128]{2,1,0:T(8,128)S(1)}, u32[]{:S(2)}, u32[]{:S(2)}) collective-permute-start(f32[7,16,128]{2,1,0:T(8,128)S(1)} %get-tuple-element.36.own), channel_id=1, source_target_pairs={{0,4},{4,0},{8,12},{12,8},{16,20},{20,16},{24,28},{28,24},{32,36},... | collective-permute-start | bytes 172040 | tf_op jit(solution)/shard_map/ppermute | solution.py:499
  11.1 7.0 %collective-permute-start.5 = (f32[7,16,128]{2,1,0:T(8,128)S(1)}, f32[7,16,128]{2,1,0:T(8,128)S(1)}, u32[]{:S(2)}, u32[]{:S(2)}) collective-permute-start(f32[7,16,128]{2,1,0:T(8,128)S(1)} %pair.1.own.own_z), channel_id=1, source_target_pairs={{0,24},{4,28},{8,0},{12,4},{16,8},{20,12},{24,16},{28,20},{32,56},... | collective-permute-start | bytes 172040 | tf_op jit(solution)/shard_map/ppermute | solution.py:457
  15.3 5.9 %collective-permute-start.4 = (f32[7,16,128]{2,1,0:T(8,128)S(1)}, f32[7,16,128]{2,1,0:T(8,128)S(1)}, u32[]{:S(2)}, u32[]{:S(2)}) collective-permute-start(f32[7,16,128]{2,1,0:T(8,128)S(1)} %pair.1.own.own_z), channel_id=1, source_target_pairs={{0,16},{4,20},{8,24},{12,28},{16,0},{20,4},{24,8},{28,12},{32,48},... | collective-permute-start | bytes 172040 | tf_op jit(solution)/shard_map/ppermute | solution.py:457
  15.3 6.1 %collective-permute-start.3 = (f32[7,16,128]{2,1,0:T(8,128)S(1)}, f32[7,16,128]{2,1,0:T(8,128)S(1)}, u32[]{:S(2)}, u32[]{:S(2)}) collective-permute-start(f32[7,16,128]{2,1,0:T(8,128)S(1)} %pair.1.own.own_z), channel_id=1, source_target_pairs={{0,8},{4,12},{8,16},{12,20},{16,24},{20,28},{24,0},{28,4},{32,40},... | collective-permute-start | bytes 172040 | tf_op jit(solution)/shard_map/ppermute | solution.py:457
  21.5 5.9 %collective-permute-start.8 = (f32[7,16,128]{2,1,0:T(8,128)S(1)}, f32[7,16,128]{2,1,0:T(8,128)S(1)}, u32[]{:S(2)}, u32[]{:S(2)}) collective-permute-start(f32[7,16,128]{2,1,0:T(8,128)S(1)} %four.1.own_y), channel_id=1, source_target_pairs={{0,96},{4,100},{8,104},{12,108},{16,112},{20,116},{24,120},{28,124... | collective-permute-start | bytes 172040 | tf_op jit(solution)/shard_map/ppermute | solution.py:457
  24.6 5.7 %collective-permute-start.7 = (f32[7,16,128]{2,1,0:T(8,128)S(1)}, f32[7,16,128]{2,1,0:T(8,128)S(1)}, u32[]{:S(2)}, u32[]{:S(2)}) collective-permute-start(f32[7,16,128]{2,1,0:T(8,128)S(1)} %four.1.own_y), channel_id=1, source_target_pairs={{0,64},{4,68},{8,72},{12,76},{16,80},{20,84},{24,88},{28,92},{32,9... | collective-permute-start | bytes 172040 | tf_op jit(solution)/shard_map/ppermute | solution.py:457
  25.2 5.7 %collective-permute-start.6 = (f32[7,16,128]{2,1,0:T(8,128)S(1)}, f32[7,16,128]{2,1,0:T(8,128)S(1)}, u32[]{:S(2)}, u32[]{:S(2)}) collective-permute-start(f32[7,16,128]{2,1,0:T(8,128)S(1)} %four.1.own_y), channel_id=1, source_target_pairs={{0,32},{4,36},{8,40},{12,44},{16,48},{20,52},{24,56},{28,60},{32,6... | collective-permute-start | bytes 172040 | tf_op jit(solution)/shard_map/ppermute | solution.py:457
  32.0 5.3 %collective-permute-start.11 = (f32[8,128]{1,0:T(8,128)S(1)}, f32[8,128]{1,0:T(8,128)S(1)}, u32[]{:S(2)}, u32[]{:S(2)}) collective-permute-start(f32[8,128]{1,0:T(8,128)S(1)} %get-tuple-element.47.own), channel_id=1, source_target_pairs={{0,3},{1,0},{2,1},{3,2},{4,7},{5,4},{6,5},{7,6},{8,11},{9,8},{10,9... | collective-permute-start | bytes 12296 | tf_op jit(solution)/shard_map/ppermute | solution.py:457
  35.9 5.1 %collective-permute-start.10 = (f32[8,128]{1,0:T(8,128)S(1)}, f32[8,128]{1,0:T(8,128)S(1)}, u32[]{:S(2)}, u32[]{:S(2)}) collective-permute-start(f32[8,128]{1,0:T(8,128)S(1)} %get-tuple-element.47.own), channel_id=1, source_target_pairs={{0,2},{1,3},{2,0},{3,1},{4,6},{5,7},{6,4},{7,5},{8,10},{9,11},{10,... | collective-permute-start | bytes 12296 | tf_op jit(solution)/shard_map/ppermute | solution.py:457
  36.5 4.8 %collective-permute-start.9 = (f32[8,128]{1,0:T(8,128)S(1)}, f32[8,128]{1,0:T(8,128)S(1)}, u32[]{:S(2)}, u32[]{:S(2)}) collective-permute-start(f32[8,128]{1,0:T(8,128)S(1)} %get-tuple-element.47.own), channel_id=1, source_target_pairs={{0,1},{1,2},{2,3},{3,0},{4,5},{5,6},{6,7},{7,4},{8,9},{9,10},{10,1... | collective-permute-start | bytes 12296 | tf_op jit(solution)/shard_map/ppermute | solution.py:457
where the time goes:
time: 43 us; the launch traced here: 42.8 us
  starting transfers between devices  21.4 us (50%)
  waiting for transfers between devices  13.8 us (32%)
  Pallas kernels  5.45 us (13%)
  local copies, waits for them, and re-layouts  2.09 us (5%)
    ppermute x9, starting transfers between devices, around(): return lax.ppermute(value, axis, pairs)  15.4 us
    ppermute x9, waiting for transfers between devices, around(): return lax.ppermute(value, axis, pairs)  12.3 us
    pallas_call x8, Pallas kernels, run(): pl.pallas_call(kernel, out_shape=outs, **windows or whole(outs, args), sc...  5.45 us
    ppermute x1, starting transfers between devices, per_device(): below = lax.ppermute(own_hi, 'gy', [(i, i + 1) for i in range(3)])  4.55 us
    unnamed x8, local copies, waits for them, and re-layouts  2.09 us
    ppermute x1, starting transfers between devices, per_device(): above = lax.ppermute(own_lo, 'gy', [(i + 1, i) for i in range(3)])  1.3 us
    ppermute x1, waiting for transfers between devices, per_device(): other = lax.ppermute(own, 'gx', [(i, i ^ 1) for i in range(32)])  1.23 us
  transfers between devices with their start and end apart: 12, of which 9 were waited for; matrix products, arithmetic and copies ran while one was open for 0% of the time, Pallas kernels for 5%

commit v1 on v0

--- a/solution.py
+++ b/solution.py
@@ -12,24 +12,29 @@
 X_LEVELS, Y_LEVELS = 2, 6
 F32 = jnp.float32
 VMEM = pl.BlockSpec(memory_space=pltpu.VMEM)
+HBM = pl.BlockSpec(memory_space=pltpu.MemorySpace.HBM)
 
 
 def struct(*shape):
     return jax.ShapeDtypeStruct(shape, F32)
 
 
+def scratch(like):
+    return pltpu.VMEM(like.shape, like.dtype)
+
+
 def whole(outs, args):
     return dict(in_specs=[VMEM] * len(args), out_specs=jax.tree.map(lambda _: VMEM, outs))
 
 
-def call(kernel, outs, scratch=(), flops=2_000_000, name=None, **windows):
+def call(kernel, outs, buffers=(), flops=2_000_000, name=None, grant=32 << 20, **windows):
     def run(*args):
         return pl.pallas_call(
             kernel,
             out_shape=outs,
             **(windows or whole(outs, args)),
-            scratch_shapes=list(scratch),
-            compiler_params=pltpu.CompilerParams(vmem_limit_bytes=32 << 20),
+            scratch_shapes=list(buffers),
+            compiler_params=pltpu.CompilerParams(vmem_limit_bytes=grant),
             cost_estimate=pl.CostEstimate(flops=flops, bytes_accessed=1 << 20, transcendentals=0),
             name=name,
         )(*args)
@@ -151,22 +156,58 @@
     return ref[8 * band : 8 * band + 8, 128 * column : 128 * column + 128]
 
 
+def flat_tile(ref, band, column):
+    at = (band * TILES + column) * 8
+    return ref[at : at + 8, :]
+
+
 def row(ref, i):
     return ref[pl.ds((i // 8) * (8 * TILES) + i % 8, TILES, stride=8), :]
 
 
-def edges_kernel(t_lo, k_lo, t_hi, k_hi, lo, hi):
+def edges_kernel(t, k, lo, hi, strips, arrived):
+    sides = (pl.ds(0, 128), pl.ds(128 * (TILES - 1), 128))
+    copies = [
+        pltpu.make_async_copy(ref.at[:, side], strips.at[n], arrived.at[n])
+        for n, (side, ref) in enumerate((side, ref) for side in sides for ref in (t, k))
+    ]
+    for copy in copies:
+        copy.start()
     lo[...] = jnp.zeros_like(lo)
     hi[...] = jnp.zeros_like(hi)
-    lo[0:1, 0:ROWS] = t_lo[...].T[0:1, :]
-    lo[1:2, 0:ROWS] = k_lo[...].T[0:1, :]
-    hi[0:1, 0:ROWS] = t_hi[...].T[127:128, :]
-    hi[1:2, 0:ROWS] = k_hi[...].T[127:128, :]
-
-
-def x_matrix_kernel(t, k, e, along, back, gain, sep, lo, hi, ends, flat):
+    for copy in copies:
+        copy.wait()
+    lo[0:1, 0:ROWS] = strips[0].T[0:1, :]
+    lo[1:2, 0:ROWS] = strips[1].T[0:1, :]
+    hi[0:1, 0:ROWS] = strips[2].T[127:128, :]
+    hi[1:2, 0:ROWS] = strips[3].T[127:128, :]
+
+
+def total(terms):
+    sums = [None] * 4
+    for n, term in enumerate(terms):
+        sums[n % 4] = plus(sums[n % 4], term)
+    return (sums[0] + sums[1]) + (sums[2] + sums[3])
+
+
+def x_matrix_kernel(
+    t_far, k_far, e, along, back, gain, sep, lo, hi, ends, t_flat, flat, t, k, arrived
+):
+    copies = []
+    for band in range(BANDS):
+        at = pl.ds(8 * band, 8)
+        copies.append(
+            [
+                pltpu.make_async_copy(far.at[at, :], near.at[at, :], arrived.at[n, band])
+                for n, (far, near) in enumerate(((t_far, t), (k_far, k)))
+            ]
+        )
+        for copy in copies[-1]:
+            copy.start()
     lane = lax.broadcasted_iota(jnp.int32, (8, 128), 1)
     for band in range(BANDS):
+        for copy in copies[band]:
+            copy.wait()
         ks = [tile(k, band, c) for c in range(TILES)]
         ts = [tile(t, band, c) for c in range(TILES)]
         k_left = [pltpu.roll(v, 127, 1) for v in ks]
@@ -175,6 +216,7 @@
         for c in range(TILES):
             at = pl.ds((band * TILES + c) * 8, 8)
             flat[at, :] = ks[c]
+            t_flat[at, :] = ts[c]
             n = min(c + 1, TILES - 1)
             k_next = jnp.where(lane == 127, k_left[n], k_left[c])
             t_next = jnp.where(lane == 127, t_left[n], t_left[c])
@@ -212,22 +254,37 @@
     args = (ROWS, X_LEVELS, x_shift, along, back, gain, sep)
     solve(at_start, *args, lo, to(lo))
     solve(at_end, *args, hi, to(hi))
-    ends[0] = lo[0]
-    ends[1] = lo[ROWS - 1]
-    ends[2] = hi[ROWS - 1]
-    ends[3] = row(flat, 0)
-    ends[4] = row(flat, ROWS - 1)
-
-
-def x_source_kernel(
-    e, along, back, gain, sep, ends, own_lo, own_hi, below, above, u, port, flat, side
-):
+    ends[0] = total(lo[i] * row(e, i) for i in range(ROWS))
+    ends[1] = total(hi[i] * row(e, i) for i in range(ROWS))
+    ends[2] = lo[0]
+    ends[3] = lo[ROWS - 1]
+    ends[4] = hi[ROWS - 1]
+    ends[5] = row(flat, 0)
+    ends[6] = row(flat, ROWS - 1)
+
+
+def x_port_kernel(ends, lo, hi, own_lo, own_hi, below, above, port, edge, side):
+    at = lax.axis_index("gy")
     side[...] = jnp.zeros_like(side)
     t_lo, k_lo = own_lo[0:1, :], own_lo[1:2, :]
     t_hi, k_hi = own_hi[0:1, :], own_hi[1:2, :]
-    side[0:1, :] = -8000.0 * (k_lo + below[1:2, :]) * (t_lo - below[0:1, :])
-    side[127:128, :] = 8000.0 * (k_hi + above[1:2, :]) * (above[0:1, :] - t_hi)
-    edge = side[...].T
+    before = jnp.where(at == 0, 0.0, below[...])
+    after = jnp.where(at == lax.axis_size("gy") - 1, 0.0, above[...])
+    side[0:1, :] = -8000.0 * (k_lo + before[1:2, :]) * (t_lo - before[0:1, :])
+    side[127:128, :] = 8000.0 * (k_hi + after[1:2, :]) * (after[0:1, :] - t_hi)
+    edge[...] = side[...].T[0:ROWS, :]
+    lane = lax.broadcasted_iota(jnp.int32, (1, 128), 1)
+    for n, response in enumerate((lo, hi)):
+        port[n] = ends[n]
+        for column, kept in ((0, 0), (TILES - 1, 127)):
+            term = edge[...] * response[:, column, :]
+            term = jnp.where(lane == kept, jnp.sum(term, axis=0, keepdims=True), 0.0)
+            port[n, column : column + 1, :] = port[n, column : column + 1, :] + term
+    for n in range(2, 7):
+        port[n] = ends[n]
+
+
+def x_solve_kernel(e, along, back, gain, sep, edge, u, flat):
     lane = lax.broadcasted_iota(jnp.int32, (8, 128), 1)
     flat[...] = e[...]
     for band in range(BANDS):
@@ -244,10 +301,6 @@
         return row(flat, l)
 
     solve(source, ROWS, X_LEVELS, x_shift, along, back, gain, sep, u, store)
-    port[0] = u[0]
-    port[1] = u[ROWS - 1]
-    for n in range(5):
-        port[2 + n] = ends[n]
 
 
 def take(ref):
@@ -340,8 +393,24 @@
     return ref[pl.ds(l, 8, stride=128), :]
 
 
-def y_matrix_kernel(k, along, back, gain, sep, lo, hi, ends, turned):
-    to_runs(lambda band, column: tile(k, band, column), turned)
+def from_runs(turned, store):
+    for p in range(TILES // 2):
+        block = turned[128 * p : 128 * p + 128, :].T
+        for half in range(2):
+            for band in range(BANDS):
+                at = ROWS * half + 8 * band
+                store(band, 2 * p + half, block[at : at + 8, :])
+
+
+def put(ref):
+    def store(band, column, value):
+        ref[8 * band : 8 * band + 8, 128 * column : 128 * column + 128] = value
+
+    return store
+
+
+def y_matrix_kernel(k, along, back, gain, sep, lo, hi, flat_lo, flat_hi, ends, turned):
+    to_runs(lambda band, column: flat_tile(k, band, column), turned)
     lane = lax.broadcasted_iota(jnp.int32, (8, 128), 1)
     sublane = lax.broadcasted_iota(jnp.int32, (8, 128), 0)
     very_last = (lane >= 64) & (sublane == 7)
@@ -377,11 +446,15 @@
     ends[2:3, :] = pltpu.roll(hi[last], 64, 1)[7:8, :]
     ends[3:4, :] = cell(turned, 0)[0:1, :]
     ends[4:5, :] = pltpu.roll(cell(turned, last), 64, 1)[7:8, :]
-
-
-def y_source_kernel(
+    for response, flat in ((lo, flat_lo), (hi, flat_hi)):
+        for l in range(Y_STEPS):
+            turned[pl.ds(l, 8, stride=128), :] = response[l]
+        from_runs(turned, put(flat))
+
+
+def y_port_kernel(
     own_y, y1, y2, y3, own_z, z1, z2, z3, own, other, u, x_lo, x_hi, t,
-    along, back, gain, sep, ends, d, port, table_y, table_z, flat, turned,
+    lo_y, hi_y, ends, turned, port, table_y, table_z, flat,
 ):
     index = lax.axis_index("gx")
     core, z, y = lax.rem(index, 2), lax.rem(lax.div(index, 2), 4), lax.div(index, 8)
@@ -400,25 +473,35 @@
         flat[at, :] = u[i] - f_lo * x_lo[i] + f_hi * x_hi[i]
 
     def block(band, column):
-        at = (band * TILES + column) * 8
-        return flat[at : at + 8, :] - 2.0 * tile(t, band, column)
+        return flat_tile(flat, band, column) - 2.0 * flat_tile(t, band, column)
 
     to_runs(block, turned)
-
+    port[...] = jnp.zeros_like(port)
+    for n, response in enumerate((lo_y, hi_y)):
+        both = total(response[l] * cell(turned, l) for l in range(Y_STEPS))
+        both = jnp.sum(both + pltpu.roll(both, 64, 1), axis=0, keepdims=True)
+        port[n : n + 1, :] = both
+    port[2:7, :] = ends[0:5, :]
+
+
+def y_solve_kernel(turned, along, back, gain, sep, t, out, d, again):
     def store(l, value):
         d[l] = value
+        again[pl.ds(l, 8, stride=128), :] = value
 
     def source(l):
         return cell(turned, l)
 
     solve(source, Y_STEPS, Y_LEVELS, y_shift, along, back, gain, sep, d, store)
-    port[...] = jnp.zeros_like(port)
-    port[0:1, :] = d[0, 0:1, :]
-    port[1:2, :] = pltpu.roll(d[Y_STEPS - 1], 64, 1)[7:8, :]
-    port[2:7, :] = ends[0:5, :]
-
-
-def finish_kernel(own, r1, r2, r3, d, y_lo, y_hi, t, out, table, turned):
+    keep = put(out)
+
+    def plus_start(band, column, value):
+        keep(band, column, value + flat_tile(t, band, column))
+
+    from_runs(again, plus_start)
+
+
+def finish_kernel(own, r1, r2, r3, base, y_lo, y_hi, out, table, side, done, sent):
     index = lax.axis_index("gy")
     place(index, own, (r1, r2, r3), table)
     lane = lax.broadcasted_iota(jnp.int32, (1, 128), 1)
@@ -430,23 +513,25 @@
     scale = 4000.0
     lo, hi = reach(index, [port_of(table.at[j]) for j in range(4)], nothing, nothing, scale)
     f_lo, f_hi = flows(port_of(own), lo, hi, scale)
-
-    def doubled(f):
-        f = jnp.broadcast_to(jnp.where(lane < ROWS, f, 0.0), (8, 128))
-        return f + pltpu.roll(f, 64, 1)
-
-    f_lo, f_hi = doubled(f_lo), doubled(f_hi)
-    for l in range(Y_STEPS):
-        turned[pl.ds(l, 8, stride=128), :] = d[l] - f_lo * y_lo[l] + f_hi * y_hi[l]
-    for p in range(TILES // 2):
-        block = turned[128 * p : 128 * p + 128, :].T
-        for half in range(2):
-            column = 2 * p + half
-            for band in range(BANDS):
-                at = 64 * half + 8 * band
-                out[8 * band : 8 * band + 8, 128 * column : 128 * column + 128] = (
-                    tile(t, band, column) + block[at : at + 8, :]
-                )
+    side[...] = jnp.zeros_like(side)
+    side[0:1, :] = f_lo
+    side[1:2, :] = f_hi
+    upright = side[...].T
+    copies = []
+    for band in range(BANDS):
+        at = slice(8 * band, 8 * band + 8)
+        down = jnp.broadcast_to(upright[at, 0:1], (8, 128))
+        up = jnp.broadcast_to(upright[at, 1:2], (8, 128))
+        keep = put(done)
+        for column in range(TILES):
+            part = tile(base, band, column)
+            part = part - down * tile(y_lo, band, column) + up * tile(y_hi, band, column)
+            keep(band, column, part)
+        copy = pltpu.make_async_copy(done.at[at, :], out.at[at, :], sent.at[band])
+        copy.start()
+        copies.append(copy)
+    for copy in copies:
+        copy.wait()
 
 
 def around(value, axis, size, stride, step):
@@ -459,48 +544,55 @@
 
 def per_device(initial_heat_state, thermal_coefficient):
     t, k = initial_heat_state[0], thermal_coefficient[0]
-    first = pl.BlockSpec((ROWS, 128), lambda n: (0, 0))
-    last = pl.BlockSpec((ROWS, 128), lambda n: (0, TILES - 1))
     own_lo, own_hi = call(
         edges_kernel,
         [struct(8, 128)] * 2,
+        [pltpu.VMEM((4, ROWS, 128), F32), pltpu.SemaphoreType.DMA((4,))],
         name="edges",
-        grid=(1,),
-        in_specs=[first, first, last, last],
-        out_specs=[pl.BlockSpec((8, 128), lambda n: (0, 0))] * 2,
-    )(t, k, t, k)
-    below = lax.ppermute(own_hi, "gy", [(i, i + 1) for i in range(3)])
-    above = lax.ppermute(own_lo, "gy", [(i + 1, i) for i in range(3)])
-    flat = pltpu.VMEM((BANDS * TILES * 8, 128), F32)
-    runs = pltpu.VMEM((TILES // 2 * 128, 128), F32)
-    x_field, y_field = struct(ROWS, TILES, 128), struct(Y_STEPS, 8, 128)
-    e, *x_coefficients, x_lo, x_hi, x_ends = call(
+        grant=56 << 20,
+        in_specs=[HBM, HBM],
+        out_specs=[VMEM, VMEM],
+    )(t, k)
+    below = around(own_hi, "gy", 4, 1, 1)
+    above = around(own_lo, "gy", 4, 1, 3)
+    flat = struct(BANDS * TILES * 8, 128)
+    runs = struct(TILES // 2 * 128, 128)
+    x_field, y_field, natural = struct(ROWS, TILES, 128), struct(Y_STEPS, 8, 128), struct(ROWS, COLS)
+    x_port = struct(7, TILES, 128)
+    e, *x_coefficients, x_lo, x_hi, x_ends, t_flat, k_flat = call(
         x_matrix_kernel,
         [
-            struct(BANDS * TILES * 8, 128),
+            flat,
             x_field,
             x_field,
             x_field,
             struct((2 * X_LEVELS + 1) * SEGMENTS, TILES, 128),
             x_field,
             x_field,
-            struct(5, TILES, 128),
+            x_port,
+            flat,
+            flat,
         ],
-        [flat],
+        [scratch(natural), scratch(natural), pltpu.SemaphoreType.DMA((2, BANDS))],
         name="x_matrix",
+        in_specs=[HBM, HBM],
+        out_specs=[VMEM] * 10,
     )(t, k)
-    x_port = struct(7, TILES, 128)
-    u, own = call(
-        x_source_kernel,
-        [x_field, x_port],
-        [flat, pltpu.VMEM((128, 128), F32)],
-        name="x_source",
-    )(e, *x_coefficients, x_ends, own_lo, own_hi, below, above)
+    own, edge = call(
+        x_port_kernel,
+        [x_port, struct(ROWS, 128)],
+        [pltpu.VMEM((128, 128), F32)],
+        flops=200_000,
+        name="x_port",
+    )(x_ends, x_lo, x_hi, own_lo, own_hi, below, above)
+    u = call(x_solve_kernel, x_field, [scratch(flat)], flops=700_000, name="x_solve")(
+        e, *x_coefficients, edge
+    )
     other = lax.ppermute(own, "gx", [(i, i ^ 1) for i in range(32)])
     own_z = call(pair_kernel, x_port, name="pair")(own, other)
-    k_y, own_z = lax.optimization_barrier((k, own_z))
+    k_y, own_z = lax.optimization_barrier((k_flat, own_z))
     from_z = [around(own_z, "gx", 32, 2, s) for s in (1, 2, 3)]
-    *y_coefficients, y_lo, y_hi, y_ends = call(
+    *y_coefficients, y_lo, y_hi, flat_lo, flat_hi, y_ends = call(
         y_matrix_kernel,
         [
             y_field,
@@ -509,27 +601,36 @@
             struct((2 * Y_LEVELS + 1) * SEGMENTS, 8, 128),
             y_field,
             y_field,
+            natural,
+            natural,
             struct(8, 128),
         ],
-        [runs],
+        [scratch(runs)],
         name="y_matrix",
     )(k_y)
     table = pltpu.VMEM((4, 7, TILES, 128), F32)
     own_y = call(four_kernel, x_port, [table], name="four")(own_z, *from_z)
     from_y = [around(own_y, "gx", 32, 8, s) for s in (1, 2, 3)]
-    d, port = call(
-        y_source_kernel,
-        [y_field, struct(8, 128)],
-        [table, table, flat, runs],
-        name="y_source",
-    )(own_y, *from_y, own_z, *from_z, own, other, u, x_lo, x_hi, t, *y_coefficients, y_ends)
+    turned, port = call(
+        y_port_kernel, [runs, struct(8, 128)], [table, table, scratch(flat)], name="y_port"
+    )(own_y, *from_y, own_z, *from_z, own, other, u, x_lo, x_hi, t_flat, y_lo, y_hi, y_ends)
     from_gy = [around(port, "gy", 4, 1, s) for s in (1, 2, 3)]
+    base = call(
+        y_solve_kernel, natural, [scratch(y_field), scratch(runs)], name="y_solve"
+    )(turned, *y_coefficients, t_flat)
     updated = call(
         finish_kernel,
-        struct(ROWS, COLS),
-        [pltpu.VMEM((4, 8, 128), F32), runs],
+        natural,
+        [
+            pltpu.VMEM((4, 8, 128), F32),
+            pltpu.VMEM((128, 128), F32),
+            scratch(natural),
+            pltpu.SemaphoreType.DMA((BANDS,)),
+        ],
         name="finish",
-    )(port, *from_gy, d, y_lo, y_hi, t)
+        in_specs=[VMEM] * 7,
+        out_specs=HBM,
+    )(port, *from_gy, base, flat_lo, flat_hi)
     return updated[None]
 
 

time: 43 us -> 40.3 us (0.937)
  Pallas kernels: 5.45 us -> 10.9 us
  starting transfers between devices: 21.4 us -> 16.3 us
  local copies, waits for them, and re-layouts: 2.09 us -> 0.02 us
  waiting for transfers between devices: 13.8 us -> 12.9 us
    ppermute x2 -> x0, starting transfers between devices: 5.85 us -> none  [the longest x1 4.55 us: per_device(): below = lax.ppermute(own_hi, 'gy', [(i, i + 1) for i in range(3)])]
    pallas_call x8 -> x10, Pallas kernels: 5.45 us -> 10.9 us  [run(): pl.pallas_call(kernel, out_shape=outs, **windows or whole(outs, args), sc...]
    unnamed x8, local copies, waits for them, and re-layouts: 2.09 us -> 0.02 us
    ppermute x9 -> x11, starting transfers between devices: 15.4 us -> 16.2 us  [around(): return lax.ppermute(value, axis, pairs)]
    ppermute x9 -> x11, waiting for transfers between devices: 12.3 us -> 11.7 us  [around(): return lax.ppermute(value, axis, pairs)]
  transfers between devices with their start and end apart: 12 -> 12, of which waited for: 9 -> 8; matrix products, arithmetic and copies ran while one was open for 0% -> 0% of each run, Pallas kernels for 5% -> 17%
where the time goes in v1:
time: 40.3 us; the launch traced here: 40.2 us
  starting transfers between devices  16.3 us (40%)
  waiting for transfers between devices  12.9 us (32%)
  Pallas kernels  10.9 us (27%)
    ppermute x11, starting transfers between devices, around(): return lax.ppermute(value, axis, pairs)  16.2 us
    ppermute x11, waiting for transfers between devices, around(): return lax.ppermute(value, axis, pairs)  11.7 us
    pallas_call x10, Pallas kernels, run(): pl.pallas_call(kernel, out_shape=outs, **windows or whole(outs, args), sc...  10.9 us
    ppermute x1, waiting for transfers between devices, per_device(): other = lax.ppermute(own, 'gx', [(i, i ^ 1) for i in range(32)])  1.23 us
  transfers between devices with their start and end apart: 12, of which 8 were waited for; matrix products, arithmetic and copies ran while one was open for 0% of the time, Pallas kernels for 17%

profile of v1, /device:TPU:0, one launch (start us, length us, event | category | flops | bytes accessed | tf_op | source)
XLA Modules:
  0.0 40.2 jit_solution(17431224107031392611)
XLA Ops:
  0.0 0.0 copy-start
  0.0 0.0 copy-start.1
  0.0 1.6 %edges.1 = (f32[8,128]{1,0:T(8,128)}, f32[8,128]{1,0:T(8,128)}) custom-call(f32[64,2048]{1,0:T(8,128)} %bitcast.3, f32[64,2048]{1,0:T(8,128)} %bitcast.5), custom_call_target="tpu_custom_call" | custom-call | flops 2000000 | bytes 1048576 | tf_op jit(solution)/shard_map/edges/pallas_call | solution.py:32
  1.6 2.9 %collective-permute-start.1 = (f32[8,128]{1,0:T(8,128)}, f32[8,128]{1,0:T(8,128)S(1)}, u32[]{:S(2)}, u32[]{:S(2)}) collective-permute-start(f32[8,128]{1,0:T(8,128)} %get-tuple-element.36.own_lo), channel_id=1, source_target_pairs={{0,3},{1,0},{2,1},{3,2},{4,7},{5,4},{6,5},{7,6},{8,11},{9,8},{10,9... | collective-permute-start | bytes 12296 | tf_op jit(solution)/shard_map/ppermute | solution.py:542
  4.6 0.0 collective-permute-start
  4.6 0.0 copy-done
  4.6 0.0 copy-done.1
  4.6 0.0 copy-start.3
  4.6 3.4 %x_matrix.1 = (f32[1024,128]{1,0:T(8,128)S(1)}, f32[64,16,128]{2,1,0:T(8,128)S(1)}, f32[64,16,128]{2,1,0:T(8,128)S(1)}, f32[64,16,128]{2,1,0:T(8,128)S(1)}, f32[...) custom-call(f32[64,2048]{1,0:T(8,128)S(1)} %bitcast.4, ...), custom_call_target="tpu_custom_call" | custom-call | flops 2000000 | bytes 1048576 | tf_op jit(solution)/shard_map/x_matrix/pallas_call | solution.py:32
  8.0 0.0 copy-start.2
  8.0 0.0 collective-permute-done.1.above
  8.0 1.6 %collective-permute-done.below = f32[8,128]{1,0:T(8,128)S(1)} collective-permute-done((f32[8,128]{1,0:T(8,128)}, f32[8,128]{1,0:T(8,128)S(1)}, u32[]{:S(2)}, u32[]{:S(2)}) %collective-permute-start) | collective-permute-done | bytes 4128 | tf_op jit(solution)/shard_map/ppermute | solution.py:542
  9.6 0.0 copy-done.3
  9.6 0.0 copy-done.2
  9.6 0.1 x_port.1
  9.7 0.1 collective-permute-start.2
  9.8 1.2 %collective-permute-done.2.other = f32[7,16,128]{2,1,0:T(8,128)S(1)} collective-permute-done((f32[7,16,128]{2,1,0:T(8,128)S(1)}, f32[7,16,128]{2,1,0:T(8,128)S(1)}, u32[]{:S(2)}, u32[]{:S(2)}) %collective-permute-start.2) | collective-permute-done | bytes 57376 | tf_op jit(solution)/shard_map/ppermute | solution.py:591
  11.1 4.1 %collective-permute-start.5 = (f32[7,16,128]{2,1,0:T(8,128)S(1)}, f32[7,16,128]{2,1,0:T(8,128)S(1)}, u32[]{:S(2)}, u32[]{:S(2)}) collective-permute-start(f32[7,16,128]{2,1,0:T(8,128)S(1)} %pair.1.own.own_z), channel_id=1, source_target_pairs={{0,24},{4,28},{8,0},{12,4},{16,8},{20,12},{24,16},{28,20},{32,56},... | collective-permute-start | bytes 172040 | tf_op jit(solution)/shard_map/ppermute | solution.py:542
  15.2 0.0 collective-permute-start.4
  15.2 1.3 %collective-permute-start.3 = (f32[7,16,128]{2,1,0:T(8,128)S(1)}, f32[7,16,128]{2,1,0:T(8,128)S(1)}, u32[]{:S(2)}, u32[]{:S(2)}) collective-permute-start(f32[7,16,128]{2,1,0:T(8,128)S(1)} %pair.1.own.own_z), channel_id=1, source_target_pairs={{0,8},{4,12},{8,16},{12,20},{16,24},{20,28},{24,0},{28,4},{32,40},... | collective-permute-start | bytes 172040 | tf_op jit(solution)/shard_map/ppermute | solution.py:542
  16.4 1.5 %collective-permute-done.5.r3.z3 = f32[7,16,128]{2,1,0:T(8,128)S(1)} collective-permute-done((f32[7,16,128]{2,1,0:T(8,128)S(1)}, f32[7,16,128]{2,1,0:T(8,128)S(1)}, u32[]{:S(2)}, u32[]{:S(2)}) %collective-permute-start.5) | collective-permute-done | bytes 57376 | tf_op jit(solution)/shard_map/ppermute | solution.py:542
  17.9 3.1 %collective-permute-done.4.r2.z2 = f32[7,16,128]{2,1,0:T(8,128)S(1)} collective-permute-done((f32[7,16,128]{2,1,0:T(8,128)S(1)}, f32[7,16,128]{2,1,0:T(8,128)S(1)}, u32[]{:S(2)}, u32[]{:S(2)}) %collective-permute-start.4) | collective-permute-done | bytes 57376 | tf_op jit(solution)/shard_map/ppermute | solution.py:542
  21.0 0.3 collective-permute-done.3.r1.z1
  21.3 0.1 four.1.own_y
  21.4 3.1 %collective-permute-start.8 = (f32[7,16,128]{2,1,0:T(8,128)S(1)}, f32[7,16,128]{2,1,0:T(8,128)S(1)}, u32[]{:S(2)}, u32[]{:S(2)}) collective-permute-start(f32[7,16,128]{2,1,0:T(8,128)S(1)} %four.1.own_y), channel_id=1, source_target_pairs={{0,96},{4,100},{8,104},{12,108},{16,112},{20,116},{24,120},{28,124... | collective-permute-start | bytes 172040 | tf_op jit(solution)/shard_map/ppermute | solution.py:542
  24.5 0.6 %collective-permute-start.7 = (f32[7,16,128]{2,1,0:T(8,128)S(1)}, f32[7,16,128]{2,1,0:T(8,128)S(1)}, u32[]{:S(2)}, u32[]{:S(2)}) collective-permute-start(f32[7,16,128]{2,1,0:T(8,128)S(1)} %four.1.own_y), channel_id=1, source_target_pairs={{0,64},{4,68},{8,72},{12,76},{16,80},{20,84},{24,88},{28,92},{32,9... | collective-permute-start | bytes 172040 | tf_op jit(solution)/shard_map/ppermute | solution.py:542
  25.1 1.0 %collective-permute-start.6 = (f32[7,16,128]{2,1,0:T(8,128)S(1)}, f32[7,16,128]{2,1,0:T(8,128)S(1)}, u32[]{:S(2)}, u32[]{:S(2)}) collective-permute-start(f32[7,16,128]{2,1,0:T(8,128)S(1)} %four.1.own_y), channel_id=1, source_target_pairs={{0,32},{4,36},{8,40},{12,44},{16,48},{20,52},{24,56},{28,60},{32,6... | collective-permute-start | bytes 172040 | tf_op jit(solution)/shard_map/ppermute | solution.py:542
  26.1 0.3 x_solve.1.u
  26.4 2.0 %y_matrix.1 = (f32[128,8,128]{2,1,0:T(8,128)S(1)}, f32[128,8,128]{2,1,0:T(8,128)S(1)}, f32[128,8,128]{2,1,0:T(8,128)S(1)}, f32[52,8,128]{2,1,0:T(8,128)S(1)}, f3...) custom-call(f32[1024,128]{1,0:T(8,128)S(1)} %get-tuple-element.47.k), custom_call_target="tpu_custom_call" | custom-call | flops 2000000 | bytes 1048576 | tf_op jit(solution)/shard_map/y_matrix/pallas_call | solution.py:32
  28.4 0.0 collective-permute-done.8.y3
  28.4 1.8 %collective-permute-done.7.y2 = f32[7,16,128]{2,1,0:T(8,128)S(1)} collective-permute-done((f32[7,16,128]{2,1,0:T(8,128)S(1)}, f32[7,16,128]{2,1,0:T(8,128)S(1)}, u32[]{:S(2)}, u32[]{:S(2)}) %collective-permute-start.7) | collective-permute-done | bytes 57376 | tf_op jit(solution)/shard_map/ppermute | solution.py:542
  30.2 0.6 %collective-permute-done.6.y1 = f32[7,16,128]{2,1,0:T(8,128)S(1)} collective-permute-done((f32[7,16,128]{2,1,0:T(8,128)S(1)}, f32[7,16,128]{2,1,0:T(8,128)S(1)}, u32[]{:S(2)}, u32[]{:S(2)}) %collective-permute-start.6) | collective-permute-done | bytes 57376 | tf_op jit(solution)/shard_map/ppermute | solution.py:542
  30.7 1.0 %y_port.1 = (f32[1024,128]{1,0:T(8,128)S(1)}, f32[8,128]{1,0:T(8,128)S(1)}) custom-call(f32[7,16,128]{2,1,0:T(8,128)S(1)} %four.1.own_y, f32[7,16,128]{2,1,0:T(8,128)S(1)} %collective-permute-done.6.y1, f32[7,16,128]{2,1,0:T(8,128)S(1)} %collective-permute-done.7.y2, f32[7,16,128]{2,1,0:T(8,128)S(1)} %collective-permute-done.8.y3, ...), custom_call_target="tpu_custom_call" | custom-call | flops 2000000 | bytes 1048576 | tf_op jit(solution)/shard_map/y_port/pallas_call | solution.py:32
  31.7 2.3 %collective-permute-start.11 = (f32[8,128]{1,0:T(8,128)S(1)}, f32[8,128]{1,0:T(8,128)S(1)}, u32[]{:S(2)}, u32[]{:S(2)}) collective-permute-start(f32[8,128]{1,0:T(8,128)S(1)} %get-tuple-element.51.own), channel_id=1, source_target_pairs={{0,3},{1,0},{2,1},{3,2},{4,7},{5,4},{6,5},{7,6},{8,11},{9,8},{10,9... | collective-permute-start | bytes 12296 | tf_op jit(solution)/shard_map/ppermute | solution.py:542
  34.0 0.0 collective-permute-start.10
  34.0 0.9 %collective-permute-start.9 = (f32[8,128]{1,0:T(8,128)S(1)}, f32[8,128]{1,0:T(8,128)S(1)}, u32[]{:S(2)}, u32[]{:S(2)}) collective-permute-start(f32[8,128]{1,0:T(8,128)S(1)} %get-tuple-element.51.own), channel_id=1, source_target_pairs={{0,1},{1,2},{2,3},{3,0},{4,5},{5,6},{6,7},{7,4},{8,9},{9,10},{10,1... | collective-permute-start | bytes 12296 | tf_op jit(solution)/shard_map/ppermute | solution.py:542
  35.0 1.3 %y_solve.1.base = f32[64,2048]{1,0:T(8,128)S(1)} custom-call(f32[1024,128]{1,0:T(8,128)S(1)} %get-tuple-element.52.turned, f32[128,8,128]{2,1,0:T(8,128)S(1)} %get-tuple-element.53.along, f32[128,8,128]{2,1,0:T(8,128)S(1)} %get-tuple-element.54.back, f32[128,8,128]{2,1,0:T(8,128)S(1)} %get-tuple-element.55.gain, f32[52,8,128]{2,1,0:T(8,128)S(1)} %get-tuple-element.56.sep, ...), custom_call_target="tpu_custom_call" | custom-call | flops 2000000 | bytes 1048576 | tf_op jit(solution)/shard_map/y_solve/pallas_call | solution.py:32
  36.3 0.0 collective-permute-done.11.r3
  36.3 2.9 %collective-permute-done.10.r2 = f32[8,128]{1,0:T(8,128)S(1)} collective-permute-done((f32[8,128]{1,0:T(8,128)S(1)}, f32[8,128]{1,0:T(8,128)S(1)}, u32[]{:S(2)}, u32[]{:S(2)}) %collective-permute-start.10) | collective-permute-done | bytes 4128 | tf_op jit(solution)/shard_map/ppermute | solution.py:542
  39.1 0.0 collective-permute-done.9.r1
  39.1 1.1 %finish.1 = f32[64,2048]{1,0:T(8,128)} custom-call(f32[8,128]{1,0:T(8,128)S(1)} %get-tuple-element.51.own, f32[8,128]{1,0:T(8,128)S(1)} %collective-permute-done.9.r1, f32[8,128]{1,0:T(8,128)S(1)} %collective-permute-done.10.r2, f32[8,128]{1,0:T(8,128)S(1)} %collective-permute-done.11.r3, f32[64,2048]{1,0:T(8,128)S(1)} %y_solve.1.base, ...), custom_call_target="tpu_custom_call" | custom-call | flops 2000000 | bytes 1048576 | tf_op jit(solution)/shard_map/finish/pallas_call | solution.py:32
  (1 shorter events, 0.0 us)
Async XLA Ops:
  0.0 4.6 %copy-start = (f32[1,64,2048]{2,1,0:T(8,128)S(1)}, f32[1,64,2048]{2,1,0:T(8,128)}, u32[]{:S(2)}) copy-start(f32[1,64,2048]{2,1,0:T(8,128)} %param.2) | copy-start | bytes 1572868
  0.0 4.6 %copy-start.1 = (f32[1,64,2048]{2,1,0:T(8,128)S(1)}, f32[1,64,2048]{2,1,0:T(8,128)}, u32[]{:S(2)}) copy-start(f32[1,64,2048]{2,1,0:T(8,128)} %param.3) | copy-start | bytes 1572868
  1.6 6.4 %collective-permute-start.1 = (f32[8,128]{1,0:T(8,128)}, f32[8,128]{1,0:T(8,128)S(1)}, u32[]{:S(2)}, u32[]{:S(2)}) collective-permute-start(f32[8,128]{1,0:T(8,128)} %get-tuple-element.36.own_lo), channel_id=1, source_target_pairs={{0,3},{1,0},{2,1},{3,2},{4,7},{5,4},{6,5},{7,6},{8,11},{9,8},{10,9... | collective-permute-start | bytes 12296 | tf_op jit(solution)/shard_map/ppermute | solution.py:542
  4.6 5.0 %collective-permute-start = (f32[8,128]{1,0:T(8,128)}, f32[8,128]{1,0:T(8,128)S(1)}, u32[]{:S(2)}, u32[]{:S(2)}) collective-permute-start(f32[8,128]{1,0:T(8,128)} %get-tuple-element.37.own_hi), channel_id=1, source_target_pairs={{0,1},{1,2},{2,3},{3,0},{4,5},{5,6},{6,7},{7,4},{8,9},{9,10},{10,1... | collective-permute-start | bytes 12296 | tf_op jit(solution)/shard_map/ppermute | solution.py:542
  4.6 5.0 %copy-start.3 = (f32[8,128]{1,0:T(8,128)S(1)}, f32[8,128]{1,0:T(8,128)}, u32[]{:S(2)}) copy-start(f32[8,128]{1,0:T(8,128)} %get-tuple-element.37.own_hi) | copy-start | bytes 12292
  8.0 1.6 %copy-start.2 = (f32[8,128]{1,0:T(8,128)S(1)}, f32[8,128]{1,0:T(8,128)}, u32[]{:S(2)}) copy-start(f32[8,128]{1,0:T(8,128)} %get-tuple-element.36.own_lo) | copy-start | bytes 12292
  9.7 1.3 %collective-permute-start.2 = (f32[7,16,128]{2,1,0:T(8,128)S(1)}, f32[7,16,128]{2,1,0:T(8,128)S(1)}, u32[]{:S(2)}, u32[]{:S(2)}) collective-permute-start(f32[7,16,128]{2,1,0:T(8,128)S(1)} %get-tuple-element.38.own), channel_id=1, source_target_pairs={{0,4},{4,0},{8,12},{12,8},{16,20},{20,16},{24,28},{28,24},{32,36},... | collective-permute-start | bytes 172040 | tf_op jit(solution)/shard_map/ppermute | solution.py:591
  11.1 6.9 %collective-permute-start.5 = (f32[7,16,128]{2,1,0:T(8,128)S(1)}, f32[7,16,128]{2,1,0:T(8,128)S(1)}, u32[]{:S(2)}, u32[]{:S(2)}) collective-permute-start(f32[7,16,128]{2,1,0:T(8,128)S(1)} %pair.1.own.own_z), channel_id=1, source_target_pairs={{0,24},{4,28},{8,0},{12,4},{16,8},{20,12},{24,16},{28,20},{32,56},... | collective-permute-start | bytes 172040 | tf_op jit(solution)/shard_map/ppermute | solution.py:542
  15.2 5.9 %collective-permute-start.4 = (f32[7,16,128]{2,1,0:T(8,128)S(1)}, f32[7,16,128]{2,1,0:T(8,128)S(1)}, u32[]{:S(2)}, u32[]{:S(2)}) collective-permute-start(f32[7,16,128]{2,1,0:T(8,128)S(1)} %pair.1.own.own_z), channel_id=1, source_target_pairs={{0,16},{4,20},{8,24},{12,28},{16,0},{20,4},{24,8},{28,12},{32,48},... | collective-permute-start | bytes 172040 | tf_op jit(solution)/shard_map/ppermute | solution.py:542
  15.2 6.1 %collective-permute-start.3 = (f32[7,16,128]{2,1,0:T(8,128)S(1)}, f32[7,16,128]{2,1,0:T(8,128)S(1)}, u32[]{:S(2)}, u32[]{:S(2)}) collective-permute-start(f32[7,16,128]{2,1,0:T(8,128)S(1)} %pair.1.own.own_z), channel_id=1, source_target_pairs={{0,8},{4,12},{8,16},{12,20},{16,24},{20,28},{24,0},{28,4},{32,40},... | collective-permute-start | bytes 172040 | tf_op jit(solution)/shard_map/ppermute | solution.py:542
  21.4 7.0 %collective-permute-start.8 = (f32[7,16,128]{2,1,0:T(8,128)S(1)}, f32[7,16,128]{2,1,0:T(8,128)S(1)}, u32[]{:S(2)}, u32[]{:S(2)}) collective-permute-start(f32[7,16,128]{2,1,0:T(8,128)S(1)} %four.1.own_y), channel_id=1, source_target_pairs={{0,96},{4,100},{8,104},{12,108},{16,112},{20,116},{24,120},{28,124... | collective-permute-start | bytes 172040 | tf_op jit(solution)/shard_map/ppermute | solution.py:542
  24.5 5.7 %collective-permute-start.7 = (f32[7,16,128]{2,1,0:T(8,128)S(1)}, f32[7,16,128]{2,1,0:T(8,128)S(1)}, u32[]{:S(2)}, u32[]{:S(2)}) collective-permute-start(f32[7,16,128]{2,1,0:T(8,128)S(1)} %four.1.own_y), channel_id=1, source_target_pairs={{0,64},{4,68},{8,72},{12,76},{16,80},{20,84},{24,88},{28,92},{32,9... | collective-permute-start | bytes 172040 | tf_op jit(solution)/shard_map/ppermute | solution.py:542
  25.1 5.7 %collective-permute-start.6 = (f32[7,16,128]{2,1,0:T(8,128)S(1)}, f32[7,16,128]{2,1,0:T(8,128)S(1)}, u32[]{:S(2)}, u32[]{:S(2)}) collective-permute-start(f32[7,16,128]{2,1,0:T(8,128)S(1)} %four.1.own_y), channel_id=1, source_target_pairs={{0,32},{4,36},{8,40},{12,44},{16,48},{20,52},{24,56},{28,60},{32,6... | collective-permute-start | bytes 172040 | tf_op jit(solution)/shard_map/ppermute | solution.py:542
  31.7 4.6 %collective-permute-start.11 = (f32[8,128]{1,0:T(8,128)S(1)}, f32[8,128]{1,0:T(8,128)S(1)}, u32[]{:S(2)}, u32[]{:S(2)}) collective-permute-start(f32[8,128]{1,0:T(8,128)S(1)} %get-tuple-element.51.own), channel_id=1, source_target_pairs={{0,3},{1,0},{2,1},{3,2},{4,7},{5,4},{6,5},{7,6},{8,11},{9,8},{10,9... | collective-permute-start | bytes 12296 | tf_op jit(solution)/shard_map/ppermute | solution.py:542
  34.0 5.1 %collective-permute-start.10 = (f32[8,128]{1,0:T(8,128)S(1)}, f32[8,128]{1,0:T(8,128)S(1)}, u32[]{:S(2)}, u32[]{:S(2)}) collective-permute-start(f32[8,128]{1,0:T(8,128)S(1)} %get-tuple-element.51.own), channel_id=1, source_target_pairs={{0,2},{1,3},{2,0},{3,1},{4,6},{5,7},{6,4},{7,5},{8,10},{9,11},{10,... | collective-permute-start | bytes 12296 | tf_op jit(solution)/shard_map/ppermute | solution.py:542
  34.0 5.1 %collective-permute-start.9 = (f32[8,128]{1,0:T(8,128)S(1)}, f32[8,128]{1,0:T(8,128)S(1)}, u32[]{:S(2)}, u32[]{:S(2)}) collective-permute-start(f32[8,128]{1,0:T(8,128)S(1)} %get-tuple-element.51.own), channel_id=1, source_target_pairs={{0,1},{1,2},{2,3},{3,0},{4,5},{5,6},{6,7},{7,4},{8,9},{9,10},{10,1... | collective-permute-start | bytes 12296 | tf_op jit(solution)/shard_map/ppermute | solution.py:542

commit v2 on v1

--- a/solution.py
+++ b/solution.py
@@ -190,24 +190,14 @@
     return (sums[0] + sums[1]) + (sums[2] + sums[3])
 
 
-def x_matrix_kernel(
-    t_far, k_far, e, along, back, gain, sep, lo, hi, ends, t_flat, flat, t, k, arrived
-):
-    copies = []
-    for band in range(BANDS):
-        at = pl.ds(8 * band, 8)
-        copies.append(
-            [
-                pltpu.make_async_copy(far.at[at, :], near.at[at, :], arrived.at[n, band])
-                for n, (far, near) in enumerate(((t_far, t), (k_far, k)))
-            ]
-        )
-        for copy in copies[-1]:
-            copy.start()
+def x_matrix_kernel(t, k, e, along, back, gain, sep, lo, hi, ends, t_flat, flat, own):
+    own[...] = jnp.zeros_like(own)
+    for n, (ref, column) in enumerate(((t, 0), (k, 0), (t, TILES - 1), (k, TILES - 1))):
+        strip = ref[:, 128 * column : 128 * column + 128].T
+        at = 127 if column else 0
+        own[n : n + 1, 0:ROWS] = strip[at : at + 1, :]
     lane = lax.broadcasted_iota(jnp.int32, (8, 128), 1)
     for band in range(BANDS):
-        for copy in copies[band]:
-            copy.wait()
         ks = [tile(k, band, c) for c in range(TILES)]
         ts = [tile(t, band, c) for c in range(TILES)]
         k_left = [pltpu.roll(v, 127, 1) for v in ks]
@@ -263,11 +253,10 @@
     ends[6] = row(flat, ROWS - 1)
 
 
-def x_port_kernel(ends, lo, hi, own_lo, own_hi, below, above, port, edge, side):
+def x_port_kernel(ends, lo, hi, own, below, above, port, edge, side):
     at = lax.axis_index("gy")
     side[...] = jnp.zeros_like(side)
-    t_lo, k_lo = own_lo[0:1, :], own_lo[1:2, :]
-    t_hi, k_hi = own_hi[0:1, :], own_hi[1:2, :]
+    t_lo, k_lo, t_hi, k_hi = (own[n : n + 1, :] for n in range(4))
     before = jnp.where(at == 0, 0.0, below[...])
     after = jnp.where(at == lax.axis_size("gy") - 1, 0.0, above[...])
     side[0:1, :] = -8000.0 * (k_lo + before[1:2, :]) * (t_lo - before[0:1, :])
@@ -559,7 +548,7 @@
     runs = struct(TILES // 2 * 128, 128)
     x_field, y_field, natural = struct(ROWS, TILES, 128), struct(Y_STEPS, 8, 128), struct(ROWS, COLS)
     x_port = struct(7, TILES, 128)
-    e, *x_coefficients, x_lo, x_hi, x_ends, t_flat, k_flat = call(
+    e, *x_coefficients, x_lo, x_hi, x_ends, t_flat, k_flat, own = call(
         x_matrix_kernel,
         [
             flat,
@@ -572,11 +561,9 @@
             x_port,
             flat,
             flat,
+            struct(8, 128),
         ],
-        [scratch(natural), scratch(natural), pltpu.SemaphoreType.DMA((2, BANDS))],
         name="x_matrix",
-        in_specs=[HBM, HBM],
-        out_specs=[VMEM] * 10,
     )(t, k)
     own, edge = call(
         x_port_kernel,
@@ -584,7 +571,7 @@
         [pltpu.VMEM((128, 128), F32)],
         flops=200_000,
         name="x_port",
-    )(x_ends, x_lo, x_hi, own_lo, own_hi, below, above)
+    )(x_ends, x_lo, x_hi, own, below, above)
     u = call(x_solve_kernel, x_field, [scratch(flat)], flops=700_000, name="x_solve")(
         e, *x_coefficients, edge
     )

time: 40.3 us -> 38.8 us (0.963)
  Pallas kernels: 10.9 us -> 8.56 us
  starting transfers between devices: 16.3 us -> 17.6 us
  waiting for transfers between devices: 12.9 us -> 12.4 us
    pallas_call x10, Pallas kernels: 10.9 us -> 8.56 us  [run(): pl.pallas_call(kernel, out_shape=outs, **windows or whole(outs, args), sc...]
    ppermute x11, starting transfers between devices: 16.2 us -> 17.5 us  [around(): return lax.ppermute(value, axis, pairs)]
    ppermute x11, waiting for transfers between devices: 11.7 us -> 11.2 us  [around(): return lax.ppermute(value, axis, pairs)]
  transfers between devices with their start and end apart: 12 -> 12, of which waited for: 8 -> 10; matrix products, arithmetic and copies ran while one was open for 0% -> 0% of each run, Pallas kernels for 17% -> 12%
where the time goes in v2:
time: 38.8 us; the launch traced here: 38.7 us
  starting transfers between devices  17.6 us (45%)
  waiting for transfers between devices  12.4 us (32%)
  Pallas kernels  8.56 us (22%)
    ppermute x11, starting transfers between devices, around(): return lax.ppermute(value, axis, pairs)  17.5 us
    ppermute x11, waiting for transfers between devices, around(): return lax.ppermute(value, axis, pairs)  11.2 us
    pallas_call x10, Pallas kernels, run(): pl.pallas_call(kernel, out_shape=outs, **windows or whole(outs, args), sc...  8.56 us
    ppermute x1, waiting for transfers between devices, per_device(): other = lax.ppermute(own, 'gx', [(i, i ^ 1) for i in range(32)])  1.23 us
  transfers between devices with their start and end apart: 12, of which 10 were waited for; matrix products, arithmetic and copies ran while one was open for 0% of the time, Pallas kernels for 12%

profile of v2, /device:TPU:0, one launch (start us, length us, event | category | flops | bytes accessed | tf_op | source)
XLA Modules:
  0.0 38.7 jit_solution(8236689852661023141)
XLA Ops:
  0.0 0.0 copy-start
  0.0 0.0 copy-start.1
  0.0 1.6 %edges.1 = (f32[8,128]{1,0:T(8,128)}, f32[8,128]{1,0:T(8,128)}) custom-call(f32[64,2048]{1,0:T(8,128)} %bitcast.3, f32[64,2048]{1,0:T(8,128)} %bitcast.5), custom_call_target="tpu_custom_call" | custom-call | flops 2000000 | bytes 1048576 | tf_op jit(solution)/shard_map/edges/pallas_call | solution.py:32
  1.6 1.6 %collective-permute-start = (f32[8,128]{1,0:T(8,128)}, f32[8,128]{1,0:T(8,128)S(1)}, u32[]{:S(2)}, u32[]{:S(2)}) collective-permute-start(f32[8,128]{1,0:T(8,128)} %get-tuple-element.38), channel_id=1, source_target_pairs={{0,1},{1,2},{2,3},{3,0},{4,5},{5,6},{6,7},{7,4},{8,9},{9,10},{10,1... | collective-permute-start | bytes 12296 | tf_op jit(solution)/shard_map/ppermute | solution.py:531
  3.3 1.7 %collective-permute-start.1 = (f32[8,128]{1,0:T(8,128)}, f32[8,128]{1,0:T(8,128)S(1)}, u32[]{:S(2)}, u32[]{:S(2)}) collective-permute-start(f32[8,128]{1,0:T(8,128)} %get-tuple-element.39), channel_id=1, source_target_pairs={{0,3},{1,0},{2,1},{3,2},{4,7},{5,4},{6,5},{7,6},{8,11},{9,8},{10,9... | collective-permute-start | bytes 12296 | tf_op jit(solution)/shard_map/ppermute | solution.py:531
  5.0 0.0 copy-done
  5.0 0.0 copy-done.1
  5.0 1.1 %x_matrix.1 = (f32[1024,128]{1,0:T(8,128)S(1)}, f32[64,16,128]{2,1,0:T(8,128)S(1)}, f32[64,16,128]{2,1,0:T(8,128)S(1)}, f32[64,16,128]{2,1,0:T(8,128)S(1)}, f32[...) custom-call(f32[64,2048]{1,0:T(8,128)S(1)} %bitcast.4, ...), custom_call_target="tpu_custom_call" | custom-call | flops 2000000 | bytes 1048576 | tf_op jit(solution)/shard_map/x_matrix/pallas_call | solution.py:32
  6.1 0.7 %collective-permute-done.below = f32[8,128]{1,0:T(8,128)S(1)} collective-permute-done((f32[8,128]{1,0:T(8,128)}, f32[8,128]{1,0:T(8,128)S(1)}, u32[]{:S(2)}, u32[]{:S(2)}) %collective-permute-start) | collective-permute-done | bytes 4128 | tf_op jit(solution)/shard_map/ppermute | solution.py:531
  6.7 0.4 collective-permute-done.1.above
  7.1 0.1 x_port.1
  7.2 0.1 collective-permute-start.2
  7.3 1.2 %collective-permute-done.2.other = f32[7,16,128]{2,1,0:T(8,128)S(1)} collective-permute-done((f32[7,16,128]{2,1,0:T(8,128)S(1)}, f32[7,16,128]{2,1,0:T(8,128)S(1)}, u32[]{:S(2)}, u32[]{:S(2)}) %collective-permute-start.2) | collective-permute-done | bytes 57376 | tf_op jit(solution)/shard_map/ppermute | solution.py:578
  8.6 4.1 %collective-permute-start.5 = (f32[7,16,128]{2,1,0:T(8,128)S(1)}, f32[7,16,128]{2,1,0:T(8,128)S(1)}, u32[]{:S(2)}, u32[]{:S(2)}) collective-permute-start(f32[7,16,128]{2,1,0:T(8,128)S(1)} %pair.1.own.own_z), channel_id=1, source_target_pairs={{0,24},{4,28},{8,0},{12,4},{16,8},{20,12},{24,16},{28,20},{32,56},... | collective-permute-start | bytes 172040 | tf_op jit(solution)/shard_map/ppermute | solution.py:531
  12.7 0.0 collective-permute-start.4
  12.7 1.3 %collective-permute-start.3 = (f32[7,16,128]{2,1,0:T(8,128)S(1)}, f32[7,16,128]{2,1,0:T(8,128)S(1)}, u32[]{:S(2)}, u32[]{:S(2)}) collective-permute-start(f32[7,16,128]{2,1,0:T(8,128)S(1)} %pair.1.own.own_z), channel_id=1, source_target_pairs={{0,8},{4,12},{8,16},{12,20},{16,24},{20,28},{24,0},{28,4},{32,40},... | collective-permute-start | bytes 172040 | tf_op jit(solution)/shard_map/ppermute | solution.py:531
  13.9 1.5 %collective-permute-done.5.r3.z3 = f32[7,16,128]{2,1,0:T(8,128)S(1)} collective-permute-done((f32[7,16,128]{2,1,0:T(8,128)S(1)}, f32[7,16,128]{2,1,0:T(8,128)S(1)}, u32[]{:S(2)}, u32[]{:S(2)}) %collective-permute-start.5) | collective-permute-done | bytes 57376 | tf_op jit(solution)/shard_map/ppermute | solution.py:531
  15.4 3.1 %collective-permute-done.4.r2.z2 = f32[7,16,128]{2,1,0:T(8,128)S(1)} collective-permute-done((f32[7,16,128]{2,1,0:T(8,128)S(1)}, f32[7,16,128]{2,1,0:T(8,128)S(1)}, u32[]{:S(2)}, u32[]{:S(2)}) %collective-permute-start.4) | collective-permute-done | bytes 57376 | tf_op jit(solution)/shard_map/ppermute | solution.py:531
  18.5 0.3 collective-permute-done.3.r1.z1
  18.8 0.1 four.1.own_y
  18.9 3.1 %collective-permute-start.8 = (f32[7,16,128]{2,1,0:T(8,128)S(1)}, f32[7,16,128]{2,1,0:T(8,128)S(1)}, u32[]{:S(2)}, u32[]{:S(2)}) collective-permute-start(f32[7,16,128]{2,1,0:T(8,128)S(1)} %four.1.own_y), channel_id=1, source_target_pairs={{0,96},{4,100},{8,104},{12,108},{16,112},{20,116},{24,120},{28,124... | collective-permute-start | bytes 172040 | tf_op jit(solution)/shard_map/ppermute | solution.py:531
  22.0 0.6 %collective-permute-start.7 = (f32[7,16,128]{2,1,0:T(8,128)S(1)}, f32[7,16,128]{2,1,0:T(8,128)S(1)}, u32[]{:S(2)}, u32[]{:S(2)}) collective-permute-start(f32[7,16,128]{2,1,0:T(8,128)S(1)} %four.1.own_y), channel_id=1, source_target_pairs={{0,64},{4,68},{8,72},{12,76},{16,80},{20,84},{24,88},{28,92},{32,9... | collective-permute-start | bytes 172040 | tf_op jit(solution)/shard_map/ppermute | solution.py:531
  22.6 1.0 %collective-permute-start.6 = (f32[7,16,128]{2,1,0:T(8,128)S(1)}, f32[7,16,128]{2,1,0:T(8,128)S(1)}, u32[]{:S(2)}, u32[]{:S(2)}) collective-permute-start(f32[7,16,128]{2,1,0:T(8,128)S(1)} %four.1.own_y), channel_id=1, source_target_pairs={{0,32},{4,36},{8,40},{12,44},{16,48},{20,52},{24,56},{28,60},{32,6... | collective-permute-start | bytes 172040 | tf_op jit(solution)/shard_map/ppermute | solution.py:531
  23.6 0.3 x_solve.1.u
  23.9 2.0 %y_matrix.1 = (f32[128,8,128]{2,1,0:T(8,128)S(1)}, f32[128,8,128]{2,1,0:T(8,128)S(1)}, f32[128,8,128]{2,1,0:T(8,128)S(1)}, f32[52,8,128]{2,1,0:T(8,128)S(1)}, f3...) custom-call(f32[1024,128]{1,0:T(8,128)S(1)} %get-tuple-element.49.k), custom_call_target="tpu_custom_call" | custom-call | flops 2000000 | bytes 1048576 | tf_op jit(solution)/shard_map/y_matrix/pallas_call | solution.py:32
  25.9 0.0 collective-permute-done.8.y3
  25.9 1.8 %collective-permute-done.7.y2 = f32[7,16,128]{2,1,0:T(8,128)S(1)} collective-permute-done((f32[7,16,128]{2,1,0:T(8,128)S(1)}, f32[7,16,128]{2,1,0:T(8,128)S(1)}, u32[]{:S(2)}, u32[]{:S(2)}) %collective-permute-start.7) | collective-permute-done | bytes 57376 | tf_op jit(solution)/shard_map/ppermute | solution.py:531
  27.7 0.6 %collective-permute-done.6.y1 = f32[7,16,128]{2,1,0:T(8,128)S(1)} collective-permute-done((f32[7,16,128]{2,1,0:T(8,128)S(1)}, f32[7,16,128]{2,1,0:T(8,128)S(1)}, u32[]{:S(2)}, u32[]{:S(2)}) %collective-permute-start.6) | collective-permute-done | bytes 57376 | tf_op jit(solution)/shard_map/ppermute | solution.py:531
  28.3 1.0 %y_port.1 = (f32[1024,128]{1,0:T(8,128)S(1)}, f32[8,128]{1,0:T(8,128)S(1)}) custom-call(f32[7,16,128]{2,1,0:T(8,128)S(1)} %four.1.own_y, f32[7,16,128]{2,1,0:T(8,128)S(1)} %collective-permute-done.6.y1, f32[7,16,128]{2,1,0:T(8,128)S(1)} %collective-permute-done.7.y2, f32[7,16,128]{2,1,0:T(8,128)S(1)} %collective-permute-done.8.y3, ...), custom_call_target="tpu_custom_call" | custom-call | flops 2000000 | bytes 1048576 | tf_op jit(solution)/shard_map/y_port/pallas_call | solution.py:32
  29.2 3.0 %collective-permute-start.11 = (f32[8,128]{1,0:T(8,128)S(1)}, f32[8,128]{1,0:T(8,128)S(1)}, u32[]{:S(2)}, u32[]{:S(2)}) collective-permute-start(f32[8,128]{1,0:T(8,128)S(1)} %get-tuple-element.53.own), channel_id=1, source_target_pairs={{0,3},{1,0},{2,1},{3,2},{4,7},{5,4},{6,5},{7,6},{8,11},{9,8},{10,9... | collective-permute-start | bytes 12296 | tf_op jit(solution)/shard_map/ppermute | solution.py:531
  32.2 0.6 %collective-permute-start.10 = (f32[8,128]{1,0:T(8,128)S(1)}, f32[8,128]{1,0:T(8,128)S(1)}, u32[]{:S(2)}, u32[]{:S(2)}) collective-permute-start(f32[8,128]{1,0:T(8,128)S(1)} %get-tuple-element.53.own), channel_id=1, source_target_pairs={{0,2},{1,3},{2,0},{3,1},{4,6},{5,7},{6,4},{7,5},{8,10},{9,11},{10,... | collective-permute-start | bytes 12296 | tf_op jit(solution)/shard_map/ppermute | solution.py:531
  32.8 0.6 %collective-permute-start.9 = (f32[8,128]{1,0:T(8,128)S(1)}, f32[8,128]{1,0:T(8,128)S(1)}, u32[]{:S(2)}, u32[]{:S(2)}) collective-permute-start(f32[8,128]{1,0:T(8,128)S(1)} %get-tuple-element.53.own), channel_id=1, source_target_pairs={{0,1},{1,2},{2,3},{3,0},{4,5},{5,6},{6,7},{7,4},{8,9},{9,10},{10,1... | collective-permute-start | bytes 12296 | tf_op jit(solution)/shard_map/ppermute | solution.py:531
  33.4 1.3 %y_solve.1.base = f32[64,2048]{1,0:T(8,128)S(1)} custom-call(f32[1024,128]{1,0:T(8,128)S(1)} %get-tuple-element.54.turned, f32[128,8,128]{2,1,0:T(8,128)S(1)} %get-tuple-element.55.along, f32[128,8,128]{2,1,0:T(8,128)S(1)} %get-tuple-element.56.back, f32[128,8,128]{2,1,0:T(8,128)S(1)} %get-tuple-element.57.gain, f32[52,8,128]{2,1,0:T(8,128)S(1)} %get-tuple-element.58.sep, ...), custom_call_target="tpu_custom_call" | custom-call | flops 2000000 | bytes 1048576 | tf_op jit(solution)/shard_map/y_solve/pallas_call | solution.py:32
  34.7 0.0 collective-permute-done.11.r3
  34.7 2.6 %collective-permute-done.10.r2 = f32[8,128]{1,0:T(8,128)S(1)} collective-permute-done((f32[8,128]{1,0:T(8,128)S(1)}, f32[8,128]{1,0:T(8,128)S(1)}, u32[]{:S(2)}, u32[]{:S(2)}) %collective-permute-start.10) | collective-permute-done | bytes 4128 | tf_op jit(solution)/shard_map/ppermute | solution.py:531
  37.3 0.3 collective-permute-done.9.r1
  37.6 1.1 %finish.1 = f32[64,2048]{1,0:T(8,128)} custom-call(f32[8,128]{1,0:T(8,128)S(1)} %get-tuple-element.53.own, f32[8,128]{1,0:T(8,128)S(1)} %collective-permute-done.9.r1, f32[8,128]{1,0:T(8,128)S(1)} %collective-permute-done.10.r2, f32[8,128]{1,0:T(8,128)S(1)} %collective-permute-done.11.r3, f32[64,2048]{1,0:T(8,128)S(1)} %y_solve.1.base, ...), custom_call_target="tpu_custom_call" | custom-call | flops 2000000 | bytes 1048576 | tf_op jit(solution)/shard_map/finish/pallas_call | solution.py:32
  (1 shorter events, 0.0 us)
Async XLA Ops:
  0.0 5.0 %copy-start = (f32[1,64,2048]{2,1,0:T(8,128)S(1)}, f32[1,64,2048]{2,1,0:T(8,128)}, u32[]{:S(2)}) copy-start(f32[1,64,2048]{2,1,0:T(8,128)} %param.2) | copy-start | bytes 1572868
  0.0 5.0 %copy-start.1 = (f32[1,64,2048]{2,1,0:T(8,128)S(1)}, f32[1,64,2048]{2,1,0:T(8,128)}, u32[]{:S(2)}) copy-start(f32[1,64,2048]{2,1,0:T(8,128)} %param.3) | copy-start | bytes 1572868
  1.6 5.1 %collective-permute-start = (f32[8,128]{1,0:T(8,128)}, f32[8,128]{1,0:T(8,128)S(1)}, u32[]{:S(2)}, u32[]{:S(2)}) collective-permute-start(f32[8,128]{1,0:T(8,128)} %get-tuple-element.38), channel_id=1, source_target_pairs={{0,1},{1,2},{2,3},{3,0},{4,5},{5,6},{6,7},{7,4},{8,9},{9,10},{10,1... | collective-permute-start | bytes 12296 | tf_op jit(solution)/shard_map/ppermute | solution.py:531
  3.3 3.8 %collective-permute-start.1 = (f32[8,128]{1,0:T(8,128)}, f32[8,128]{1,0:T(8,128)S(1)}, u32[]{:S(2)}, u32[]{:S(2)}) collective-permute-start(f32[8,128]{1,0:T(8,128)} %get-tuple-element.39), channel_id=1, source_target_pairs={{0,3},{1,0},{2,1},{3,2},{4,7},{5,4},{6,5},{7,6},{8,11},{9,8},{10,9... | collective-permute-start | bytes 12296 | tf_op jit(solution)/shard_map/ppermute | solution.py:531
  7.2 1.3 %collective-permute-start.2 = (f32[7,16,128]{2,1,0:T(8,128)S(1)}, f32[7,16,128]{2,1,0:T(8,128)S(1)}, u32[]{:S(2)}, u32[]{:S(2)}) collective-permute-start(f32[7,16,128]{2,1,0:T(8,128)S(1)} %get-tuple-element.40.own), channel_id=1, source_target_pairs={{0,4},{4,0},{8,12},{12,8},{16,20},{20,16},{24,28},{28,24},{32,36},... | collective-permute-start | bytes 172040 | tf_op jit(solution)/shard_map/ppermute | solution.py:578
  8.6 6.9 %collective-permute-start.5 = (f32[7,16,128]{2,1,0:T(8,128)S(1)}, f32[7,16,128]{2,1,0:T(8,128)S(1)}, u32[]{:S(2)}, u32[]{:S(2)}) collective-permute-start(f32[7,16,128]{2,1,0:T(8,128)S(1)} %pair.1.own.own_z), channel_id=1, source_target_pairs={{0,24},{4,28},{8,0},{12,4},{16,8},{20,12},{24,16},{28,20},{32,56},... | collective-permute-start | bytes 172040 | tf_op jit(solution)/shard_map/ppermute | solution.py:531
  12.7 5.9 %collective-permute-start.4 = (f32[7,16,128]{2,1,0:T(8,128)S(1)}, f32[7,16,128]{2,1,0:T(8,128)S(1)}, u32[]{:S(2)}, u32[]{:S(2)}) collective-permute-start(f32[7,16,128]{2,1,0:T(8,128)S(1)} %pair.1.own.own_z), channel_id=1, source_target_pairs={{0,16},{4,20},{8,24},{12,28},{16,0},{20,4},{24,8},{28,12},{32,48},... | collective-permute-start | bytes 172040 | tf_op jit(solution)/shard_map/ppermute | solution.py:531
  12.7 6.1 %collective-permute-start.3 = (f32[7,16,128]{2,1,0:T(8,128)S(1)}, f32[7,16,128]{2,1,0:T(8,128)S(1)}, u32[]{:S(2)}, u32[]{:S(2)}) collective-permute-start(f32[7,16,128]{2,1,0:T(8,128)S(1)} %pair.1.own.own_z), channel_id=1, source_target_pairs={{0,8},{4,12},{8,16},{12,20},{16,24},{20,28},{24,0},{28,4},{32,40},... | collective-permute-start | bytes 172040 | tf_op jit(solution)/shard_map/ppermute | solution.py:531
  18.9 7.0 %collective-permute-start.8 = (f32[7,16,128]{2,1,0:T(8,128)S(1)}, f32[7,16,128]{2,1,0:T(8,128)S(1)}, u32[]{:S(2)}, u32[]{:S(2)}) collective-permute-start(f32[7,16,128]{2,1,0:T(8,128)S(1)} %four.1.own_y), channel_id=1, source_target_pairs={{0,96},{4,100},{8,104},{12,108},{16,112},{20,116},{24,120},{28,124... | collective-permute-start | bytes 172040 | tf_op jit(solution)/shard_map/ppermute | solution.py:531
  22.0 5.7 %collective-permute-start.7 = (f32[7,16,128]{2,1,0:T(8,128)S(1)}, f32[7,16,128]{2,1,0:T(8,128)S(1)}, u32[]{:S(2)}, u32[]{:S(2)}) collective-permute-start(f32[7,16,128]{2,1,0:T(8,128)S(1)} %four.1.own_y), channel_id=1, source_target_pairs={{0,64},{4,68},{8,72},{12,76},{16,80},{20,84},{24,88},{28,92},{32,9... | collective-permute-start | bytes 172040 | tf_op jit(solution)/shard_map/ppermute | solution.py:531
  22.6 5.7 %collective-permute-start.6 = (f32[7,16,128]{2,1,0:T(8,128)S(1)}, f32[7,16,128]{2,1,0:T(8,128)S(1)}, u32[]{:S(2)}, u32[]{:S(2)}) collective-permute-start(f32[7,16,128]{2,1,0:T(8,128)S(1)} %four.1.own_y), channel_id=1, source_target_pairs={{0,32},{4,36},{8,40},{12,44},{16,48},{20,52},{24,56},{28,60},{32,6... | collective-permute-start | bytes 172040 | tf_op jit(solution)/shard_map/ppermute | solution.py:531
  29.2 5.5 %collective-permute-start.11 = (f32[8,128]{1,0:T(8,128)S(1)}, f32[8,128]{1,0:T(8,128)S(1)}, u32[]{:S(2)}, u32[]{:S(2)}) collective-permute-start(f32[8,128]{1,0:T(8,128)S(1)} %get-tuple-element.53.own), channel_id=1, source_target_pairs={{0,3},{1,0},{2,1},{3,2},{4,7},{5,4},{6,5},{7,6},{8,11},{9,8},{10,9... | collective-permute-start | bytes 12296 | tf_op jit(solution)/shard_map/ppermute | solution.py:531
  32.2 5.1 %collective-permute-start.10 = (f32[8,128]{1,0:T(8,128)S(1)}, f32[8,128]{1,0:T(8,128)S(1)}, u32[]{:S(2)}, u32[]{:S(2)}) collective-permute-start(f32[8,128]{1,0:T(8,128)S(1)} %get-tuple-element.53.own), channel_id=1, source_target_pairs={{0,2},{1,3},{2,0},{3,1},{4,6},{5,7},{6,4},{7,5},{8,10},{9,11},{10,... | collective-permute-start | bytes 12296 | tf_op jit(solution)/shard_map/ppermute | solution.py:531
  32.8 4.8 %collective-permute-start.9 = (f32[8,128]{1,0:T(8,128)S(1)}, f32[8,128]{1,0:T(8,128)S(1)}, u32[]{:S(2)}, u32[]{:S(2)}) collective-permute-start(f32[8,128]{1,0:T(8,128)S(1)} %get-tuple-element.53.own), channel_id=1, source_target_pairs={{0,1},{1,2},{2,3},{3,0},{4,5},{5,6},{6,7},{7,4},{8,9},{9,10},{10,1... | collective-permute-start | bytes 12296 | tf_op jit(solution)/shard_map/ppermute | solution.py:531

commit v3 on v2

--- a/solution.py
+++ b/solution.py
@@ -523,11 +523,11 @@
         copy.wait()
 
 
-def around(value, axis, size, stride, step):
+def around(value, axis, size, stride, step, cross=0):
     pairs = []
     for i in range(size):
         digit = (i // stride) % 4
-        pairs.append((i, i + ((digit + step) % 4 - digit) * stride))
+        pairs.append((i, (i + ((digit + step) % 4 - digit) * stride) ^ cross))
     return lax.ppermute(value, axis, pairs)
 
 
@@ -578,7 +578,7 @@
     other = lax.ppermute(own, "gx", [(i, i ^ 1) for i in range(32)])
     own_z = call(pair_kernel, x_port, name="pair")(own, other)
     k_y, own_z = lax.optimization_barrier((k_flat, own_z))
-    from_z = [around(own_z, "gx", 32, 2, s) for s in (1, 2, 3)]
+    from_z = [around(own_z, "gx", 32, 2, s, 1) for s in (1, 2, 3)]
     *y_coefficients, y_lo, y_hi, flat_lo, flat_hi, y_ends = call(
         y_matrix_kernel,
         [
@@ -597,7 +597,7 @@
     )(k_y)
     table = pltpu.VMEM((4, 7, TILES, 128), F32)
     own_y = call(four_kernel, x_port, [table], name="four")(own_z, *from_z)
-    from_y = [around(own_y, "gx", 32, 8, s) for s in (1, 2, 3)]
+    from_y = [around(own_y, "gx", 32, 8, s, 1) for s in (1, 2, 3)]
     turned, port = call(
         y_port_kernel, [runs, struct(8, 128)], [table, table, scratch(flat)], name="y_port"
     )(own_y, *from_y, own_z, *from_z, own, other, u, x_lo, x_hi, t_flat, y_lo, y_hi, y_ends)

time: 38.8 us -> 39.1 us (level)
  waiting for transfers between devices: 12.4 us -> 13.8 us
  starting transfers between devices: 17.6 us -> 16.6 us
    ppermute x11, waiting for transfers between devices: 11.2 us -> 12.6 us  [around(): return lax.ppermute(value, axis, pairs)]
    ppermute x11, starting transfers between devices: 17.5 us -> 16.5 us  [around(): return lax.ppermute(value, axis, pairs)]
where the time goes in v3:
time: 39.1 us; the launch traced here: 39 us
  starting transfers between devices  16.6 us (42%)
  waiting for transfers between devices  13.8 us (35%)
  Pallas kernels  8.56 us (22%)
    ppermute x11, starting transfers between devices, around(): return lax.ppermute(value, axis, pairs)  16.5 us
    ppermute x11, waiting for transfers between devices, around(): return lax.ppermute(value, axis, pairs)  12.6 us
    pallas_call x10, Pallas kernels, run(): pl.pallas_call(kernel, out_shape=outs, **windows or whole(outs, args), sc...  8.56 us
    ppermute x1, waiting for transfers between devices, per_device(): other = lax.ppermute(own, 'gx', [(i, i ^ 1) for i in range(32)])  1.23 us
  transfers between devices with their start and end apart: 12, of which 10 were waited for; matrix products, arithmetic and copies ran while one was open for 0% of the time, Pallas kernels for 12%

profile of v3, /device:TPU:0, one launch (start us, length us, event | category | flops | bytes accessed | tf_op | source)
XLA Modules:
  0.0 39.0 jit_solution(5404809662849741004)
XLA Ops:
  0.0 0.0 copy-start
  0.0 0.0 copy-start.1
  0.0 1.6 %edges.1 = (f32[8,128]{1,0:T(8,128)}, f32[8,128]{1,0:T(8,128)}) custom-call(f32[64,2048]{1,0:T(8,128)} %bitcast.3, f32[64,2048]{1,0:T(8,128)} %bitcast.5), custom_call_target="tpu_custom_call" | custom-call | flops 2000000 | bytes 1048576 | tf_op jit(solution)/shard_map/edges/pallas_call | solution.py:32
  1.6 1.6 %collective-permute-start = (f32[8,128]{1,0:T(8,128)}, f32[8,128]{1,0:T(8,128)S(1)}, u32[]{:S(2)}, u32[]{:S(2)}) collective-permute-start(f32[8,128]{1,0:T(8,128)} %get-tuple-element.38), channel_id=1, source_target_pairs={{0,1},{1,2},{2,3},{3,0},{4,5},{5,6},{6,7},{7,4},{8,9},{9,10},{10,1... | collective-permute-start | bytes 12296 | tf_op jit(solution)/shard_map/ppermute | solution.py:531
  3.3 1.7 %collective-permute-start.1 = (f32[8,128]{1,0:T(8,128)}, f32[8,128]{1,0:T(8,128)S(1)}, u32[]{:S(2)}, u32[]{:S(2)}) collective-permute-start(f32[8,128]{1,0:T(8,128)} %get-tuple-element.39), channel_id=1, source_target_pairs={{0,3},{1,0},{2,1},{3,2},{4,7},{5,4},{6,5},{7,6},{8,11},{9,8},{10,9... | collective-permute-start | bytes 12296 | tf_op jit(solution)/shard_map/ppermute | solution.py:531
  5.0 0.0 copy-done
  5.0 0.0 copy-done.1
  5.0 1.1 %x_matrix.1 = (f32[1024,128]{1,0:T(8,128)S(1)}, f32[64,16,128]{2,1,0:T(8,128)S(1)}, f32[64,16,128]{2,1,0:T(8,128)S(1)}, f32[64,16,128]{2,1,0:T(8,128)S(1)}, f32[...) custom-call(f32[64,2048]{1,0:T(8,128)S(1)} %bitcast.4, ...), custom_call_target="tpu_custom_call" | custom-call | flops 2000000 | bytes 1048576 | tf_op jit(solution)/shard_map/x_matrix/pallas_call | solution.py:32
  6.1 0.7 %collective-permute-done.below = f32[8,128]{1,0:T(8,128)S(1)} collective-permute-done((f32[8,128]{1,0:T(8,128)}, f32[8,128]{1,0:T(8,128)S(1)}, u32[]{:S(2)}, u32[]{:S(2)}) %collective-permute-start) | collective-permute-done | bytes 4128 | tf_op jit(solution)/shard_map/ppermute | solution.py:531
  6.7 0.4 collective-permute-done.1.above
  7.1 0.1 x_port.1
  7.2 0.1 collective-permute-start.2
  7.3 1.2 %collective-permute-done.2.other = f32[7,16,128]{2,1,0:T(8,128)S(1)} collective-permute-done((f32[7,16,128]{2,1,0:T(8,128)S(1)}, f32[7,16,128]{2,1,0:T(8,128)S(1)}, u32[]{:S(2)}, u32[]{:S(2)}) %collective-permute-start.2) | collective-permute-done | bytes 57376 | tf_op jit(solution)/shard_map/ppermute | solution.py:578
  8.6 3.9 %collective-permute-start.5 = (f32[7,16,128]{2,1,0:T(8,128)S(1)}, f32[7,16,128]{2,1,0:T(8,128)S(1)}, u32[]{:S(2)}, u32[]{:S(2)}) collective-permute-start(f32[7,16,128]{2,1,0:T(8,128)S(1)} %pair.1.own.own_z), channel_id=1, source_target_pairs={{0,28},{4,24},{8,4},{12,0},{16,12},{20,8},{24,20},{28,16},{32,60},... | collective-permute-start | bytes 172040 | tf_op jit(solution)/shard_map/ppermute | solution.py:531
  12.4 0.0 collective-permute-start.4
  12.4 1.0 %collective-permute-start.3 = (f32[7,16,128]{2,1,0:T(8,128)S(1)}, f32[7,16,128]{2,1,0:T(8,128)S(1)}, u32[]{:S(2)}, u32[]{:S(2)}) collective-permute-start(f32[7,16,128]{2,1,0:T(8,128)S(1)} %pair.1.own.own_z), channel_id=1, source_target_pairs={{0,12},{4,8},{8,20},{12,16},{16,28},{20,24},{24,4},{28,0},{32,44},... | collective-permute-start | bytes 172040 | tf_op jit(solution)/shard_map/ppermute | solution.py:531
  13.4 2.3 %collective-permute-done.5.r3.z3 = f32[7,16,128]{2,1,0:T(8,128)S(1)} collective-permute-done((f32[7,16,128]{2,1,0:T(8,128)S(1)}, f32[7,16,128]{2,1,0:T(8,128)S(1)}, u32[]{:S(2)}, u32[]{:S(2)}) %collective-permute-start.5) | collective-permute-done | bytes 57376 | tf_op jit(solution)/shard_map/ppermute | solution.py:531
  15.7 2.1 %collective-permute-done.4.r2.z2 = f32[7,16,128]{2,1,0:T(8,128)S(1)} collective-permute-done((f32[7,16,128]{2,1,0:T(8,128)S(1)}, f32[7,16,128]{2,1,0:T(8,128)S(1)}, u32[]{:S(2)}, u32[]{:S(2)}) %collective-permute-start.4) | collective-permute-done | bytes 57376 | tf_op jit(solution)/shard_map/ppermute | solution.py:531
  17.8 1.0 %collective-permute-done.3.r1.z1 = f32[7,16,128]{2,1,0:T(8,128)S(1)} collective-permute-done((f32[7,16,128]{2,1,0:T(8,128)S(1)}, f32[7,16,128]{2,1,0:T(8,128)S(1)}, u32[]{:S(2)}, u32[]{:S(2)}) %collective-permute-start.3) | collective-permute-done | bytes 57376 | tf_op jit(solution)/shard_map/ppermute | solution.py:531
  18.8 0.1 four.1.own_y
  18.8 2.8 %collective-permute-start.8 = (f32[7,16,128]{2,1,0:T(8,128)S(1)}, f32[7,16,128]{2,1,0:T(8,128)S(1)}, u32[]{:S(2)}, u32[]{:S(2)}) collective-permute-start(f32[7,16,128]{2,1,0:T(8,128)S(1)} %four.1.own_y), channel_id=1, source_target_pairs={{0,100},{4,96},{8,108},{12,104},{16,116},{20,112},{24,124},{28,120... | collective-permute-start | bytes 172040 | tf_op jit(solution)/shard_map/ppermute | solution.py:531
  21.7 0.6 %collective-permute-start.7 = (f32[7,16,128]{2,1,0:T(8,128)S(1)}, f32[7,16,128]{2,1,0:T(8,128)S(1)}, u32[]{:S(2)}, u32[]{:S(2)}) collective-permute-start(f32[7,16,128]{2,1,0:T(8,128)S(1)} %four.1.own_y), channel_id=1, source_target_pairs={{0,68},{4,64},{8,76},{12,72},{16,84},{20,80},{24,92},{28,88},{32,1... | collective-permute-start | bytes 172040 | tf_op jit(solution)/shard_map/ppermute | solution.py:531
  22.3 0.7 %collective-permute-start.6 = (f32[7,16,128]{2,1,0:T(8,128)S(1)}, f32[7,16,128]{2,1,0:T(8,128)S(1)}, u32[]{:S(2)}, u32[]{:S(2)}) collective-permute-start(f32[7,16,128]{2,1,0:T(8,128)S(1)} %four.1.own_y), channel_id=1, source_target_pairs={{0,36},{4,32},{8,44},{12,40},{16,52},{20,48},{24,60},{28,56},{32,6... | collective-permute-start | bytes 172040 | tf_op jit(solution)/shard_map/ppermute | solution.py:531
  23.0 0.3 x_solve.1.u
  23.3 2.0 %y_matrix.1 = (f32[128,8,128]{2,1,0:T(8,128)S(1)}, f32[128,8,128]{2,1,0:T(8,128)S(1)}, f32[128,8,128]{2,1,0:T(8,128)S(1)}, f32[52,8,128]{2,1,0:T(8,128)S(1)}, f3...) custom-call(f32[1024,128]{1,0:T(8,128)S(1)} %get-tuple-element.49.k), custom_call_target="tpu_custom_call" | custom-call | flops 2000000 | bytes 1048576 | tf_op jit(solution)/shard_map/y_matrix/pallas_call | solution.py:32
  25.3 0.0 collective-permute-done.8.y3
  25.4 1.6 %collective-permute-done.7.y2 = f32[7,16,128]{2,1,0:T(8,128)S(1)} collective-permute-done((f32[7,16,128]{2,1,0:T(8,128)S(1)}, f32[7,16,128]{2,1,0:T(8,128)S(1)}, u32[]{:S(2)}, u32[]{:S(2)}) %collective-permute-start.7) | collective-permute-done | bytes 57376 | tf_op jit(solution)/shard_map/ppermute | solution.py:531
  27.0 1.6 %collective-permute-done.6.y1 = f32[7,16,128]{2,1,0:T(8,128)S(1)} collective-permute-done((f32[7,16,128]{2,1,0:T(8,128)S(1)}, f32[7,16,128]{2,1,0:T(8,128)S(1)}, u32[]{:S(2)}, u32[]{:S(2)}) %collective-permute-start.6) | collective-permute-done | bytes 57376 | tf_op jit(solution)/shard_map/ppermute | solution.py:531
  28.6 1.0 %y_port.1 = (f32[1024,128]{1,0:T(8,128)S(1)}, f32[8,128]{1,0:T(8,128)S(1)}) custom-call(f32[7,16,128]{2,1,0:T(8,128)S(1)} %four.1.own_y, f32[7,16,128]{2,1,0:T(8,128)S(1)} %collective-permute-done.6.y1, f32[7,16,128]{2,1,0:T(8,128)S(1)} %collective-permute-done.7.y2, f32[7,16,128]{2,1,0:T(8,128)S(1)} %collective-permute-done.8.y3, ...), custom_call_target="tpu_custom_call" | custom-call | flops 2000000 | bytes 1048576 | tf_op jit(solution)/shard_map/y_port/pallas_call | solution.py:32
  29.6 3.0 %collective-permute-start.11 = (f32[8,128]{1,0:T(8,128)S(1)}, f32[8,128]{1,0:T(8,128)S(1)}, u32[]{:S(2)}, u32[]{:S(2)}) collective-permute-start(f32[8,128]{1,0:T(8,128)S(1)} %get-tuple-element.53.own), channel_id=1, source_target_pairs={{0,3},{1,0},{2,1},{3,2},{4,7},{5,4},{6,5},{7,6},{8,11},{9,8},{10,9... | collective-permute-start | bytes 12296 | tf_op jit(solution)/shard_map/ppermute | solution.py:531
  32.5 0.6 %collective-permute-start.10 = (f32[8,128]{1,0:T(8,128)S(1)}, f32[8,128]{1,0:T(8,128)S(1)}, u32[]{:S(2)}, u32[]{:S(2)}) collective-permute-start(f32[8,128]{1,0:T(8,128)S(1)} %get-tuple-element.53.own), channel_id=1, source_target_pairs={{0,2},{1,3},{2,0},{3,1},{4,6},{5,7},{6,4},{7,5},{8,10},{9,11},{10,... | collective-permute-start | bytes 12296 | tf_op jit(solution)/shard_map/ppermute | solution.py:531
  33.1 0.6 %collective-permute-start.9 = (f32[8,128]{1,0:T(8,128)S(1)}, f32[8,128]{1,0:T(8,128)S(1)}, u32[]{:S(2)}, u32[]{:S(2)}) collective-permute-start(f32[8,128]{1,0:T(8,128)S(1)} %get-tuple-element.53.own), channel_id=1, source_target_pairs={{0,1},{1,2},{2,3},{3,0},{4,5},{5,6},{6,7},{7,4},{8,9},{9,10},{10,1... | collective-permute-start | bytes 12296 | tf_op jit(solution)/shard_map/ppermute | solution.py:531
  33.7 1.3 %y_solve.1.base = f32[64,2048]{1,0:T(8,128)S(1)} custom-call(f32[1024,128]{1,0:T(8,128)S(1)} %get-tuple-element.54.turned, f32[128,8,128]{2,1,0:T(8,128)S(1)} %get-tuple-element.55.along, f32[128,8,128]{2,1,0:T(8,128)S(1)} %get-tuple-element.56.back, f32[128,8,128]{2,1,0:T(8,128)S(1)} %get-tuple-element.57.gain, f32[52,8,128]{2,1,0:T(8,128)S(1)} %get-tuple-element.58.sep, ...), custom_call_target="tpu_custom_call" | custom-call | flops 2000000 | bytes 1048576 | tf_op jit(solution)/shard_map/y_solve/pallas_call | solution.py:32
  35.0 0.0 collective-permute-done.11.r3
  35.0 2.6 %collective-permute-done.10.r2 = f32[8,128]{1,0:T(8,128)S(1)} collective-permute-done((f32[8,128]{1,0:T(8,128)S(1)}, f32[8,128]{1,0:T(8,128)S(1)}, u32[]{:S(2)}, u32[]{:S(2)}) %collective-permute-start.10) | collective-permute-done | bytes 4128 | tf_op jit(solution)/shard_map/ppermute | solution.py:531
  37.7 0.3 collective-permute-done.9.r1
  38.0 1.1 %finish.1 = f32[64,2048]{1,0:T(8,128)} custom-call(f32[8,128]{1,0:T(8,128)S(1)} %get-tuple-element.53.own, f32[8,128]{1,0:T(8,128)S(1)} %collective-permute-done.9.r1, f32[8,128]{1,0:T(8,128)S(1)} %collective-permute-done.10.r2, f32[8,128]{1,0:T(8,128)S(1)} %collective-permute-done.11.r3, f32[64,2048]{1,0:T(8,128)S(1)} %y_solve.1.base, ...), custom_call_target="tpu_custom_call" | custom-call | flops 2000000 | bytes 1048576 | tf_op jit(solution)/shard_map/finish/pallas_call | solution.py:32
  (1 shorter events, 0.0 us)
Async XLA Ops:
  0.0 5.0 %copy-start = (f32[1,64,2048]{2,1,0:T(8,128)S(1)}, f32[1,64,2048]{2,1,0:T(8,128)}, u32[]{:S(2)}) copy-start(f32[1,64,2048]{2,1,0:T(8,128)} %param.2) | copy-start | bytes 1572868
  0.0 5.0 %copy-start.1 = (f32[1,64,2048]{2,1,0:T(8,128)S(1)}, f32[1,64,2048]{2,1,0:T(8,128)}, u32[]{:S(2)}) copy-start(f32[1,64,2048]{2,1,0:T(8,128)} %param.3) | copy-start | bytes 1572868
  1.6 5.1 %collective-permute-start = (f32[8,128]{1,0:T(8,128)}, f32[8,128]{1,0:T(8,128)S(1)}, u32[]{:S(2)}, u32[]{:S(2)}) collective-permute-start(f32[8,128]{1,0:T(8,128)} %get-tuple-element.38), channel_id=1, source_target_pairs={{0,1},{1,2},{2,3},{3,0},{4,5},{5,6},{6,7},{7,4},{8,9},{9,10},{10,1... | collective-permute-start | bytes 12296 | tf_op jit(solution)/shard_map/ppermute | solution.py:531
  3.3 3.8 %collective-permute-start.1 = (f32[8,128]{1,0:T(8,128)}, f32[8,128]{1,0:T(8,128)S(1)}, u32[]{:S(2)}, u32[]{:S(2)}) collective-permute-start(f32[8,128]{1,0:T(8,128)} %get-tuple-element.39), channel_id=1, source_target_pairs={{0,3},{1,0},{2,1},{3,2},{4,7},{5,4},{6,5},{7,6},{8,11},{9,8},{10,9... | collective-permute-start | bytes 12296 | tf_op jit(solution)/shard_map/ppermute | solution.py:531
  7.2 1.3 %collective-permute-start.2 = (f32[7,16,128]{2,1,0:T(8,128)S(1)}, f32[7,16,128]{2,1,0:T(8,128)S(1)}, u32[]{:S(2)}, u32[]{:S(2)}) collective-permute-start(f32[7,16,128]{2,1,0:T(8,128)S(1)} %get-tuple-element.40.own), channel_id=1, source_target_pairs={{0,4},{4,0},{8,12},{12,8},{16,20},{20,16},{24,28},{28,24},{32,36},... | collective-permute-start | bytes 172040 | tf_op jit(solution)/shard_map/ppermute | solution.py:578
  8.6 7.1 %collective-permute-start.5 = (f32[7,16,128]{2,1,0:T(8,128)S(1)}, f32[7,16,128]{2,1,0:T(8,128)S(1)}, u32[]{:S(2)}, u32[]{:S(2)}) collective-permute-start(f32[7,16,128]{2,1,0:T(8,128)S(1)} %pair.1.own.own_z), channel_id=1, source_target_pairs={{0,28},{4,24},{8,4},{12,0},{16,12},{20,8},{24,20},{28,16},{32,60},... | collective-permute-start | bytes 172040 | tf_op jit(solution)/shard_map/ppermute | solution.py:531
  12.4 5.4 %collective-permute-start.4 = (f32[7,16,128]{2,1,0:T(8,128)S(1)}, f32[7,16,128]{2,1,0:T(8,128)S(1)}, u32[]{:S(2)}, u32[]{:S(2)}) collective-permute-start(f32[7,16,128]{2,1,0:T(8,128)S(1)} %pair.1.own.own_z), channel_id=1, source_target_pairs={{0,20},{4,16},{8,28},{12,24},{16,4},{20,0},{24,12},{28,8},{32,52},... | collective-permute-start | bytes 172040 | tf_op jit(solution)/shard_map/ppermute | solution.py:531
  12.4 6.3 %collective-permute-start.3 = (f32[7,16,128]{2,1,0:T(8,128)S(1)}, f32[7,16,128]{2,1,0:T(8,128)S(1)}, u32[]{:S(2)}, u32[]{:S(2)}) collective-permute-start(f32[7,16,128]{2,1,0:T(8,128)S(1)} %pair.1.own.own_z), channel_id=1, source_target_pairs={{0,12},{4,8},{8,20},{12,16},{16,28},{20,24},{24,4},{28,0},{32,44},... | collective-permute-start | bytes 172040 | tf_op jit(solution)/shard_map/ppermute | solution.py:531
  18.8 6.5 %collective-permute-start.8 = (f32[7,16,128]{2,1,0:T(8,128)S(1)}, f32[7,16,128]{2,1,0:T(8,128)S(1)}, u32[]{:S(2)}, u32[]{:S(2)}) collective-permute-start(f32[7,16,128]{2,1,0:T(8,128)S(1)} %four.1.own_y), channel_id=1, source_target_pairs={{0,100},{4,96},{8,108},{12,104},{16,116},{20,112},{24,124},{28,120... | collective-permute-start | bytes 172040 | tf_op jit(solution)/shard_map/ppermute | solution.py:531
  21.7 5.3 %collective-permute-start.7 = (f32[7,16,128]{2,1,0:T(8,128)S(1)}, f32[7,16,128]{2,1,0:T(8,128)S(1)}, u32[]{:S(2)}, u32[]{:S(2)}) collective-permute-start(f32[7,16,128]{2,1,0:T(8,128)S(1)} %four.1.own_y), channel_id=1, source_target_pairs={{0,68},{4,64},{8,76},{12,72},{16,84},{20,80},{24,92},{28,88},{32,1... | collective-permute-start | bytes 172040 | tf_op jit(solution)/shard_map/ppermute | solution.py:531
  22.3 6.3 %collective-permute-start.6 = (f32[7,16,128]{2,1,0:T(8,128)S(1)}, f32[7,16,128]{2,1,0:T(8,128)S(1)}, u32[]{:S(2)}, u32[]{:S(2)}) collective-permute-start(f32[7,16,128]{2,1,0:T(8,128)S(1)} %four.1.own_y), channel_id=1, source_target_pairs={{0,36},{4,32},{8,44},{12,40},{16,52},{20,48},{24,60},{28,56},{32,6... | collective-permute-start | bytes 172040 | tf_op jit(solution)/shard_map/ppermute | solution.py:531
  29.6 5.5 %collective-permute-start.11 = (f32[8,128]{1,0:T(8,128)S(1)}, f32[8,128]{1,0:T(8,128)S(1)}, u32[]{:S(2)}, u32[]{:S(2)}) collective-permute-start(f32[8,128]{1,0:T(8,128)S(1)} %get-tuple-element.53.own), channel_id=1, source_target_pairs={{0,3},{1,0},{2,1},{3,2},{4,7},{5,4},{6,5},{7,6},{8,11},{9,8},{10,9... | collective-permute-start | bytes 12296 | tf_op jit(solution)/shard_map/ppermute | solution.py:531
  32.5 5.1 %collective-permute-start.10 = (f32[8,128]{1,0:T(8,128)S(1)}, f32[8,128]{1,0:T(8,128)S(1)}, u32[]{:S(2)}, u32[]{:S(2)}) collective-permute-start(f32[8,128]{1,0:T(8,128)S(1)} %get-tuple-element.53.own), channel_id=1, source_target_pairs={{0,2},{1,3},{2,0},{3,1},{4,6},{5,7},{6,4},{7,5},{8,10},{9,11},{10,... | collective-permute-start | bytes 12296 | tf_op jit(solution)/shard_map/ppermute | solution.py:531
  33.1 4.8 %collective-permute-start.9 = (f32[8,128]{1,0:T(8,128)S(1)}, f32[8,128]{1,0:T(8,128)S(1)}, u32[]{:S(2)}, u32[]{:S(2)}) collective-permute-start(f32[8,128]{1,0:T(8,128)S(1)} %get-tuple-element.53.own), channel_id=1, source_target_pairs={{0,1},{1,2},{2,3},{3,0},{4,5},{5,6},{6,7},{7,4},{8,9},{9,10},{10,1... | collective-permute-start | bytes 12296 | tf_op jit(solution)/shard_map/ppermute | solution.py:531

commit v4 on v2

--- a/solution.py
+++ b/solution.py
@@ -10,6 +10,7 @@
 SEGMENTS = 4
 Y_STEPS = 128
 X_LEVELS, Y_LEVELS = 2, 6
+RING = (2, 1, 3)
 F32 = jnp.float32
 VMEM = pl.BlockSpec(memory_space=pltpu.VMEM)
 HBM = pl.BlockSpec(memory_space=pltpu.MemorySpace.HBM)
@@ -350,8 +351,8 @@
 
 def place(index, own, received, table):
     table[index] = own[...]
-    for s in (1, 2, 3):
-        table[lax.rem(index + 4 - s, 4)] = received[s - 1][...]
+    for s, value in zip(RING, received):
+        table[lax.rem(index + 4 - s, 4)] = value[...]
 
 
 def pair_kernel(own, other, out):
@@ -441,9 +442,30 @@
         from_runs(turned, put(flat))
 
 
+def blend_kernel(u, x_lo, x_hi, y_lo, y_hi, t, source, lo, hi, mixed, known, flat, side):
+    for ref, out in ((u, flat), (x_lo, lo), (x_hi, hi)):
+        for i in range(ROWS):
+            at = pl.ds((i // 8) * (8 * TILES) + i % 8, TILES, stride=8)
+            out[at, :] = ref[i]
+    for band in range(BANDS):
+        sums = [None, None]
+        for column in range(TILES):
+            at = pl.ds((band * TILES + column) * 8, 8)
+            value = flat[at, :] - 2.0 * t[at, :]
+            source[at, :] = value
+            for n, response in enumerate((y_lo, y_hi)):
+                r = tile(response, band, column)
+                sums[n] = plus(sums[n], r * value)
+                mixed[2 * n, at, :] = r * lo[at, :]
+                mixed[2 * n + 1, at, :] = r * hi[at, :]
+        for n in range(2):
+            side[64 * n + 8 * band : 64 * n + 8 * band + 8, :] = sums[n]
+    known[...] = jnp.broadcast_to(jnp.sum(side[...].T, axis=0, keepdims=True), (8, 128))
+
+
 def y_port_kernel(
-    own_y, y1, y2, y3, own_z, z1, z2, z3, own, other, u, x_lo, x_hi, t,
-    lo_y, hi_y, ends, turned, port, table_y, table_z, flat,
+    own_y, y1, y2, y3, own_z, z1, z2, z3, own, other, mixed, known, ends,
+    port, flow, table_y, table_z, side,
 ):
     index = lax.axis_index("gx")
     core, z, y = lax.rem(index, 2), lax.rem(lax.div(index, 2), 4), lax.div(index, 8)
@@ -456,38 +478,53 @@
     mine, theirs = take(own), take(other)
     lo = choose(core == 1, past_up(lo, theirs, scale), lo)
     hi = choose(core == 0, past_down(hi, theirs, scale), hi)
-    f_lo, f_hi = flows(mine, lo, hi, scale)
-    for i in range(ROWS):
-        at = pl.ds((i // 8) * (8 * TILES) + i % 8, TILES, stride=8)
-        flat[at, :] = u[i] - f_lo * x_lo[i] + f_hi * x_hi[i]
-
+    flow[0], flow[1] = flows(mine, lo, hi, scale)
+    sums = [None] * (2 * BANDS)
+    for column in range(TILES):
+        down, up = across(flow, column)
+        for band in range(BANDS):
+            at = pl.ds((band * TILES + column) * 8, 8)
+            for n in range(2):
+                part = up * mixed[2 * n + 1, at, :] - down * mixed[2 * n, at, :]
+                sums[BANDS * n + band] = plus(sums[BANDS * n + band], part)
+    for n, value in enumerate(sums):
+        side[8 * n : 8 * n + 8, :] = value
+    both = jnp.sum(side[...].T, axis=0, keepdims=True) + known[0:1, :]
+    port[...] = jnp.zeros_like(port)
+    port[0:1, :] = both
+    port[1:2, :] = pltpu.roll(both, 64, 1)
+    port[2:7, :] = ends[0:5, :]
+
+
+def across(flow, column):
+    return tuple(
+        jnp.broadcast_to(flow[n, column : column + 1, :], (8, 128)) for n in range(2)
+    )
+
+
+def y_solve_kernel(source, lo, hi, flow, along, back, gain, sep, t, out, d, turned):
     def block(band, column):
-        return flat_tile(flat, band, column) - 2.0 * flat_tile(t, band, column)
+        down, up = across(flow, column)
+        x = flat_tile(source, band, column)
+        return x - down * flat_tile(lo, band, column) + up * flat_tile(hi, band, column)
 
     to_runs(block, turned)
-    port[...] = jnp.zeros_like(port)
-    for n, response in enumerate((lo_y, hi_y)):
-        both = total(response[l] * cell(turned, l) for l in range(Y_STEPS))
-        both = jnp.sum(both + pltpu.roll(both, 64, 1), axis=0, keepdims=True)
-        port[n : n + 1, :] = both
-    port[2:7, :] = ends[0:5, :]
-
-
-def y_solve_kernel(turned, along, back, gain, sep, t, out, d, again):
+
     def store(l, value):
         d[l] = value
-        again[pl.ds(l, 8, stride=128), :] = value
-
-    def source(l):
+
+    def cells(l):
         return cell(turned, l)
 
-    solve(source, Y_STEPS, Y_LEVELS, y_shift, along, back, gain, sep, d, store)
+    solve(cells, Y_STEPS, Y_LEVELS, y_shift, along, back, gain, sep, d, store)
+    for l in range(Y_STEPS):
+        turned[pl.ds(l, 8, stride=128), :] = d[l]
     keep = put(out)
 
     def plus_start(band, column, value):
         keep(band, column, value + flat_tile(t, band, column))
 
-    from_runs(again, plus_start)
+    from_runs(turned, plus_start)
 
 
 def finish_kernel(own, r1, r2, r3, base, y_lo, y_hi, out, table, side, done, sent):
@@ -578,7 +615,7 @@
     other = lax.ppermute(own, "gx", [(i, i ^ 1) for i in range(32)])
     own_z = call(pair_kernel, x_port, name="pair")(own, other)
     k_y, own_z = lax.optimization_barrier((k_flat, own_z))
-    from_z = [around(own_z, "gx", 32, 2, s) for s in (1, 2, 3)]
+    from_z = [around(own_z, "gx", 32, 2, s) for s in RING]
     *y_coefficients, y_lo, y_hi, flat_lo, flat_hi, y_ends = call(
         y_matrix_kernel,
         [
@@ -595,16 +632,27 @@
         [scratch(runs)],
         name="y_matrix",
     )(k_y)
+    *from_z, y_ends, u = lax.optimization_barrier((*from_z, y_ends, u))
     table = pltpu.VMEM((4, 7, TILES, 128), F32)
     own_y = call(four_kernel, x_port, [table], name="four")(own_z, *from_z)
-    from_y = [around(own_y, "gx", 32, 8, s) for s in (1, 2, 3)]
-    turned, port = call(
-        y_port_kernel, [runs, struct(8, 128)], [table, table, scratch(flat)], name="y_port"
-    )(own_y, *from_y, own_z, *from_z, own, other, u, x_lo, x_hi, t_flat, y_lo, y_hi, y_ends)
-    from_gy = [around(port, "gy", 4, 1, s) for s in (1, 2, 3)]
+    from_y = [around(own_y, "gx", 32, 8, s) for s in RING]
+    square = pltpu.VMEM((128, 128), F32)
+    source, lo_flat, hi_flat, mixed, known = call(
+        blend_kernel,
+        [flat, flat, flat, struct(4, BANDS * TILES * 8, 128), struct(8, 128)],
+        [scratch(flat), square],
+        name="blend",
+    )(u, x_lo, x_hi, flat_lo, flat_hi, t_flat)
+    port, flow = call(
+        y_port_kernel,
+        [struct(8, 128), struct(2, TILES, 128)],
+        [table, table, square],
+        name="y_port",
+    )(own_y, *from_y, own_z, *from_z, own, other, mixed, known, y_ends)
+    from_gy = [around(port, "gy", 4, 1, s) for s in RING]
     base = call(
         y_solve_kernel, natural, [scratch(y_field), scratch(runs)], name="y_solve"
-    )(turned, *y_coefficients, t_flat)
+    )(source, lo_flat, hi_flat, flow, *y_coefficients, t_flat)
     updated = call(
         finish_kernel,
         natural,

time: 38.8 us -> 38.8 us (level)
  waiting for transfers between devices: 12.4 us -> 5.81 us
  starting transfers between devices: 17.6 us -> 21 us
  local copies, waits for them, and re-layouts: 0.01 us -> 2.08 us
  Pallas kernels: 8.56 us -> 9.36 us
    ppermute x11, waiting for transfers between devices: 11.2 us -> 4.58 us  [around(): return lax.ppermute(value, axis, pairs)]
    ppermute x11, starting transfers between devices: 17.5 us -> 20.9 us  [around(): return lax.ppermute(value, axis, pairs)]
    unnamed x4, local copies, waits for them, and re-layouts: 0.01 us -> 2.08 us
    pallas_call x10 -> x11, Pallas kernels: 8.56 us -> 9.36 us  [run(): pl.pallas_call(kernel, out_shape=outs, **windows or whole(outs, args), sc...]
  transfers between devices with their start and end apart: 12 -> 12, of which waited for: 10 -> 3; matrix products, arithmetic and copies ran while one was open for 0% -> 0% of each run, Pallas kernels for 12% -> 16%
where the time goes in v4:
time: 38.8 us; the launch traced here: 38.4 us
  starting transfers between devices  21 us (54%)
  Pallas kernels  9.36 us (24%)
  waiting for transfers between devices  5.81 us (15%)
  local copies, waits for them, and re-layouts  2.08 us (5%)
    ppermute x11, starting transfers between devices, around(): return lax.ppermute(value, axis, pairs)  20.9 us
    pallas_call x11, Pallas kernels, run(): pl.pallas_call(kernel, out_shape=outs, **windows or whole(outs, args), sc...  9.36 us
    ppermute x11, waiting for transfers between devices, around(): return lax.ppermute(value, axis, pairs)  4.58 us
    unnamed x4, local copies, waits for them, and re-layouts  2.08 us
    ppermute x1, waiting for transfers between devices, per_device(): other = lax.ppermute(own, 'gx', [(i, i ^ 1) for i in range(32)])  1.23 us
  transfers between devices with their start and end apart: 12, of which 3 were waited for; matrix products, arithmetic and copies ran while one was open for 0% of the time, Pallas kernels for 16%

profile of v4, /device:TPU:0, one launch (start us, length us, event | category | flops | bytes accessed | tf_op | source)
XLA Modules:
  0.0 38.4 jit_solution(17658846006093145475)
XLA Ops:
  0.0 1.5 %edges.1 = (f32[8,128]{1,0:T(8,128)}, f32[8,128]{1,0:T(8,128)}) custom-call(f32[64,2048]{1,0:T(8,128)} %bitcast.3, f32[64,2048]{1,0:T(8,128)} %bitcast.5), custom_call_target="tpu_custom_call" | custom-call | flops 2000000 | bytes 1048576 | tf_op jit(solution)/shard_map/edges/pallas_call | solution.py:33
  1.6 1.6 %collective-permute-start = (f32[8,128]{1,0:T(8,128)}, f32[8,128]{1,0:T(8,128)S(1)}, u32[]{:S(2)}, u32[]{:S(2)}) collective-permute-start(f32[8,128]{1,0:T(8,128)} %get-tuple-element.46), channel_id=1, source_target_pairs={{0,1},{1,2},{2,3},{3,0},{4,5},{5,6},{6,7},{7,4},{8,9},{9,10},{10,1... | collective-permute-start | bytes 12296 | tf_op jit(solution)/shard_map/ppermute | solution.py:568
  3.2 1.7 %collective-permute-start.1 = (f32[8,128]{1,0:T(8,128)}, f32[8,128]{1,0:T(8,128)S(1)}, u32[]{:S(2)}, u32[]{:S(2)}) collective-permute-start(f32[8,128]{1,0:T(8,128)} %get-tuple-element.47), channel_id=1, source_target_pairs={{0,3},{1,0},{2,1},{3,2},{4,7},{5,4},{6,5},{7,6},{8,11},{9,8},{10,9... | collective-permute-start | bytes 12296 | tf_op jit(solution)/shard_map/ppermute | solution.py:568
  4.9 0.0 copy-start
  4.9 1.0 %copy-done = f32[1,64,2048]{2,1,0:T(8,128)S(1)} copy-done((f32[1,64,2048]{2,1,0:T(8,128)S(1)}, f32[1,64,2048]{2,1,0:T(8,128)}, u32[]{:S(2)}) %copy-start) | copy-done | bytes 524312
  5.9 0.0 copy-start.1
  5.9 1.0 %copy-done.1 = f32[1,64,2048]{2,1,0:T(8,128)S(1)} copy-done((f32[1,64,2048]{2,1,0:T(8,128)S(1)}, f32[1,64,2048]{2,1,0:T(8,128)}, u32[]{:S(2)}) %copy-start.1) | copy-done | bytes 524312
  6.9 1.1 %x_matrix.1 = (f32[1024,128]{1,0:T(8,128)S(1)}, f32[64,16,128]{2,1,0:T(8,128)S(1)}, f32[64,16,128]{2,1,0:T(8,128)S(1)}, f32[64,16,128]{2,1,0:T(8,128)S(1)}, f32[...) custom-call(f32[64,2048]{1,0:T(8,128)S(1)} %bitcast.4, ...), custom_call_target="tpu_custom_call" | custom-call | flops 2000000 | bytes 1048576 | tf_op jit(solution)/shard_map/x_matrix/pallas_call | solution.py:33
  8.1 0.0 collective-permute-done.below
  8.1 0.0 collective-permute-done.1.above
  8.1 0.1 x_port.1
  8.2 0.1 collective-permute-start.2
  8.3 1.2 %collective-permute-done.2.other = f32[7,16,128]{2,1,0:T(8,128)S(1)} collective-permute-done((f32[7,16,128]{2,1,0:T(8,128)S(1)}, f32[7,16,128]{2,1,0:T(8,128)S(1)}, u32[]{:S(2)}, u32[]{:S(2)}) %collective-permute-start.2) | collective-permute-done | bytes 57376 | tf_op jit(solution)/shard_map/ppermute | solution.py:615
  9.5 4.0 %collective-permute-start.3 = (f32[7,16,128]{2,1,0:T(8,128)S(1)}, f32[7,16,128]{2,1,0:T(8,128)S(1)}, u32[]{:S(2)}, u32[]{:S(2)}) collective-permute-start(f32[7,16,128]{2,1,0:T(8,128)S(1)} %pair.1.own.own_z), channel_id=1, source_target_pairs={{0,16},{4,20},{8,24},{12,28},{16,0},{20,4},{24,8},{28,12},{32,48},... | collective-permute-start | bytes 172040 | tf_op jit(solution)/shard_map/ppermute | solution.py:568
  13.6 1.0 %collective-permute-start.4 = (f32[7,16,128]{2,1,0:T(8,128)S(1)}, f32[7,16,128]{2,1,0:T(8,128)S(1)}, u32[]{:S(2)}, u32[]{:S(2)}) collective-permute-start(f32[7,16,128]{2,1,0:T(8,128)S(1)} %pair.1.own.own_z), channel_id=1, source_target_pairs={{0,8},{4,12},{8,16},{12,20},{16,24},{20,28},{24,0},{28,4},{32,40},... | collective-permute-start | bytes 172040 | tf_op jit(solution)/shard_map/ppermute | solution.py:568
  14.6 2.2 %collective-permute-start.5 = (f32[7,16,128]{2,1,0:T(8,128)S(1)}, f32[7,16,128]{2,1,0:T(8,128)S(1)}, u32[]{:S(2)}, u32[]{:S(2)}) collective-permute-start(f32[7,16,128]{2,1,0:T(8,128)S(1)} %pair.1.own.own_z), channel_id=1, source_target_pairs={{0,24},{4,28},{8,0},{12,4},{16,8},{20,12},{24,16},{28,20},{32,56},... | collective-permute-start | bytes 172040 | tf_op jit(solution)/shard_map/ppermute | solution.py:568
  16.8 0.3 x_solve.1.u
  17.1 2.6 %y_matrix.1 = (f32[128,8,128]{2,1,0:T(8,128)S(1)}, f32[128,8,128]{2,1,0:T(8,128)S(1)}, f32[128,8,128]{2,1,0:T(8,128)S(1)}, f32[52,8,128]{2,1,0:T(8,128)S(1)}, f3...) custom-call(f32[1024,128]{1,0:T(8,128)S(1)} %get-tuple-element.50.k), custom_call_target="tpu_custom_call" | custom-call | flops 2000000 | bytes 1048576 | tf_op jit(solution)/shard_map/y_matrix/pallas_call | solution.py:33
  19.8 0.0 collective-permute-done.3.r1.z1
  19.8 0.0 collective-permute-done.4.r2.z2
  19.8 0.0 collective-permute-done.5.r3.z3
  19.8 0.1 four.1.own_y
  19.9 3.3 %collective-permute-start.6 = (f32[7,16,128]{2,1,0:T(8,128)S(1)}, f32[7,16,128]{2,1,0:T(8,128)S(1)}, u32[]{:S(2)}, u32[]{:S(2)}) collective-permute-start(f32[7,16,128]{2,1,0:T(8,128)S(1)} %four.1.own_y), channel_id=1, source_target_pairs={{0,64},{4,68},{8,72},{12,76},{16,80},{20,84},{24,88},{28,92},{32,9... | collective-permute-start | bytes 172040 | tf_op jit(solution)/shard_map/ppermute | solution.py:568
  23.1 0.7 %collective-permute-start.7 = (f32[7,16,128]{2,1,0:T(8,128)S(1)}, f32[7,16,128]{2,1,0:T(8,128)S(1)}, u32[]{:S(2)}, u32[]{:S(2)}) collective-permute-start(f32[7,16,128]{2,1,0:T(8,128)S(1)} %four.1.own_y), channel_id=1, source_target_pairs={{0,32},{4,36},{8,40},{12,44},{16,48},{20,52},{24,56},{28,60},{32,6... | collective-permute-start | bytes 172040 | tf_op jit(solution)/shard_map/ppermute | solution.py:568
  23.8 2.6 %collective-permute-start.8 = (f32[7,16,128]{2,1,0:T(8,128)S(1)}, f32[7,16,128]{2,1,0:T(8,128)S(1)}, u32[]{:S(2)}, u32[]{:S(2)}) collective-permute-start(f32[7,16,128]{2,1,0:T(8,128)S(1)} %four.1.own_y), channel_id=1, source_target_pairs={{0,96},{4,100},{8,104},{12,108},{16,112},{20,116},{24,120},{28,124... | collective-permute-start | bytes 172040 | tf_op jit(solution)/shard_map/ppermute | solution.py:568
  26.4 0.6 %blend.1 = (f32[1024,128]{1,0:T(8,128)S(1)}, f32[1024,128]{1,0:T(8,128)S(1)}, f32[1024,128]{1,0:T(8,128)S(1)}, f32[4,1024,128]{2,1,0:T(8,128)S(1)}, f32[8,128]{1,0:T(8,128)S(1)}) custom-call(f32[64,16,128]{2,1,0:T(8,128)S(1)} %x_solve.1.u, f32[64,16,128]{2,1,0:T(8,128)S(1)} %get-tuple-element.43.lo.x_lo, f32[64,16,128]{2,1,0:T(8,128)S(1)} %get-tuple-element.44.hi.x_hi, ...), custom_call_target="tpu_custom_call" | custom-call | flops 2000000 | bytes 1048576 | tf_op jit(solution)/shard_map/blend/pallas_call | solution.py:33
  26.9 0.0 collective-permute-done.6.y1
  26.9 1.6 %collective-permute-done.7.y2 = f32[7,16,128]{2,1,0:T(8,128)S(1)} collective-permute-done((f32[7,16,128]{2,1,0:T(8,128)S(1)}, f32[7,16,128]{2,1,0:T(8,128)S(1)}, u32[]{:S(2)}, u32[]{:S(2)}) %collective-permute-start.7) | collective-permute-done | bytes 57376 | tf_op jit(solution)/shard_map/ppermute | solution.py:568
  28.5 0.0 collective-permute-done.8.y3
  28.5 0.4 %y_port.1 = (f32[8,128]{1,0:T(8,128)S(1)}, f32[2,16,128]{2,1,0:T(8,128)S(1)}) custom-call(f32[7,16,128]{2,1,0:T(8,128)S(1)} %four.1.own_y, f32[7,16,128]{2,1,0:T(8,128)S(1)} %collective-permute-done.6.y1, f32[7,16,128]{2,1,0:T(8,128)S(1)} %collective-permute-done.7.y2, f32[7,16,128]{2,1,0:T(8,128)S(1)} %collective-permute-done.8.y3, ...), custom_call_target="tpu_custom_call" | custom-call | flops 2000000 | bytes 1048576 | tf_op jit(solution)/shard_map/y_port/pallas_call | solution.py:33
  29.0 0.4 collective-permute-start.10
  29.3 2.9 %collective-permute-start.11 = (f32[8,128]{1,0:T(8,128)S(1)}, f32[8,128]{1,0:T(8,128)S(1)}, u32[]{:S(2)}, u32[]{:S(2)}) collective-permute-start(f32[8,128]{1,0:T(8,128)S(1)} %get-tuple-element.68.own), channel_id=1, source_target_pairs={{0,3},{1,0},{2,1},{3,2},{4,7},{5,4},{6,5},{7,6},{8,11},{9,8},{10,9... | collective-permute-start | bytes 12296 | tf_op jit(solution)/shard_map/ppermute | solution.py:568
  32.2 0.6 %collective-permute-start.9 = (f32[8,128]{1,0:T(8,128)S(1)}, f32[8,128]{1,0:T(8,128)S(1)}, u32[]{:S(2)}, u32[]{:S(2)}) collective-permute-start(f32[8,128]{1,0:T(8,128)S(1)} %get-tuple-element.68.own), channel_id=1, source_target_pairs={{0,2},{1,3},{2,0},{3,1},{4,6},{5,7},{6,4},{7,5},{8,10},{9,11},{10,... | collective-permute-start | bytes 12296 | tf_op jit(solution)/shard_map/ppermute | solution.py:568
  32.8 1.5 %y_solve.1.base = f32[64,2048]{1,0:T(8,128)S(1)} custom-call(f32[1024,128]{1,0:T(8,128)S(1)} %get-tuple-element.69.source, f32[1024,128]{1,0:T(8,128)S(1)} %get-tuple-element.70.lo, f32[1024,128]{1,0:T(8,128)S(1)} %get-tuple-element.71.hi, f32[2,16,128]{2,1,0:T(8,128)S(1)} %get-tuple-element.72.flow, f32[128,8,128]{2,1,0:T(8,128)S(1)} %get-tuple-element.73.along, ...), custom_call_target="tpu_custom_call" | custom-call | flops 2000000 | bytes 1048576 | tf_op jit(solution)/shard_map/y_solve/pallas_call | solution.py:33
  34.3 0.0 collective-permute-done.10.r2
  34.3 0.0 collective-permute-done.11.r3
  34.3 3.0 %collective-permute-done.9.r1 = f32[8,128]{1,0:T(8,128)S(1)} collective-permute-done((f32[8,128]{1,0:T(8,128)S(1)}, f32[8,128]{1,0:T(8,128)S(1)}, u32[]{:S(2)}, u32[]{:S(2)}) %collective-permute-start.9) | collective-permute-done | bytes 4128 | tf_op jit(solution)/shard_map/ppermute | solution.py:568
  37.3 1.1 %finish.1 = f32[64,2048]{1,0:T(8,128)} custom-call(f32[8,128]{1,0:T(8,128)S(1)} %get-tuple-element.68.own, f32[8,128]{1,0:T(8,128)S(1)} %collective-permute-done.9.r1, f32[8,128]{1,0:T(8,128)S(1)} %collective-permute-done.10.r2, f32[8,128]{1,0:T(8,128)S(1)} %collective-permute-done.11.r3, f32[64,2048]{1,0:T(8,128)S(1)} %y_solve.1.base, ...), custom_call_target="tpu_custom_call" | custom-call | flops 2000000 | bytes 1048576 | tf_op jit(solution)/shard_map/finish/pallas_call | solution.py:33
  (1 shorter events, 0.0 us)
Async XLA Ops:
  1.6 6.5 %collective-permute-start = (f32[8,128]{1,0:T(8,128)}, f32[8,128]{1,0:T(8,128)S(1)}, u32[]{:S(2)}, u32[]{:S(2)}) collective-permute-start(f32[8,128]{1,0:T(8,128)} %get-tuple-element.46), channel_id=1, source_target_pairs={{0,1},{1,2},{2,3},{3,0},{4,5},{5,6},{6,7},{7,4},{8,9},{9,10},{10,1... | collective-permute-start | bytes 12296 | tf_op jit(solution)/shard_map/ppermute | solution.py:568
  3.2 4.9 %collective-permute-start.1 = (f32[8,128]{1,0:T(8,128)}, f32[8,128]{1,0:T(8,128)S(1)}, u32[]{:S(2)}, u32[]{:S(2)}) collective-permute-start(f32[8,128]{1,0:T(8,128)} %get-tuple-element.47), channel_id=1, source_target_pairs={{0,3},{1,0},{2,1},{3,2},{4,7},{5,4},{6,5},{7,6},{8,11},{9,8},{10,9... | collective-permute-start | bytes 12296 | tf_op jit(solution)/shard_map/ppermute | solution.py:568
  4.9 1.0 %copy-start = (f32[1,64,2048]{2,1,0:T(8,128)S(1)}, f32[1,64,2048]{2,1,0:T(8,128)}, u32[]{:S(2)}) copy-start(f32[1,64,2048]{2,1,0:T(8,128)} %param.2) | copy-start | bytes 1572868
  5.9 1.0 %copy-start.1 = (f32[1,64,2048]{2,1,0:T(8,128)S(1)}, f32[1,64,2048]{2,1,0:T(8,128)}, u32[]{:S(2)}) copy-start(f32[1,64,2048]{2,1,0:T(8,128)} %param.3) | copy-start | bytes 1572868
  8.2 1.3 %collective-permute-start.2 = (f32[7,16,128]{2,1,0:T(8,128)S(1)}, f32[7,16,128]{2,1,0:T(8,128)S(1)}, u32[]{:S(2)}, u32[]{:S(2)}) collective-permute-start(f32[7,16,128]{2,1,0:T(8,128)S(1)} %get-tuple-element.48.own), channel_id=1, source_target_pairs={{0,4},{4,0},{8,12},{12,8},{16,20},{20,16},{24,28},{28,24},{32,36},... | collective-permute-start | bytes 172040 | tf_op jit(solution)/shard_map/ppermute | solution.py:615
  9.5 10.2 %collective-permute-start.3 = (f32[7,16,128]{2,1,0:T(8,128)S(1)}, f32[7,16,128]{2,1,0:T(8,128)S(1)}, u32[]{:S(2)}, u32[]{:S(2)}) collective-permute-start(f32[7,16,128]{2,1,0:T(8,128)S(1)} %pair.1.own.own_z), channel_id=1, source_target_pairs={{0,16},{4,20},{8,24},{12,28},{16,0},{20,4},{24,8},{28,12},{32,48},... | collective-permute-start | bytes 172040 | tf_op jit(solution)/shard_map/ppermute | solution.py:568
  13.6 6.2 %collective-permute-start.4 = (f32[7,16,128]{2,1,0:T(8,128)S(1)}, f32[7,16,128]{2,1,0:T(8,128)S(1)}, u32[]{:S(2)}, u32[]{:S(2)}) collective-permute-start(f32[7,16,128]{2,1,0:T(8,128)S(1)} %pair.1.own.own_z), channel_id=1, source_target_pairs={{0,8},{4,12},{8,16},{12,20},{16,24},{20,28},{24,0},{28,4},{32,40},... | collective-permute-start | bytes 172040 | tf_op jit(solution)/shard_map/ppermute | solution.py:568
  14.6 5.2 %collective-permute-start.5 = (f32[7,16,128]{2,1,0:T(8,128)S(1)}, f32[7,16,128]{2,1,0:T(8,128)S(1)}, u32[]{:S(2)}, u32[]{:S(2)}) collective-permute-start(f32[7,16,128]{2,1,0:T(8,128)S(1)} %pair.1.own.own_z), channel_id=1, source_target_pairs={{0,24},{4,28},{8,0},{12,4},{16,8},{20,12},{24,16},{28,20},{32,56},... | collective-permute-start | bytes 172040 | tf_op jit(solution)/shard_map/ppermute | solution.py:568
  19.9 7.1 %collective-permute-start.6 = (f32[7,16,128]{2,1,0:T(8,128)S(1)}, f32[7,16,128]{2,1,0:T(8,128)S(1)}, u32[]{:S(2)}, u32[]{:S(2)}) collective-permute-start(f32[7,16,128]{2,1,0:T(8,128)S(1)} %four.1.own_y), channel_id=1, source_target_pairs={{0,64},{4,68},{8,72},{12,76},{16,80},{20,84},{24,88},{28,92},{32,9... | collective-permute-start | bytes 172040 | tf_op jit(solution)/shard_map/ppermute | solution.py:568
  23.1 5.4 %collective-permute-start.7 = (f32[7,16,128]{2,1,0:T(8,128)S(1)}, f32[7,16,128]{2,1,0:T(8,128)S(1)}, u32[]{:S(2)}, u32[]{:S(2)}) collective-permute-start(f32[7,16,128]{2,1,0:T(8,128)S(1)} %four.1.own_y), channel_id=1, source_target_pairs={{0,32},{4,36},{8,40},{12,44},{16,48},{20,52},{24,56},{28,60},{32,6... | collective-permute-start | bytes 172040 | tf_op jit(solution)/shard_map/ppermute | solution.py:568
  23.8 4.7 %collective-permute-start.8 = (f32[7,16,128]{2,1,0:T(8,128)S(1)}, f32[7,16,128]{2,1,0:T(8,128)S(1)}, u32[]{:S(2)}, u32[]{:S(2)}) collective-permute-start(f32[7,16,128]{2,1,0:T(8,128)S(1)} %four.1.own_y), channel_id=1, source_target_pairs={{0,96},{4,100},{8,104},{12,108},{16,112},{20,116},{24,120},{28,124... | collective-permute-start | bytes 172040 | tf_op jit(solution)/shard_map/ppermute | solution.py:568
  29.0 5.4 %collective-permute-start.10 = (f32[8,128]{1,0:T(8,128)S(1)}, f32[8,128]{1,0:T(8,128)S(1)}, u32[]{:S(2)}, u32[]{:S(2)}) collective-permute-start(f32[8,128]{1,0:T(8,128)S(1)} %get-tuple-element.68.own), channel_id=1, source_target_pairs={{0,1},{1,2},{2,3},{3,0},{4,5},{5,6},{6,7},{7,4},{8,9},{9,10},{10,1... | collective-permute-start | bytes 12296 | tf_op jit(solution)/shard_map/ppermute | solution.py:568
  29.3 5.0 %collective-permute-start.11 = (f32[8,128]{1,0:T(8,128)S(1)}, f32[8,128]{1,0:T(8,128)S(1)}, u32[]{:S(2)}, u32[]{:S(2)}) collective-permute-start(f32[8,128]{1,0:T(8,128)S(1)} %get-tuple-element.68.own), channel_id=1, source_target_pairs={{0,3},{1,0},{2,1},{3,2},{4,7},{5,4},{6,5},{7,6},{8,11},{9,8},{10,9... | collective-permute-start | bytes 12296 | tf_op jit(solution)/shard_map/ppermute | solution.py:568
  32.2 5.1 %collective-permute-start.9 = (f32[8,128]{1,0:T(8,128)S(1)}, f32[8,128]{1,0:T(8,128)S(1)}, u32[]{:S(2)}, u32[]{:S(2)}) collective-permute-start(f32[8,128]{1,0:T(8,128)S(1)} %get-tuple-element.68.own), channel_id=1, source_target_pairs={{0,2},{1,3},{2,0},{3,1},{4,6},{5,7},{6,4},{7,5},{8,10},{9,11},{10,... | collective-permute-start | bytes 12296 | tf_op jit(solution)/shard_map/ppermute | solution.py:568

commit v5 on v4

--- a/solution.py
+++ b/solution.py
@@ -10,6 +10,7 @@
 SEGMENTS = 4
 Y_STEPS = 128
 X_LEVELS, Y_LEVELS = 2, 6
+GRANT = (527 << 20) // 10
 RING = (2, 1, 3)
 F32 = jnp.float32
 VMEM = pl.BlockSpec(memory_space=pltpu.VMEM)
@@ -166,22 +167,24 @@
     return ref[pl.ds((i // 8) * (8 * TILES) + i % 8, TILES, stride=8), :]
 
 
-def edges_kernel(t, k, lo, hi, strips, arrived):
-    sides = (pl.ds(0, 128), pl.ds(128 * (TILES - 1), 128))
-    copies = [
-        pltpu.make_async_copy(ref.at[:, side], strips.at[n], arrived.at[n])
-        for n, (side, ref) in enumerate((side, ref) for side in sides for ref in (t, k))
-    ]
-    for copy in copies:
-        copy.start()
-    lo[...] = jnp.zeros_like(lo)
-    hi[...] = jnp.zeros_like(hi)
+def load_kernel(t_far, k_far, t, k, lo, hi, own, arrived):
+    copies = []
+    for band in range(BANDS):
+        at = pl.ds(8 * band, 8)
+        for n, (far, near) in enumerate(((t_far, t), (k_far, k))):
+            copy = pltpu.make_async_copy(far.at[at, :], near.at[at, :], arrived.at[n, band])
+            copy.start()
+            copies.append(copy)
+    for ref in (lo, hi, own):
+        ref[...] = jnp.zeros_like(ref)
     for copy in copies:
         copy.wait()
-    lo[0:1, 0:ROWS] = strips[0].T[0:1, :]
-    lo[1:2, 0:ROWS] = strips[1].T[0:1, :]
-    hi[0:1, 0:ROWS] = strips[2].T[127:128, :]
-    hi[1:2, 0:ROWS] = strips[3].T[127:128, :]
+    for n, (ref, column) in enumerate(((t, 0), (k, 0), (t, TILES - 1), (k, TILES - 1))):
+        strip = ref[:, 128 * column : 128 * column + 128].T
+        at = 127 if column else 0
+        edge = strip[at : at + 1, :]
+        own[n : n + 1, 0:ROWS] = edge
+        (hi if column else lo)[n % 2 : n % 2 + 1, 0:ROWS] = edge
 
 
 def total(terms):
@@ -191,12 +194,7 @@
     return (sums[0] + sums[1]) + (sums[2] + sums[3])
 
 
-def x_matrix_kernel(t, k, e, along, back, gain, sep, lo, hi, ends, t_flat, flat, own):
-    own[...] = jnp.zeros_like(own)
-    for n, (ref, column) in enumerate(((t, 0), (k, 0), (t, TILES - 1), (k, TILES - 1))):
-        strip = ref[:, 128 * column : 128 * column + 128].T
-        at = 127 if column else 0
-        own[n : n + 1, 0:ROWS] = strip[at : at + 1, :]
+def x_matrix_kernel(t, k, e, along, back, gain, sep, lo, hi, ends, t_flat, flat):
     lane = lax.broadcasted_iota(jnp.int32, (8, 128), 1)
     for band in range(BANDS):
         ks = [tile(k, band, c) for c in range(TILES)]
@@ -399,8 +397,8 @@
     return store
 
 
-def y_matrix_kernel(k, along, back, gain, sep, lo, hi, flat_lo, flat_hi, ends, turned):
-    to_runs(lambda band, column: flat_tile(k, band, column), turned)
+def y_matrix_kernel(k, along, back, gain, sep, lo, hi, ends, turned):
+    to_runs(lambda band, column: tile(k, band, column), turned)
     lane = lax.broadcasted_iota(jnp.int32, (8, 128), 1)
     sublane = lax.broadcasted_iota(jnp.int32, (8, 128), 0)
     very_last = (lane >= 64) & (sublane == 7)
@@ -436,10 +434,13 @@
     ends[2:3, :] = pltpu.roll(hi[last], 64, 1)[7:8, :]
     ends[3:4, :] = cell(turned, 0)[0:1, :]
     ends[4:5, :] = pltpu.roll(cell(turned, last), 64, 1)[7:8, :]
-    for response, flat in ((lo, flat_lo), (hi, flat_hi)):
+
+
+def upright_kernel(lo, hi, flat_lo, flat_hi, turned):
+    for n, (response, flat) in enumerate(((lo, flat_lo), (hi, flat_hi))):
         for l in range(Y_STEPS):
-            turned[pl.ds(l, 8, stride=128), :] = response[l]
-        from_runs(turned, put(flat))
+            turned[n, pl.ds(l, 8, stride=128), :] = response[l]
+        from_runs(turned.at[n], put(flat))
 
 
 def blend_kernel(u, x_lo, x_hi, y_lo, y_hi, t, source, lo, hi, mixed, known, flat, side):
@@ -570,22 +571,23 @@
 
 def per_device(initial_heat_state, thermal_coefficient):
     t, k = initial_heat_state[0], thermal_coefficient[0]
-    own_lo, own_hi = call(
-        edges_kernel,
-        [struct(8, 128)] * 2,
-        [pltpu.VMEM((4, ROWS, 128), F32), pltpu.SemaphoreType.DMA((4,))],
-        name="edges",
-        grant=56 << 20,
+    natural = struct(ROWS, COLS)
+    t, k, own_lo, own_hi, own_edges = call(
+        load_kernel,
+        [natural, natural] + [struct(8, 128)] * 3,
+        [pltpu.SemaphoreType.DMA((2, BANDS))],
+        name="load",
+        grant=GRANT,
         in_specs=[HBM, HBM],
-        out_specs=[VMEM, VMEM],
+        out_specs=[VMEM] * 5,
     )(t, k)
     below = around(own_hi, "gy", 4, 1, 1)
     above = around(own_lo, "gy", 4, 1, 3)
     flat = struct(BANDS * TILES * 8, 128)
     runs = struct(TILES // 2 * 128, 128)
-    x_field, y_field, natural = struct(ROWS, TILES, 128), struct(Y_STEPS, 8, 128), struct(ROWS, COLS)
+    x_field, y_field = struct(ROWS, TILES, 128), struct(Y_STEPS, 8, 128)
     x_port = struct(7, TILES, 128)
-    e, *x_coefficients, x_lo, x_hi, x_ends, t_flat, k_flat, own = call(
+    e, *x_coefficients, x_lo, x_hi, x_ends, t_flat, k_flat = call(
         x_matrix_kernel,
         [
             flat,
@@ -598,25 +600,10 @@
             x_port,
             flat,
             flat,
-            struct(8, 128),
         ],
         name="x_matrix",
     )(t, k)
-    own, edge = call(
-        x_port_kernel,
-        [x_port, struct(ROWS, 128)],
-        [pltpu.VMEM((128, 128), F32)],
-        flops=200_000,
-        name="x_port",
-    )(x_ends, x_lo, x_hi, own, below, above)
-    u = call(x_solve_kernel, x_field, [scratch(flat)], flops=700_000, name="x_solve")(
-        e, *x_coefficients, edge
-    )
-    other = lax.ppermute(own, "gx", [(i, i ^ 1) for i in range(32)])
-    own_z = call(pair_kernel, x_port, name="pair")(own, other)
-    k_y, own_z = lax.optimization_barrier((k_flat, own_z))
-    from_z = [around(own_z, "gx", 32, 2, s) for s in RING]
-    *y_coefficients, y_lo, y_hi, flat_lo, flat_hi, y_ends = call(
+    *y_coefficients, y_lo, y_hi, y_ends = call(
         y_matrix_kernel,
         [
             y_field,
@@ -625,14 +612,33 @@
             struct((2 * Y_LEVELS + 1) * SEGMENTS, 8, 128),
             y_field,
             y_field,
-            natural,
-            natural,
             struct(8, 128),
         ],
         [scratch(runs)],
         name="y_matrix",
-    )(k_y)
-    *from_z, y_ends, u = lax.optimization_barrier((*from_z, y_ends, u))
+    )(k)
+    below, above, y_lo = lax.optimization_barrier((below, above, y_lo))
+    own, edge = call(
+        x_port_kernel,
+        [x_port, struct(ROWS, 128)],
+        [pltpu.VMEM((128, 128), F32)],
+        flops=200_000,
+        name="x_port",
+    )(x_ends, x_lo, x_hi, own_edges, below, above)
+    u = call(x_solve_kernel, x_field, [scratch(flat)], flops=700_000, name="x_solve")(
+        e, *x_coefficients, edge
+    )
+    other = lax.ppermute(own, "gx", [(i, i ^ 1) for i in range(32)])
+    other, u = lax.optimization_barrier((other, u))
+    own_z = call(pair_kernel, x_port, name="pair")(own, other)
+    from_z = [around(own_z, "gx", 32, 2, s) for s in RING]
+    flat_lo, flat_hi = call(
+        upright_kernel,
+        [natural, natural],
+        [pltpu.VMEM((2, TILES // 2 * 128, 128), F32)],
+        name="upright",
+    )(y_lo, y_hi)
+    *from_z, flat_lo = lax.optimization_barrier((*from_z, flat_lo))
     table = pltpu.VMEM((4, 7, TILES, 128), F32)
     own_y = call(four_kernel, x_port, [table], name="four")(own_z, *from_z)
     from_y = [around(own_y, "gx", 32, 8, s) for s in RING]

time: 38.8 us -> 36.9 us (0.951)
  local copies, waits for them, and re-layouts: 2.08 us -> 0 us
  Pallas kernels: 9.36 us -> 8.77 us
  starting transfers between devices: 21 us -> 21.5 us
    unnamed x4 -> x0, local copies, waits for them, and re-layouts: 2.08 us -> none
    ppermute x11, waiting for transfers between devices: 4.58 us -> 5.24 us  [around(): return lax.ppermute(value, axis, pairs)]
    pallas_call x11 -> x12, Pallas kernels: 9.36 us -> 8.77 us  [run(): pl.pallas_call(kernel, out_shape=outs, **windows or whole(outs, args), sc...]
    ppermute x11, starting transfers between devices: 20.9 us -> 21.4 us  [around(): return lax.ppermute(value, axis, pairs)]
  transfers between devices with their start and end apart: 12 -> 12, of which waited for: 3 -> 4; matrix products, arithmetic and copies ran while one was open for 0% -> 0% of each run, Pallas kernels for 16% -> 15%
where the time goes in v5:
time: 36.9 us; the launch traced here: 36.6 us
  starting transfers between devices  21.5 us (58%)
  Pallas kernels  8.77 us (24%)
  waiting for transfers between devices  6.17 us (17%)
    ppermute x11, starting transfers between devices, around(): return lax.ppermute(value, axis, pairs)  21.4 us
    pallas_call x12, Pallas kernels, run(): pl.pallas_call(kernel, out_shape=outs, **windows or whole(outs, args), sc...  8.77 us
    ppermute x11, waiting for transfers between devices, around(): return lax.ppermute(value, axis, pairs)  5.24 us
    ppermute x1, waiting for transfers between devices, per_device(): other = lax.ppermute(own, 'gx', [(i, i ^ 1) for i in range(32)])  0.93 us
  transfers between devices with their start and end apart: 12, of which 4 were waited for; matrix products, arithmetic and copies ran while one was open for 0% of the time, Pallas kernels for 15%

profile of v5, /device:TPU:0, one launch (start us, length us, event | category | flops | bytes accessed | tf_op | source)
XLA Modules:
  0.0 36.6 jit_solution(701788845566464651)
XLA Ops:
  0.0 1.5 %load.1 = (f32[64,2048]{1,0:T(8,128)S(1)}, f32[64,2048]{1,0:T(8,128)S(1)}, f32[8,128]{1,0:T(8,128)S(1)}, f32[8,128]{1,0:T(8,128)S(1)}, f32[8,128]{1,0:T(8,128)S(1)}) custom-call(f32[64,2048]{1,0:T(8,128)} %bitcast.3, f32[64,2048]{1,0:T(8,128)} %bitcast.4), custom_call_target="tpu_custom_call" | custom-call | flops 2000000 | bytes 1048576 | tf_op jit(solution)/shard_map/load/pallas_call | solution.py:34
  1.5 1.6 %collective-permute-start = (f32[8,128]{1,0:T(8,128)S(1)}, f32[8,128]{1,0:T(8,128)S(1)}, u32[]{:S(2)}, u32[]{:S(2)}) collective-permute-start(f32[8,128]{1,0:T(8,128)S(1)} %get-tuple-element.52), channel_id=1, source_target_pairs={{0,1},{1,2},{2,3},{3,0},{4,5},{5,6},{6,7},{7,4},{8,9},{9,10},{10,1... | collective-permute-start | bytes 12296 | tf_op jit(solution)/shard_map/ppermute | solution.py:569
  3.1 1.7 %collective-permute-start.1 = (f32[8,128]{1,0:T(8,128)S(1)}, f32[8,128]{1,0:T(8,128)S(1)}, u32[]{:S(2)}, u32[]{:S(2)}) collective-permute-start(f32[8,128]{1,0:T(8,128)S(1)} %get-tuple-element.53), channel_id=1, source_target_pairs={{0,3},{1,0},{2,1},{3,2},{4,7},{5,4},{6,5},{7,6},{8,11},{9,8},{10,9... | collective-permute-start | bytes 12296 | tf_op jit(solution)/shard_map/ppermute | solution.py:569
  4.8 1.2 %y_matrix.1 = (f32[128,8,128]{2,1,0:T(8,128)S(1)}, f32[128,8,128]{2,1,0:T(8,128)S(1)}, f32[128,8,128]{2,1,0:T(8,128)S(1)}, f32[52,8,128]{2,1,0:T(8,128)S(1)}, f3...) custom-call(f32[64,2048]{1,0:T(8,128)S(1)} %get-tuple-element.47.k), custom_call_target="tpu_custom_call" | custom-call | flops 2000000 | bytes 1048576 | tf_op jit(solution)/shard_map/y_matrix/pallas_call | solution.py:34
  6.0 1.1 %x_matrix.1 = (f32[1024,128]{1,0:T(8,128)S(1)}, f32[64,16,128]{2,1,0:T(8,128)S(1)}, f32[64,16,128]{2,1,0:T(8,128)S(1)}, f32[64,16,128]{2,1,0:T(8,128)S(1)}, f32[...) custom-call(f32[64,2048]{1,0:T(8,128)S(1)} %get-tuple-element.46.t, ...), custom_call_target="tpu_custom_call" | custom-call | flops 2000000 | bytes 1048576 | tf_op jit(solution)/shard_map/x_matrix/pallas_call | solution.py:34
  7.1 0.0 collective-permute-done.below
  7.1 0.0 collective-permute-done.1.above
  7.1 0.1 x_port.1
  7.2 0.1 collective-permute-start.2
  7.3 0.3 x_solve.1.u
  7.6 0.9 %collective-permute-done.2.other = f32[7,16,128]{2,1,0:T(8,128)S(1)} collective-permute-done((f32[7,16,128]{2,1,0:T(8,128)S(1)}, f32[7,16,128]{2,1,0:T(8,128)S(1)}, u32[]{:S(2)}, u32[]{:S(2)}) %collective-permute-start.2) | collective-permute-done | bytes 57376 | tf_op jit(solution)/shard_map/ppermute | solution.py:631
  8.5 4.0 %collective-permute-start.3 = (f32[7,16,128]{2,1,0:T(8,128)S(1)}, f32[7,16,128]{2,1,0:T(8,128)S(1)}, u32[]{:S(2)}, u32[]{:S(2)}) collective-permute-start(f32[7,16,128]{2,1,0:T(8,128)S(1)} %pair.1.own.own_z), channel_id=1, source_target_pairs={{0,16},{4,20},{8,24},{12,28},{16,0},{20,4},{24,8},{28,12},{32,48},... | collective-permute-start | bytes 172040 | tf_op jit(solution)/shard_map/ppermute | solution.py:569
  12.6 1.0 %collective-permute-start.4 = (f32[7,16,128]{2,1,0:T(8,128)S(1)}, f32[7,16,128]{2,1,0:T(8,128)S(1)}, u32[]{:S(2)}, u32[]{:S(2)}) collective-permute-start(f32[7,16,128]{2,1,0:T(8,128)S(1)} %pair.1.own.own_z), channel_id=1, source_target_pairs={{0,8},{4,12},{8,16},{12,20},{16,24},{20,28},{24,0},{28,4},{32,40},... | collective-permute-start | bytes 172040 | tf_op jit(solution)/shard_map/ppermute | solution.py:569
  13.6 2.2 %collective-permute-start.5 = (f32[7,16,128]{2,1,0:T(8,128)S(1)}, f32[7,16,128]{2,1,0:T(8,128)S(1)}, u32[]{:S(2)}, u32[]{:S(2)}) collective-permute-start(f32[7,16,128]{2,1,0:T(8,128)S(1)} %pair.1.own.own_z), channel_id=1, source_target_pairs={{0,24},{4,28},{8,0},{12,4},{16,8},{20,12},{24,16},{28,20},{32,56},... | collective-permute-start | bytes 172040 | tf_op jit(solution)/shard_map/ppermute | solution.py:569
  15.8 0.9 %upright.1 = (f32[64,2048]{1,0:T(8,128)S(1)}, f32[64,2048]{1,0:T(8,128)S(1)}) custom-call(f32[128,8,128]{2,1,0:T(8,128)S(1)} %get-tuple-element.65.lo, f32[128,8,128]{2,1,0:T(8,128)S(1)} %get-tuple-element.66.hi), custom_call_target="tpu_custom_call" | custom-call | flops 2000000 | bytes 1048576 | tf_op jit(solution)/shard_map/upright/pallas_call | solution.py:34
  16.7 0.0 collective-permute-done.3.r1.z1
  16.7 1.3 %collective-permute-done.4.r2.z2 = f32[7,16,128]{2,1,0:T(8,128)S(1)} collective-permute-done((f32[7,16,128]{2,1,0:T(8,128)S(1)}, f32[7,16,128]{2,1,0:T(8,128)S(1)}, u32[]{:S(2)}, u32[]{:S(2)}) %collective-permute-start.4) | collective-permute-done | bytes 57376 | tf_op jit(solution)/shard_map/ppermute | solution.py:569
  18.0 0.0 collective-permute-done.5.r3.z3
  18.0 0.1 four.1.own_y
  18.0 3.3 %collective-permute-start.6 = (f32[7,16,128]{2,1,0:T(8,128)S(1)}, f32[7,16,128]{2,1,0:T(8,128)S(1)}, u32[]{:S(2)}, u32[]{:S(2)}) collective-permute-start(f32[7,16,128]{2,1,0:T(8,128)S(1)} %four.1.own_y), channel_id=1, source_target_pairs={{0,64},{4,68},{8,72},{12,76},{16,80},{20,84},{24,88},{28,92},{32,9... | collective-permute-start | bytes 172040 | tf_op jit(solution)/shard_map/ppermute | solution.py:569
  21.3 0.7 %collective-permute-start.7 = (f32[7,16,128]{2,1,0:T(8,128)S(1)}, f32[7,16,128]{2,1,0:T(8,128)S(1)}, u32[]{:S(2)}, u32[]{:S(2)}) collective-permute-start(f32[7,16,128]{2,1,0:T(8,128)S(1)} %four.1.own_y), channel_id=1, source_target_pairs={{0,32},{4,36},{8,40},{12,44},{16,48},{20,52},{24,56},{28,60},{32,6... | collective-permute-start | bytes 172040 | tf_op jit(solution)/shard_map/ppermute | solution.py:569
  22.0 2.6 %collective-permute-start.8 = (f32[7,16,128]{2,1,0:T(8,128)S(1)}, f32[7,16,128]{2,1,0:T(8,128)S(1)}, u32[]{:S(2)}, u32[]{:S(2)}) collective-permute-start(f32[7,16,128]{2,1,0:T(8,128)S(1)} %four.1.own_y), channel_id=1, source_target_pairs={{0,96},{4,100},{8,104},{12,108},{16,112},{20,116},{24,120},{28,124... | collective-permute-start | bytes 172040 | tf_op jit(solution)/shard_map/ppermute | solution.py:569
  24.6 0.6 %blend.1 = (f32[1024,128]{1,0:T(8,128)S(1)}, f32[1024,128]{1,0:T(8,128)S(1)}, f32[1024,128]{1,0:T(8,128)S(1)}, f32[4,1024,128]{2,1,0:T(8,128)S(1)}, f32[8,128]{1,0:T(8,128)S(1)}) custom-call(f32[64,16,128]{2,1,0:T(8,128)S(1)} %x_solve.1.u, f32[64,16,128]{2,1,0:T(8,128)S(1)} %get-tuple-element.49.lo.x_lo, f32[64,16,128]{2,1,0:T(8,128)S(1)} %get-tuple-element.50.hi.x_hi, ...), custom_call_target="tpu_custom_call" | custom-call | flops 2000000 | bytes 1048576 | tf_op jit(solution)/shard_map/blend/pallas_call | solution.py:34
  25.2 0.0 collective-permute-done.6.y1
  25.2 1.5 %collective-permute-done.7.y2 = f32[7,16,128]{2,1,0:T(8,128)S(1)} collective-permute-done((f32[7,16,128]{2,1,0:T(8,128)S(1)}, f32[7,16,128]{2,1,0:T(8,128)S(1)}, u32[]{:S(2)}, u32[]{:S(2)}) %collective-permute-start.7) | collective-permute-done | bytes 57376 | tf_op jit(solution)/shard_map/ppermute | solution.py:569
  26.7 0.0 collective-permute-done.8.y3
  26.7 0.4 %y_port.1 = (f32[8,128]{1,0:T(8,128)S(1)}, f32[2,16,128]{2,1,0:T(8,128)S(1)}) custom-call(f32[7,16,128]{2,1,0:T(8,128)S(1)} %four.1.own_y, f32[7,16,128]{2,1,0:T(8,128)S(1)} %collective-permute-done.6.y1, f32[7,16,128]{2,1,0:T(8,128)S(1)} %collective-permute-done.7.y2, f32[7,16,128]{2,1,0:T(8,128)S(1)} %collective-permute-done.8.y3, ...), custom_call_target="tpu_custom_call" | custom-call | flops 2000000 | bytes 1048576 | tf_op jit(solution)/shard_map/y_port/pallas_call | solution.py:34
  27.1 1.1 %collective-permute-start.10 = (f32[8,128]{1,0:T(8,128)S(1)}, f32[8,128]{1,0:T(8,128)S(1)}, u32[]{:S(2)}, u32[]{:S(2)}) collective-permute-start(f32[8,128]{1,0:T(8,128)S(1)} %get-tuple-element.78.own), channel_id=1, source_target_pairs={{0,1},{1,2},{2,3},{3,0},{4,5},{5,6},{6,7},{7,4},{8,9},{9,10},{10,1... | collective-permute-start | bytes 12296 | tf_op jit(solution)/shard_map/ppermute | solution.py:569
  28.2 2.2 %collective-permute-start.11 = (f32[8,128]{1,0:T(8,128)S(1)}, f32[8,128]{1,0:T(8,128)S(1)}, u32[]{:S(2)}, u32[]{:S(2)}) collective-permute-start(f32[8,128]{1,0:T(8,128)S(1)} %get-tuple-element.78.own), channel_id=1, source_target_pairs={{0,3},{1,0},{2,1},{3,2},{4,7},{5,4},{6,5},{7,6},{8,11},{9,8},{10,9... | collective-permute-start | bytes 12296 | tf_op jit(solution)/shard_map/ppermute | solution.py:569
  30.4 1.1 %collective-permute-start.9 = (f32[8,128]{1,0:T(8,128)S(1)}, f32[8,128]{1,0:T(8,128)S(1)}, u32[]{:S(2)}, u32[]{:S(2)}) collective-permute-start(f32[8,128]{1,0:T(8,128)S(1)} %get-tuple-element.78.own), channel_id=1, source_target_pairs={{0,2},{1,3},{2,0},{3,1},{4,6},{5,7},{6,4},{7,5},{8,10},{9,11},{10,... | collective-permute-start | bytes 12296 | tf_op jit(solution)/shard_map/ppermute | solution.py:569
  31.5 1.6 %y_solve.1.base = f32[64,2048]{1,0:T(8,128)S(1)} custom-call(f32[1024,128]{1,0:T(8,128)S(1)} %get-tuple-element.79.source, f32[1024,128]{1,0:T(8,128)S(1)} %get-tuple-element.80.lo, f32[1024,128]{1,0:T(8,128)S(1)} %get-tuple-element.81.hi, f32[2,16,128]{2,1,0:T(8,128)S(1)} %get-tuple-element.82.flow, f32[128,8,128]{2,1,0:T(8,128)S(1)} %get-tuple-element.83.along, ...), custom_call_target="tpu_custom_call" | custom-call | flops 2000000 | bytes 1048576 | tf_op jit(solution)/shard_map/y_solve/pallas_call | solution.py:34
  33.1 0.0 collective-permute-done.10.r2
  33.1 0.0 collective-permute-done.11.r3
  33.1 2.4 %collective-permute-done.9.r1 = f32[8,128]{1,0:T(8,128)S(1)} collective-permute-done((f32[8,128]{1,0:T(8,128)S(1)}, f32[8,128]{1,0:T(8,128)S(1)}, u32[]{:S(2)}, u32[]{:S(2)}) %collective-permute-start.9) | collective-permute-done | bytes 4128 | tf_op jit(solution)/shard_map/ppermute | solution.py:569
  35.5 1.1 %finish.1 = f32[64,2048]{1,0:T(8,128)} custom-call(f32[8,128]{1,0:T(8,128)S(1)} %get-tuple-element.78.own, f32[8,128]{1,0:T(8,128)S(1)} %collective-permute-done.9.r1, f32[8,128]{1,0:T(8,128)S(1)} %collective-permute-done.10.r2, f32[8,128]{1,0:T(8,128)S(1)} %collective-permute-done.11.r3, f32[64,2048]{1,0:T(8,128)S(1)} %y_solve.1.base, ...), custom_call_target="tpu_custom_call" | custom-call | flops 2000000 | bytes 1048576 | tf_op jit(solution)/shard_map/finish/pallas_call | solution.py:34
  (1 shorter events, 0.0 us)
Async XLA Ops:
  1.5 5.6 %collective-permute-start = (f32[8,128]{1,0:T(8,128)S(1)}, f32[8,128]{1,0:T(8,128)S(1)}, u32[]{:S(2)}, u32[]{:S(2)}) collective-permute-start(f32[8,128]{1,0:T(8,128)S(1)} %get-tuple-element.52), channel_id=1, source_target_pairs={{0,1},{1,2},{2,3},{3,0},{4,5},{5,6},{6,7},{7,4},{8,9},{9,10},{10,1... | collective-permute-start | bytes 12296 | tf_op jit(solution)/shard_map/ppermute | solution.py:569
  3.1 3.9 %collective-permute-start.1 = (f32[8,128]{1,0:T(8,128)S(1)}, f32[8,128]{1,0:T(8,128)S(1)}, u32[]{:S(2)}, u32[]{:S(2)}) collective-permute-start(f32[8,128]{1,0:T(8,128)S(1)} %get-tuple-element.53), channel_id=1, source_target_pairs={{0,3},{1,0},{2,1},{3,2},{4,7},{5,4},{6,5},{7,6},{8,11},{9,8},{10,9... | collective-permute-start | bytes 12296 | tf_op jit(solution)/shard_map/ppermute | solution.py:569
  7.2 1.3 %collective-permute-start.2 = (f32[7,16,128]{2,1,0:T(8,128)S(1)}, f32[7,16,128]{2,1,0:T(8,128)S(1)}, u32[]{:S(2)}, u32[]{:S(2)}) collective-permute-start(f32[7,16,128]{2,1,0:T(8,128)S(1)} %get-tuple-element.57.own), channel_id=1, source_target_pairs={{0,4},{4,0},{8,12},{12,8},{16,20},{20,16},{24,28},{28,24},{32,36},... | collective-permute-start | bytes 172040 | tf_op jit(solution)/shard_map/ppermute | solution.py:631
  8.5 8.1 %collective-permute-start.3 = (f32[7,16,128]{2,1,0:T(8,128)S(1)}, f32[7,16,128]{2,1,0:T(8,128)S(1)}, u32[]{:S(2)}, u32[]{:S(2)}) collective-permute-start(f32[7,16,128]{2,1,0:T(8,128)S(1)} %pair.1.own.own_z), channel_id=1, source_target_pairs={{0,16},{4,20},{8,24},{12,28},{16,0},{20,4},{24,8},{28,12},{32,48},... | collective-permute-start | bytes 172040 | tf_op jit(solution)/shard_map/ppermute | solution.py:569
  12.6 5.4 %collective-permute-start.4 = (f32[7,16,128]{2,1,0:T(8,128)S(1)}, f32[7,16,128]{2,1,0:T(8,128)S(1)}, u32[]{:S(2)}, u32[]{:S(2)}) collective-permute-start(f32[7,16,128]{2,1,0:T(8,128)S(1)} %pair.1.own.own_z), channel_id=1, source_target_pairs={{0,8},{4,12},{8,16},{12,20},{16,24},{20,28},{24,0},{28,4},{32,40},... | collective-permute-start | bytes 172040 | tf_op jit(solution)/shard_map/ppermute | solution.py:569
  13.6 4.4 %collective-permute-start.5 = (f32[7,16,128]{2,1,0:T(8,128)S(1)}, f32[7,16,128]{2,1,0:T(8,128)S(1)}, u32[]{:S(2)}, u32[]{:S(2)}) collective-permute-start(f32[7,16,128]{2,1,0:T(8,128)S(1)} %pair.1.own.own_z), channel_id=1, source_target_pairs={{0,24},{4,28},{8,0},{12,4},{16,8},{20,12},{24,16},{28,20},{32,56},... | collective-permute-start | bytes 172040 | tf_op jit(solution)/shard_map/ppermute | solution.py:569
  18.0 7.1 %collective-permute-start.6 = (f32[7,16,128]{2,1,0:T(8,128)S(1)}, f32[7,16,128]{2,1,0:T(8,128)S(1)}, u32[]{:S(2)}, u32[]{:S(2)}) collective-permute-start(f32[7,16,128]{2,1,0:T(8,128)S(1)} %four.1.own_y), channel_id=1, source_target_pairs={{0,64},{4,68},{8,72},{12,76},{16,80},{20,84},{24,88},{28,92},{32,9... | collective-permute-start | bytes 172040 | tf_op jit(solution)/shard_map/ppermute | solution.py:569
  21.3 5.4 %collective-permute-start.7 = (f32[7,16,128]{2,1,0:T(8,128)S(1)}, f32[7,16,128]{2,1,0:T(8,128)S(1)}, u32[]{:S(2)}, u32[]{:S(2)}) collective-permute-start(f32[7,16,128]{2,1,0:T(8,128)S(1)} %four.1.own_y), channel_id=1, source_target_pairs={{0,32},{4,36},{8,40},{12,44},{16,48},{20,52},{24,56},{28,60},{32,6... | collective-permute-start | bytes 172040 | tf_op jit(solution)/shard_map/ppermute | solution.py:569
  22.0 4.7 %collective-permute-start.8 = (f32[7,16,128]{2,1,0:T(8,128)S(1)}, f32[7,16,128]{2,1,0:T(8,128)S(1)}, u32[]{:S(2)}, u32[]{:S(2)}) collective-permute-start(f32[7,16,128]{2,1,0:T(8,128)S(1)} %four.1.own_y), channel_id=1, source_target_pairs={{0,96},{4,100},{8,104},{12,108},{16,112},{20,116},{24,120},{28,124... | collective-permute-start | bytes 172040 | tf_op jit(solution)/shard_map/ppermute | solution.py:569
  27.1 5.9 %collective-permute-start.10 = (f32[8,128]{1,0:T(8,128)S(1)}, f32[8,128]{1,0:T(8,128)S(1)}, u32[]{:S(2)}, u32[]{:S(2)}) collective-permute-start(f32[8,128]{1,0:T(8,128)S(1)} %get-tuple-element.78.own), channel_id=1, source_target_pairs={{0,1},{1,2},{2,3},{3,0},{4,5},{5,6},{6,7},{7,4},{8,9},{9,10},{10,1... | collective-permute-start | bytes 12296 | tf_op jit(solution)/shard_map/ppermute | solution.py:569
  28.2 4.9 %collective-permute-start.11 = (f32[8,128]{1,0:T(8,128)S(1)}, f32[8,128]{1,0:T(8,128)S(1)}, u32[]{:S(2)}, u32[]{:S(2)}) collective-permute-start(f32[8,128]{1,0:T(8,128)S(1)} %get-tuple-element.78.own), channel_id=1, source_target_pairs={{0,3},{1,0},{2,1},{3,2},{4,7},{5,4},{6,5},{7,6},{8,11},{9,8},{10,9... | collective-permute-start | bytes 12296 | tf_op jit(solution)/shard_map/ppermute | solution.py:569
  30.4 5.1 %collective-permute-start.9 = (f32[8,128]{1,0:T(8,128)S(1)}, f32[8,128]{1,0:T(8,128)S(1)}, u32[]{:S(2)}, u32[]{:S(2)}) collective-permute-start(f32[8,128]{1,0:T(8,128)S(1)} %get-tuple-element.78.own), channel_id=1, source_target_pairs={{0,2},{1,3},{2,0},{3,1},{4,6},{5,7},{6,4},{7,5},{8,10},{9,11},{10,... | collective-permute-start | bytes 12296 | tf_op jit(solution)/shard_map/ppermute | solution.py:569

commit v6 on v5

--- a/solution.py
+++ b/solution.py
@@ -252,7 +252,7 @@
     ends[6] = row(flat, ROWS - 1)
 
 
-def x_port_kernel(ends, lo, hi, own, below, above, port, edge, side):
+def x_port_kernel(ends, lo, hi, own, below, above, keep, give, edge, port, side):
     at = lax.axis_index("gy")
     side[...] = jnp.zeros_like(side)
     t_lo, k_lo, t_hi, k_hi = (own[n : n + 1, :] for n in range(4))
@@ -268,8 +268,14 @@
             term = edge[...] * response[:, column, :]
             term = jnp.where(lane == kept, jnp.sum(term, axis=0, keepdims=True), 0.0)
             port[n, column : column + 1, :] = port[n, column : column + 1, :] + term
-    for n in range(2, 7):
-        port[n] = ends[n]
+    core = lax.rem(lax.axis_index("gx"), 2)
+    for n in range(7):
+        ref = port if n < 2 else ends
+        keep[n], give[n] = choose(core == 0, halves(ref, n), halves(ref, n)[::-1])
+
+
+def halves(ref, n):
+    return ref[n, : TILES // 2, :], ref[n, TILES // 2 :, :]
 
 
 def x_solve_kernel(e, along, back, gain, sep, edge, u, flat):
@@ -464,22 +470,31 @@
     known[...] = jnp.broadcast_to(jnp.sum(side[...].T, axis=0, keepdims=True), (8, 128))
 
 
-def y_port_kernel(
-    own_y, y1, y2, y3, own_z, z1, z2, z3, own, other, mixed, known, ends,
-    port, flow, table_y, table_z, side,
+def through_kernel(
+    own_y, y1, y2, y3, own_z, z1, z2, z3, own, other, keep, give, table_y, table_z
 ):
     index = lax.axis_index("gx")
     core, z, y = lax.rem(index, 2), lax.rem(lax.div(index, 2), 4), lax.div(index, 8)
     place(y, own_y, (y1, y2, y3), table_y)
     place(z, own_z, (z1, z2, z3), table_z)
-    nothing = (jnp.zeros((TILES, 128), F32),) * 3
+    nothing = (jnp.zeros(own.shape[1:], F32),) * 3
     scale = 1000.0
     lo, hi = reach(y, [take(table_y.at[j]) for j in range(4)], nothing, nothing, scale)
     lo, hi = reach(z, [take(table_z.at[j]) for j in range(4)], lo, hi, scale)
     mine, theirs = take(own), take(other)
-    lo = choose(core == 1, past_up(lo, theirs, scale), lo)
-    hi = choose(core == 0, past_down(hi, theirs, scale), hi)
-    flow[0], flow[1] = flows(mine, lo, hi, scale)
+    first = choose(core == 0, mine, theirs)
+    second = choose(core == 0, theirs, mine)
+    at_first = flows(first, lo, past_down(hi, second, scale), scale)
+    at_second = flows(second, past_up(lo, first, scale), hi, scale)
+    keep[0], keep[1] = choose(core == 0, at_first, at_second)
+    give[0], give[1] = choose(core == 0, at_second, at_first)
+
+
+def y_port_kernel(keep, got, mixed, known, ends, port, flow, side):
+    core = lax.rem(lax.axis_index("gx"), 2)
+    for n in range(2):
+        flow[n, : TILES // 2, :] = jnp.where(core == 0, keep[n], got[n])
+        flow[n, TILES // 2 :, :] = jnp.where(core == 0, got[n], keep[n])
     sums = [None] * (2 * BANDS)
     for column in range(TILES):
         down, up = across(flow, column)
@@ -618,19 +633,21 @@
         name="y_matrix",
     )(k)
     below, above, y_lo = lax.optimization_barrier((below, above, y_lo))
-    own, edge = call(
+    half = struct(7, TILES // 2, 128)
+    own, give, edge = call(
         x_port_kernel,
-        [x_port, struct(ROWS, 128)],
-        [pltpu.VMEM((128, 128), F32)],
+        [half, half, struct(ROWS, 128)],
+        [scratch(x_port), pltpu.VMEM((128, 128), F32)],
         flops=200_000,
         name="x_port",
     )(x_ends, x_lo, x_hi, own_edges, below, above)
     u = call(x_solve_kernel, x_field, [scratch(flat)], flops=700_000, name="x_solve")(
         e, *x_coefficients, edge
     )
-    other = lax.ppermute(own, "gx", [(i, i ^ 1) for i in range(32)])
+    pairs = [(i, i ^ 1) for i in range(32)]
+    other = lax.ppermute(give, "gx", pairs)
     other, u = lax.optimization_barrier((other, u))
-    own_z = call(pair_kernel, x_port, name="pair")(own, other)
+    own_z = call(pair_kernel, half, name="pair")(own, other)
     from_z = [around(own_z, "gx", 32, 2, s) for s in RING]
     flat_lo, flat_hi = call(
         upright_kernel,
@@ -639,8 +656,8 @@
         name="upright",
     )(y_lo, y_hi)
     *from_z, flat_lo = lax.optimization_barrier((*from_z, flat_lo))
-    table = pltpu.VMEM((4, 7, TILES, 128), F32)
-    own_y = call(four_kernel, x_port, [table], name="four")(own_z, *from_z)
+    table = pltpu.VMEM((4, 7, TILES // 2, 128), F32)
+    own_y = call(four_kernel, half, [table], name="four")(own_z, *from_z)
     from_y = [around(own_y, "gx", 32, 8, s) for s in RING]
     square = pltpu.VMEM((128, 128), F32)
     source, lo_flat, hi_flat, mixed, known = call(
@@ -649,12 +666,14 @@
         [scratch(flat), square],
         name="blend",
     )(u, x_lo, x_hi, flat_lo, flat_hi, t_flat)
+    some = struct(2, TILES // 2, 128)
+    keep, give = call(through_kernel, [some, some], [table, table], name="through")(
+        own_y, *from_y, own_z, *from_z, own, other
+    )
+    got = lax.ppermute(give, "gx", pairs)
     port, flow = call(
-        y_port_kernel,
-        [struct(8, 128), struct(2, TILES, 128)],
-        [table, table, square],
-        name="y_port",
-    )(own_y, *from_y, own_z, *from_z, own, other, mixed, known, y_ends)
+        y_port_kernel, [struct(8, 128), struct(2, TILES, 128)], [square], name="y_port"
+    )(keep, got, mixed, known, y_ends)
     from_gy = [around(port, "gy", 4, 1, s) for s in RING]
     base = call(
         y_solve_kernel, natural, [scratch(y_field), scratch(runs)], name="y_solve"

time: 36.9 us -> 37.8 us (1.024)
  the two profiles are of different devices: /device:TPU:0 before, /device:TPU:30 now
where the time goes in v6:
time: 37.8 us; the launch traced here: 37.6 us
  starting transfers between devices  14.8 us (39%)
  waiting for transfers between devices  13.9 us (37%)
  Pallas kernels  8.74 us (23%)
    ppermute x11, starting transfers between devices, around(): return lax.ppermute(value, axis, pairs)  14.6 us
    ppermute x11, waiting for transfers between devices, around(): return lax.ppermute(value, axis, pairs)  12.5 us
    pallas_call x13, Pallas kernels, run(): pl.pallas_call(kernel, out_shape=outs, **windows or whole(outs, args), sc...  8.74 us
    ppermute x1, waiting for transfers between devices, per_device(): other = lax.ppermute(give, 'gx', pairs)  0.89 us
  transfers between devices with their start and end apart: 13, of which 8 were waited for; matrix products, arithmetic and copies ran while one was open for 0% of the time, Pallas kernels for 15%

profile of v6, /device:TPU:30, one launch (start us, length us, event | category | flops | bytes accessed | tf_op | source)
XLA Modules:
  0.0 37.6 jit_solution(7755083858435136098)
XLA Ops:
  0.0 1.5 %load.1 = (f32[64,2048]{1,0:T(8,128)S(1)}, f32[64,2048]{1,0:T(8,128)S(1)}, f32[8,128]{1,0:T(8,128)S(1)}, f32[8,128]{1,0:T(8,128)S(1)}, f32[8,128]{1,0:T(8,128)S(1)}) custom-call(f32[64,2048]{1,0:T(8,128)} %bitcast.3, f32[64,2048]{1,0:T(8,128)} %bitcast.4), custom_call_target="tpu_custom_call" | custom-call | flops 2000000 | bytes 1048576 | tf_op jit(solution)/shard_map/load/pallas_call | solution.py:34
  1.5 0.5 %collective-permute-start = (f32[8,128]{1,0:T(8,128)S(1)}, f32[8,128]{1,0:T(8,128)S(1)}, u32[]{:S(2)}, u32[]{:S(2)}) collective-permute-start(f32[8,128]{1,0:T(8,128)S(1)} %get-tuple-element.55), channel_id=1, source_target_pairs={{0,1},{1,2},{2,3},{3,0},{4,5},{5,6},{6,7},{7,4},{8,9},{9,10},{10,1... | collective-permute-start | bytes 12296 | tf_op jit(solution)/shard_map/ppermute | solution.py:584
  2.0 1.5 %collective-permute-start.1 = (f32[8,128]{1,0:T(8,128)S(1)}, f32[8,128]{1,0:T(8,128)S(1)}, u32[]{:S(2)}, u32[]{:S(2)}) collective-permute-start(f32[8,128]{1,0:T(8,128)S(1)} %get-tuple-element.56), channel_id=1, source_target_pairs={{0,3},{1,0},{2,1},{3,2},{4,7},{5,4},{6,5},{7,6},{8,11},{9,8},{10,9... | collective-permute-start | bytes 12296 | tf_op jit(solution)/shard_map/ppermute | solution.py:584
  3.6 1.2 %y_matrix.1 = (f32[128,8,128]{2,1,0:T(8,128)S(1)}, f32[128,8,128]{2,1,0:T(8,128)S(1)}, f32[128,8,128]{2,1,0:T(8,128)S(1)}, f32[52,8,128]{2,1,0:T(8,128)S(1)}, f3...) custom-call(f32[64,2048]{1,0:T(8,128)S(1)} %get-tuple-element.50.k), custom_call_target="tpu_custom_call" | custom-call | flops 2000000 | bytes 1048576 | tf_op jit(solution)/shard_map/y_matrix/pallas_call | solution.py:34
  4.8 1.1 %x_matrix.1 = (f32[1024,128]{1,0:T(8,128)S(1)}, f32[64,16,128]{2,1,0:T(8,128)S(1)}, f32[64,16,128]{2,1,0:T(8,128)S(1)}, f32[64,16,128]{2,1,0:T(8,128)S(1)}, f32[...) custom-call(f32[64,2048]{1,0:T(8,128)S(1)} %get-tuple-element.49.t, ...), custom_call_target="tpu_custom_call" | custom-call | flops 2000000 | bytes 1048576 | tf_op jit(solution)/shard_map/x_matrix/pallas_call | solution.py:34
  5.9 0.0 collective-permute-done.below
  5.9 1.0 %collective-permute-done.1.above = f32[8,128]{1,0:T(8,128)S(1)} collective-permute-done((f32[8,128]{1,0:T(8,128)S(1)}, f32[8,128]{1,0:T(8,128)S(1)}, u32[]{:S(2)}, u32[]{:S(2)}) %collective-permute-start.1) | collective-permute-done | bytes 4128 | tf_op jit(solution)/shard_map/ppermute | solution.py:584
  6.9 0.1 x_port.1
  7.0 0.1 collective-permute-start.2
  7.1 0.3 x_solve.1.u
  7.4 0.9 %collective-permute-done.2.other = f32[7,8,128]{2,1,0:T(8,128)S(1)} collective-permute-done((f32[7,8,128]{2,1,0:T(8,128)S(1)}, f32[7,8,128]{2,1,0:T(8,128)S(1)}, u32[]{:S(2)}, u32[]{:S(2)}) %collective-permute-start.2) | collective-permute-done | bytes 28704 | tf_op jit(solution)/shard_map/ppermute | solution.py:648
  8.3 4.1 %collective-permute-start.5 = (f32[7,8,128]{2,1,0:T(8,128)S(1)}, f32[7,8,128]{2,1,0:T(8,128)S(1)}, u32[]{:S(2)}, u32[]{:S(2)}) collective-permute-start(f32[7,8,128]{2,1,0:T(8,128)S(1)} %pair.1.own.own_z), channel_id=1, source_target_pairs={{0,24},{4,28},{8,0},{12,4},{16,8},{20,12},{24,16},{28,20},{32,56},... | collective-permute-start | bytes 86024 | tf_op jit(solution)/shard_map/ppermute | solution.py:584
  12.4 0.0 collective-permute-start.4
  12.4 1.9 %collective-permute-start.3 = (f32[7,8,128]{2,1,0:T(8,128)S(1)}, f32[7,8,128]{2,1,0:T(8,128)S(1)}, u32[]{:S(2)}, u32[]{:S(2)}) collective-permute-start(f32[7,8,128]{2,1,0:T(8,128)S(1)} %pair.1.own.own_z), channel_id=1, source_target_pairs={{0,16},{4,20},{8,24},{12,28},{16,0},{20,4},{24,8},{28,12},{32,48},... | collective-permute-start | bytes 86024 | tf_op jit(solution)/shard_map/ppermute | solution.py:584
  14.3 0.9 %upright.1 = (f32[64,2048]{1,0:T(8,128)S(1)}, f32[64,2048]{1,0:T(8,128)S(1)}) custom-call(f32[128,8,128]{2,1,0:T(8,128)S(1)} %get-tuple-element.69.lo, f32[128,8,128]{2,1,0:T(8,128)S(1)} %get-tuple-element.70.hi), custom_call_target="tpu_custom_call" | custom-call | flops 2000000 | bytes 1048576 | tf_op jit(solution)/shard_map/upright/pallas_call | solution.py:34
  15.1 0.0 collective-permute-done.5.r3.z3
  15.1 2.4 %collective-permute-done.4.r2.z2 = f32[7,8,128]{2,1,0:T(8,128)S(1)} collective-permute-done((f32[7,8,128]{2,1,0:T(8,128)S(1)}, f32[7,8,128]{2,1,0:T(8,128)S(1)}, u32[]{:S(2)}, u32[]{:S(2)}) %collective-permute-start.4) | collective-permute-done | bytes 28704 | tf_op jit(solution)/shard_map/ppermute | solution.py:584
  17.5 0.3 collective-permute-done.3.r1.z1
  17.8 0.8 %collective-permute-start.8 = (f32[7,8,128]{2,1,0:T(8,128)S(1)}, f32[7,8,128]{2,1,0:T(8,128)S(1)}, u32[]{:S(2)}, u32[]{:S(2)}) collective-permute-start(f32[7,8,128]{2,1,0:T(8,128)S(1)} %four.1.own_y), channel_id=1, source_target_pairs={{0,96},{4,100},{8,104},{12,108},{16,112},{20,116},{24,120},{28,124... | collective-permute-start | bytes 86024 | tf_op jit(solution)/shard_map/ppermute | solution.py:584
  18.6 2.5 %collective-permute-start.7 = (f32[7,8,128]{2,1,0:T(8,128)S(1)}, f32[7,8,128]{2,1,0:T(8,128)S(1)}, u32[]{:S(2)}, u32[]{:S(2)}) collective-permute-start(f32[7,8,128]{2,1,0:T(8,128)S(1)} %four.1.own_y), channel_id=1, source_target_pairs={{0,32},{4,36},{8,40},{12,44},{16,48},{20,52},{24,56},{28,60},{32,6... | collective-permute-start | bytes 86024 | tf_op jit(solution)/shard_map/ppermute | solution.py:584
  21.1 0.0 collective-permute-start.6
  21.2 1.8 %collective-permute-done.8.y3 = f32[7,8,128]{2,1,0:T(8,128)S(1)} collective-permute-done((f32[7,8,128]{2,1,0:T(8,128)S(1)}, f32[7,8,128]{2,1,0:T(8,128)S(1)}, u32[]{:S(2)}, u32[]{:S(2)}) %collective-permute-start.8) | collective-permute-done | bytes 28704 | tf_op jit(solution)/shard_map/ppermute | solution.py:584
  23.0 0.0 collective-permute-done.7.y2
  23.0 3.5 %collective-permute-done.6.y1 = f32[7,8,128]{2,1,0:T(8,128)S(1)} collective-permute-done((f32[7,8,128]{2,1,0:T(8,128)S(1)}, f32[7,8,128]{2,1,0:T(8,128)S(1)}, u32[]{:S(2)}, u32[]{:S(2)}) %collective-permute-start.6) | collective-permute-done | bytes 28704 | tf_op jit(solution)/shard_map/ppermute | solution.py:584
  26.5 0.1 through.1
  26.6 0.1 collective-permute-start.9
  26.7 0.6 %blend.1 = (f32[1024,128]{1,0:T(8,128)S(1)}, f32[1024,128]{1,0:T(8,128)S(1)}, f32[1024,128]{1,0:T(8,128)S(1)}, f32[4,1024,128]{2,1,0:T(8,128)S(1)}, f32[8,128]{1,0:T(8,128)S(1)}) custom-call(f32[64,16,128]{2,1,0:T(8,128)S(1)} %x_solve.1.u, f32[64,16,128]{2,1,0:T(8,128)S(1)} %get-tuple-element.52.lo.x_lo, f32[64,16,128]{2,1,0:T(8,128)S(1)} %get-tuple-element.53.hi.x_hi, ...), custom_call_target="tpu_custom_call" | custom-call | flops 2000000 | bytes 1048576 | tf_op jit(solution)/shard_map/blend/pallas_call | solution.py:34
  27.3 0.5 %collective-permute-done.9.got = f32[2,8,128]{2,1,0:T(8,128)S(1)} collective-permute-done((f32[2,8,128]{2,1,0:T(8,128)S(1)}, f32[2,8,128]{2,1,0:T(8,128)S(1)}, u32[]{:S(2)}, u32[]{:S(2)}) %collective-permute-start.9) | collective-permute-done | bytes 8224 | tf_op jit(solution)/shard_map/ppermute | solution.py:673
  27.9 0.3 y_port.1
  28.2 0.3 collective-permute-start.12
  28.5 2.9 %collective-permute-start.11 = (f32[8,128]{1,0:T(8,128)S(1)}, f32[8,128]{1,0:T(8,128)S(1)}, u32[]{:S(2)}, u32[]{:S(2)}) collective-permute-start(f32[8,128]{1,0:T(8,128)S(1)} %get-tuple-element.84.own), channel_id=1, source_target_pairs={{0,1},{1,2},{2,3},{3,0},{4,5},{5,6},{6,7},{7,4},{8,9},{9,10},{10,1... | collective-permute-start | bytes 12296 | tf_op jit(solution)/shard_map/ppermute | solution.py:584
  31.4 0.0 collective-permute-start.10
  31.4 1.6 %y_solve.1.base = f32[64,2048]{1,0:T(8,128)S(1)} custom-call(f32[1024,128]{1,0:T(8,128)S(1)} %get-tuple-element.85.source, f32[1024,128]{1,0:T(8,128)S(1)} %get-tuple-element.86.lo, f32[1024,128]{1,0:T(8,128)S(1)} %get-tuple-element.87.hi, f32[2,16,128]{2,1,0:T(8,128)S(1)} %get-tuple-element.88.flow, f32[128,8,128]{2,1,0:T(8,128)S(1)} %get-tuple-element.89.along, ...), custom_call_target="tpu_custom_call" | custom-call | flops 2000000 | bytes 1048576 | tf_op jit(solution)/shard_map/y_solve/pallas_call | solution.py:34
  33.0 0.0 collective-permute-done.12.r3
  33.0 0.0 collective-permute-done.11.r2
  33.0 3.5 %collective-permute-done.10.r1 = f32[8,128]{1,0:T(8,128)S(1)} collective-permute-done((f32[8,128]{1,0:T(8,128)S(1)}, f32[8,128]{1,0:T(8,128)S(1)}, u32[]{:S(2)}, u32[]{:S(2)}) %collective-permute-start.10) | collective-permute-done | bytes 4128 | tf_op jit(solution)/shard_map/ppermute | solution.py:584
  36.5 1.1 %finish.1 = f32[64,2048]{1,0:T(8,128)} custom-call(f32[8,128]{1,0:T(8,128)S(1)} %get-tuple-element.84.own, f32[8,128]{1,0:T(8,128)S(1)} %collective-permute-done.10.r1, f32[8,128]{1,0:T(8,128)S(1)} %collective-permute-done.11.r2, f32[8,128]{1,0:T(8,128)S(1)} %collective-permute-done.12.r3, f32[64,2048]{1,0:T(8,128)S(1)} %y_solve.1.base, ...), custom_call_target="tpu_custom_call" | custom-call | flops 2000000 | bytes 1048576 | tf_op jit(solution)/shard_map/finish/pallas_call | solution.py:34
  (2 shorter events, 0.1 us)
Async XLA Ops:
  1.5 4.4 %collective-permute-start = (f32[8,128]{1,0:T(8,128)S(1)}, f32[8,128]{1,0:T(8,128)S(1)}, u32[]{:S(2)}, u32[]{:S(2)}) collective-permute-start(f32[8,128]{1,0:T(8,128)S(1)} %get-tuple-element.55), channel_id=1, source_target_pairs={{0,1},{1,2},{2,3},{3,0},{4,5},{5,6},{6,7},{7,4},{8,9},{9,10},{10,1... | collective-permute-start | bytes 12296 | tf_op jit(solution)/shard_map/ppermute | solution.py:584
  2.0 4.8 %collective-permute-start.1 = (f32[8,128]{1,0:T(8,128)S(1)}, f32[8,128]{1,0:T(8,128)S(1)}, u32[]{:S(2)}, u32[]{:S(2)}) collective-permute-start(f32[8,128]{1,0:T(8,128)S(1)} %get-tuple-element.56), channel_id=1, source_target_pairs={{0,3},{1,0},{2,1},{3,2},{4,7},{5,4},{6,5},{7,6},{8,11},{9,8},{10,9... | collective-permute-start | bytes 12296 | tf_op jit(solution)/shard_map/ppermute | solution.py:584
  7.0 1.3 %collective-permute-start.2 = (f32[7,8,128]{2,1,0:T(8,128)S(1)}, f32[7,8,128]{2,1,0:T(8,128)S(1)}, u32[]{:S(2)}, u32[]{:S(2)}) collective-permute-start(f32[7,8,128]{2,1,0:T(8,128)S(1)} %get-tuple-element.61), channel_id=1, source_target_pairs={{0,4},{4,0},{8,12},{12,8},{16,20},{20,16},{24,28},{28,24},{32,36},... | collective-permute-start | bytes 86024 | tf_op jit(solution)/shard_map/ppermute | solution.py:648
  8.3 6.8 %collective-permute-start.5 = (f32[7,8,128]{2,1,0:T(8,128)S(1)}, f32[7,8,128]{2,1,0:T(8,128)S(1)}, u32[]{:S(2)}, u32[]{:S(2)}) collective-permute-start(f32[7,8,128]{2,1,0:T(8,128)S(1)} %pair.1.own.own_z), channel_id=1, source_target_pairs={{0,24},{4,28},{8,0},{12,4},{16,8},{20,12},{24,16},{28,20},{32,56},... | collective-permute-start | bytes 86024 | tf_op jit(solution)/shard_map/ppermute | solution.py:584
  12.4 5.1 %collective-permute-start.4 = (f32[7,8,128]{2,1,0:T(8,128)S(1)}, f32[7,8,128]{2,1,0:T(8,128)S(1)}, u32[]{:S(2)}, u32[]{:S(2)}) collective-permute-start(f32[7,8,128]{2,1,0:T(8,128)S(1)} %pair.1.own.own_z), channel_id=1, source_target_pairs={{0,8},{4,12},{8,16},{12,20},{16,24},{20,28},{24,0},{28,4},{32,40},... | collective-permute-start | bytes 86024 | tf_op jit(solution)/shard_map/ppermute | solution.py:584
  12.4 5.4 %collective-permute-start.3 = (f32[7,8,128]{2,1,0:T(8,128)S(1)}, f32[7,8,128]{2,1,0:T(8,128)S(1)}, u32[]{:S(2)}, u32[]{:S(2)}) collective-permute-start(f32[7,8,128]{2,1,0:T(8,128)S(1)} %pair.1.own.own_z), channel_id=1, source_target_pairs={{0,16},{4,20},{8,24},{12,28},{16,0},{20,4},{24,8},{28,12},{32,48},... | collective-permute-start | bytes 86024 | tf_op jit(solution)/shard_map/ppermute | solution.py:584
  17.8 5.2 %collective-permute-start.8 = (f32[7,8,128]{2,1,0:T(8,128)S(1)}, f32[7,8,128]{2,1,0:T(8,128)S(1)}, u32[]{:S(2)}, u32[]{:S(2)}) collective-permute-start(f32[7,8,128]{2,1,0:T(8,128)S(1)} %four.1.own_y), channel_id=1, source_target_pairs={{0,96},{4,100},{8,104},{12,108},{16,112},{20,116},{24,120},{28,124... | collective-permute-start | bytes 86024 | tf_op jit(solution)/shard_map/ppermute | solution.py:584
  18.6 4.3 %collective-permute-start.7 = (f32[7,8,128]{2,1,0:T(8,128)S(1)}, f32[7,8,128]{2,1,0:T(8,128)S(1)}, u32[]{:S(2)}, u32[]{:S(2)}) collective-permute-start(f32[7,8,128]{2,1,0:T(8,128)S(1)} %four.1.own_y), channel_id=1, source_target_pairs={{0,32},{4,36},{8,40},{12,44},{16,48},{20,52},{24,56},{28,60},{32,6... | collective-permute-start | bytes 86024 | tf_op jit(solution)/shard_map/ppermute | solution.py:584
  21.1 5.4 %collective-permute-start.6 = (f32[7,8,128]{2,1,0:T(8,128)S(1)}, f32[7,8,128]{2,1,0:T(8,128)S(1)}, u32[]{:S(2)}, u32[]{:S(2)}) collective-permute-start(f32[7,8,128]{2,1,0:T(8,128)S(1)} %four.1.own_y), channel_id=1, source_target_pairs={{0,64},{4,68},{8,72},{12,76},{16,80},{20,84},{24,88},{28,92},{32,9... | collective-permute-start | bytes 86024 | tf_op jit(solution)/shard_map/ppermute | solution.py:584
  26.6 1.3 %collective-permute-start.9 = (f32[2,8,128]{2,1,0:T(8,128)S(1)}, f32[2,8,128]{2,1,0:T(8,128)S(1)}, u32[]{:S(2)}, u32[]{:S(2)}) collective-permute-start(f32[2,8,128]{2,1,0:T(8,128)S(1)} %get-tuple-element.76), channel_id=1, source_target_pairs={{0,4},{4,0},{8,12},{12,8},{16,20},{20,16},{24,28},{28,24},{32,36},... | collective-permute-start | bytes 24584 | tf_op jit(solution)/shard_map/ppermute | solution.py:673
  28.2 4.8 %collective-permute-start.12 = (f32[8,128]{1,0:T(8,128)S(1)}, f32[8,128]{1,0:T(8,128)S(1)}, u32[]{:S(2)}, u32[]{:S(2)}) collective-permute-start(f32[8,128]{1,0:T(8,128)S(1)} %get-tuple-element.84.own), channel_id=1, source_target_pairs={{0,3},{1,0},{2,1},{3,2},{4,7},{5,4},{6,5},{7,6},{8,11},{9,8},{10,9... | collective-permute-start | bytes 12296 | tf_op jit(solution)/shard_map/ppermute | solution.py:584
  28.5 4.5 %collective-permute-start.11 = (f32[8,128]{1,0:T(8,128)S(1)}, f32[8,128]{1,0:T(8,128)S(1)}, u32[]{:S(2)}, u32[]{:S(2)}) collective-permute-start(f32[8,128]{1,0:T(8,128)S(1)} %get-tuple-element.84.own), channel_id=1, source_target_pairs={{0,1},{1,2},{2,3},{3,0},{4,5},{5,6},{6,7},{7,4},{8,9},{9,10},{10,1... | collective-permute-start | bytes 12296 | tf_op jit(solution)/shard_map/ppermute | solution.py:584
  31.4 5.1 %collective-permute-start.10 = (f32[8,128]{1,0:T(8,128)S(1)}, f32[8,128]{1,0:T(8,128)S(1)}, u32[]{:S(2)}, u32[]{:S(2)}) collective-permute-start(f32[8,128]{1,0:T(8,128)S(1)} %get-tuple-element.84.own), channel_id=1, source_target_pairs={{0,2},{1,3},{2,0},{3,1},{4,6},{5,7},{6,4},{7,5},{8,10},{9,11},{10,... | collective-permute-start | bytes 12296 | tf_op jit(solution)/shard_map/ppermute | solution.py:584

commit v7 on v6

--- a/solution.py
+++ b/solution.py
@@ -11,7 +11,7 @@
 Y_STEPS = 128
 X_LEVELS, Y_LEVELS = 2, 6
 GRANT = (527 << 20) // 10
-RING = (2, 1, 3)
+RING = (3, 1, 2)
 F32 = jnp.float32
 VMEM = pl.BlockSpec(memory_space=pltpu.VMEM)
 HBM = pl.BlockSpec(memory_space=pltpu.MemorySpace.HBM)

time: 37.8 us -> 36.7 us (0.971)
  waiting for transfers between devices: 13.9 us -> 11.5 us
  starting transfers between devices: 14.8 us -> 16.2 us
    ppermute x11, waiting for transfers between devices: 12.5 us -> 10.1 us  [around(): return lax.ppermute(value, axis, pairs)]
    ppermute x11, starting transfers between devices: 14.6 us -> 16 us  [around(): return lax.ppermute(value, axis, pairs)]
where the time goes in v7:
time: 36.7 us; the launch traced here: 36.5 us
  starting transfers between devices  16.2 us (44%)
  waiting for transfers between devices  11.5 us (31%)
  Pallas kernels  8.75 us (24%)
    ppermute x11, starting transfers between devices, around(): return lax.ppermute(value, axis, pairs)  16 us
    ppermute x11, waiting for transfers between devices, around(): return lax.ppermute(value, axis, pairs)  10.1 us
    pallas_call x13, Pallas kernels, run(): pl.pallas_call(kernel, out_shape=outs, **windows or whole(outs, args), sc...  8.75 us
    ppermute x1, waiting for transfers between devices, per_device(): other = lax.ppermute(give, 'gx', pairs)  0.89 us
  transfers between devices with their start and end apart: 13, of which 8 were waited for; matrix products, arithmetic and copies ran while one was open for 0% of the time, Pallas kernels for 15%

profile of v7, /device:TPU:30, one launch (start us, length us, event | category | flops | bytes accessed | tf_op | source)
XLA Modules:
  0.0 36.5 jit_solution(12483285446913022845)
XLA Ops:
  0.0 1.5 %load.1 = (f32[64,2048]{1,0:T(8,128)S(1)}, f32[64,2048]{1,0:T(8,128)S(1)}, f32[8,128]{1,0:T(8,128)S(1)}, f32[8,128]{1,0:T(8,128)S(1)}, f32[8,128]{1,0:T(8,128)S(1)}) custom-call(f32[64,2048]{1,0:T(8,128)} %bitcast.3, f32[64,2048]{1,0:T(8,128)} %bitcast.4), custom_call_target="tpu_custom_call" | custom-call | flops 2000000 | bytes 1048576 | tf_op jit(solution)/shard_map/load/pallas_call | solution.py:34
  1.5 0.5 %collective-permute-start = (f32[8,128]{1,0:T(8,128)S(1)}, f32[8,128]{1,0:T(8,128)S(1)}, u32[]{:S(2)}, u32[]{:S(2)}) collective-permute-start(f32[8,128]{1,0:T(8,128)S(1)} %get-tuple-element.55), channel_id=1, source_target_pairs={{0,1},{1,2},{2,3},{3,0},{4,5},{5,6},{6,7},{7,4},{8,9},{9,10},{10,1... | collective-permute-start | bytes 12296 | tf_op jit(solution)/shard_map/ppermute | solution.py:584
  2.0 1.5 %collective-permute-start.1 = (f32[8,128]{1,0:T(8,128)S(1)}, f32[8,128]{1,0:T(8,128)S(1)}, u32[]{:S(2)}, u32[]{:S(2)}) collective-permute-start(f32[8,128]{1,0:T(8,128)S(1)} %get-tuple-element.56), channel_id=1, source_target_pairs={{0,3},{1,0},{2,1},{3,2},{4,7},{5,4},{6,5},{7,6},{8,11},{9,8},{10,9... | collective-permute-start | bytes 12296 | tf_op jit(solution)/shard_map/ppermute | solution.py:584
  3.6 1.2 %y_matrix.1 = (f32[128,8,128]{2,1,0:T(8,128)S(1)}, f32[128,8,128]{2,1,0:T(8,128)S(1)}, f32[128,8,128]{2,1,0:T(8,128)S(1)}, f32[52,8,128]{2,1,0:T(8,128)S(1)}, f3...) custom-call(f32[64,2048]{1,0:T(8,128)S(1)} %get-tuple-element.50.k), custom_call_target="tpu_custom_call" | custom-call | flops 2000000 | bytes 1048576 | tf_op jit(solution)/shard_map/y_matrix/pallas_call | solution.py:34
  4.8 1.1 %x_matrix.1 = (f32[1024,128]{1,0:T(8,128)S(1)}, f32[64,16,128]{2,1,0:T(8,128)S(1)}, f32[64,16,128]{2,1,0:T(8,128)S(1)}, f32[64,16,128]{2,1,0:T(8,128)S(1)}, f32[...) custom-call(f32[64,2048]{1,0:T(8,128)S(1)} %get-tuple-element.49.t, ...), custom_call_target="tpu_custom_call" | custom-call | flops 2000000 | bytes 1048576 | tf_op jit(solution)/shard_map/x_matrix/pallas_call | solution.py:34
  5.9 0.0 collective-permute-done.below
  5.9 1.0 %collective-permute-done.1.above = f32[8,128]{1,0:T(8,128)S(1)} collective-permute-done((f32[8,128]{1,0:T(8,128)S(1)}, f32[8,128]{1,0:T(8,128)S(1)}, u32[]{:S(2)}, u32[]{:S(2)}) %collective-permute-start.1) | collective-permute-done | bytes 4128 | tf_op jit(solution)/shard_map/ppermute | solution.py:584
  6.9 0.1 x_port.1
  7.0 0.1 collective-permute-start.2
  7.1 0.3 x_solve.1.u
  7.4 0.9 %collective-permute-done.2.other = f32[7,8,128]{2,1,0:T(8,128)S(1)} collective-permute-done((f32[7,8,128]{2,1,0:T(8,128)S(1)}, f32[7,8,128]{2,1,0:T(8,128)S(1)}, u32[]{:S(2)}, u32[]{:S(2)}) %collective-permute-start.2) | collective-permute-done | bytes 28704 | tf_op jit(solution)/shard_map/ppermute | solution.py:648
  8.3 4.0 %collective-permute-start.5 = (f32[7,8,128]{2,1,0:T(8,128)S(1)}, f32[7,8,128]{2,1,0:T(8,128)S(1)}, u32[]{:S(2)}, u32[]{:S(2)}) collective-permute-start(f32[7,8,128]{2,1,0:T(8,128)S(1)} %pair.1.own.own_z), channel_id=1, source_target_pairs={{0,16},{4,20},{8,24},{12,28},{16,0},{20,4},{24,8},{28,12},{32,48},... | collective-permute-start | bytes 86024 | tf_op jit(solution)/shard_map/ppermute | solution.py:584
  12.2 1.0 %collective-permute-start.4 = (f32[7,8,128]{2,1,0:T(8,128)S(1)}, f32[7,8,128]{2,1,0:T(8,128)S(1)}, u32[]{:S(2)}, u32[]{:S(2)}) collective-permute-start(f32[7,8,128]{2,1,0:T(8,128)S(1)} %pair.1.own.own_z), channel_id=1, source_target_pairs={{0,8},{4,12},{8,16},{12,20},{16,24},{20,28},{24,0},{28,4},{32,40},... | collective-permute-start | bytes 86024 | tf_op jit(solution)/shard_map/ppermute | solution.py:584
  13.3 2.2 %collective-permute-start.3 = (f32[7,8,128]{2,1,0:T(8,128)S(1)}, f32[7,8,128]{2,1,0:T(8,128)S(1)}, u32[]{:S(2)}, u32[]{:S(2)}) collective-permute-start(f32[7,8,128]{2,1,0:T(8,128)S(1)} %pair.1.own.own_z), channel_id=1, source_target_pairs={{0,24},{4,28},{8,0},{12,4},{16,8},{20,12},{24,16},{28,20},{32,56},... | collective-permute-start | bytes 86024 | tf_op jit(solution)/shard_map/ppermute | solution.py:584
  15.5 0.9 %upright.1 = (f32[64,2048]{1,0:T(8,128)S(1)}, f32[64,2048]{1,0:T(8,128)S(1)}) custom-call(f32[128,8,128]{2,1,0:T(8,128)S(1)} %get-tuple-element.69.lo, f32[128,8,128]{2,1,0:T(8,128)S(1)} %get-tuple-element.70.hi), custom_call_target="tpu_custom_call" | custom-call | flops 2000000 | bytes 1048576 | tf_op jit(solution)/shard_map/upright/pallas_call | solution.py:34
  16.3 0.0 collective-permute-done.5.r3.z3
  16.4 1.0 %collective-permute-done.4.r2.z2 = f32[7,8,128]{2,1,0:T(8,128)S(1)} collective-permute-done((f32[7,8,128]{2,1,0:T(8,128)S(1)}, f32[7,8,128]{2,1,0:T(8,128)S(1)}, u32[]{:S(2)}, u32[]{:S(2)}) %collective-permute-start.4) | collective-permute-done | bytes 28704 | tf_op jit(solution)/shard_map/ppermute | solution.py:584
  17.3 0.0 collective-permute-done.3.r1.z1
  17.4 1.3 %collective-permute-start.8 = (f32[7,8,128]{2,1,0:T(8,128)S(1)}, f32[7,8,128]{2,1,0:T(8,128)S(1)}, u32[]{:S(2)}, u32[]{:S(2)}) collective-permute-start(f32[7,8,128]{2,1,0:T(8,128)S(1)} %four.1.own_y), channel_id=1, source_target_pairs={{0,64},{4,68},{8,72},{12,76},{16,80},{20,84},{24,88},{28,92},{32,9... | collective-permute-start | bytes 86024 | tf_op jit(solution)/shard_map/ppermute | solution.py:584
  18.7 2.2 %collective-permute-start.7 = (f32[7,8,128]{2,1,0:T(8,128)S(1)}, f32[7,8,128]{2,1,0:T(8,128)S(1)}, u32[]{:S(2)}, u32[]{:S(2)}) collective-permute-start(f32[7,8,128]{2,1,0:T(8,128)S(1)} %four.1.own_y), channel_id=1, source_target_pairs={{0,32},{4,36},{8,40},{12,44},{16,48},{20,52},{24,56},{28,60},{32,6... | collective-permute-start | bytes 86024 | tf_op jit(solution)/shard_map/ppermute | solution.py:584
  20.9 0.0 collective-permute-start.6
  20.9 2.0 %collective-permute-done.8.y3 = f32[7,8,128]{2,1,0:T(8,128)S(1)} collective-permute-done((f32[7,8,128]{2,1,0:T(8,128)S(1)}, f32[7,8,128]{2,1,0:T(8,128)S(1)}, u32[]{:S(2)}, u32[]{:S(2)}) %collective-permute-start.8) | collective-permute-done | bytes 28704 | tf_op jit(solution)/shard_map/ppermute | solution.py:584
  22.8 0.0 collective-permute-done.7.y2
  22.8 3.1 %collective-permute-done.6.y1 = f32[7,8,128]{2,1,0:T(8,128)S(1)} collective-permute-done((f32[7,8,128]{2,1,0:T(8,128)S(1)}, f32[7,8,128]{2,1,0:T(8,128)S(1)}, u32[]{:S(2)}, u32[]{:S(2)}) %collective-permute-start.6) | collective-permute-done | bytes 28704 | tf_op jit(solution)/shard_map/ppermute | solution.py:584
  26.0 0.1 through.1
  26.1 0.1 collective-permute-start.9
  26.2 0.6 %blend.1 = (f32[1024,128]{1,0:T(8,128)S(1)}, f32[1024,128]{1,0:T(8,128)S(1)}, f32[1024,128]{1,0:T(8,128)S(1)}, f32[4,1024,128]{2,1,0:T(8,128)S(1)}, f32[8,128]{1,0:T(8,128)S(1)}) custom-call(f32[64,16,128]{2,1,0:T(8,128)S(1)} %x_solve.1.u, f32[64,16,128]{2,1,0:T(8,128)S(1)} %get-tuple-element.52.lo.x_lo, f32[64,16,128]{2,1,0:T(8,128)S(1)} %get-tuple-element.53.hi.x_hi, ...), custom_call_target="tpu_custom_call" | custom-call | flops 2000000 | bytes 1048576 | tf_op jit(solution)/shard_map/blend/pallas_call | solution.py:34
  26.8 0.5 %collective-permute-done.9.got = f32[2,8,128]{2,1,0:T(8,128)S(1)} collective-permute-done((f32[2,8,128]{2,1,0:T(8,128)S(1)}, f32[2,8,128]{2,1,0:T(8,128)S(1)}, u32[]{:S(2)}, u32[]{:S(2)}) %collective-permute-start.9) | collective-permute-done | bytes 8224 | tf_op jit(solution)/shard_map/ppermute | solution.py:673
  27.3 0.3 y_port.1
  27.6 1.2 %collective-permute-start.12 = (f32[8,128]{1,0:T(8,128)S(1)}, f32[8,128]{1,0:T(8,128)S(1)}, u32[]{:S(2)}, u32[]{:S(2)}) collective-permute-start(f32[8,128]{1,0:T(8,128)S(1)} %get-tuple-element.84.own), channel_id=1, source_target_pairs={{0,2},{1,3},{2,0},{3,1},{4,6},{5,7},{6,4},{7,5},{8,10},{9,11},{10,... | collective-permute-start | bytes 12296 | tf_op jit(solution)/shard_map/ppermute | solution.py:584
  28.8 1.8 %collective-permute-start.11 = (f32[8,128]{1,0:T(8,128)S(1)}, f32[8,128]{1,0:T(8,128)S(1)}, u32[]{:S(2)}, u32[]{:S(2)}) collective-permute-start(f32[8,128]{1,0:T(8,128)S(1)} %get-tuple-element.84.own), channel_id=1, source_target_pairs={{0,1},{1,2},{2,3},{3,0},{4,5},{5,6},{6,7},{7,4},{8,9},{9,10},{10,1... | collective-permute-start | bytes 12296 | tf_op jit(solution)/shard_map/ppermute | solution.py:584
  30.6 0.2 collective-permute-start.10
  30.9 1.6 %y_solve.1.base = f32[64,2048]{1,0:T(8,128)S(1)} custom-call(f32[1024,128]{1,0:T(8,128)S(1)} %get-tuple-element.85.source, f32[1024,128]{1,0:T(8,128)S(1)} %get-tuple-element.86.lo, f32[1024,128]{1,0:T(8,128)S(1)} %get-tuple-element.87.hi, f32[2,16,128]{2,1,0:T(8,128)S(1)} %get-tuple-element.88.flow, f32[128,8,128]{2,1,0:T(8,128)S(1)} %get-tuple-element.89.along, ...), custom_call_target="tpu_custom_call" | custom-call | flops 2000000 | bytes 1048576 | tf_op jit(solution)/shard_map/y_solve/pallas_call | solution.py:34
  32.4 0.3 collective-permute-done.12.r3
  32.7 0.0 collective-permute-done.11.r2
  32.7 2.7 %collective-permute-done.10.r1 = f32[8,128]{1,0:T(8,128)S(1)} collective-permute-done((f32[8,128]{1,0:T(8,128)S(1)}, f32[8,128]{1,0:T(8,128)S(1)}, u32[]{:S(2)}, u32[]{:S(2)}) %collective-permute-start.10) | collective-permute-done | bytes 4128 | tf_op jit(solution)/shard_map/ppermute | solution.py:584
  35.5 1.1 %finish.1 = f32[64,2048]{1,0:T(8,128)} custom-call(f32[8,128]{1,0:T(8,128)S(1)} %get-tuple-element.84.own, f32[8,128]{1,0:T(8,128)S(1)} %collective-permute-done.10.r1, f32[8,128]{1,0:T(8,128)S(1)} %collective-permute-done.11.r2, f32[8,128]{1,0:T(8,128)S(1)} %collective-permute-done.12.r3, f32[64,2048]{1,0:T(8,128)S(1)} %y_solve.1.base, ...), custom_call_target="tpu_custom_call" | custom-call | flops 2000000 | bytes 1048576 | tf_op jit(solution)/shard_map/finish/pallas_call | solution.py:34
  (2 shorter events, 0.1 us)
Async XLA Ops:
  1.5 4.4 %collective-permute-start = (f32[8,128]{1,0:T(8,128)S(1)}, f32[8,128]{1,0:T(8,128)S(1)}, u32[]{:S(2)}, u32[]{:S(2)}) collective-permute-start(f32[8,128]{1,0:T(8,128)S(1)} %get-tuple-element.55), channel_id=1, source_target_pairs={{0,1},{1,2},{2,3},{3,0},{4,5},{5,6},{6,7},{7,4},{8,9},{9,10},{10,1... | collective-permute-start | bytes 12296 | tf_op jit(solution)/shard_map/ppermute | solution.py:584
  2.0 4.8 %collective-permute-start.1 = (f32[8,128]{1,0:T(8,128)S(1)}, f32[8,128]{1,0:T(8,128)S(1)}, u32[]{:S(2)}, u32[]{:S(2)}) collective-permute-start(f32[8,128]{1,0:T(8,128)S(1)} %get-tuple-element.56), channel_id=1, source_target_pairs={{0,3},{1,0},{2,1},{3,2},{4,7},{5,4},{6,5},{7,6},{8,11},{9,8},{10,9... | collective-permute-start | bytes 12296 | tf_op jit(solution)/shard_map/ppermute | solution.py:584
  7.0 1.3 %collective-permute-start.2 = (f32[7,8,128]{2,1,0:T(8,128)S(1)}, f32[7,8,128]{2,1,0:T(8,128)S(1)}, u32[]{:S(2)}, u32[]{:S(2)}) collective-permute-start(f32[7,8,128]{2,1,0:T(8,128)S(1)} %get-tuple-element.61), channel_id=1, source_target_pairs={{0,4},{4,0},{8,12},{12,8},{16,20},{20,16},{24,28},{28,24},{32,36},... | collective-permute-start | bytes 86024 | tf_op jit(solution)/shard_map/ppermute | solution.py:648
  8.3 8.1 %collective-permute-start.5 = (f32[7,8,128]{2,1,0:T(8,128)S(1)}, f32[7,8,128]{2,1,0:T(8,128)S(1)}, u32[]{:S(2)}, u32[]{:S(2)}) collective-permute-start(f32[7,8,128]{2,1,0:T(8,128)S(1)} %pair.1.own.own_z), channel_id=1, source_target_pairs={{0,16},{4,20},{8,24},{12,28},{16,0},{20,4},{24,8},{28,12},{32,48},... | collective-permute-start | bytes 86024 | tf_op jit(solution)/shard_map/ppermute | solution.py:584
  12.2 5.1 %collective-permute-start.4 = (f32[7,8,128]{2,1,0:T(8,128)S(1)}, f32[7,8,128]{2,1,0:T(8,128)S(1)}, u32[]{:S(2)}, u32[]{:S(2)}) collective-permute-start(f32[7,8,128]{2,1,0:T(8,128)S(1)} %pair.1.own.own_z), channel_id=1, source_target_pairs={{0,8},{4,12},{8,16},{12,20},{16,24},{20,28},{24,0},{28,4},{32,40},... | collective-permute-start | bytes 86024 | tf_op jit(solution)/shard_map/ppermute | solution.py:584
  13.3 4.1 %collective-permute-start.3 = (f32[7,8,128]{2,1,0:T(8,128)S(1)}, f32[7,8,128]{2,1,0:T(8,128)S(1)}, u32[]{:S(2)}, u32[]{:S(2)}) collective-permute-start(f32[7,8,128]{2,1,0:T(8,128)S(1)} %pair.1.own.own_z), channel_id=1, source_target_pairs={{0,24},{4,28},{8,0},{12,4},{16,8},{20,12},{24,16},{28,20},{32,56},... | collective-permute-start | bytes 86024 | tf_op jit(solution)/shard_map/ppermute | solution.py:584
  17.4 5.5 %collective-permute-start.8 = (f32[7,8,128]{2,1,0:T(8,128)S(1)}, f32[7,8,128]{2,1,0:T(8,128)S(1)}, u32[]{:S(2)}, u32[]{:S(2)}) collective-permute-start(f32[7,8,128]{2,1,0:T(8,128)S(1)} %four.1.own_y), channel_id=1, source_target_pairs={{0,64},{4,68},{8,72},{12,76},{16,80},{20,84},{24,88},{28,92},{32,9... | collective-permute-start | bytes 86024 | tf_op jit(solution)/shard_map/ppermute | solution.py:584
  18.7 4.1 %collective-permute-start.7 = (f32[7,8,128]{2,1,0:T(8,128)S(1)}, f32[7,8,128]{2,1,0:T(8,128)S(1)}, u32[]{:S(2)}, u32[]{:S(2)}) collective-permute-start(f32[7,8,128]{2,1,0:T(8,128)S(1)} %four.1.own_y), channel_id=1, source_target_pairs={{0,32},{4,36},{8,40},{12,44},{16,48},{20,52},{24,56},{28,60},{32,6... | collective-permute-start | bytes 86024 | tf_op jit(solution)/shard_map/ppermute | solution.py:584
  20.9 5.1 %collective-permute-start.6 = (f32[7,8,128]{2,1,0:T(8,128)S(1)}, f32[7,8,128]{2,1,0:T(8,128)S(1)}, u32[]{:S(2)}, u32[]{:S(2)}) collective-permute-start(f32[7,8,128]{2,1,0:T(8,128)S(1)} %four.1.own_y), channel_id=1, source_target_pairs={{0,96},{4,100},{8,104},{12,108},{16,112},{20,116},{24,120},{28,124... | collective-permute-start | bytes 86024 | tf_op jit(solution)/shard_map/ppermute | solution.py:584
  26.1 1.3 %collective-permute-start.9 = (f32[2,8,128]{2,1,0:T(8,128)S(1)}, f32[2,8,128]{2,1,0:T(8,128)S(1)}, u32[]{:S(2)}, u32[]{:S(2)}) collective-permute-start(f32[2,8,128]{2,1,0:T(8,128)S(1)} %get-tuple-element.76), channel_id=1, source_target_pairs={{0,4},{4,0},{8,12},{12,8},{16,20},{20,16},{24,28},{28,24},{32,36},... | collective-permute-start | bytes 24584 | tf_op jit(solution)/shard_map/ppermute | solution.py:673
  27.6 5.1 %collective-permute-start.12 = (f32[8,128]{1,0:T(8,128)S(1)}, f32[8,128]{1,0:T(8,128)S(1)}, u32[]{:S(2)}, u32[]{:S(2)}) collective-permute-start(f32[8,128]{1,0:T(8,128)S(1)} %get-tuple-element.84.own), channel_id=1, source_target_pairs={{0,2},{1,3},{2,0},{3,1},{4,6},{5,7},{6,4},{7,5},{8,10},{9,11},{10,... | collective-permute-start | bytes 12296 | tf_op jit(solution)/shard_map/ppermute | solution.py:584
  28.8 3.9 %collective-permute-start.11 = (f32[8,128]{1,0:T(8,128)S(1)}, f32[8,128]{1,0:T(8,128)S(1)}, u32[]{:S(2)}, u32[]{:S(2)}) collective-permute-start(f32[8,128]{1,0:T(8,128)S(1)} %get-tuple-element.84.own), channel_id=1, source_target_pairs={{0,1},{1,2},{2,3},{3,0},{4,5},{5,6},{6,7},{7,4},{8,9},{9,10},{10,1... | collective-permute-start | bytes 12296 | tf_op jit(solution)/shard_map/ppermute | solution.py:584
  30.6 4.8 %collective-permute-start.10 = (f32[8,128]{1,0:T(8,128)S(1)}, f32[8,128]{1,0:T(8,128)S(1)}, u32[]{:S(2)}, u32[]{:S(2)}) collective-permute-start(f32[8,128]{1,0:T(8,128)S(1)} %get-tuple-element.84.own), channel_id=1, source_target_pairs={{0,3},{1,0},{2,1},{3,2},{4,7},{5,4},{6,5},{7,6},{8,11},{9,8},{10,9... | collective-permute-start | bytes 12296 | tf_op jit(solution)/shard_map/ppermute | solution.py:584

commit v8 on v7

--- a/solution.py
+++ b/solution.py
@@ -11,7 +11,7 @@
 Y_STEPS = 128
 X_LEVELS, Y_LEVELS = 2, 6
 GRANT = (527 << 20) // 10
-RING = (3, 1, 2)
+RING = (1, 3, 2)
 F32 = jnp.float32
 VMEM = pl.BlockSpec(memory_space=pltpu.VMEM)
 HBM = pl.BlockSpec(memory_space=pltpu.MemorySpace.HBM)
@@ -356,7 +356,7 @@
 def place(index, own, received, table):
     table[index] = own[...]
     for s, value in zip(RING, received):
-        table[lax.rem(index + 4 - s, 4)] = value[...]
+        table[lax.bitwise_xor(index, s)] = value[...]
 
 
 def pair_kernel(own, other, out):
@@ -580,7 +580,7 @@
     pairs = []
     for i in range(size):
         digit = (i // stride) % 4
-        pairs.append((i, i + ((digit + step) % 4 - digit) * stride))
+        pairs.append((i, i + ((digit ^ step) - digit) * stride))
     return lax.ppermute(value, axis, pairs)
 
 
@@ -596,8 +596,8 @@
         in_specs=[HBM, HBM],
         out_specs=[VMEM] * 5,
     )(t, k)
-    below = around(own_hi, "gy", 4, 1, 1)
-    above = around(own_lo, "gy", 4, 1, 3)
+    below = lax.ppermute(own_hi, "gy", [(i, (i + 1) % 4) for i in range(4)])
+    above = lax.ppermute(own_lo, "gy", [((i + 1) % 4, i) for i in range(4)])
     flat = struct(BANDS * TILES * 8, 128)
     runs = struct(TILES // 2 * 128, 128)
     x_field, y_field = struct(ROWS, TILES, 128), struct(Y_STEPS, 8, 128)

time: 36.7 us -> 36.3 us (0.989)
  the two profiles are of different devices: /device:TPU:30 before, /device:TPU:0 now
where the time goes in v8:
time: 36.3 us; the launch traced here: 36.1 us
  starting transfers between devices  16.6 us (46%)
  waiting for transfers between devices  10.7 us (29%)
  Pallas kernels  8.74 us (24%)
    ppermute x9, starting transfers between devices, around(): return lax.ppermute(value, axis, pairs)  13.1 us
    ppermute x9, waiting for transfers between devices, around(): return lax.ppermute(value, axis, pairs)  9.24 us
    pallas_call x13, Pallas kernels, run(): pl.pallas_call(kernel, out_shape=outs, **windows or whole(outs, args), sc...  8.74 us
    ppermute x1, starting transfers between devices, per_device(): above = lax.ppermute(own_lo, 'gy', [((i + 1) % 4, i) for i in range(4)])  1.66 us
    ppermute x1, starting transfers between devices, per_device(): below = lax.ppermute(own_hi, 'gy', [(i, (i + 1) % 4) for i in range(4)])  1.64 us
    ppermute x1, waiting for transfers between devices, per_device(): other = lax.ppermute(give, 'gx', pairs)  0.89 us
  transfers between devices with their start and end apart: 13, of which 7 were waited for; matrix products, arithmetic and copies ran while one was open for 0% of the time, Pallas kernels for 16%

profile of v8, /device:TPU:0, one launch (start us, length us, event | category | flops | bytes accessed | tf_op | source)
XLA Modules:
  0.0 36.1 jit_solution(1879363650515065481)
XLA Ops:
  0.0 1.5 %load.1 = (f32[64,2048]{1,0:T(8,128)S(1)}, f32[64,2048]{1,0:T(8,128)S(1)}, f32[8,128]{1,0:T(8,128)S(1)}, f32[8,128]{1,0:T(8,128)S(1)}, f32[8,128]{1,0:T(8,128)S(1)}) custom-call(f32[64,2048]{1,0:T(8,128)} %bitcast.3, f32[64,2048]{1,0:T(8,128)} %bitcast.4), custom_call_target="tpu_custom_call" | custom-call | flops 2000000 | bytes 1048576 | tf_op jit(solution)/shard_map/load/pallas_call | solution.py:34
  1.5 1.6 %collective-permute-start = (f32[8,128]{1,0:T(8,128)S(1)}, f32[8,128]{1,0:T(8,128)S(1)}, u32[]{:S(2)}, u32[]{:S(2)}) collective-permute-start(f32[8,128]{1,0:T(8,128)S(1)} %get-tuple-element.55), channel_id=1, source_target_pairs={{0,1},{1,2},{2,3},{3,0},{4,5},{5,6},{6,7},{7,4},{8,9},{9,10},{10,1... | collective-permute-start | bytes 12296 | tf_op jit(solution)/shard_map/ppermute | solution.py:599
  3.1 1.7 %collective-permute-start.1 = (f32[8,128]{1,0:T(8,128)S(1)}, f32[8,128]{1,0:T(8,128)S(1)}, u32[]{:S(2)}, u32[]{:S(2)}) collective-permute-start(f32[8,128]{1,0:T(8,128)S(1)} %get-tuple-element.56), channel_id=1, source_target_pairs={{1,0},{2,1},{3,2},{0,3},{5,4},{6,5},{7,6},{4,7},{9,8},{10,9},{11,1... | collective-permute-start | bytes 12296 | tf_op jit(solution)/shard_map/ppermute | solution.py:600
  4.8 1.2 %y_matrix.1 = (f32[128,8,128]{2,1,0:T(8,128)S(1)}, f32[128,8,128]{2,1,0:T(8,128)S(1)}, f32[128,8,128]{2,1,0:T(8,128)S(1)}, f32[52,8,128]{2,1,0:T(8,128)S(1)}, f3...) custom-call(f32[64,2048]{1,0:T(8,128)S(1)} %get-tuple-element.50.k), custom_call_target="tpu_custom_call" | custom-call | flops 2000000 | bytes 1048576 | tf_op jit(solution)/shard_map/y_matrix/pallas_call | solution.py:34
  6.0 1.1 %x_matrix.1 = (f32[1024,128]{1,0:T(8,128)S(1)}, f32[64,16,128]{2,1,0:T(8,128)S(1)}, f32[64,16,128]{2,1,0:T(8,128)S(1)}, f32[64,16,128]{2,1,0:T(8,128)S(1)}, f32[...) custom-call(f32[64,2048]{1,0:T(8,128)S(1)} %get-tuple-element.49.t, ...), custom_call_target="tpu_custom_call" | custom-call | flops 2000000 | bytes 1048576 | tf_op jit(solution)/shard_map/x_matrix/pallas_call | solution.py:34
  7.1 0.0 collective-permute-done.below
  7.1 0.0 collective-permute-done.1.above
  7.1 0.1 x_port.1
  7.2 0.1 collective-permute-start.2
  7.3 0.3 x_solve.1.u
  7.6 0.9 %collective-permute-done.2.other = f32[7,8,128]{2,1,0:T(8,128)S(1)} collective-permute-done((f32[7,8,128]{2,1,0:T(8,128)S(1)}, f32[7,8,128]{2,1,0:T(8,128)S(1)}, u32[]{:S(2)}, u32[]{:S(2)}) %collective-permute-start.2) | collective-permute-done | bytes 28704 | tf_op jit(solution)/shard_map/ppermute | solution.py:648
  8.5 4.0 %collective-permute-start.5 = (f32[7,8,128]{2,1,0:T(8,128)S(1)}, f32[7,8,128]{2,1,0:T(8,128)S(1)}, u32[]{:S(2)}, u32[]{:S(2)}) collective-permute-start(f32[7,8,128]{2,1,0:T(8,128)S(1)} %pair.1.own.own_z), channel_id=1, source_target_pairs={{0,16},{4,20},{8,24},{12,28},{16,0},{20,4},{24,8},{28,12},{32,48},... | collective-permute-start | bytes 86024 | tf_op jit(solution)/shard_map/ppermute | solution.py:584
  12.5 0.7 %collective-permute-start.4 = (f32[7,8,128]{2,1,0:T(8,128)S(1)}, f32[7,8,128]{2,1,0:T(8,128)S(1)}, u32[]{:S(2)}, u32[]{:S(2)}) collective-permute-start(f32[7,8,128]{2,1,0:T(8,128)S(1)} %pair.1.own.own_z), channel_id=1, source_target_pairs={{0,24},{4,28},{8,16},{12,20},{16,8},{20,12},{24,0},{28,4},{32,56},... | collective-permute-start | bytes 86024 | tf_op jit(solution)/shard_map/ppermute | solution.py:584
  13.3 0.3 collective-permute-start.3
  13.6 0.9 %upright.1 = (f32[64,2048]{1,0:T(8,128)S(1)}, f32[64,2048]{1,0:T(8,128)S(1)}) custom-call(f32[128,8,128]{2,1,0:T(8,128)S(1)} %get-tuple-element.69.lo, f32[128,8,128]{2,1,0:T(8,128)S(1)} %get-tuple-element.70.hi), custom_call_target="tpu_custom_call" | custom-call | flops 2000000 | bytes 1048576 | tf_op jit(solution)/shard_map/upright/pallas_call | solution.py:34
  14.4 0.0 collective-permute-done.5.r3.z3
  14.4 3.2 %collective-permute-done.4.r2.z2 = f32[7,8,128]{2,1,0:T(8,128)S(1)} collective-permute-done((f32[7,8,128]{2,1,0:T(8,128)S(1)}, f32[7,8,128]{2,1,0:T(8,128)S(1)}, u32[]{:S(2)}, u32[]{:S(2)}) %collective-permute-start.4) | collective-permute-done | bytes 28704 | tf_op jit(solution)/shard_map/ppermute | solution.py:584
  17.6 0.0 collective-permute-done.3.r1.z1
  17.7 3.3 %collective-permute-start.8 = (f32[7,8,128]{2,1,0:T(8,128)S(1)}, f32[7,8,128]{2,1,0:T(8,128)S(1)}, u32[]{:S(2)}, u32[]{:S(2)}) collective-permute-start(f32[7,8,128]{2,1,0:T(8,128)S(1)} %four.1.own_y), channel_id=1, source_target_pairs={{0,64},{4,68},{8,72},{12,76},{16,80},{20,84},{24,88},{28,92},{32,9... | collective-permute-start | bytes 86024 | tf_op jit(solution)/shard_map/ppermute | solution.py:584
  21.0 1.1 %collective-permute-start.7 = (f32[7,8,128]{2,1,0:T(8,128)S(1)}, f32[7,8,128]{2,1,0:T(8,128)S(1)}, u32[]{:S(2)}, u32[]{:S(2)}) collective-permute-start(f32[7,8,128]{2,1,0:T(8,128)S(1)} %four.1.own_y), channel_id=1, source_target_pairs={{0,96},{4,100},{8,104},{12,108},{16,112},{20,116},{24,120},{28,124... | collective-permute-start | bytes 86024 | tf_op jit(solution)/shard_map/ppermute | solution.py:584
  22.0 0.0 collective-permute-start.6
  22.0 1.1 %collective-permute-done.8.y3 = f32[7,8,128]{2,1,0:T(8,128)S(1)} collective-permute-done((f32[7,8,128]{2,1,0:T(8,128)S(1)}, f32[7,8,128]{2,1,0:T(8,128)S(1)}, u32[]{:S(2)}, u32[]{:S(2)}) %collective-permute-start.8) | collective-permute-done | bytes 28704 | tf_op jit(solution)/shard_map/ppermute | solution.py:584
  23.1 2.9 %collective-permute-done.7.y2 = f32[7,8,128]{2,1,0:T(8,128)S(1)} collective-permute-done((f32[7,8,128]{2,1,0:T(8,128)S(1)}, f32[7,8,128]{2,1,0:T(8,128)S(1)}, u32[]{:S(2)}, u32[]{:S(2)}) %collective-permute-start.7) | collective-permute-done | bytes 28704 | tf_op jit(solution)/shard_map/ppermute | solution.py:584
  26.0 0.0 collective-permute-done.6.y1
  26.0 0.1 through.1
  26.2 0.1 collective-permute-start.9
  26.2 0.6 %blend.1 = (f32[1024,128]{1,0:T(8,128)S(1)}, f32[1024,128]{1,0:T(8,128)S(1)}, f32[1024,128]{1,0:T(8,128)S(1)}, f32[4,1024,128]{2,1,0:T(8,128)S(1)}, f32[8,128]{1,0:T(8,128)S(1)}) custom-call(f32[64,16,128]{2,1,0:T(8,128)S(1)} %x_solve.1.u, f32[64,16,128]{2,1,0:T(8,128)S(1)} %get-tuple-element.52.lo.x_lo, f32[64,16,128]{2,1,0:T(8,128)S(1)} %get-tuple-element.53.hi.x_hi, ...), custom_call_target="tpu_custom_call" | custom-call | flops 2000000 | bytes 1048576 | tf_op jit(solution)/shard_map/blend/pallas_call | solution.py:34
  26.9 0.5 %collective-permute-done.9.got = f32[2,8,128]{2,1,0:T(8,128)S(1)} collective-permute-done((f32[2,8,128]{2,1,0:T(8,128)S(1)}, f32[2,8,128]{2,1,0:T(8,128)S(1)}, u32[]{:S(2)}, u32[]{:S(2)}) %collective-permute-start.9) | collective-permute-done | bytes 8224 | tf_op jit(solution)/shard_map/ppermute | solution.py:673
  27.4 0.3 y_port.1
  27.7 2.3 %collective-permute-start.12 = (f32[8,128]{1,0:T(8,128)S(1)}, f32[8,128]{1,0:T(8,128)S(1)}, u32[]{:S(2)}, u32[]{:S(2)}) collective-permute-start(f32[8,128]{1,0:T(8,128)S(1)} %get-tuple-element.84.own), channel_id=1, source_target_pairs={{0,2},{1,3},{2,0},{3,1},{4,6},{5,7},{6,4},{7,5},{8,10},{9,11},{10,... | collective-permute-start | bytes 12296 | tf_op jit(solution)/shard_map/ppermute | solution.py:584
  30.0 1.4 %collective-permute-start.11 = (f32[8,128]{1,0:T(8,128)S(1)}, f32[8,128]{1,0:T(8,128)S(1)}, u32[]{:S(2)}, u32[]{:S(2)}) collective-permute-start(f32[8,128]{1,0:T(8,128)S(1)} %get-tuple-element.84.own), channel_id=1, source_target_pairs={{0,3},{1,2},{2,1},{3,0},{4,7},{5,6},{6,5},{7,4},{8,11},{9,10},{10,... | collective-permute-start | bytes 12296 | tf_op jit(solution)/shard_map/ppermute | solution.py:584
  31.5 0.0 collective-permute-start.10
  31.5 1.6 %y_solve.1.base = f32[64,2048]{1,0:T(8,128)S(1)} custom-call(f32[1024,128]{1,0:T(8,128)S(1)} %get-tuple-element.85.source, f32[1024,128]{1,0:T(8,128)S(1)} %get-tuple-element.86.lo, f32[1024,128]{1,0:T(8,128)S(1)} %get-tuple-element.87.hi, f32[2,16,128]{2,1,0:T(8,128)S(1)} %get-tuple-element.88.flow, f32[128,8,128]{2,1,0:T(8,128)S(1)} %get-tuple-element.89.along, ...), custom_call_target="tpu_custom_call" | custom-call | flops 2000000 | bytes 1048576 | tf_op jit(solution)/shard_map/y_solve/pallas_call | solution.py:34
  33.0 0.0 collective-permute-done.12.r3
  33.0 1.8 %collective-permute-done.11.r2 = f32[8,128]{1,0:T(8,128)S(1)} collective-permute-done((f32[8,128]{1,0:T(8,128)S(1)}, f32[8,128]{1,0:T(8,128)S(1)}, u32[]{:S(2)}, u32[]{:S(2)}) %collective-permute-start.11) | collective-permute-done | bytes 4128 | tf_op jit(solution)/shard_map/ppermute | solution.py:584
  34.8 0.2 collective-permute-done.10.r1
  35.1 1.1 %finish.1 = f32[64,2048]{1,0:T(8,128)} custom-call(f32[8,128]{1,0:T(8,128)S(1)} %get-tuple-element.84.own, f32[8,128]{1,0:T(8,128)S(1)} %collective-permute-done.10.r1, f32[8,128]{1,0:T(8,128)S(1)} %collective-permute-done.11.r2, f32[8,128]{1,0:T(8,128)S(1)} %collective-permute-done.12.r3, f32[64,2048]{1,0:T(8,128)S(1)} %y_solve.1.base, ...), custom_call_target="tpu_custom_call" | custom-call | flops 2000000 | bytes 1048576 | tf_op jit(solution)/shard_map/finish/pallas_call | solution.py:34
  (2 shorter events, 0.1 us)
Async XLA Ops:
  1.5 5.6 %collective-permute-start = (f32[8,128]{1,0:T(8,128)S(1)}, f32[8,128]{1,0:T(8,128)S(1)}, u32[]{:S(2)}, u32[]{:S(2)}) collective-permute-start(f32[8,128]{1,0:T(8,128)S(1)} %get-tuple-element.55), channel_id=1, source_target_pairs={{0,1},{1,2},{2,3},{3,0},{4,5},{5,6},{6,7},{7,4},{8,9},{9,10},{10,1... | collective-permute-start | bytes 12296 | tf_op jit(solution)/shard_map/ppermute | solution.py:599
  3.1 3.9 %collective-permute-start.1 = (f32[8,128]{1,0:T(8,128)S(1)}, f32[8,128]{1,0:T(8,128)S(1)}, u32[]{:S(2)}, u32[]{:S(2)}) collective-permute-start(f32[8,128]{1,0:T(8,128)S(1)} %get-tuple-element.56), channel_id=1, source_target_pairs={{1,0},{2,1},{3,2},{0,3},{5,4},{6,5},{7,6},{4,7},{9,8},{10,9},{11,1... | collective-permute-start | bytes 12296 | tf_op jit(solution)/shard_map/ppermute | solution.py:600
  7.2 1.3 %collective-permute-start.2 = (f32[7,8,128]{2,1,0:T(8,128)S(1)}, f32[7,8,128]{2,1,0:T(8,128)S(1)}, u32[]{:S(2)}, u32[]{:S(2)}) collective-permute-start(f32[7,8,128]{2,1,0:T(8,128)S(1)} %get-tuple-element.61), channel_id=1, source_target_pairs={{0,4},{4,0},{8,12},{12,8},{16,20},{20,16},{24,28},{28,24},{32,36},... | collective-permute-start | bytes 86024 | tf_op jit(solution)/shard_map/ppermute | solution.py:648
  8.5 5.9 %collective-permute-start.5 = (f32[7,8,128]{2,1,0:T(8,128)S(1)}, f32[7,8,128]{2,1,0:T(8,128)S(1)}, u32[]{:S(2)}, u32[]{:S(2)}) collective-permute-start(f32[7,8,128]{2,1,0:T(8,128)S(1)} %pair.1.own.own_z), channel_id=1, source_target_pairs={{0,16},{4,20},{8,24},{12,28},{16,0},{20,4},{24,8},{28,12},{32,48},... | collective-permute-start | bytes 86024 | tf_op jit(solution)/shard_map/ppermute | solution.py:584
  12.5 5.1 %collective-permute-start.4 = (f32[7,8,128]{2,1,0:T(8,128)S(1)}, f32[7,8,128]{2,1,0:T(8,128)S(1)}, u32[]{:S(2)}, u32[]{:S(2)}) collective-permute-start(f32[7,8,128]{2,1,0:T(8,128)S(1)} %pair.1.own.own_z), channel_id=1, source_target_pairs={{0,24},{4,28},{8,16},{12,20},{16,8},{20,12},{24,0},{28,4},{32,56},... | collective-permute-start | bytes 86024 | tf_op jit(solution)/shard_map/ppermute | solution.py:584
  13.3 4.4 %collective-permute-start.3 = (f32[7,8,128]{2,1,0:T(8,128)S(1)}, f32[7,8,128]{2,1,0:T(8,128)S(1)}, u32[]{:S(2)}, u32[]{:S(2)}) collective-permute-start(f32[7,8,128]{2,1,0:T(8,128)S(1)} %pair.1.own.own_z), channel_id=1, source_target_pairs={{0,8},{4,12},{8,0},{12,4},{16,24},{20,28},{24,16},{28,20},{32,40},... | collective-permute-start | bytes 86024 | tf_op jit(solution)/shard_map/ppermute | solution.py:584
  17.7 5.5 %collective-permute-start.8 = (f32[7,8,128]{2,1,0:T(8,128)S(1)}, f32[7,8,128]{2,1,0:T(8,128)S(1)}, u32[]{:S(2)}, u32[]{:S(2)}) collective-permute-start(f32[7,8,128]{2,1,0:T(8,128)S(1)} %four.1.own_y), channel_id=1, source_target_pairs={{0,64},{4,68},{8,72},{12,76},{16,80},{20,84},{24,88},{28,92},{32,9... | collective-permute-start | bytes 86024 | tf_op jit(solution)/shard_map/ppermute | solution.py:584
  21.0 5.1 %collective-permute-start.7 = (f32[7,8,128]{2,1,0:T(8,128)S(1)}, f32[7,8,128]{2,1,0:T(8,128)S(1)}, u32[]{:S(2)}, u32[]{:S(2)}) collective-permute-start(f32[7,8,128]{2,1,0:T(8,128)S(1)} %four.1.own_y), channel_id=1, source_target_pairs={{0,96},{4,100},{8,104},{12,108},{16,112},{20,116},{24,120},{28,124... | collective-permute-start | bytes 86024 | tf_op jit(solution)/shard_map/ppermute | solution.py:584
  22.0 4.0 %collective-permute-start.6 = (f32[7,8,128]{2,1,0:T(8,128)S(1)}, f32[7,8,128]{2,1,0:T(8,128)S(1)}, u32[]{:S(2)}, u32[]{:S(2)}) collective-permute-start(f32[7,8,128]{2,1,0:T(8,128)S(1)} %four.1.own_y), channel_id=1, source_target_pairs={{0,32},{4,36},{8,40},{12,44},{16,48},{20,52},{24,56},{28,60},{32,0... | collective-permute-start | bytes 86024 | tf_op jit(solution)/shard_map/ppermute | solution.py:584
  26.2 1.3 %collective-permute-start.9 = (f32[2,8,128]{2,1,0:T(8,128)S(1)}, f32[2,8,128]{2,1,0:T(8,128)S(1)}, u32[]{:S(2)}, u32[]{:S(2)}) collective-permute-start(f32[2,8,128]{2,1,0:T(8,128)S(1)} %get-tuple-element.76), channel_id=1, source_target_pairs={{0,4},{4,0},{8,12},{12,8},{16,20},{20,16},{24,28},{28,24},{32,36},... | collective-permute-start | bytes 24584 | tf_op jit(solution)/shard_map/ppermute | solution.py:673
  27.7 5.3 %collective-permute-start.12 = (f32[8,128]{1,0:T(8,128)S(1)}, f32[8,128]{1,0:T(8,128)S(1)}, u32[]{:S(2)}, u32[]{:S(2)}) collective-permute-start(f32[8,128]{1,0:T(8,128)S(1)} %get-tuple-element.84.own), channel_id=1, source_target_pairs={{0,2},{1,3},{2,0},{3,1},{4,6},{5,7},{6,4},{7,5},{8,10},{9,11},{10,... | collective-permute-start | bytes 12296 | tf_op jit(solution)/shard_map/ppermute | solution.py:584
  30.0 4.8 %collective-permute-start.11 = (f32[8,128]{1,0:T(8,128)S(1)}, f32[8,128]{1,0:T(8,128)S(1)}, u32[]{:S(2)}, u32[]{:S(2)}) collective-permute-start(f32[8,128]{1,0:T(8,128)S(1)} %get-tuple-element.84.own), channel_id=1, source_target_pairs={{0,3},{1,2},{2,1},{3,0},{4,7},{5,6},{6,5},{7,4},{8,11},{9,10},{10,... | collective-permute-start | bytes 12296 | tf_op jit(solution)/shard_map/ppermute | solution.py:584
  31.5 3.6 %collective-permute-start.10 = (f32[8,128]{1,0:T(8,128)S(1)}, f32[8,128]{1,0:T(8,128)S(1)}, u32[]{:S(2)}, u32[]{:S(2)}) collective-permute-start(f32[8,128]{1,0:T(8,128)S(1)} %get-tuple-element.84.own), channel_id=1, source_target_pairs={{0,1},{1,0},{2,3},{3,2},{4,5},{5,4},{6,7},{7,6},{8,9},{9,8},{10,11... | collective-permute-start | bytes 12296 | tf_op jit(solution)/shard_map/ppermute | solution.py:584

commit v9 on v8

--- a/solution.py
+++ b/solution.py
@@ -11,7 +11,7 @@
 Y_STEPS = 128
 X_LEVELS, Y_LEVELS = 2, 6
 GRANT = (527 << 20) // 10
-RING = (1, 3, 2)
+RING = (1, 2, 3)
 F32 = jnp.float32
 VMEM = pl.BlockSpec(memory_space=pltpu.VMEM)
 HBM = pl.BlockSpec(memory_space=pltpu.MemorySpace.HBM)

time: 36.3 us -> 37.2 us (1.025)
  waiting for transfers between devices: 10.7 us -> 11.3 us
    ppermute x9, waiting for transfers between devices: 9.24 us -> 9.83 us  [around(): return lax.ppermute(value, axis, pairs)]
  transfers between devices with their start and end apart: 13 -> 13, of which waited for: 7 -> 6; matrix products, arithmetic and copies ran while one was open for 0% -> 0% of each run, Pallas kernels for 16% -> 15%
where the time goes in v9:
time: 37.2 us; the launch traced here: 37 us
  starting transfers between devices  16.9 us (45%)
  waiting for transfers between devices  11.3 us (30%)
  Pallas kernels  8.74 us (23%)
    ppermute x9, starting transfers between devices, around(): return lax.ppermute(value, axis, pairs)  13.4 us
    ppermute x9, waiting for transfers between devices, around(): return lax.ppermute(value, axis, pairs)  9.83 us
    pallas_call x13, Pallas kernels, run(): pl.pallas_call(kernel, out_shape=outs, **windows or whole(outs, args), sc...  8.74 us
    ppermute x1, starting transfers between devices, per_device(): above = lax.ppermute(own_lo, 'gy', [((i + 1) % 4, i) for i in range(4)])  1.66 us
    ppermute x1, starting transfers between devices, per_device(): below = lax.ppermute(own_hi, 'gy', [(i, (i + 1) % 4) for i in range(4)])  1.64 us
    ppermute x1, waiting for transfers between devices, per_device(): other = lax.ppermute(give, 'gx', pairs)  0.89 us
  transfers between devices with their start and end apart: 13, of which 6 were waited for; matrix products, arithmetic and copies ran while one was open for 0% of the time, Pallas kernels for 15%

profile of v9, /device:TPU:0, one launch (start us, length us, event | category | flops | bytes accessed | tf_op | source)
XLA Modules:
  0.0 37.0 jit_solution(10965157651381184693)
XLA Ops:
  0.0 1.5 %load.1 = (f32[64,2048]{1,0:T(8,128)S(1)}, f32[64,2048]{1,0:T(8,128)S(1)}, f32[8,128]{1,0:T(8,128)S(1)}, f32[8,128]{1,0:T(8,128)S(1)}, f32[8,128]{1,0:T(8,128)S(1)}) custom-call(f32[64,2048]{1,0:T(8,128)} %bitcast.3, f32[64,2048]{1,0:T(8,128)} %bitcast.4), custom_call_target="tpu_custom_call" | custom-call | flops 2000000 | bytes 1048576 | tf_op jit(solution)/shard_map/load/pallas_call | solution.py:34
  1.5 1.6 %collective-permute-start = (f32[8,128]{1,0:T(8,128)S(1)}, f32[8,128]{1,0:T(8,128)S(1)}, u32[]{:S(2)}, u32[]{:S(2)}) collective-permute-start(f32[8,128]{1,0:T(8,128)S(1)} %get-tuple-element.55), channel_id=1, source_target_pairs={{0,1},{1,2},{2,3},{3,0},{4,5},{5,6},{6,7},{7,4},{8,9},{9,10},{10,1... | collective-permute-start | bytes 12296 | tf_op jit(solution)/shard_map/ppermute | solution.py:599
  3.1 1.7 %collective-permute-start.1 = (f32[8,128]{1,0:T(8,128)S(1)}, f32[8,128]{1,0:T(8,128)S(1)}, u32[]{:S(2)}, u32[]{:S(2)}) collective-permute-start(f32[8,128]{1,0:T(8,128)S(1)} %get-tuple-element.56), channel_id=1, source_target_pairs={{1,0},{2,1},{3,2},{0,3},{5,4},{6,5},{7,6},{4,7},{9,8},{10,9},{11,1... | collective-permute-start | bytes 12296 | tf_op jit(solution)/shard_map/ppermute | solution.py:600
  4.8 1.2 %y_matrix.1 = (f32[128,8,128]{2,1,0:T(8,128)S(1)}, f32[128,8,128]{2,1,0:T(8,128)S(1)}, f32[128,8,128]{2,1,0:T(8,128)S(1)}, f32[52,8,128]{2,1,0:T(8,128)S(1)}, f3...) custom-call(f32[64,2048]{1,0:T(8,128)S(1)} %get-tuple-element.50.k), custom_call_target="tpu_custom_call" | custom-call | flops 2000000 | bytes 1048576 | tf_op jit(solution)/shard_map/y_matrix/pallas_call | solution.py:34
  6.0 1.1 %x_matrix.1 = (f32[1024,128]{1,0:T(8,128)S(1)}, f32[64,16,128]{2,1,0:T(8,128)S(1)}, f32[64,16,128]{2,1,0:T(8,128)S(1)}, f32[64,16,128]{2,1,0:T(8,128)S(1)}, f32[...) custom-call(f32[64,2048]{1,0:T(8,128)S(1)} %get-tuple-element.49.t, ...), custom_call_target="tpu_custom_call" | custom-call | flops 2000000 | bytes 1048576 | tf_op jit(solution)/shard_map/x_matrix/pallas_call | solution.py:34
  7.1 0.0 collective-permute-done.below
  7.1 0.0 collective-permute-done.1.above
  7.1 0.1 x_port.1
  7.2 0.1 collective-permute-start.2
  7.3 0.3 x_solve.1.u
  7.6 0.9 %collective-permute-done.2.other = f32[7,8,128]{2,1,0:T(8,128)S(1)} collective-permute-done((f32[7,8,128]{2,1,0:T(8,128)S(1)}, f32[7,8,128]{2,1,0:T(8,128)S(1)}, u32[]{:S(2)}, u32[]{:S(2)}) %collective-permute-start.2) | collective-permute-done | bytes 28704 | tf_op jit(solution)/shard_map/ppermute | solution.py:648
  8.5 4.2 %collective-permute-start.5 = (f32[7,8,128]{2,1,0:T(8,128)S(1)}, f32[7,8,128]{2,1,0:T(8,128)S(1)}, u32[]{:S(2)}, u32[]{:S(2)}) collective-permute-start(f32[7,8,128]{2,1,0:T(8,128)S(1)} %pair.1.own.own_z), channel_id=1, source_target_pairs={{0,24},{4,28},{8,16},{12,20},{16,8},{20,12},{24,0},{28,4},{32,56},... | collective-permute-start | bytes 86024 | tf_op jit(solution)/shard_map/ppermute | solution.py:584
  12.7 0.0 collective-permute-start.4
  12.7 0.9 %collective-permute-start.3 = (f32[7,8,128]{2,1,0:T(8,128)S(1)}, f32[7,8,128]{2,1,0:T(8,128)S(1)}, u32[]{:S(2)}, u32[]{:S(2)}) collective-permute-start(f32[7,8,128]{2,1,0:T(8,128)S(1)} %pair.1.own.own_z), channel_id=1, source_target_pairs={{0,8},{4,12},{8,0},{12,4},{16,24},{20,28},{24,16},{28,20},{32,40},... | collective-permute-start | bytes 86024 | tf_op jit(solution)/shard_map/ppermute | solution.py:584
  13.7 0.9 %upright.1 = (f32[64,2048]{1,0:T(8,128)S(1)}, f32[64,2048]{1,0:T(8,128)S(1)}) custom-call(f32[128,8,128]{2,1,0:T(8,128)S(1)} %get-tuple-element.69.lo, f32[128,8,128]{2,1,0:T(8,128)S(1)} %get-tuple-element.70.hi), custom_call_target="tpu_custom_call" | custom-call | flops 2000000 | bytes 1048576 | tf_op jit(solution)/shard_map/upright/pallas_call | solution.py:34
  14.5 0.0 collective-permute-done.5.r3.z3
  14.6 3.5 %collective-permute-done.4.r2.z2 = f32[7,8,128]{2,1,0:T(8,128)S(1)} collective-permute-done((f32[7,8,128]{2,1,0:T(8,128)S(1)}, f32[7,8,128]{2,1,0:T(8,128)S(1)}, u32[]{:S(2)}, u32[]{:S(2)}) %collective-permute-start.4) | collective-permute-done | bytes 28704 | tf_op jit(solution)/shard_map/ppermute | solution.py:584
  18.1 0.0 collective-permute-done.3.r1.z1
  18.1 3.1 %collective-permute-start.8 = (f32[7,8,128]{2,1,0:T(8,128)S(1)}, f32[7,8,128]{2,1,0:T(8,128)S(1)}, u32[]{:S(2)}, u32[]{:S(2)}) collective-permute-start(f32[7,8,128]{2,1,0:T(8,128)S(1)} %four.1.own_y), channel_id=1, source_target_pairs={{0,96},{4,100},{8,104},{12,108},{16,112},{20,116},{24,120},{28,124... | collective-permute-start | bytes 86024 | tf_op jit(solution)/shard_map/ppermute | solution.py:584
  21.2 0.6 %collective-permute-start.7 = (f32[7,8,128]{2,1,0:T(8,128)S(1)}, f32[7,8,128]{2,1,0:T(8,128)S(1)}, u32[]{:S(2)}, u32[]{:S(2)}) collective-permute-start(f32[7,8,128]{2,1,0:T(8,128)S(1)} %four.1.own_y), channel_id=1, source_target_pairs={{0,64},{4,68},{8,72},{12,76},{16,80},{20,84},{24,88},{28,92},{32,9... | collective-permute-start | bytes 86024 | tf_op jit(solution)/shard_map/ppermute | solution.py:584
  21.9 0.5 %collective-permute-start.6 = (f32[7,8,128]{2,1,0:T(8,128)S(1)}, f32[7,8,128]{2,1,0:T(8,128)S(1)}, u32[]{:S(2)}, u32[]{:S(2)}) collective-permute-start(f32[7,8,128]{2,1,0:T(8,128)S(1)} %four.1.own_y), channel_id=1, source_target_pairs={{0,32},{4,36},{8,40},{12,44},{16,48},{20,52},{24,56},{28,60},{32,0... | collective-permute-start | bytes 86024 | tf_op jit(solution)/shard_map/ppermute | solution.py:584
  22.3 1.0 %collective-permute-done.8.y3 = f32[7,8,128]{2,1,0:T(8,128)S(1)} collective-permute-done((f32[7,8,128]{2,1,0:T(8,128)S(1)}, f32[7,8,128]{2,1,0:T(8,128)S(1)}, u32[]{:S(2)}, u32[]{:S(2)}) %collective-permute-start.8) | collective-permute-done | bytes 28704 | tf_op jit(solution)/shard_map/ppermute | solution.py:584
  23.3 3.3 %collective-permute-done.7.y2 = f32[7,8,128]{2,1,0:T(8,128)S(1)} collective-permute-done((f32[7,8,128]{2,1,0:T(8,128)S(1)}, f32[7,8,128]{2,1,0:T(8,128)S(1)}, u32[]{:S(2)}, u32[]{:S(2)}) %collective-permute-start.7) | collective-permute-done | bytes 28704 | tf_op jit(solution)/shard_map/ppermute | solution.py:584
  26.6 0.0 collective-permute-done.6.y1
  26.6 0.1 through.1
  26.7 0.1 collective-permute-start.9
  26.8 0.6 %blend.1 = (f32[1024,128]{1,0:T(8,128)S(1)}, f32[1024,128]{1,0:T(8,128)S(1)}, f32[1024,128]{1,0:T(8,128)S(1)}, f32[4,1024,128]{2,1,0:T(8,128)S(1)}, f32[8,128]{1,0:T(8,128)S(1)}) custom-call(f32[64,16,128]{2,1,0:T(8,128)S(1)} %x_solve.1.u, f32[64,16,128]{2,1,0:T(8,128)S(1)} %get-tuple-element.52.lo.x_lo, f32[64,16,128]{2,1,0:T(8,128)S(1)} %get-tuple-element.53.hi.x_hi, ...), custom_call_target="tpu_custom_call" | custom-call | flops 2000000 | bytes 1048576 | tf_op jit(solution)/shard_map/blend/pallas_call | solution.py:34
  27.4 0.5 %collective-permute-done.9.got = f32[2,8,128]{2,1,0:T(8,128)S(1)} collective-permute-done((f32[2,8,128]{2,1,0:T(8,128)S(1)}, f32[2,8,128]{2,1,0:T(8,128)S(1)}, u32[]{:S(2)}, u32[]{:S(2)}) %collective-permute-start.9) | collective-permute-done | bytes 8224 | tf_op jit(solution)/shard_map/ppermute | solution.py:673
  28.0 0.3 y_port.1
  28.3 2.5 %collective-permute-start.12 = (f32[8,128]{1,0:T(8,128)S(1)}, f32[8,128]{1,0:T(8,128)S(1)}, u32[]{:S(2)}, u32[]{:S(2)}) collective-permute-start(f32[8,128]{1,0:T(8,128)S(1)} %get-tuple-element.84.own), channel_id=1, source_target_pairs={{0,3},{1,2},{2,1},{3,0},{4,7},{5,6},{6,5},{7,4},{8,11},{9,10},{10,... | collective-permute-start | bytes 12296 | tf_op jit(solution)/shard_map/ppermute | solution.py:584
  30.8 0.6 %collective-permute-start.11 = (f32[8,128]{1,0:T(8,128)S(1)}, f32[8,128]{1,0:T(8,128)S(1)}, u32[]{:S(2)}, u32[]{:S(2)}) collective-permute-start(f32[8,128]{1,0:T(8,128)S(1)} %get-tuple-element.84.own), channel_id=1, source_target_pairs={{0,2},{1,3},{2,0},{3,1},{4,6},{5,7},{6,4},{7,5},{8,10},{9,11},{10,... | collective-permute-start | bytes 12296 | tf_op jit(solution)/shard_map/ppermute | solution.py:584
  31.4 1.0 %collective-permute-start.10 = (f32[8,128]{1,0:T(8,128)S(1)}, f32[8,128]{1,0:T(8,128)S(1)}, u32[]{:S(2)}, u32[]{:S(2)}) collective-permute-start(f32[8,128]{1,0:T(8,128)S(1)} %get-tuple-element.84.own), channel_id=1, source_target_pairs={{0,1},{1,0},{2,3},{3,2},{4,5},{5,4},{6,7},{7,6},{8,9},{9,8},{10,11... | collective-permute-start | bytes 12296 | tf_op jit(solution)/shard_map/ppermute | solution.py:584
  32.4 1.6 %y_solve.1.base = f32[64,2048]{1,0:T(8,128)S(1)} custom-call(f32[1024,128]{1,0:T(8,128)S(1)} %get-tuple-element.85.source, f32[1024,128]{1,0:T(8,128)S(1)} %get-tuple-element.86.lo, f32[1024,128]{1,0:T(8,128)S(1)} %get-tuple-element.87.hi, f32[2,16,128]{2,1,0:T(8,128)S(1)} %get-tuple-element.88.flow, f32[128,8,128]{2,1,0:T(8,128)S(1)} %get-tuple-element.89.along, ...), custom_call_target="tpu_custom_call" | custom-call | flops 2000000 | bytes 1048576 | tf_op jit(solution)/shard_map/y_solve/pallas_call | solution.py:34
  34.0 0.0 collective-permute-done.12.r3
  34.0 2.0 %collective-permute-done.11.r2 = f32[8,128]{1,0:T(8,128)S(1)} collective-permute-done((f32[8,128]{1,0:T(8,128)S(1)}, f32[8,128]{1,0:T(8,128)S(1)}, u32[]{:S(2)}, u32[]{:S(2)}) %collective-permute-start.11) | collective-permute-done | bytes 4128 | tf_op jit(solution)/shard_map/ppermute | solution.py:584
  35.9 0.0 collective-permute-done.10.r1
  35.9 1.1 %finish.1 = f32[64,2048]{1,0:T(8,128)} custom-call(f32[8,128]{1,0:T(8,128)S(1)} %get-tuple-element.84.own, f32[8,128]{1,0:T(8,128)S(1)} %collective-permute-done.10.r1, f32[8,128]{1,0:T(8,128)S(1)} %collective-permute-done.11.r2, f32[8,128]{1,0:T(8,128)S(1)} %collective-permute-done.12.r3, f32[64,2048]{1,0:T(8,128)S(1)} %y_solve.1.base, ...), custom_call_target="tpu_custom_call" | custom-call | flops 2000000 | bytes 1048576 | tf_op jit(solution)/shard_map/finish/pallas_call | solution.py:34
  (2 shorter events, 0.1 us)
Async XLA Ops:
  1.5 5.6 %collective-permute-start = (f32[8,128]{1,0:T(8,128)S(1)}, f32[8,128]{1,0:T(8,128)S(1)}, u32[]{:S(2)}, u32[]{:S(2)}) collective-permute-start(f32[8,128]{1,0:T(8,128)S(1)} %get-tuple-element.55), channel_id=1, source_target_pairs={{0,1},{1,2},{2,3},{3,0},{4,5},{5,6},{6,7},{7,4},{8,9},{9,10},{10,1... | collective-permute-start | bytes 12296 | tf_op jit(solution)/shard_map/ppermute | solution.py:599
  3.1 3.9 %collective-permute-start.1 = (f32[8,128]{1,0:T(8,128)S(1)}, f32[8,128]{1,0:T(8,128)S(1)}, u32[]{:S(2)}, u32[]{:S(2)}) collective-permute-start(f32[8,128]{1,0:T(8,128)S(1)} %get-tuple-element.56), channel_id=1, source_target_pairs={{1,0},{2,1},{3,2},{0,3},{5,4},{6,5},{7,6},{4,7},{9,8},{10,9},{11,1... | collective-permute-start | bytes 12296 | tf_op jit(solution)/shard_map/ppermute | solution.py:600
  7.2 1.3 %collective-permute-start.2 = (f32[7,8,128]{2,1,0:T(8,128)S(1)}, f32[7,8,128]{2,1,0:T(8,128)S(1)}, u32[]{:S(2)}, u32[]{:S(2)}) collective-permute-start(f32[7,8,128]{2,1,0:T(8,128)S(1)} %get-tuple-element.61), channel_id=1, source_target_pairs={{0,4},{4,0},{8,12},{12,8},{16,20},{20,16},{24,28},{28,24},{32,36},... | collective-permute-start | bytes 86024 | tf_op jit(solution)/shard_map/ppermute | solution.py:648
  8.5 6.1 %collective-permute-start.5 = (f32[7,8,128]{2,1,0:T(8,128)S(1)}, f32[7,8,128]{2,1,0:T(8,128)S(1)}, u32[]{:S(2)}, u32[]{:S(2)}) collective-permute-start(f32[7,8,128]{2,1,0:T(8,128)S(1)} %pair.1.own.own_z), channel_id=1, source_target_pairs={{0,24},{4,28},{8,16},{12,20},{16,8},{20,12},{24,0},{28,4},{32,56},... | collective-permute-start | bytes 86024 | tf_op jit(solution)/shard_map/ppermute | solution.py:584
  12.7 5.4 %collective-permute-start.4 = (f32[7,8,128]{2,1,0:T(8,128)S(1)}, f32[7,8,128]{2,1,0:T(8,128)S(1)}, u32[]{:S(2)}, u32[]{:S(2)}) collective-permute-start(f32[7,8,128]{2,1,0:T(8,128)S(1)} %pair.1.own.own_z), channel_id=1, source_target_pairs={{0,16},{4,20},{8,24},{12,28},{16,0},{20,4},{24,8},{28,12},{32,48},... | collective-permute-start | bytes 86024 | tf_op jit(solution)/shard_map/ppermute | solution.py:584
  12.7 5.4 %collective-permute-start.3 = (f32[7,8,128]{2,1,0:T(8,128)S(1)}, f32[7,8,128]{2,1,0:T(8,128)S(1)}, u32[]{:S(2)}, u32[]{:S(2)}) collective-permute-start(f32[7,8,128]{2,1,0:T(8,128)S(1)} %pair.1.own.own_z), channel_id=1, source_target_pairs={{0,8},{4,12},{8,0},{12,4},{16,24},{20,28},{24,16},{28,20},{32,40},... | collective-permute-start | bytes 86024 | tf_op jit(solution)/shard_map/ppermute | solution.py:584
  18.1 5.2 %collective-permute-start.8 = (f32[7,8,128]{2,1,0:T(8,128)S(1)}, f32[7,8,128]{2,1,0:T(8,128)S(1)}, u32[]{:S(2)}, u32[]{:S(2)}) collective-permute-start(f32[7,8,128]{2,1,0:T(8,128)S(1)} %four.1.own_y), channel_id=1, source_target_pairs={{0,96},{4,100},{8,104},{12,108},{16,112},{20,116},{24,120},{28,124... | collective-permute-start | bytes 86024 | tf_op jit(solution)/shard_map/ppermute | solution.py:584
  21.2 5.4 %collective-permute-start.7 = (f32[7,8,128]{2,1,0:T(8,128)S(1)}, f32[7,8,128]{2,1,0:T(8,128)S(1)}, u32[]{:S(2)}, u32[]{:S(2)}) collective-permute-start(f32[7,8,128]{2,1,0:T(8,128)S(1)} %four.1.own_y), channel_id=1, source_target_pairs={{0,64},{4,68},{8,72},{12,76},{16,80},{20,84},{24,88},{28,92},{32,9... | collective-permute-start | bytes 86024 | tf_op jit(solution)/shard_map/ppermute | solution.py:584
  21.9 4.7 %collective-permute-start.6 = (f32[7,8,128]{2,1,0:T(8,128)S(1)}, f32[7,8,128]{2,1,0:T(8,128)S(1)}, u32[]{:S(2)}, u32[]{:S(2)}) collective-permute-start(f32[7,8,128]{2,1,0:T(8,128)S(1)} %four.1.own_y), channel_id=1, source_target_pairs={{0,32},{4,36},{8,40},{12,44},{16,48},{20,52},{24,56},{28,60},{32,0... | collective-permute-start | bytes 86024 | tf_op jit(solution)/shard_map/ppermute | solution.py:584
  26.7 1.3 %collective-permute-start.9 = (f32[2,8,128]{2,1,0:T(8,128)S(1)}, f32[2,8,128]{2,1,0:T(8,128)S(1)}, u32[]{:S(2)}, u32[]{:S(2)}) collective-permute-start(f32[2,8,128]{2,1,0:T(8,128)S(1)} %get-tuple-element.76), channel_id=1, source_target_pairs={{0,4},{4,0},{8,12},{12,8},{16,20},{20,16},{24,28},{28,24},{32,36},... | collective-permute-start | bytes 24584 | tf_op jit(solution)/shard_map/ppermute | solution.py:673
  28.3 5.7 %collective-permute-start.12 = (f32[8,128]{1,0:T(8,128)S(1)}, f32[8,128]{1,0:T(8,128)S(1)}, u32[]{:S(2)}, u32[]{:S(2)}) collective-permute-start(f32[8,128]{1,0:T(8,128)S(1)} %get-tuple-element.84.own), channel_id=1, source_target_pairs={{0,3},{1,2},{2,1},{3,0},{4,7},{5,6},{6,5},{7,4},{8,11},{9,10},{10,... | collective-permute-start | bytes 12296 | tf_op jit(solution)/shard_map/ppermute | solution.py:584
  30.8 5.1 %collective-permute-start.11 = (f32[8,128]{1,0:T(8,128)S(1)}, f32[8,128]{1,0:T(8,128)S(1)}, u32[]{:S(2)}, u32[]{:S(2)}) collective-permute-start(f32[8,128]{1,0:T(8,128)S(1)} %get-tuple-element.84.own), channel_id=1, source_target_pairs={{0,2},{1,3},{2,0},{3,1},{4,6},{5,7},{6,4},{7,5},{8,10},{9,11},{10,... | collective-permute-start | bytes 12296 | tf_op jit(solution)/shard_map/ppermute | solution.py:584
  31.4 4.5 %collective-permute-start.10 = (f32[8,128]{1,0:T(8,128)S(1)}, f32[8,128]{1,0:T(8,128)S(1)}, u32[]{:S(2)}, u32[]{:S(2)}) collective-permute-start(f32[8,128]{1,0:T(8,128)S(1)} %get-tuple-element.84.own), channel_id=1, source_target_pairs={{0,1},{1,0},{2,3},{3,2},{4,5},{5,4},{6,7},{7,6},{8,9},{9,8},{10,11... | collective-permute-start | bytes 12296 | tf_op jit(solution)/shard_map/ppermute | solution.py:584

commit v10 on v5

--- a/solution.py
+++ b/solution.py
@@ -11,7 +11,7 @@
 Y_STEPS = 128
 X_LEVELS, Y_LEVELS = 2, 6
 GRANT = (527 << 20) // 10
-RING = (2, 1, 3)
+RING, LAST_RING = (2, 3, 1), (1, 2, 3)
 F32 = jnp.float32
 VMEM = pl.BlockSpec(memory_space=pltpu.VMEM)
 HBM = pl.BlockSpec(memory_space=pltpu.MemorySpace.HBM)
@@ -347,10 +347,10 @@
     return (d_hi * c_lo + be * c_hi) * inverse, (d_lo * c_hi + be * c_lo) * inverse
 
 
-def place(index, own, received, table):
+def place(index, own, received, table, ring=RING):
     table[index] = own[...]
-    for s, value in zip(RING, received):
-        table[lax.rem(index + 4 - s, 4)] = value[...]
+    for s, value in zip(ring, received):
+        table[lax.bitwise_xor(index, s)] = value[...]
 
 
 def pair_kernel(own, other, out):
@@ -530,7 +530,7 @@
 
 def finish_kernel(own, r1, r2, r3, base, y_lo, y_hi, out, table, side, done, sent):
     index = lax.axis_index("gy")
-    place(index, own, (r1, r2, r3), table)
+    place(index, own, (r1, r2, r3), table, LAST_RING)
     lane = lax.broadcasted_iota(jnp.int32, (1, 128), 1)
 
     def port_of(ref):
@@ -565,7 +565,7 @@
     pairs = []
     for i in range(size):
         digit = (i // stride) % 4
-        pairs.append((i, i + ((digit + step) % 4 - digit) * stride))
+        pairs.append((i, i + ((digit ^ step) - digit) * stride))
     return lax.ppermute(value, axis, pairs)
 
 
@@ -581,8 +581,8 @@
         in_specs=[HBM, HBM],
         out_specs=[VMEM] * 5,
     )(t, k)
-    below = around(own_hi, "gy", 4, 1, 1)
-    above = around(own_lo, "gy", 4, 1, 3)
+    below = lax.ppermute(own_hi, "gy", [(i, (i + 1) % 4) for i in range(4)])
+    above = lax.ppermute(own_lo, "gy", [((i + 1) % 4, i) for i in range(4)])
     flat = struct(BANDS * TILES * 8, 128)
     runs = struct(TILES // 2 * 128, 128)
     x_field, y_field = struct(ROWS, TILES, 128), struct(Y_STEPS, 8, 128)
@@ -655,7 +655,7 @@
         [table, table, square],
         name="y_port",
     )(own_y, *from_y, own_z, *from_z, own, other, mixed, known, y_ends)
-    from_gy = [around(port, "gy", 4, 1, s) for s in RING]
+    from_gy = [around(port, "gy", 4, 1, s) for s in LAST_RING]
     base = call(
         y_solve_kernel, natural, [scratch(y_field), scratch(runs)], name="y_solve"
     )(source, lo_flat, hi_flat, flow, *y_coefficients, t_flat)

time: 36.9 us -> 35.7 us (0.967)
  starting transfers between devices: 21.5 us -> 16.5 us
  waiting for transfers between devices: 6.17 us -> 10.2 us
    ppermute x11 -> x9, starting transfers between devices: 21.4 us -> 13.2 us  [around(): return lax.ppermute(value, axis, pairs)]
    ppermute x11 -> x9, waiting for transfers between devices: 5.24 us -> 9.24 us  [around(): return lax.ppermute(value, axis, pairs)]
    ppermute x0 -> x2, starting transfers between devices: none -> 3.31 us  [the longest x1 1.66 us: per_device(): above = lax.ppermute(own_lo, 'gy', [((i + 1) % 4, i) for i in range(4)])]
  transfers between devices with their start and end apart: 12 -> 12, of which waited for: 4 -> 7; matrix products, arithmetic and copies ran while one was open for 0% -> 0% of each run, Pallas kernels for 15% -> 16%
where the time goes in v10:
time: 35.7 us; the launch traced here: 35.6 us
  starting transfers between devices  16.5 us (46%)
  waiting for transfers between devices  10.2 us (29%)
  Pallas kernels  8.77 us (25%)
    ppermute x9, starting transfers between devices, around(): return lax.ppermute(value, axis, pairs)  13.2 us
    ppermute x9, waiting for transfers between devices, around(): return lax.ppermute(value, axis, pairs)  9.24 us
    pallas_call x12, Pallas kernels, run(): pl.pallas_call(kernel, out_shape=outs, **windows or whole(outs, args), sc...  8.77 us
    ppermute x1, starting transfers between devices, per_device(): above = lax.ppermute(own_lo, 'gy', [((i + 1) % 4, i) for i in range(4)])  1.66 us
    ppermute x1, starting transfers between devices, per_device(): below = lax.ppermute(own_hi, 'gy', [(i, (i + 1) % 4) for i in range(4)])  1.64 us
    ppermute x1, waiting for transfers between devices, per_device(): other = lax.ppermute(own, 'gx', [(i, i ^ 1) for i in range(32)])  0.93 us
  transfers between devices with their start and end apart: 12, of which 7 were waited for; matrix products, arithmetic and copies ran while one was open for 0% of the time, Pallas kernels for 16%

profile of v10, /device:TPU:0, one launch (start us, length us, event | category | flops | bytes accessed | tf_op | source)
XLA Modules:
  0.0 35.6 jit_solution(16759446577582226923)
XLA Ops:
  0.0 1.5 %load.1 = (f32[64,2048]{1,0:T(8,128)S(1)}, f32[64,2048]{1,0:T(8,128)S(1)}, f32[8,128]{1,0:T(8,128)S(1)}, f32[8,128]{1,0:T(8,128)S(1)}, f32[8,128]{1,0:T(8,128)S(1)}) custom-call(f32[64,2048]{1,0:T(8,128)} %bitcast.3, f32[64,2048]{1,0:T(8,128)} %bitcast.4), custom_call_target="tpu_custom_call" | custom-call | flops 2000000 | bytes 1048576 | tf_op jit(solution)/shard_map/load/pallas_call | solution.py:34
  1.5 1.6 %collective-permute-start = (f32[8,128]{1,0:T(8,128)S(1)}, f32[8,128]{1,0:T(8,128)S(1)}, u32[]{:S(2)}, u32[]{:S(2)}) collective-permute-start(f32[8,128]{1,0:T(8,128)S(1)} %get-tuple-element.52), channel_id=1, source_target_pairs={{0,1},{1,2},{2,3},{3,0},{4,5},{5,6},{6,7},{7,4},{8,9},{9,10},{10,1... | collective-permute-start | bytes 12296 | tf_op jit(solution)/shard_map/ppermute | solution.py:584
  3.1 1.7 %collective-permute-start.1 = (f32[8,128]{1,0:T(8,128)S(1)}, f32[8,128]{1,0:T(8,128)S(1)}, u32[]{:S(2)}, u32[]{:S(2)}) collective-permute-start(f32[8,128]{1,0:T(8,128)S(1)} %get-tuple-element.53), channel_id=1, source_target_pairs={{1,0},{2,1},{3,2},{0,3},{5,4},{6,5},{7,6},{4,7},{9,8},{10,9},{11,1... | collective-permute-start | bytes 12296 | tf_op jit(solution)/shard_map/ppermute | solution.py:585
  4.8 1.2 %y_matrix.1 = (f32[128,8,128]{2,1,0:T(8,128)S(1)}, f32[128,8,128]{2,1,0:T(8,128)S(1)}, f32[128,8,128]{2,1,0:T(8,128)S(1)}, f32[52,8,128]{2,1,0:T(8,128)S(1)}, f3...) custom-call(f32[64,2048]{1,0:T(8,128)S(1)} %get-tuple-element.47.k), custom_call_target="tpu_custom_call" | custom-call | flops 2000000 | bytes 1048576 | tf_op jit(solution)/shard_map/y_matrix/pallas_call | solution.py:34
  6.0 1.1 %x_matrix.1 = (f32[1024,128]{1,0:T(8,128)S(1)}, f32[64,16,128]{2,1,0:T(8,128)S(1)}, f32[64,16,128]{2,1,0:T(8,128)S(1)}, f32[64,16,128]{2,1,0:T(8,128)S(1)}, f32[...) custom-call(f32[64,2048]{1,0:T(8,128)S(1)} %get-tuple-element.46.t, ...), custom_call_target="tpu_custom_call" | custom-call | flops 2000000 | bytes 1048576 | tf_op jit(solution)/shard_map/x_matrix/pallas_call | solution.py:34
  7.1 0.0 collective-permute-done.below
  7.1 0.0 collective-permute-done.1.above
  7.1 0.1 x_port.1
  7.2 0.1 collective-permute-start.2
  7.3 0.3 x_solve.1.u
  7.6 0.9 %collective-permute-done.2.other = f32[7,16,128]{2,1,0:T(8,128)S(1)} collective-permute-done((f32[7,16,128]{2,1,0:T(8,128)S(1)}, f32[7,16,128]{2,1,0:T(8,128)S(1)}, u32[]{:S(2)}, u32[]{:S(2)}) %collective-permute-start.2) | collective-permute-done | bytes 57376 | tf_op jit(solution)/shard_map/ppermute | solution.py:631
  8.5 4.0 %collective-permute-start.3 = (f32[7,16,128]{2,1,0:T(8,128)S(1)}, f32[7,16,128]{2,1,0:T(8,128)S(1)}, u32[]{:S(2)}, u32[]{:S(2)}) collective-permute-start(f32[7,16,128]{2,1,0:T(8,128)S(1)} %pair.1.own.own_z), channel_id=1, source_target_pairs={{0,16},{4,20},{8,24},{12,28},{16,0},{20,4},{24,8},{28,12},{32,48},... | collective-permute-start | bytes 172040 | tf_op jit(solution)/shard_map/ppermute | solution.py:569
  12.6 0.7 %collective-permute-start.4 = (f32[7,16,128]{2,1,0:T(8,128)S(1)}, f32[7,16,128]{2,1,0:T(8,128)S(1)}, u32[]{:S(2)}, u32[]{:S(2)}) collective-permute-start(f32[7,16,128]{2,1,0:T(8,128)S(1)} %pair.1.own.own_z), channel_id=1, source_target_pairs={{0,24},{4,28},{8,16},{12,20},{16,8},{20,12},{24,0},{28,4},{32,56},... | collective-permute-start | bytes 172040 | tf_op jit(solution)/shard_map/ppermute | solution.py:569
  13.3 0.3 collective-permute-start.5
  13.6 0.9 %upright.1 = (f32[64,2048]{1,0:T(8,128)S(1)}, f32[64,2048]{1,0:T(8,128)S(1)}) custom-call(f32[128,8,128]{2,1,0:T(8,128)S(1)} %get-tuple-element.65.lo, f32[128,8,128]{2,1,0:T(8,128)S(1)} %get-tuple-element.66.hi), custom_call_target="tpu_custom_call" | custom-call | flops 2000000 | bytes 1048576 | tf_op jit(solution)/shard_map/upright/pallas_call | solution.py:34
  14.5 0.4 %collective-permute-done.3.r1.z1 = f32[7,16,128]{2,1,0:T(8,128)S(1)} collective-permute-done((f32[7,16,128]{2,1,0:T(8,128)S(1)}, f32[7,16,128]{2,1,0:T(8,128)S(1)}, u32[]{:S(2)}, u32[]{:S(2)}) %collective-permute-start.3) | collective-permute-done | bytes 57376 | tf_op jit(solution)/shard_map/ppermute | solution.py:569
  14.8 3.1 %collective-permute-done.4.r2.z2 = f32[7,16,128]{2,1,0:T(8,128)S(1)} collective-permute-done((f32[7,16,128]{2,1,0:T(8,128)S(1)}, f32[7,16,128]{2,1,0:T(8,128)S(1)}, u32[]{:S(2)}, u32[]{:S(2)}) %collective-permute-start.4) | collective-permute-done | bytes 57376 | tf_op jit(solution)/shard_map/ppermute | solution.py:569
  18.0 0.0 collective-permute-done.5.r3.z3
  18.0 0.1 four.1.own_y
  18.0 3.3 %collective-permute-start.6 = (f32[7,16,128]{2,1,0:T(8,128)S(1)}, f32[7,16,128]{2,1,0:T(8,128)S(1)}, u32[]{:S(2)}, u32[]{:S(2)}) collective-permute-start(f32[7,16,128]{2,1,0:T(8,128)S(1)} %four.1.own_y), channel_id=1, source_target_pairs={{0,64},{4,68},{8,72},{12,76},{16,80},{20,84},{24,88},{28,92},{32,9... | collective-permute-start | bytes 172040 | tf_op jit(solution)/shard_map/ppermute | solution.py:569
  21.3 1.1 %collective-permute-start.7 = (f32[7,16,128]{2,1,0:T(8,128)S(1)}, f32[7,16,128]{2,1,0:T(8,128)S(1)}, u32[]{:S(2)}, u32[]{:S(2)}) collective-permute-start(f32[7,16,128]{2,1,0:T(8,128)S(1)} %four.1.own_y), channel_id=1, source_target_pairs={{0,96},{4,100},{8,104},{12,108},{16,112},{20,116},{24,120},{28,124... | collective-permute-start | bytes 172040 | tf_op jit(solution)/shard_map/ppermute | solution.py:569
  22.4 0.0 collective-permute-start.8
  22.4 0.6 %blend.1 = (f32[1024,128]{1,0:T(8,128)S(1)}, f32[1024,128]{1,0:T(8,128)S(1)}, f32[1024,128]{1,0:T(8,128)S(1)}, f32[4,1024,128]{2,1,0:T(8,128)S(1)}, f32[8,128]{1,0:T(8,128)S(1)}) custom-call(f32[64,16,128]{2,1,0:T(8,128)S(1)} %x_solve.1.u, f32[64,16,128]{2,1,0:T(8,128)S(1)} %get-tuple-element.49.lo.x_lo, f32[64,16,128]{2,1,0:T(8,128)S(1)} %get-tuple-element.50.hi.x_hi, ...), custom_call_target="tpu_custom_call" | custom-call | flops 2000000 | bytes 1048576 | tf_op jit(solution)/shard_map/blend/pallas_call | solution.py:34
  23.0 0.8 %collective-permute-done.6.y1 = f32[7,16,128]{2,1,0:T(8,128)S(1)} collective-permute-done((f32[7,16,128]{2,1,0:T(8,128)S(1)}, f32[7,16,128]{2,1,0:T(8,128)S(1)}, u32[]{:S(2)}, u32[]{:S(2)}) %collective-permute-start.6) | collective-permute-done | bytes 57376 | tf_op jit(solution)/shard_map/ppermute | solution.py:569
  23.8 2.9 %collective-permute-done.7.y2 = f32[7,16,128]{2,1,0:T(8,128)S(1)} collective-permute-done((f32[7,16,128]{2,1,0:T(8,128)S(1)}, f32[7,16,128]{2,1,0:T(8,128)S(1)}, u32[]{:S(2)}, u32[]{:S(2)}) %collective-permute-start.7) | collective-permute-done | bytes 57376 | tf_op jit(solution)/shard_map/ppermute | solution.py:569
  26.7 0.0 collective-permute-done.8.y3
  26.7 0.4 %y_port.1 = (f32[8,128]{1,0:T(8,128)S(1)}, f32[2,16,128]{2,1,0:T(8,128)S(1)}) custom-call(f32[7,16,128]{2,1,0:T(8,128)S(1)} %four.1.own_y, f32[7,16,128]{2,1,0:T(8,128)S(1)} %collective-permute-done.6.y1, f32[7,16,128]{2,1,0:T(8,128)S(1)} %collective-permute-done.7.y2, f32[7,16,128]{2,1,0:T(8,128)S(1)} %collective-permute-done.8.y3, ...), custom_call_target="tpu_custom_call" | custom-call | flops 2000000 | bytes 1048576 | tf_op jit(solution)/shard_map/y_port/pallas_call | solution.py:34
  27.1 2.3 %collective-permute-start.10 = (f32[8,128]{1,0:T(8,128)S(1)}, f32[8,128]{1,0:T(8,128)S(1)}, u32[]{:S(2)}, u32[]{:S(2)}) collective-permute-start(f32[8,128]{1,0:T(8,128)S(1)} %get-tuple-element.78.own), channel_id=1, source_target_pairs={{0,2},{1,3},{2,0},{3,1},{4,6},{5,7},{6,4},{7,5},{8,10},{9,11},{10,... | collective-permute-start | bytes 12296 | tf_op jit(solution)/shard_map/ppermute | solution.py:569
  29.5 1.4 %collective-permute-start.11 = (f32[8,128]{1,0:T(8,128)S(1)}, f32[8,128]{1,0:T(8,128)S(1)}, u32[]{:S(2)}, u32[]{:S(2)}) collective-permute-start(f32[8,128]{1,0:T(8,128)S(1)} %get-tuple-element.78.own), channel_id=1, source_target_pairs={{0,3},{1,2},{2,1},{3,0},{4,7},{5,6},{6,5},{7,4},{8,11},{9,10},{10,... | collective-permute-start | bytes 12296 | tf_op jit(solution)/shard_map/ppermute | solution.py:569
  30.9 0.0 collective-permute-start.9
  30.9 1.6 %y_solve.1.base = f32[64,2048]{1,0:T(8,128)S(1)} custom-call(f32[1024,128]{1,0:T(8,128)S(1)} %get-tuple-element.79.source, f32[1024,128]{1,0:T(8,128)S(1)} %get-tuple-element.80.lo, f32[1024,128]{1,0:T(8,128)S(1)} %get-tuple-element.81.hi, f32[2,16,128]{2,1,0:T(8,128)S(1)} %get-tuple-element.82.flow, f32[128,8,128]{2,1,0:T(8,128)S(1)} %get-tuple-element.83.along, ...), custom_call_target="tpu_custom_call" | custom-call | flops 2000000 | bytes 1048576 | tf_op jit(solution)/shard_map/y_solve/pallas_call | solution.py:34
  32.5 0.0 collective-permute-done.10.r2
  32.5 1.8 %collective-permute-done.11.r3 = f32[8,128]{1,0:T(8,128)S(1)} collective-permute-done((f32[8,128]{1,0:T(8,128)S(1)}, f32[8,128]{1,0:T(8,128)S(1)}, u32[]{:S(2)}, u32[]{:S(2)}) %collective-permute-start.11) | collective-permute-done | bytes 4128 | tf_op jit(solution)/shard_map/ppermute | solution.py:569
  34.3 0.2 collective-permute-done.9.r1
  34.5 1.1 %finish.1 = f32[64,2048]{1,0:T(8,128)} custom-call(f32[8,128]{1,0:T(8,128)S(1)} %get-tuple-element.78.own, f32[8,128]{1,0:T(8,128)S(1)} %collective-permute-done.9.r1, f32[8,128]{1,0:T(8,128)S(1)} %collective-permute-done.10.r2, f32[8,128]{1,0:T(8,128)S(1)} %collective-permute-done.11.r3, f32[64,2048]{1,0:T(8,128)S(1)} %y_solve.1.base, ...), custom_call_target="tpu_custom_call" | custom-call | flops 2000000 | bytes 1048576 | tf_op jit(solution)/shard_map/finish/pallas_call | solution.py:34
  (1 shorter events, 0.0 us)
Async XLA Ops:
  1.5 5.6 %collective-permute-start = (f32[8,128]{1,0:T(8,128)S(1)}, f32[8,128]{1,0:T(8,128)S(1)}, u32[]{:S(2)}, u32[]{:S(2)}) collective-permute-start(f32[8,128]{1,0:T(8,128)S(1)} %get-tuple-element.52), channel_id=1, source_target_pairs={{0,1},{1,2},{2,3},{3,0},{4,5},{5,6},{6,7},{7,4},{8,9},{9,10},{10,1... | collective-permute-start | bytes 12296 | tf_op jit(solution)/shard_map/ppermute | solution.py:584
  3.1 3.9 %collective-permute-start.1 = (f32[8,128]{1,0:T(8,128)S(1)}, f32[8,128]{1,0:T(8,128)S(1)}, u32[]{:S(2)}, u32[]{:S(2)}) collective-permute-start(f32[8,128]{1,0:T(8,128)S(1)} %get-tuple-element.53), channel_id=1, source_target_pairs={{1,0},{2,1},{3,2},{0,3},{5,4},{6,5},{7,6},{4,7},{9,8},{10,9},{11,1... | collective-permute-start | bytes 12296 | tf_op jit(solution)/shard_map/ppermute | solution.py:585
  7.2 1.3 %collective-permute-start.2 = (f32[7,16,128]{2,1,0:T(8,128)S(1)}, f32[7,16,128]{2,1,0:T(8,128)S(1)}, u32[]{:S(2)}, u32[]{:S(2)}) collective-permute-start(f32[7,16,128]{2,1,0:T(8,128)S(1)} %get-tuple-element.57.own), channel_id=1, source_target_pairs={{0,4},{4,0},{8,12},{12,8},{16,20},{20,16},{24,28},{28,24},{32,36},... | collective-permute-start | bytes 172040 | tf_op jit(solution)/shard_map/ppermute | solution.py:631
  8.5 6.3 %collective-permute-start.3 = (f32[7,16,128]{2,1,0:T(8,128)S(1)}, f32[7,16,128]{2,1,0:T(8,128)S(1)}, u32[]{:S(2)}, u32[]{:S(2)}) collective-permute-start(f32[7,16,128]{2,1,0:T(8,128)S(1)} %pair.1.own.own_z), channel_id=1, source_target_pairs={{0,16},{4,20},{8,24},{12,28},{16,0},{20,4},{24,8},{28,12},{32,48},... | collective-permute-start | bytes 172040 | tf_op jit(solution)/shard_map/ppermute | solution.py:569
  12.6 5.4 %collective-permute-start.4 = (f32[7,16,128]{2,1,0:T(8,128)S(1)}, f32[7,16,128]{2,1,0:T(8,128)S(1)}, u32[]{:S(2)}, u32[]{:S(2)}) collective-permute-start(f32[7,16,128]{2,1,0:T(8,128)S(1)} %pair.1.own.own_z), channel_id=1, source_target_pairs={{0,24},{4,28},{8,16},{12,20},{16,8},{20,12},{24,0},{28,4},{32,56},... | collective-permute-start | bytes 172040 | tf_op jit(solution)/shard_map/ppermute | solution.py:569
  13.3 4.7 %collective-permute-start.5 = (f32[7,16,128]{2,1,0:T(8,128)S(1)}, f32[7,16,128]{2,1,0:T(8,128)S(1)}, u32[]{:S(2)}, u32[]{:S(2)}) collective-permute-start(f32[7,16,128]{2,1,0:T(8,128)S(1)} %pair.1.own.own_z), channel_id=1, source_target_pairs={{0,8},{4,12},{8,0},{12,4},{16,24},{20,28},{24,16},{28,20},{32,40},... | collective-permute-start | bytes 172040 | tf_op jit(solution)/shard_map/ppermute | solution.py:569
  18.0 5.8 %collective-permute-start.6 = (f32[7,16,128]{2,1,0:T(8,128)S(1)}, f32[7,16,128]{2,1,0:T(8,128)S(1)}, u32[]{:S(2)}, u32[]{:S(2)}) collective-permute-start(f32[7,16,128]{2,1,0:T(8,128)S(1)} %four.1.own_y), channel_id=1, source_target_pairs={{0,64},{4,68},{8,72},{12,76},{16,80},{20,84},{24,88},{28,92},{32,9... | collective-permute-start | bytes 172040 | tf_op jit(solution)/shard_map/ppermute | solution.py:569
  21.3 5.4 %collective-permute-start.7 = (f32[7,16,128]{2,1,0:T(8,128)S(1)}, f32[7,16,128]{2,1,0:T(8,128)S(1)}, u32[]{:S(2)}, u32[]{:S(2)}) collective-permute-start(f32[7,16,128]{2,1,0:T(8,128)S(1)} %four.1.own_y), channel_id=1, source_target_pairs={{0,96},{4,100},{8,104},{12,108},{16,112},{20,116},{24,120},{28,124... | collective-permute-start | bytes 172040 | tf_op jit(solution)/shard_map/ppermute | solution.py:569
  22.4 4.3 %collective-permute-start.8 = (f32[7,16,128]{2,1,0:T(8,128)S(1)}, f32[7,16,128]{2,1,0:T(8,128)S(1)}, u32[]{:S(2)}, u32[]{:S(2)}) collective-permute-start(f32[7,16,128]{2,1,0:T(8,128)S(1)} %four.1.own_y), channel_id=1, source_target_pairs={{0,32},{4,36},{8,40},{12,44},{16,48},{20,52},{24,56},{28,60},{32,0... | collective-permute-start | bytes 172040 | tf_op jit(solution)/shard_map/ppermute | solution.py:569
  27.1 5.3 %collective-permute-start.10 = (f32[8,128]{1,0:T(8,128)S(1)}, f32[8,128]{1,0:T(8,128)S(1)}, u32[]{:S(2)}, u32[]{:S(2)}) collective-permute-start(f32[8,128]{1,0:T(8,128)S(1)} %get-tuple-element.78.own), channel_id=1, source_target_pairs={{0,2},{1,3},{2,0},{3,1},{4,6},{5,7},{6,4},{7,5},{8,10},{9,11},{10,... | collective-permute-start | bytes 12296 | tf_op jit(solution)/shard_map/ppermute | solution.py:569
  29.5 4.8 %collective-permute-start.11 = (f32[8,128]{1,0:T(8,128)S(1)}, f32[8,128]{1,0:T(8,128)S(1)}, u32[]{:S(2)}, u32[]{:S(2)}) collective-permute-start(f32[8,128]{1,0:T(8,128)S(1)} %get-tuple-element.78.own), channel_id=1, source_target_pairs={{0,3},{1,2},{2,1},{3,0},{4,7},{5,6},{6,5},{7,4},{8,11},{9,10},{10,... | collective-permute-start | bytes 12296 | tf_op jit(solution)/shard_map/ppermute | solution.py:569
  30.9 3.6 %collective-permute-start.9 = (f32[8,128]{1,0:T(8,128)S(1)}, f32[8,128]{1,0:T(8,128)S(1)}, u32[]{:S(2)}, u32[]{:S(2)}) collective-permute-start(f32[8,128]{1,0:T(8,128)S(1)} %get-tuple-element.78.own), channel_id=1, source_target_pairs={{0,1},{1,0},{2,3},{3,2},{4,5},{5,4},{6,7},{7,6},{8,9},{9,8},{10,11... | collective-permute-start | bytes 12296 | tf_op jit(solution)/shard_map/ppermute | solution.py:569

commit v11 on v10

--- a/solution.py
+++ b/solution.py
@@ -167,7 +167,7 @@
     return ref[pl.ds((i // 8) * (8 * TILES) + i % 8, TILES, stride=8), :]
 
 
-def load_kernel(t_far, k_far, t, k, lo, hi, own, arrived):
+def load_kernel(t_far, k_far, t, k, one, three, own, arrived):
     copies = []
     for band in range(BANDS):
         at = pl.ds(8 * band, 8)
@@ -175,16 +175,21 @@
             copy = pltpu.make_async_copy(far.at[at, :], near.at[at, :], arrived.at[n, band])
             copy.start()
             copies.append(copy)
-    for ref in (lo, hi, own):
+    for ref in (one, three, own):
         ref[...] = jnp.zeros_like(ref)
     for copy in copies:
         copy.wait()
+    edges = []
     for n, (ref, column) in enumerate(((t, 0), (k, 0), (t, TILES - 1), (k, TILES - 1))):
         strip = ref[:, 128 * column : 128 * column + 128].T
         at = 127 if column else 0
-        edge = strip[at : at + 1, :]
-        own[n : n + 1, 0:ROWS] = edge
-        (hi if column else lo)[n % 2 : n % 2 + 1, 0:ROWS] = edge
+        edges.append(strip[at : at + 1, :])
+        own[n : n + 1, 0:ROWS] = edges[n]
+    even = lax.rem(lax.axis_index("gy"), 2) == 0
+    for n in range(2):
+        lo, hi = edges[n], edges[2 + n]
+        one[n : n + 1, 0:ROWS] = jnp.where(even, hi, lo)
+        three[n : n + 1, 0:ROWS] = jnp.where(even, lo, hi)
 
 
 def total(terms):
@@ -252,12 +257,15 @@
     ends[6] = row(flat, ROWS - 1)
 
 
-def x_port_kernel(ends, lo, hi, own, below, above, port, edge, side):
+def x_port_kernel(ends, lo, hi, own, from_one, from_three, port, edge, side):
     at = lax.axis_index("gy")
     side[...] = jnp.zeros_like(side)
     t_lo, k_lo, t_hi, k_hi = (own[n : n + 1, :] for n in range(4))
-    before = jnp.where(at == 0, 0.0, below[...])
-    after = jnp.where(at == lax.axis_size("gy") - 1, 0.0, above[...])
+    even = lax.rem(at, 2) == 0
+    below = jnp.where(even, from_three[...], from_one[...])
+    above = jnp.where(even, from_one[...], from_three[...])
+    before = jnp.where(at == 0, 0.0, below)
+    after = jnp.where(at == lax.axis_size("gy") - 1, 0.0, above)
     side[0:1, :] = -8000.0 * (k_lo + before[1:2, :]) * (t_lo - before[0:1, :])
     side[127:128, :] = 8000.0 * (k_hi + after[1:2, :]) * (after[0:1, :] - t_hi)
     edge[...] = side[...].T[0:ROWS, :]
@@ -572,7 +580,7 @@
 def per_device(initial_heat_state, thermal_coefficient):
     t, k = initial_heat_state[0], thermal_coefficient[0]
     natural = struct(ROWS, COLS)
-    t, k, own_lo, own_hi, own_edges = call(
+    t, k, to_one, to_three, own_edges = call(
         load_kernel,
         [natural, natural] + [struct(8, 128)] * 3,
         [pltpu.SemaphoreType.DMA((2, BANDS))],
@@ -581,8 +589,8 @@
         in_specs=[HBM, HBM],
         out_specs=[VMEM] * 5,
     )(t, k)
-    below = lax.ppermute(own_hi, "gy", [(i, (i + 1) % 4) for i in range(4)])
-    above = lax.ppermute(own_lo, "gy", [((i + 1) % 4, i) for i in range(4)])
+    from_three = around(to_three, "gy", 4, 1, 3)
+    from_one = around(to_one, "gy", 4, 1, 1)
     flat = struct(BANDS * TILES * 8, 128)
     runs = struct(TILES // 2 * 128, 128)
     x_field, y_field = struct(ROWS, TILES, 128), struct(Y_STEPS, 8, 128)
@@ -603,6 +611,21 @@
         ],
         name="x_matrix",
     )(t, k)
+    own, edge = call(
+        x_port_kernel,
+        [x_port, struct(ROWS, 128)],
+        [pltpu.VMEM((128, 128), F32)],
+        flops=200_000,
+        name="x_port",
+    )(x_ends, x_lo, x_hi, own_edges, from_one, from_three)
+    u = call(x_solve_kernel, x_field, [scratch(flat)], flops=700_000, name="x_solve")(
+        e, *x_coefficients, edge
+    )
+    other = lax.ppermute(own, "gx", [(i, i ^ 1) for i in range(32)])
+    other, u = lax.optimization_barrier((other, u))
+    own_z = call(pair_kernel, x_port, name="pair")(own, other)
+    k_y, own_z = lax.optimization_barrier((k, own_z))
+    from_z = [around(own_z, "gx", 32, 2, s) for s in RING]
     *y_coefficients, y_lo, y_hi, y_ends = call(
         y_matrix_kernel,
         [
@@ -616,22 +639,7 @@
         ],
         [scratch(runs)],
         name="y_matrix",
-    )(k)
-    below, above, y_lo = lax.optimization_barrier((below, above, y_lo))
-    own, edge = call(
-        x_port_kernel,
-        [x_port, struct(ROWS, 128)],
-        [pltpu.VMEM((128, 128), F32)],
-        flops=200_000,
-        name="x_port",
-    )(x_ends, x_lo, x_hi, own_edges, below, above)
-    u = call(x_solve_kernel, x_field, [scratch(flat)], flops=700_000, name="x_solve")(
-        e, *x_coefficients, edge
-    )
-    other = lax.ppermute(own, "gx", [(i, i ^ 1) for i in range(32)])
-    other, u = lax.optimization_barrier((other, u))
-    own_z = call(pair_kernel, x_port, name="pair")(own, other)
-    from_z = [around(own_z, "gx", 32, 2, s) for s in RING]
+    )(k_y)
     flat_lo, flat_hi = call(
         upright_kernel,
         [natural, natural],

time: 35.7 us -> 35.5 us (level)
    ppermute x9 -> x11, starting transfers between devices: 13.2 us -> 16.6 us  [around(): return lax.ppermute(value, axis, pairs)]
    ppermute x2 -> x0, starting transfers between devices: 3.31 us -> none  [the longest x1 1.66 us: per_device(): above = lax.ppermute(own_lo, 'gy', [((i + 1) % 4, i) for i in range(4)])]
    ppermute x9 -> x11, waiting for transfers between devices: 9.24 us -> 9.06 us  [around(): return lax.ppermute(value, axis, pairs)]
where the time goes in v11:
time: 35.5 us; the launch traced here: 35.4 us
  starting transfers between devices  16.6 us (47%)
  waiting for transfers between devices  9.98 us (28%)
  Pallas kernels  8.68 us (24%)
    ppermute x11, starting transfers between devices, around(): return lax.ppermute(value, axis, pairs)  16.6 us
    ppermute x11, waiting for transfers between devices, around(): return lax.ppermute(value, axis, pairs)  9.06 us
    pallas_call x12, Pallas kernels, run(): pl.pallas_call(kernel, out_shape=outs, **windows or whole(outs, args), sc...  8.68 us
    ppermute x1, waiting for transfers between devices, per_device(): other = lax.ppermute(own, 'gx', [(i, i ^ 1) for i in range(32)])  0.92 us
  transfers between devices with their start and end apart: 12, of which 7 were waited for; matrix products, arithmetic and copies ran while one was open for 0% of the time, Pallas kernels for 16%

profile of v11, /device:TPU:0, one launch (start us, length us, event | category | flops | bytes accessed | tf_op | source)
XLA Modules:
  0.0 35.4 jit_solution(8567356659640641079)
XLA Ops:
  0.0 1.5 %load.1 = (f32[64,2048]{1,0:T(8,128)S(1)}, f32[64,2048]{1,0:T(8,128)S(1)}, f32[8,128]{1,0:T(8,128)S(1)}, f32[8,128]{1,0:T(8,128)S(1)}, f32[8,128]{1,0:T(8,128)S(1)}) custom-call(f32[64,2048]{1,0:T(8,128)} %bitcast.3, f32[64,2048]{1,0:T(8,128)} %bitcast.4), custom_call_target="tpu_custom_call" | custom-call | flops 2000000 | bytes 1048576 | tf_op jit(solution)/shard_map/load/pallas_call | solution.py:34
  1.5 1.7 %collective-permute-start = (f32[8,128]{1,0:T(8,128)S(1)}, f32[8,128]{1,0:T(8,128)S(1)}, u32[]{:S(2)}, u32[]{:S(2)}) collective-permute-start(f32[8,128]{1,0:T(8,128)S(1)} %get-tuple-element.51), channel_id=1, source_target_pairs={{0,1},{1,0},{2,3},{3,2},{4,5},{5,4},{6,7},{7,6},{8,9},{9,8},{10,11... | collective-permute-start | bytes 12296 | tf_op jit(solution)/shard_map/ppermute | solution.py:577
  3.2 2.1 %collective-permute-start.1 = (f32[8,128]{1,0:T(8,128)S(1)}, f32[8,128]{1,0:T(8,128)S(1)}, u32[]{:S(2)}, u32[]{:S(2)}) collective-permute-start(f32[8,128]{1,0:T(8,128)S(1)} %get-tuple-element.52), channel_id=1, source_target_pairs={{0,3},{1,2},{2,1},{3,0},{4,7},{5,6},{6,5},{7,4},{8,11},{9,10},{10,... | collective-permute-start | bytes 12296 | tf_op jit(solution)/shard_map/ppermute | solution.py:577
  5.2 1.0 %x_matrix.1 = (f32[1024,128]{1,0:T(8,128)S(1)}, f32[64,16,128]{2,1,0:T(8,128)S(1)}, f32[64,16,128]{2,1,0:T(8,128)S(1)}, f32[64,16,128]{2,1,0:T(8,128)S(1)}, f32[...) custom-call(f32[64,2048]{1,0:T(8,128)S(1)} %get-tuple-element.46.t, ...), custom_call_target="tpu_custom_call" | custom-call | flops 2000000 | bytes 1048576 | tf_op jit(solution)/shard_map/x_matrix/pallas_call | solution.py:34
  6.3 0.0 collective-permute-done.from_one
  6.3 1.7 %collective-permute-done.1.from_three = f32[8,128]{1,0:T(8,128)S(1)} collective-permute-done((f32[8,128]{1,0:T(8,128)S(1)}, f32[8,128]{1,0:T(8,128)S(1)}, u32[]{:S(2)}, u32[]{:S(2)}) %collective-permute-start.1) | collective-permute-done | bytes 4128 | tf_op jit(solution)/shard_map/ppermute | solution.py:577
  8.0 0.1 x_port.1
  8.1 0.1 collective-permute-start.2
  8.2 0.3 x_solve.1.u
  8.5 0.9 %collective-permute-done.2.other = f32[7,16,128]{2,1,0:T(8,128)S(1)} collective-permute-done((f32[7,16,128]{2,1,0:T(8,128)S(1)}, f32[7,16,128]{2,1,0:T(8,128)S(1)}, u32[]{:S(2)}, u32[]{:S(2)}) %collective-permute-start.2) | collective-permute-done | bytes 57376 | tf_op jit(solution)/shard_map/ppermute | solution.py:624
  9.4 4.0 %collective-permute-start.3 = (f32[7,16,128]{2,1,0:T(8,128)S(1)}, f32[7,16,128]{2,1,0:T(8,128)S(1)}, u32[]{:S(2)}, u32[]{:S(2)}) collective-permute-start(f32[7,16,128]{2,1,0:T(8,128)S(1)} %pair.1.own.own_z), channel_id=1, source_target_pairs={{0,16},{4,20},{8,24},{12,28},{16,0},{20,4},{24,8},{28,12},{32,48},... | collective-permute-start | bytes 172040 | tf_op jit(solution)/shard_map/ppermute | solution.py:577
  13.4 0.7 %collective-permute-start.4 = (f32[7,16,128]{2,1,0:T(8,128)S(1)}, f32[7,16,128]{2,1,0:T(8,128)S(1)}, u32[]{:S(2)}, u32[]{:S(2)}) collective-permute-start(f32[7,16,128]{2,1,0:T(8,128)S(1)} %pair.1.own.own_z), channel_id=1, source_target_pairs={{0,24},{4,28},{8,16},{12,20},{16,8},{20,12},{24,0},{28,4},{32,56},... | collective-permute-start | bytes 172040 | tf_op jit(solution)/shard_map/ppermute | solution.py:577
  14.1 0.3 collective-permute-start.5
  14.4 1.2 %y_matrix.1 = (f32[128,8,128]{2,1,0:T(8,128)S(1)}, f32[128,8,128]{2,1,0:T(8,128)S(1)}, f32[128,8,128]{2,1,0:T(8,128)S(1)}, f32[52,8,128]{2,1,0:T(8,128)S(1)}, f3...) custom-call(f32[64,2048]{1,0:T(8,128)S(1)} %get-tuple-element.62.k), custom_call_target="tpu_custom_call" | custom-call | flops 2000000 | bytes 1048576 | tf_op jit(solution)/shard_map/y_matrix/pallas_call | solution.py:34
  15.6 0.8 %upright.1 = (f32[64,2048]{1,0:T(8,128)S(1)}, f32[64,2048]{1,0:T(8,128)S(1)}) custom-call(f32[128,8,128]{2,1,0:T(8,128)S(1)} %get-tuple-element.63.lo, f32[128,8,128]{2,1,0:T(8,128)S(1)} %get-tuple-element.64.hi), custom_call_target="tpu_custom_call" | custom-call | flops 2000000 | bytes 1048576 | tf_op jit(solution)/shard_map/upright/pallas_call | solution.py:34
  16.5 0.0 collective-permute-done.3.r1.z1
  16.5 2.3 %collective-permute-done.4.r2.z2 = f32[7,16,128]{2,1,0:T(8,128)S(1)} collective-permute-done((f32[7,16,128]{2,1,0:T(8,128)S(1)}, f32[7,16,128]{2,1,0:T(8,128)S(1)}, u32[]{:S(2)}, u32[]{:S(2)}) %collective-permute-start.4) | collective-permute-done | bytes 57376 | tf_op jit(solution)/shard_map/ppermute | solution.py:577
  18.8 0.0 collective-permute-done.5.r3.z3
  18.8 0.1 four.1.own_y
  18.9 3.3 %collective-permute-start.6 = (f32[7,16,128]{2,1,0:T(8,128)S(1)}, f32[7,16,128]{2,1,0:T(8,128)S(1)}, u32[]{:S(2)}, u32[]{:S(2)}) collective-permute-start(f32[7,16,128]{2,1,0:T(8,128)S(1)} %four.1.own_y), channel_id=1, source_target_pairs={{0,64},{4,68},{8,72},{12,76},{16,80},{20,84},{24,88},{28,92},{32,9... | collective-permute-start | bytes 172040 | tf_op jit(solution)/shard_map/ppermute | solution.py:577
  22.1 1.1 %collective-permute-start.7 = (f32[7,16,128]{2,1,0:T(8,128)S(1)}, f32[7,16,128]{2,1,0:T(8,128)S(1)}, u32[]{:S(2)}, u32[]{:S(2)}) collective-permute-start(f32[7,16,128]{2,1,0:T(8,128)S(1)} %four.1.own_y), channel_id=1, source_target_pairs={{0,96},{4,100},{8,104},{12,108},{16,112},{20,116},{24,120},{28,124... | collective-permute-start | bytes 172040 | tf_op jit(solution)/shard_map/ppermute | solution.py:577
  23.2 0.0 collective-permute-start.8
  23.2 0.6 %blend.1 = (f32[1024,128]{1,0:T(8,128)S(1)}, f32[1024,128]{1,0:T(8,128)S(1)}, f32[1024,128]{1,0:T(8,128)S(1)}, f32[4,1024,128]{2,1,0:T(8,128)S(1)}, f32[8,128]{1,0:T(8,128)S(1)}) custom-call(f32[64,16,128]{2,1,0:T(8,128)S(1)} %x_solve.1.u, f32[64,16,128]{2,1,0:T(8,128)S(1)} %get-tuple-element.48.lo.x_lo, f32[64,16,128]{2,1,0:T(8,128)S(1)} %get-tuple-element.49.hi.x_hi, ...), custom_call_target="tpu_custom_call" | custom-call | flops 2000000 | bytes 1048576 | tf_op jit(solution)/shard_map/blend/pallas_call | solution.py:34
  23.7 0.9 %collective-permute-done.6.y1 = f32[7,16,128]{2,1,0:T(8,128)S(1)} collective-permute-done((f32[7,16,128]{2,1,0:T(8,128)S(1)}, f32[7,16,128]{2,1,0:T(8,128)S(1)}, u32[]{:S(2)}, u32[]{:S(2)}) %collective-permute-start.6) | collective-permute-done | bytes 57376 | tf_op jit(solution)/shard_map/ppermute | solution.py:577
  24.6 2.9 %collective-permute-done.7.y2 = f32[7,16,128]{2,1,0:T(8,128)S(1)} collective-permute-done((f32[7,16,128]{2,1,0:T(8,128)S(1)}, f32[7,16,128]{2,1,0:T(8,128)S(1)}, u32[]{:S(2)}, u32[]{:S(2)}) %collective-permute-start.7) | collective-permute-done | bytes 57376 | tf_op jit(solution)/shard_map/ppermute | solution.py:577
  27.5 0.0 collective-permute-done.8.y3
  27.5 0.4 %y_port.1 = (f32[8,128]{1,0:T(8,128)S(1)}, f32[2,16,128]{2,1,0:T(8,128)S(1)}) custom-call(f32[7,16,128]{2,1,0:T(8,128)S(1)} %four.1.own_y, f32[7,16,128]{2,1,0:T(8,128)S(1)} %collective-permute-done.6.y1, f32[7,16,128]{2,1,0:T(8,128)S(1)} %collective-permute-done.7.y2, f32[7,16,128]{2,1,0:T(8,128)S(1)} %collective-permute-done.8.y3, ...), custom_call_target="tpu_custom_call" | custom-call | flops 2000000 | bytes 1048576 | tf_op jit(solution)/shard_map/y_port/pallas_call | solution.py:34
  28.0 1.5 %collective-permute-start.10 = (f32[8,128]{1,0:T(8,128)S(1)}, f32[8,128]{1,0:T(8,128)S(1)}, u32[]{:S(2)}, u32[]{:S(2)}) collective-permute-start(f32[8,128]{1,0:T(8,128)S(1)} %get-tuple-element.76.own), channel_id=1, source_target_pairs={{0,2},{1,3},{2,0},{3,1},{4,6},{5,7},{6,4},{7,5},{8,10},{9,11},{10,... | collective-permute-start | bytes 12296 | tf_op jit(solution)/shard_map/ppermute | solution.py:577
  29.5 0.7 %collective-permute-start.11 = (f32[8,128]{1,0:T(8,128)S(1)}, f32[8,128]{1,0:T(8,128)S(1)}, u32[]{:S(2)}, u32[]{:S(2)}) collective-permute-start(f32[8,128]{1,0:T(8,128)S(1)} %get-tuple-element.76.own), channel_id=1, source_target_pairs={{0,3},{1,2},{2,1},{3,0},{4,7},{5,6},{6,5},{7,4},{8,11},{9,10},{10,... | collective-permute-start | bytes 12296 | tf_op jit(solution)/shard_map/ppermute | solution.py:577
  30.2 1.3 %collective-permute-start.9 = (f32[8,128]{1,0:T(8,128)S(1)}, f32[8,128]{1,0:T(8,128)S(1)}, u32[]{:S(2)}, u32[]{:S(2)}) collective-permute-start(f32[8,128]{1,0:T(8,128)S(1)} %get-tuple-element.76.own), channel_id=1, source_target_pairs={{0,1},{1,0},{2,3},{3,2},{4,5},{5,4},{6,7},{7,6},{8,9},{9,8},{10,11... | collective-permute-start | bytes 12296 | tf_op jit(solution)/shard_map/ppermute | solution.py:577
  31.5 1.5 %y_solve.1.base = f32[64,2048]{1,0:T(8,128)S(1)} custom-call(f32[1024,128]{1,0:T(8,128)S(1)} %get-tuple-element.77.source, f32[1024,128]{1,0:T(8,128)S(1)} %get-tuple-element.78.lo, f32[1024,128]{1,0:T(8,128)S(1)} %get-tuple-element.79.hi, f32[2,16,128]{2,1,0:T(8,128)S(1)} %get-tuple-element.80.flow, f32[128,8,128]{2,1,0:T(8,128)S(1)} %get-tuple-element.81.along, ...), custom_call_target="tpu_custom_call" | custom-call | flops 2000000 | bytes 1048576 | tf_op jit(solution)/shard_map/y_solve/pallas_call | solution.py:34
  33.0 0.1 collective-permute-done.10.r2
  33.1 1.2 %collective-permute-done.11.r3 = f32[8,128]{1,0:T(8,128)S(1)} collective-permute-done((f32[8,128]{1,0:T(8,128)S(1)}, f32[8,128]{1,0:T(8,128)S(1)}, u32[]{:S(2)}, u32[]{:S(2)}) %collective-permute-start.11) | collective-permute-done | bytes 4128 | tf_op jit(solution)/shard_map/ppermute | solution.py:577
  34.3 0.0 collective-permute-done.9.r1
  34.3 1.1 %finish.1 = f32[64,2048]{1,0:T(8,128)} custom-call(f32[8,128]{1,0:T(8,128)S(1)} %get-tuple-element.76.own, f32[8,128]{1,0:T(8,128)S(1)} %collective-permute-done.9.r1, f32[8,128]{1,0:T(8,128)S(1)} %collective-permute-done.10.r2, f32[8,128]{1,0:T(8,128)S(1)} %collective-permute-done.11.r3, f32[64,2048]{1,0:T(8,128)S(1)} %y_solve.1.base, ...), custom_call_target="tpu_custom_call" | custom-call | flops 2000000 | bytes 1048576 | tf_op jit(solution)/shard_map/finish/pallas_call | solution.py:34
  (1 shorter events, 0.0 us)
Async XLA Ops:
  1.5 4.8 %collective-permute-start = (f32[8,128]{1,0:T(8,128)S(1)}, f32[8,128]{1,0:T(8,128)S(1)}, u32[]{:S(2)}, u32[]{:S(2)}) collective-permute-start(f32[8,128]{1,0:T(8,128)S(1)} %get-tuple-element.51), channel_id=1, source_target_pairs={{0,1},{1,0},{2,3},{3,2},{4,5},{5,4},{6,7},{7,6},{8,9},{9,8},{10,11... | collective-permute-start | bytes 12296 | tf_op jit(solution)/shard_map/ppermute | solution.py:577
  3.2 4.8 %collective-permute-start.1 = (f32[8,128]{1,0:T(8,128)S(1)}, f32[8,128]{1,0:T(8,128)S(1)}, u32[]{:S(2)}, u32[]{:S(2)}) collective-permute-start(f32[8,128]{1,0:T(8,128)S(1)} %get-tuple-element.52), channel_id=1, source_target_pairs={{0,3},{1,2},{2,1},{3,0},{4,7},{5,6},{6,5},{7,4},{8,11},{9,10},{10,... | collective-permute-start | bytes 12296 | tf_op jit(solution)/shard_map/ppermute | solution.py:577
  8.1 1.3 %collective-permute-start.2 = (f32[7,16,128]{2,1,0:T(8,128)S(1)}, f32[7,16,128]{2,1,0:T(8,128)S(1)}, u32[]{:S(2)}, u32[]{:S(2)}) collective-permute-start(f32[7,16,128]{2,1,0:T(8,128)S(1)} %get-tuple-element.53.own), channel_id=1, source_target_pairs={{0,4},{4,0},{8,12},{12,8},{16,20},{20,16},{24,28},{28,24},{32,36},... | collective-permute-start | bytes 172040 | tf_op jit(solution)/shard_map/ppermute | solution.py:624
  9.4 7.1 %collective-permute-start.3 = (f32[7,16,128]{2,1,0:T(8,128)S(1)}, f32[7,16,128]{2,1,0:T(8,128)S(1)}, u32[]{:S(2)}, u32[]{:S(2)}) collective-permute-start(f32[7,16,128]{2,1,0:T(8,128)S(1)} %pair.1.own.own_z), channel_id=1, source_target_pairs={{0,16},{4,20},{8,24},{12,28},{16,0},{20,4},{24,8},{28,12},{32,48},... | collective-permute-start | bytes 172040 | tf_op jit(solution)/shard_map/ppermute | solution.py:577
  13.4 5.4 %collective-permute-start.4 = (f32[7,16,128]{2,1,0:T(8,128)S(1)}, f32[7,16,128]{2,1,0:T(8,128)S(1)}, u32[]{:S(2)}, u32[]{:S(2)}) collective-permute-start(f32[7,16,128]{2,1,0:T(8,128)S(1)} %pair.1.own.own_z), channel_id=1, source_target_pairs={{0,24},{4,28},{8,16},{12,20},{16,8},{20,12},{24,0},{28,4},{32,56},... | collective-permute-start | bytes 172040 | tf_op jit(solution)/shard_map/ppermute | solution.py:577
  14.1 4.7 %collective-permute-start.5 = (f32[7,16,128]{2,1,0:T(8,128)S(1)}, f32[7,16,128]{2,1,0:T(8,128)S(1)}, u32[]{:S(2)}, u32[]{:S(2)}) collective-permute-start(f32[7,16,128]{2,1,0:T(8,128)S(1)} %pair.1.own.own_z), channel_id=1, source_target_pairs={{0,8},{4,12},{8,0},{12,4},{16,24},{20,28},{24,16},{28,20},{32,40},... | collective-permute-start | bytes 172040 | tf_op jit(solution)/shard_map/ppermute | solution.py:577
  18.9 5.8 %collective-permute-start.6 = (f32[7,16,128]{2,1,0:T(8,128)S(1)}, f32[7,16,128]{2,1,0:T(8,128)S(1)}, u32[]{:S(2)}, u32[]{:S(2)}) collective-permute-start(f32[7,16,128]{2,1,0:T(8,128)S(1)} %four.1.own_y), channel_id=1, source_target_pairs={{0,64},{4,68},{8,72},{12,76},{16,80},{20,84},{24,88},{28,92},{32,9... | collective-permute-start | bytes 172040 | tf_op jit(solution)/shard_map/ppermute | solution.py:577
  22.1 5.4 %collective-permute-start.7 = (f32[7,16,128]{2,1,0:T(8,128)S(1)}, f32[7,16,128]{2,1,0:T(8,128)S(1)}, u32[]{:S(2)}, u32[]{:S(2)}) collective-permute-start(f32[7,16,128]{2,1,0:T(8,128)S(1)} %four.1.own_y), channel_id=1, source_target_pairs={{0,96},{4,100},{8,104},{12,108},{16,112},{20,116},{24,120},{28,124... | collective-permute-start | bytes 172040 | tf_op jit(solution)/shard_map/ppermute | solution.py:577
  23.2 4.3 %collective-permute-start.8 = (f32[7,16,128]{2,1,0:T(8,128)S(1)}, f32[7,16,128]{2,1,0:T(8,128)S(1)}, u32[]{:S(2)}, u32[]{:S(2)}) collective-permute-start(f32[7,16,128]{2,1,0:T(8,128)S(1)} %four.1.own_y), channel_id=1, source_target_pairs={{0,32},{4,36},{8,40},{12,44},{16,48},{20,52},{24,56},{28,60},{32,0... | collective-permute-start | bytes 172040 | tf_op jit(solution)/shard_map/ppermute | solution.py:577
  28.0 5.1 %collective-permute-start.10 = (f32[8,128]{1,0:T(8,128)S(1)}, f32[8,128]{1,0:T(8,128)S(1)}, u32[]{:S(2)}, u32[]{:S(2)}) collective-permute-start(f32[8,128]{1,0:T(8,128)S(1)} %get-tuple-element.76.own), channel_id=1, source_target_pairs={{0,2},{1,3},{2,0},{3,1},{4,6},{5,7},{6,4},{7,5},{8,10},{9,11},{10,... | collective-permute-start | bytes 12296 | tf_op jit(solution)/shard_map/ppermute | solution.py:577
  29.5 4.8 %collective-permute-start.11 = (f32[8,128]{1,0:T(8,128)S(1)}, f32[8,128]{1,0:T(8,128)S(1)}, u32[]{:S(2)}, u32[]{:S(2)}) collective-permute-start(f32[8,128]{1,0:T(8,128)S(1)} %get-tuple-element.76.own), channel_id=1, source_target_pairs={{0,3},{1,2},{2,1},{3,0},{4,7},{5,6},{6,5},{7,4},{8,11},{9,10},{10,... | collective-permute-start | bytes 12296 | tf_op jit(solution)/shard_map/ppermute | solution.py:577
  30.2 4.2 %collective-permute-start.9 = (f32[8,128]{1,0:T(8,128)S(1)}, f32[8,128]{1,0:T(8,128)S(1)}, u32[]{:S(2)}, u32[]{:S(2)}) collective-permute-start(f32[8,128]{1,0:T(8,128)S(1)} %get-tuple-element.76.own), channel_id=1, source_target_pairs={{0,1},{1,0},{2,3},{3,2},{4,5},{5,4},{6,7},{7,6},{8,9},{9,8},{10,11... | collective-permute-start | bytes 12296 | tf_op jit(solution)/shard_map/ppermute | solution.py:577

commit v12 on v10

--- a/solution.py
+++ b/solution.py
@@ -167,7 +167,14 @@
     return ref[pl.ds((i // 8) * (8 * TILES) + i % 8, TILES, stride=8), :]
 
 
-def load_kernel(t_far, k_far, t, k, lo, hi, own, arrived):
+def load_kernel(t_far, k_far, t, k, lo, hi, own, strips, early, arrived):
+    first = []
+    for n, (far, column) in enumerate(
+        ((t_far, 0), (k_far, 0), (t_far, TILES - 1), (k_far, TILES - 1))
+    ):
+        side = pl.ds(128 * column, 128)
+        first.append(pltpu.make_async_copy(far.at[:, side], strips.at[n], early.at[n]))
+        first[n].start()
     copies = []
     for band in range(BANDS):
         at = pl.ds(8 * band, 8)
@@ -177,14 +184,15 @@
             copies.append(copy)
     for ref in (lo, hi, own):
         ref[...] = jnp.zeros_like(ref)
+    for n, copy in enumerate(first):
+        copy.wait()
+        high = n // 2
+        at = 127 * high
+        edge = strips[n].T[at : at + 1, :]
+        own[n : n + 1, 0:ROWS] = edge
+        (hi if high else lo)[n % 2 : n % 2 + 1, 0:ROWS] = edge
     for copy in copies:
         copy.wait()
-    for n, (ref, column) in enumerate(((t, 0), (k, 0), (t, TILES - 1), (k, TILES - 1))):
-        strip = ref[:, 128 * column : 128 * column + 128].T
-        at = 127 if column else 0
-        edge = strip[at : at + 1, :]
-        own[n : n + 1, 0:ROWS] = edge
-        (hi if column else lo)[n % 2 : n % 2 + 1, 0:ROWS] = edge
 
 
 def total(terms):
@@ -575,7 +583,11 @@
     t, k, own_lo, own_hi, own_edges = call(
         load_kernel,
         [natural, natural] + [struct(8, 128)] * 3,
-        [pltpu.SemaphoreType.DMA((2, BANDS))],
+        [
+            pltpu.VMEM((4, ROWS, 128), F32),
+            pltpu.SemaphoreType.DMA((4,)),
+            pltpu.SemaphoreType.DMA((2, BANDS)),
+        ],
         name="load",
         grant=GRANT,
         in_specs=[HBM, HBM],

time: 35.7 us -> 35.9 us (level)
  no operation moved by 1% of the time
where the time goes in v12:
time: 35.9 us; the launch traced here: 35.7 us
  starting transfers between devices  16.5 us (46%)
  waiting for transfers between devices  10.2 us (28%)
  Pallas kernels  8.91 us (25%)
    ppermute x9, starting transfers between devices, around(): return lax.ppermute(value, axis, pairs)  13.2 us
    ppermute x9, waiting for transfers between devices, around(): return lax.ppermute(value, axis, pairs)  9.24 us
    pallas_call x12, Pallas kernels, run(): pl.pallas_call(kernel, out_shape=outs, **windows or whole(outs, args), sc...  8.91 us
    ppermute x1, starting transfers between devices, per_device(): above = lax.ppermute(own_lo, 'gy', [((i + 1) % 4, i) for i in range(4)])  1.66 us
    ppermute x1, starting transfers between devices, per_device(): below = lax.ppermute(own_hi, 'gy', [(i, (i + 1) % 4) for i in range(4)])  1.64 us
    ppermute x1, waiting for transfers between devices, per_device(): other = lax.ppermute(own, 'gx', [(i, i ^ 1) for i in range(32)])  0.93 us
  transfers between devices with their start and end apart: 12, of which 7 were waited for; matrix products, arithmetic and copies ran while one was open for 0% of the time, Pallas kernels for 16%

profile of v12, /device:TPU:0, one launch (start us, length us, event | category | flops | bytes accessed | tf_op | source)
XLA Modules:
  0.0 35.7 jit_solution(11559143778012360921)
XLA Ops:
  0.0 1.6 %load.1 = (f32[64,2048]{1,0:T(8,128)S(1)}, f32[64,2048]{1,0:T(8,128)S(1)}, f32[8,128]{1,0:T(8,128)S(1)}, f32[8,128]{1,0:T(8,128)S(1)}, f32[8,128]{1,0:T(8,128)S(1)}) custom-call(f32[64,2048]{1,0:T(8,128)} %bitcast.3, f32[64,2048]{1,0:T(8,128)} %bitcast.4), custom_call_target="tpu_custom_call" | custom-call | flops 2000000 | bytes 1048576 | tf_op jit(solution)/shard_map/load/pallas_call | solution.py:34
  1.6 1.6 %collective-permute-start = (f32[8,128]{1,0:T(8,128)S(1)}, f32[8,128]{1,0:T(8,128)S(1)}, u32[]{:S(2)}, u32[]{:S(2)}) collective-permute-start(f32[8,128]{1,0:T(8,128)S(1)} %get-tuple-element.52), channel_id=1, source_target_pairs={{0,1},{1,2},{2,3},{3,0},{4,5},{5,6},{6,7},{7,4},{8,9},{9,10},{10,1... | collective-permute-start | bytes 12296 | tf_op jit(solution)/shard_map/ppermute | solution.py:596
  3.3 1.7 %collective-permute-start.1 = (f32[8,128]{1,0:T(8,128)S(1)}, f32[8,128]{1,0:T(8,128)S(1)}, u32[]{:S(2)}, u32[]{:S(2)}) collective-permute-start(f32[8,128]{1,0:T(8,128)S(1)} %get-tuple-element.53), channel_id=1, source_target_pairs={{1,0},{2,1},{3,2},{0,3},{5,4},{6,5},{7,6},{4,7},{9,8},{10,9},{11,1... | collective-permute-start | bytes 12296 | tf_op jit(solution)/shard_map/ppermute | solution.py:597
  4.9 1.2 %y_matrix.1 = (f32[128,8,128]{2,1,0:T(8,128)S(1)}, f32[128,8,128]{2,1,0:T(8,128)S(1)}, f32[128,8,128]{2,1,0:T(8,128)S(1)}, f32[52,8,128]{2,1,0:T(8,128)S(1)}, f3...) custom-call(f32[64,2048]{1,0:T(8,128)S(1)} %get-tuple-element.47.k), custom_call_target="tpu_custom_call" | custom-call | flops 2000000 | bytes 1048576 | tf_op jit(solution)/shard_map/y_matrix/pallas_call | solution.py:34
  6.2 1.1 %x_matrix.1 = (f32[1024,128]{1,0:T(8,128)S(1)}, f32[64,16,128]{2,1,0:T(8,128)S(1)}, f32[64,16,128]{2,1,0:T(8,128)S(1)}, f32[64,16,128]{2,1,0:T(8,128)S(1)}, f32[...) custom-call(f32[64,2048]{1,0:T(8,128)S(1)} %get-tuple-element.46.t, ...), custom_call_target="tpu_custom_call" | custom-call | flops 2000000 | bytes 1048576 | tf_op jit(solution)/shard_map/x_matrix/pallas_call | solution.py:34
  7.2 0.0 collective-permute-done.below
  7.2 0.0 collective-permute-done.1.above
  7.2 0.1 x_port.1
  7.3 0.1 collective-permute-start.2
  7.4 0.3 x_solve.1.u
  7.7 0.9 %collective-permute-done.2.other = f32[7,16,128]{2,1,0:T(8,128)S(1)} collective-permute-done((f32[7,16,128]{2,1,0:T(8,128)S(1)}, f32[7,16,128]{2,1,0:T(8,128)S(1)}, u32[]{:S(2)}, u32[]{:S(2)}) %collective-permute-start.2) | collective-permute-done | bytes 57376 | tf_op jit(solution)/shard_map/ppermute | solution.py:643
  8.7 4.0 %collective-permute-start.3 = (f32[7,16,128]{2,1,0:T(8,128)S(1)}, f32[7,16,128]{2,1,0:T(8,128)S(1)}, u32[]{:S(2)}, u32[]{:S(2)}) collective-permute-start(f32[7,16,128]{2,1,0:T(8,128)S(1)} %pair.1.own.own_z), channel_id=1, source_target_pairs={{0,16},{4,20},{8,24},{12,28},{16,0},{20,4},{24,8},{28,12},{32,48},... | collective-permute-start | bytes 172040 | tf_op jit(solution)/shard_map/ppermute | solution.py:577
  12.7 0.7 %collective-permute-start.4 = (f32[7,16,128]{2,1,0:T(8,128)S(1)}, f32[7,16,128]{2,1,0:T(8,128)S(1)}, u32[]{:S(2)}, u32[]{:S(2)}) collective-permute-start(f32[7,16,128]{2,1,0:T(8,128)S(1)} %pair.1.own.own_z), channel_id=1, source_target_pairs={{0,24},{4,28},{8,16},{12,20},{16,8},{20,12},{24,0},{28,4},{32,56},... | collective-permute-start | bytes 172040 | tf_op jit(solution)/shard_map/ppermute | solution.py:577
  13.4 0.3 collective-permute-start.5
  13.7 0.9 %upright.1 = (f32[64,2048]{1,0:T(8,128)S(1)}, f32[64,2048]{1,0:T(8,128)S(1)}) custom-call(f32[128,8,128]{2,1,0:T(8,128)S(1)} %get-tuple-element.65.lo, f32[128,8,128]{2,1,0:T(8,128)S(1)} %get-tuple-element.66.hi), custom_call_target="tpu_custom_call" | custom-call | flops 2000000 | bytes 1048576 | tf_op jit(solution)/shard_map/upright/pallas_call | solution.py:34
  14.6 0.4 collective-permute-done.3.r1.z1
  15.0 3.1 %collective-permute-done.4.r2.z2 = f32[7,16,128]{2,1,0:T(8,128)S(1)} collective-permute-done((f32[7,16,128]{2,1,0:T(8,128)S(1)}, f32[7,16,128]{2,1,0:T(8,128)S(1)}, u32[]{:S(2)}, u32[]{:S(2)}) %collective-permute-start.4) | collective-permute-done | bytes 57376 | tf_op jit(solution)/shard_map/ppermute | solution.py:577
  18.1 0.0 collective-permute-done.5.r3.z3
  18.1 0.1 four.1.own_y
  18.2 3.3 %collective-permute-start.6 = (f32[7,16,128]{2,1,0:T(8,128)S(1)}, f32[7,16,128]{2,1,0:T(8,128)S(1)}, u32[]{:S(2)}, u32[]{:S(2)}) collective-permute-start(f32[7,16,128]{2,1,0:T(8,128)S(1)} %four.1.own_y), channel_id=1, source_target_pairs={{0,64},{4,68},{8,72},{12,76},{16,80},{20,84},{24,88},{28,92},{32,9... | collective-permute-start | bytes 172040 | tf_op jit(solution)/shard_map/ppermute | solution.py:577
  21.5 1.1 %collective-permute-start.7 = (f32[7,16,128]{2,1,0:T(8,128)S(1)}, f32[7,16,128]{2,1,0:T(8,128)S(1)}, u32[]{:S(2)}, u32[]{:S(2)}) collective-permute-start(f32[7,16,128]{2,1,0:T(8,128)S(1)} %four.1.own_y), channel_id=1, source_target_pairs={{0,96},{4,100},{8,104},{12,108},{16,112},{20,116},{24,120},{28,124... | collective-permute-start | bytes 172040 | tf_op jit(solution)/shard_map/ppermute | solution.py:577
  22.5 0.0 collective-permute-start.8
  22.5 0.6 %blend.1 = (f32[1024,128]{1,0:T(8,128)S(1)}, f32[1024,128]{1,0:T(8,128)S(1)}, f32[1024,128]{1,0:T(8,128)S(1)}, f32[4,1024,128]{2,1,0:T(8,128)S(1)}, f32[8,128]{1,0:T(8,128)S(1)}) custom-call(f32[64,16,128]{2,1,0:T(8,128)S(1)} %x_solve.1.u, f32[64,16,128]{2,1,0:T(8,128)S(1)} %get-tuple-element.49.lo.x_lo, f32[64,16,128]{2,1,0:T(8,128)S(1)} %get-tuple-element.50.hi.x_hi, ...), custom_call_target="tpu_custom_call" | custom-call | flops 2000000 | bytes 1048576 | tf_op jit(solution)/shard_map/blend/pallas_call | solution.py:34
  23.1 0.8 %collective-permute-done.6.y1 = f32[7,16,128]{2,1,0:T(8,128)S(1)} collective-permute-done((f32[7,16,128]{2,1,0:T(8,128)S(1)}, f32[7,16,128]{2,1,0:T(8,128)S(1)}, u32[]{:S(2)}, u32[]{:S(2)}) %collective-permute-start.6) | collective-permute-done | bytes 57376 | tf_op jit(solution)/shard_map/ppermute | solution.py:577
  24.0 2.9 %collective-permute-done.7.y2 = f32[7,16,128]{2,1,0:T(8,128)S(1)} collective-permute-done((f32[7,16,128]{2,1,0:T(8,128)S(1)}, f32[7,16,128]{2,1,0:T(8,128)S(1)}, u32[]{:S(2)}, u32[]{:S(2)}) %collective-permute-start.7) | collective-permute-done | bytes 57376 | tf_op jit(solution)/shard_map/ppermute | solution.py:577
  26.8 0.0 collective-permute-done.8.y3
  26.8 0.4 %y_port.1 = (f32[8,128]{1,0:T(8,128)S(1)}, f32[2,16,128]{2,1,0:T(8,128)S(1)}) custom-call(f32[7,16,128]{2,1,0:T(8,128)S(1)} %four.1.own_y, f32[7,16,128]{2,1,0:T(8,128)S(1)} %collective-permute-done.6.y1, f32[7,16,128]{2,1,0:T(8,128)S(1)} %collective-permute-done.7.y2, f32[7,16,128]{2,1,0:T(8,128)S(1)} %collective-permute-done.8.y3, ...), custom_call_target="tpu_custom_call" | custom-call | flops 2000000 | bytes 1048576 | tf_op jit(solution)/shard_map/y_port/pallas_call | solution.py:34
  27.3 2.3 %collective-permute-start.10 = (f32[8,128]{1,0:T(8,128)S(1)}, f32[8,128]{1,0:T(8,128)S(1)}, u32[]{:S(2)}, u32[]{:S(2)}) collective-permute-start(f32[8,128]{1,0:T(8,128)S(1)} %get-tuple-element.78.own), channel_id=1, source_target_pairs={{0,2},{1,3},{2,0},{3,1},{4,6},{5,7},{6,4},{7,5},{8,10},{9,11},{10,... | collective-permute-start | bytes 12296 | tf_op jit(solution)/shard_map/ppermute | solution.py:577
  29.6 1.4 %collective-permute-start.11 = (f32[8,128]{1,0:T(8,128)S(1)}, f32[8,128]{1,0:T(8,128)S(1)}, u32[]{:S(2)}, u32[]{:S(2)}) collective-permute-start(f32[8,128]{1,0:T(8,128)S(1)} %get-tuple-element.78.own), channel_id=1, source_target_pairs={{0,3},{1,2},{2,1},{3,0},{4,7},{5,6},{6,5},{7,4},{8,11},{9,10},{10,... | collective-permute-start | bytes 12296 | tf_op jit(solution)/shard_map/ppermute | solution.py:577
  31.0 0.0 collective-permute-start.9
  31.0 1.6 %y_solve.1.base = f32[64,2048]{1,0:T(8,128)S(1)} custom-call(f32[1024,128]{1,0:T(8,128)S(1)} %get-tuple-element.79.source, f32[1024,128]{1,0:T(8,128)S(1)} %get-tuple-element.80.lo, f32[1024,128]{1,0:T(8,128)S(1)} %get-tuple-element.81.hi, f32[2,16,128]{2,1,0:T(8,128)S(1)} %get-tuple-element.82.flow, f32[128,8,128]{2,1,0:T(8,128)S(1)} %get-tuple-element.83.along, ...), custom_call_target="tpu_custom_call" | custom-call | flops 2000000 | bytes 1048576 | tf_op jit(solution)/shard_map/y_solve/pallas_call | solution.py:34
  32.6 0.0 collective-permute-done.10.r2
  32.6 1.8 %collective-permute-done.11.r3 = f32[8,128]{1,0:T(8,128)S(1)} collective-permute-done((f32[8,128]{1,0:T(8,128)S(1)}, f32[8,128]{1,0:T(8,128)S(1)}, u32[]{:S(2)}, u32[]{:S(2)}) %collective-permute-start.11) | collective-permute-done | bytes 4128 | tf_op jit(solution)/shard_map/ppermute | solution.py:577
  34.4 0.2 collective-permute-done.9.r1
  34.6 1.1 %finish.1 = f32[64,2048]{1,0:T(8,128)} custom-call(f32[8,128]{1,0:T(8,128)S(1)} %get-tuple-element.78.own, f32[8,128]{1,0:T(8,128)S(1)} %collective-permute-done.9.r1, f32[8,128]{1,0:T(8,128)S(1)} %collective-permute-done.10.r2, f32[8,128]{1,0:T(8,128)S(1)} %collective-permute-done.11.r3, f32[64,2048]{1,0:T(8,128)S(1)} %y_solve.1.base, ...), custom_call_target="tpu_custom_call" | custom-call | flops 2000000 | bytes 1048576 | tf_op jit(solution)/shard_map/finish/pallas_call | solution.py:34
  (1 shorter events, 0.0 us)
Async XLA Ops:
  1.6 5.6 %collective-permute-start = (f32[8,128]{1,0:T(8,128)S(1)}, f32[8,128]{1,0:T(8,128)S(1)}, u32[]{:S(2)}, u32[]{:S(2)}) collective-permute-start(f32[8,128]{1,0:T(8,128)S(1)} %get-tuple-element.52), channel_id=1, source_target_pairs={{0,1},{1,2},{2,3},{3,0},{4,5},{5,6},{6,7},{7,4},{8,9},{9,10},{10,1... | collective-permute-start | bytes 12296 | tf_op jit(solution)/shard_map/ppermute | solution.py:596
  3.3 3.9 %collective-permute-start.1 = (f32[8,128]{1,0:T(8,128)S(1)}, f32[8,128]{1,0:T(8,128)S(1)}, u32[]{:S(2)}, u32[]{:S(2)}) collective-permute-start(f32[8,128]{1,0:T(8,128)S(1)} %get-tuple-element.53), channel_id=1, source_target_pairs={{1,0},{2,1},{3,2},{0,3},{5,4},{6,5},{7,6},{4,7},{9,8},{10,9},{11,1... | collective-permute-start | bytes 12296 | tf_op jit(solution)/shard_map/ppermute | solution.py:597
  7.3 1.3 %collective-permute-start.2 = (f32[7,16,128]{2,1,0:T(8,128)S(1)}, f32[7,16,128]{2,1,0:T(8,128)S(1)}, u32[]{:S(2)}, u32[]{:S(2)}) collective-permute-start(f32[7,16,128]{2,1,0:T(8,128)S(1)} %get-tuple-element.57.own), channel_id=1, source_target_pairs={{0,4},{4,0},{8,12},{12,8},{16,20},{20,16},{24,28},{28,24},{32,36},... | collective-permute-start | bytes 172040 | tf_op jit(solution)/shard_map/ppermute | solution.py:643
  8.7 6.3 %collective-permute-start.3 = (f32[7,16,128]{2,1,0:T(8,128)S(1)}, f32[7,16,128]{2,1,0:T(8,128)S(1)}, u32[]{:S(2)}, u32[]{:S(2)}) collective-permute-start(f32[7,16,128]{2,1,0:T(8,128)S(1)} %pair.1.own.own_z), channel_id=1, source_target_pairs={{0,16},{4,20},{8,24},{12,28},{16,0},{20,4},{24,8},{28,12},{32,48},... | collective-permute-start | bytes 172040 | tf_op jit(solution)/shard_map/ppermute | solution.py:577
  12.7 5.4 %collective-permute-start.4 = (f32[7,16,128]{2,1,0:T(8,128)S(1)}, f32[7,16,128]{2,1,0:T(8,128)S(1)}, u32[]{:S(2)}, u32[]{:S(2)}) collective-permute-start(f32[7,16,128]{2,1,0:T(8,128)S(1)} %pair.1.own.own_z), channel_id=1, source_target_pairs={{0,24},{4,28},{8,16},{12,20},{16,8},{20,12},{24,0},{28,4},{32,56},... | collective-permute-start | bytes 172040 | tf_op jit(solution)/shard_map/ppermute | solution.py:577
  13.4 4.7 %collective-permute-start.5 = (f32[7,16,128]{2,1,0:T(8,128)S(1)}, f32[7,16,128]{2,1,0:T(8,128)S(1)}, u32[]{:S(2)}, u32[]{:S(2)}) collective-permute-start(f32[7,16,128]{2,1,0:T(8,128)S(1)} %pair.1.own.own_z), channel_id=1, source_target_pairs={{0,8},{4,12},{8,0},{12,4},{16,24},{20,28},{24,16},{28,20},{32,40},... | collective-permute-start | bytes 172040 | tf_op jit(solution)/shard_map/ppermute | solution.py:577
  18.2 5.8 %collective-permute-start.6 = (f32[7,16,128]{2,1,0:T(8,128)S(1)}, f32[7,16,128]{2,1,0:T(8,128)S(1)}, u32[]{:S(2)}, u32[]{:S(2)}) collective-permute-start(f32[7,16,128]{2,1,0:T(8,128)S(1)} %four.1.own_y), channel_id=1, source_target_pairs={{0,64},{4,68},{8,72},{12,76},{16,80},{20,84},{24,88},{28,92},{32,9... | collective-permute-start | bytes 172040 | tf_op jit(solution)/shard_map/ppermute | solution.py:577
  21.5 5.4 %collective-permute-start.7 = (f32[7,16,128]{2,1,0:T(8,128)S(1)}, f32[7,16,128]{2,1,0:T(8,128)S(1)}, u32[]{:S(2)}, u32[]{:S(2)}) collective-permute-start(f32[7,16,128]{2,1,0:T(8,128)S(1)} %four.1.own_y), channel_id=1, source_target_pairs={{0,96},{4,100},{8,104},{12,108},{16,112},{20,116},{24,120},{28,124... | collective-permute-start | bytes 172040 | tf_op jit(solution)/shard_map/ppermute | solution.py:577
  22.5 4.3 %collective-permute-start.8 = (f32[7,16,128]{2,1,0:T(8,128)S(1)}, f32[7,16,128]{2,1,0:T(8,128)S(1)}, u32[]{:S(2)}, u32[]{:S(2)}) collective-permute-start(f32[7,16,128]{2,1,0:T(8,128)S(1)} %four.1.own_y), channel_id=1, source_target_pairs={{0,32},{4,36},{8,40},{12,44},{16,48},{20,52},{24,56},{28,60},{32,0... | collective-permute-start | bytes 172040 | tf_op jit(solution)/shard_map/ppermute | solution.py:577
  27.3 5.3 %collective-permute-start.10 = (f32[8,128]{1,0:T(8,128)S(1)}, f32[8,128]{1,0:T(8,128)S(1)}, u32[]{:S(2)}, u32[]{:S(2)}) collective-permute-start(f32[8,128]{1,0:T(8,128)S(1)} %get-tuple-element.78.own), channel_id=1, source_target_pairs={{0,2},{1,3},{2,0},{3,1},{4,6},{5,7},{6,4},{7,5},{8,10},{9,11},{10,... | collective-permute-start | bytes 12296 | tf_op jit(solution)/shard_map/ppermute | solution.py:577
  29.6 4.8 %collective-permute-start.11 = (f32[8,128]{1,0:T(8,128)S(1)}, f32[8,128]{1,0:T(8,128)S(1)}, u32[]{:S(2)}, u32[]{:S(2)}) collective-permute-start(f32[8,128]{1,0:T(8,128)S(1)} %get-tuple-element.78.own), channel_id=1, source_target_pairs={{0,3},{1,2},{2,1},{3,0},{4,7},{5,6},{6,5},{7,4},{8,11},{9,10},{10,... | collective-permute-start | bytes 12296 | tf_op jit(solution)/shard_map/ppermute | solution.py:577
  31.0 3.6 %collective-permute-start.9 = (f32[8,128]{1,0:T(8,128)S(1)}, f32[8,128]{1,0:T(8,128)S(1)}, u32[]{:S(2)}, u32[]{:S(2)}) collective-permute-start(f32[8,128]{1,0:T(8,128)S(1)} %get-tuple-element.78.own), channel_id=1, source_target_pairs={{0,1},{1,0},{2,3},{3,2},{4,5},{5,4},{6,7},{7,6},{8,9},{9,8},{10,11... | collective-permute-start | bytes 12296 | tf_op jit(solution)/shard_map/ppermute | solution.py:577

commit v13 on v10

--- a/solution.py
+++ b/solution.py
@@ -8,6 +8,7 @@
 ROWS, COLS = 64, 2048
 BANDS, TILES = ROWS // 8, COLS // 128
 SEGMENTS = 4
+PARTS = 2
 Y_STEPS = 128
 X_LEVELS, Y_LEVELS = 2, 6
 GRANT = (527 << 20) // 10
@@ -169,10 +170,10 @@
 
 def load_kernel(t_far, k_far, t, k, lo, hi, own, arrived):
     copies = []
-    for band in range(BANDS):
-        at = pl.ds(8 * band, 8)
+    for part in range(PARTS):
+        at = pl.ds(ROWS // PARTS * part, ROWS // PARTS)
         for n, (far, near) in enumerate(((t_far, t), (k_far, k))):
-            copy = pltpu.make_async_copy(far.at[at, :], near.at[at, :], arrived.at[n, band])
+            copy = pltpu.make_async_copy(far.at[at, :], near.at[at, :], arrived.at[n, part])
             copy.start()
             copies.append(copy)
     for ref in (lo, hi, own):
@@ -554,9 +555,11 @@
             part = tile(base, band, column)
             part = part - down * tile(y_lo, band, column) + up * tile(y_hi, band, column)
             keep(band, column, part)
-        copy = pltpu.make_async_copy(done.at[at, :], out.at[at, :], sent.at[band])
-        copy.start()
-        copies.append(copy)
+        if band % 2:
+            pair = pl.ds(8 * band - 8, 16)
+            copy = pltpu.make_async_copy(done.at[pair, :], out.at[pair, :], sent.at[band // 2])
+            copy.start()
+            copies.append(copy)
     for copy in copies:
         copy.wait()
 
@@ -575,7 +578,7 @@
     t, k, own_lo, own_hi, own_edges = call(
         load_kernel,
         [natural, natural] + [struct(8, 128)] * 3,
-        [pltpu.SemaphoreType.DMA((2, BANDS))],
+        [pltpu.SemaphoreType.DMA((2, PARTS))],
         name="load",
         grant=GRANT,
         in_specs=[HBM, HBM],
@@ -666,7 +669,7 @@
             pltpu.VMEM((4, 8, 128), F32),
             pltpu.VMEM((128, 128), F32),
             scratch(natural),
-            pltpu.SemaphoreType.DMA((BANDS,)),
+            pltpu.SemaphoreType.DMA((BANDS // 2,)),
         ],
         name="finish",
         in_specs=[VMEM] * 7,

time: 35.7 us -> 35.5 us (level)
  no operation moved by 1% of the time
where the time goes in v13:
time: 35.5 us; the launch traced here: 35.4 us
  starting transfers between devices  16.5 us (46%)
  waiting for transfers between devices  10.2 us (29%)
  Pallas kernels  8.6 us (24%)
    ppermute x9, starting transfers between devices, around(): return lax.ppermute(value, axis, pairs)  13.2 us
    ppermute x9, waiting for transfers between devices, around(): return lax.ppermute(value, axis, pairs)  9.24 us
    pallas_call x12, Pallas kernels, run(): pl.pallas_call(kernel, out_shape=outs, **windows or whole(outs, args), sc...  8.6 us
    ppermute x1, starting transfers between devices, per_device(): above = lax.ppermute(own_lo, 'gy', [((i + 1) % 4, i) for i in range(4)])  1.66 us
    ppermute x1, starting transfers between devices, per_device(): below = lax.ppermute(own_hi, 'gy', [(i, (i + 1) % 4) for i in range(4)])  1.64 us
    ppermute x1, waiting for transfers between devices, per_device(): other = lax.ppermute(own, 'gx', [(i, i ^ 1) for i in range(32)])  0.93 us
  transfers between devices with their start and end apart: 12, of which 7 were waited for; matrix products, arithmetic and copies ran while one was open for 0% of the time, Pallas kernels for 16%

profile of v13, /device:TPU:0, one launch (start us, length us, event | category | flops | bytes accessed | tf_op | source)
XLA Modules:
  0.0 35.4 jit_solution(11120334628343571553)
XLA Ops:
  0.0 1.3 %load.1 = (f32[64,2048]{1,0:T(8,128)S(1)}, f32[64,2048]{1,0:T(8,128)S(1)}, f32[8,128]{1,0:T(8,128)S(1)}, f32[8,128]{1,0:T(8,128)S(1)}, f32[8,128]{1,0:T(8,128)S(1)}) custom-call(f32[64,2048]{1,0:T(8,128)} %bitcast.3, f32[64,2048]{1,0:T(8,128)} %bitcast.4), custom_call_target="tpu_custom_call" | custom-call | flops 2000000 | bytes 1048576 | tf_op jit(solution)/shard_map/load/pallas_call | solution.py:35
  1.3 1.6 %collective-permute-start = (f32[8,128]{1,0:T(8,128)S(1)}, f32[8,128]{1,0:T(8,128)S(1)}, u32[]{:S(2)}, u32[]{:S(2)}) collective-permute-start(f32[8,128]{1,0:T(8,128)S(1)} %get-tuple-element.52), channel_id=1, source_target_pairs={{0,1},{1,2},{2,3},{3,0},{4,5},{5,6},{6,7},{7,4},{8,9},{9,10},{10,1... | collective-permute-start | bytes 12296 | tf_op jit(solution)/shard_map/ppermute | solution.py:587
  3.0 1.7 %collective-permute-start.1 = (f32[8,128]{1,0:T(8,128)S(1)}, f32[8,128]{1,0:T(8,128)S(1)}, u32[]{:S(2)}, u32[]{:S(2)}) collective-permute-start(f32[8,128]{1,0:T(8,128)S(1)} %get-tuple-element.53), channel_id=1, source_target_pairs={{1,0},{2,1},{3,2},{0,3},{5,4},{6,5},{7,6},{4,7},{9,8},{10,9},{11,1... | collective-permute-start | bytes 12296 | tf_op jit(solution)/shard_map/ppermute | solution.py:588
  4.7 1.2 %y_matrix.1 = (f32[128,8,128]{2,1,0:T(8,128)S(1)}, f32[128,8,128]{2,1,0:T(8,128)S(1)}, f32[128,8,128]{2,1,0:T(8,128)S(1)}, f32[52,8,128]{2,1,0:T(8,128)S(1)}, f3...) custom-call(f32[64,2048]{1,0:T(8,128)S(1)} %get-tuple-element.47.k), custom_call_target="tpu_custom_call" | custom-call | flops 2000000 | bytes 1048576 | tf_op jit(solution)/shard_map/y_matrix/pallas_call | solution.py:35
  5.9 1.1 %x_matrix.1 = (f32[1024,128]{1,0:T(8,128)S(1)}, f32[64,16,128]{2,1,0:T(8,128)S(1)}, f32[64,16,128]{2,1,0:T(8,128)S(1)}, f32[64,16,128]{2,1,0:T(8,128)S(1)}, f32[...) custom-call(f32[64,2048]{1,0:T(8,128)S(1)} %get-tuple-element.46.t, ...), custom_call_target="tpu_custom_call" | custom-call | flops 2000000 | bytes 1048576 | tf_op jit(solution)/shard_map/x_matrix/pallas_call | solution.py:35
  6.9 0.0 collective-permute-done.below
  6.9 0.0 collective-permute-done.1.above
  6.9 0.1 x_port.1
  7.0 0.1 collective-permute-start.2
  7.1 0.3 x_solve.1.u
  7.4 0.9 %collective-permute-done.2.other = f32[7,16,128]{2,1,0:T(8,128)S(1)} collective-permute-done((f32[7,16,128]{2,1,0:T(8,128)S(1)}, f32[7,16,128]{2,1,0:T(8,128)S(1)}, u32[]{:S(2)}, u32[]{:S(2)}) %collective-permute-start.2) | collective-permute-done | bytes 57376 | tf_op jit(solution)/shard_map/ppermute | solution.py:634
  8.4 4.0 %collective-permute-start.3 = (f32[7,16,128]{2,1,0:T(8,128)S(1)}, f32[7,16,128]{2,1,0:T(8,128)S(1)}, u32[]{:S(2)}, u32[]{:S(2)}) collective-permute-start(f32[7,16,128]{2,1,0:T(8,128)S(1)} %pair.1.own.own_z), channel_id=1, source_target_pairs={{0,16},{4,20},{8,24},{12,28},{16,0},{20,4},{24,8},{28,12},{32,48},... | collective-permute-start | bytes 172040 | tf_op jit(solution)/shard_map/ppermute | solution.py:572
  12.4 0.7 %collective-permute-start.4 = (f32[7,16,128]{2,1,0:T(8,128)S(1)}, f32[7,16,128]{2,1,0:T(8,128)S(1)}, u32[]{:S(2)}, u32[]{:S(2)}) collective-permute-start(f32[7,16,128]{2,1,0:T(8,128)S(1)} %pair.1.own.own_z), channel_id=1, source_target_pairs={{0,24},{4,28},{8,16},{12,20},{16,8},{20,12},{24,0},{28,4},{32,56},... | collective-permute-start | bytes 172040 | tf_op jit(solution)/shard_map/ppermute | solution.py:572
  13.1 0.3 collective-permute-start.5
  13.5 0.9 %upright.1 = (f32[64,2048]{1,0:T(8,128)S(1)}, f32[64,2048]{1,0:T(8,128)S(1)}) custom-call(f32[128,8,128]{2,1,0:T(8,128)S(1)} %get-tuple-element.65.lo, f32[128,8,128]{2,1,0:T(8,128)S(1)} %get-tuple-element.66.hi), custom_call_target="tpu_custom_call" | custom-call | flops 2000000 | bytes 1048576 | tf_op jit(solution)/shard_map/upright/pallas_call | solution.py:35
  14.3 0.4 %collective-permute-done.3.r1.z1 = f32[7,16,128]{2,1,0:T(8,128)S(1)} collective-permute-done((f32[7,16,128]{2,1,0:T(8,128)S(1)}, f32[7,16,128]{2,1,0:T(8,128)S(1)}, u32[]{:S(2)}, u32[]{:S(2)}) %collective-permute-start.3) | collective-permute-done | bytes 57376 | tf_op jit(solution)/shard_map/ppermute | solution.py:572
  14.7 3.1 %collective-permute-done.4.r2.z2 = f32[7,16,128]{2,1,0:T(8,128)S(1)} collective-permute-done((f32[7,16,128]{2,1,0:T(8,128)S(1)}, f32[7,16,128]{2,1,0:T(8,128)S(1)}, u32[]{:S(2)}, u32[]{:S(2)}) %collective-permute-start.4) | collective-permute-done | bytes 57376 | tf_op jit(solution)/shard_map/ppermute | solution.py:572
  17.8 0.0 collective-permute-done.5.r3.z3
  17.8 0.1 four.1.own_y
  17.9 3.3 %collective-permute-start.6 = (f32[7,16,128]{2,1,0:T(8,128)S(1)}, f32[7,16,128]{2,1,0:T(8,128)S(1)}, u32[]{:S(2)}, u32[]{:S(2)}) collective-permute-start(f32[7,16,128]{2,1,0:T(8,128)S(1)} %four.1.own_y), channel_id=1, source_target_pairs={{0,64},{4,68},{8,72},{12,76},{16,80},{20,84},{24,88},{28,92},{32,9... | collective-permute-start | bytes 172040 | tf_op jit(solution)/shard_map/ppermute | solution.py:572
  21.2 1.1 %collective-permute-start.7 = (f32[7,16,128]{2,1,0:T(8,128)S(1)}, f32[7,16,128]{2,1,0:T(8,128)S(1)}, u32[]{:S(2)}, u32[]{:S(2)}) collective-permute-start(f32[7,16,128]{2,1,0:T(8,128)S(1)} %four.1.own_y), channel_id=1, source_target_pairs={{0,96},{4,100},{8,104},{12,108},{16,112},{20,116},{24,120},{28,124... | collective-permute-start | bytes 172040 | tf_op jit(solution)/shard_map/ppermute | solution.py:572
  22.2 0.0 collective-permute-start.8
  22.2 0.6 %blend.1 = (f32[1024,128]{1,0:T(8,128)S(1)}, f32[1024,128]{1,0:T(8,128)S(1)}, f32[1024,128]{1,0:T(8,128)S(1)}, f32[4,1024,128]{2,1,0:T(8,128)S(1)}, f32[8,128]{1,0:T(8,128)S(1)}) custom-call(f32[64,16,128]{2,1,0:T(8,128)S(1)} %x_solve.1.u, f32[64,16,128]{2,1,0:T(8,128)S(1)} %get-tuple-element.49.lo.x_lo, f32[64,16,128]{2,1,0:T(8,128)S(1)} %get-tuple-element.50.hi.x_hi, ...), custom_call_target="tpu_custom_call" | custom-call | flops 2000000 | bytes 1048576 | tf_op jit(solution)/shard_map/blend/pallas_call | solution.py:35
  22.8 0.8 %collective-permute-done.6.y1 = f32[7,16,128]{2,1,0:T(8,128)S(1)} collective-permute-done((f32[7,16,128]{2,1,0:T(8,128)S(1)}, f32[7,16,128]{2,1,0:T(8,128)S(1)}, u32[]{:S(2)}, u32[]{:S(2)}) %collective-permute-start.6) | collective-permute-done | bytes 57376 | tf_op jit(solution)/shard_map/ppermute | solution.py:572
  23.7 2.9 %collective-permute-done.7.y2 = f32[7,16,128]{2,1,0:T(8,128)S(1)} collective-permute-done((f32[7,16,128]{2,1,0:T(8,128)S(1)}, f32[7,16,128]{2,1,0:T(8,128)S(1)}, u32[]{:S(2)}, u32[]{:S(2)}) %collective-permute-start.7) | collective-permute-done | bytes 57376 | tf_op jit(solution)/shard_map/ppermute | solution.py:572
  26.6 0.0 collective-permute-done.8.y3
  26.6 0.4 %y_port.1 = (f32[8,128]{1,0:T(8,128)S(1)}, f32[2,16,128]{2,1,0:T(8,128)S(1)}) custom-call(f32[7,16,128]{2,1,0:T(8,128)S(1)} %four.1.own_y, f32[7,16,128]{2,1,0:T(8,128)S(1)} %collective-permute-done.6.y1, f32[7,16,128]{2,1,0:T(8,128)S(1)} %collective-permute-done.7.y2, f32[7,16,128]{2,1,0:T(8,128)S(1)} %collective-permute-done.8.y3, ...), custom_call_target="tpu_custom_call" | custom-call | flops 2000000 | bytes 1048576 | tf_op jit(solution)/shard_map/y_port/pallas_call | solution.py:35
  27.0 2.3 %collective-permute-start.10 = (f32[8,128]{1,0:T(8,128)S(1)}, f32[8,128]{1,0:T(8,128)S(1)}, u32[]{:S(2)}, u32[]{:S(2)}) collective-permute-start(f32[8,128]{1,0:T(8,128)S(1)} %get-tuple-element.78.own), channel_id=1, source_target_pairs={{0,2},{1,3},{2,0},{3,1},{4,6},{5,7},{6,4},{7,5},{8,10},{9,11},{10,... | collective-permute-start | bytes 12296 | tf_op jit(solution)/shard_map/ppermute | solution.py:572
  29.3 1.4 %collective-permute-start.11 = (f32[8,128]{1,0:T(8,128)S(1)}, f32[8,128]{1,0:T(8,128)S(1)}, u32[]{:S(2)}, u32[]{:S(2)}) collective-permute-start(f32[8,128]{1,0:T(8,128)S(1)} %get-tuple-element.78.own), channel_id=1, source_target_pairs={{0,3},{1,2},{2,1},{3,0},{4,7},{5,6},{6,5},{7,4},{8,11},{9,10},{10,... | collective-permute-start | bytes 12296 | tf_op jit(solution)/shard_map/ppermute | solution.py:572
  30.7 0.0 collective-permute-start.9
  30.7 1.6 %y_solve.1.base = f32[64,2048]{1,0:T(8,128)S(1)} custom-call(f32[1024,128]{1,0:T(8,128)S(1)} %get-tuple-element.79.source, f32[1024,128]{1,0:T(8,128)S(1)} %get-tuple-element.80.lo, f32[1024,128]{1,0:T(8,128)S(1)} %get-tuple-element.81.hi, f32[2,16,128]{2,1,0:T(8,128)S(1)} %get-tuple-element.82.flow, f32[128,8,128]{2,1,0:T(8,128)S(1)} %get-tuple-element.83.along, ...), custom_call_target="tpu_custom_call" | custom-call | flops 2000000 | bytes 1048576 | tf_op jit(solution)/shard_map/y_solve/pallas_call | solution.py:35
  32.3 0.0 collective-permute-done.10.r2
  32.3 1.8 %collective-permute-done.11.r3 = f32[8,128]{1,0:T(8,128)S(1)} collective-permute-done((f32[8,128]{1,0:T(8,128)S(1)}, f32[8,128]{1,0:T(8,128)S(1)}, u32[]{:S(2)}, u32[]{:S(2)}) %collective-permute-start.11) | collective-permute-done | bytes 4128 | tf_op jit(solution)/shard_map/ppermute | solution.py:572
  34.1 0.2 collective-permute-done.9.r1
  34.4 1.0 %finish.1 = f32[64,2048]{1,0:T(8,128)} custom-call(f32[8,128]{1,0:T(8,128)S(1)} %get-tuple-element.78.own, f32[8,128]{1,0:T(8,128)S(1)} %collective-permute-done.9.r1, f32[8,128]{1,0:T(8,128)S(1)} %collective-permute-done.10.r2, f32[8,128]{1,0:T(8,128)S(1)} %collective-permute-done.11.r3, f32[64,2048]{1,0:T(8,128)S(1)} %y_solve.1.base, ...), custom_call_target="tpu_custom_call" | custom-call | flops 2000000 | bytes 1048576 | tf_op jit(solution)/shard_map/finish/pallas_call | solution.py:35
  (1 shorter events, 0.0 us)
Async XLA Ops:
  1.3 5.6 %collective-permute-start = (f32[8,128]{1,0:T(8,128)S(1)}, f32[8,128]{1,0:T(8,128)S(1)}, u32[]{:S(2)}, u32[]{:S(2)}) collective-permute-start(f32[8,128]{1,0:T(8,128)S(1)} %get-tuple-element.52), channel_id=1, source_target_pairs={{0,1},{1,2},{2,3},{3,0},{4,5},{5,6},{6,7},{7,4},{8,9},{9,10},{10,1... | collective-permute-start | bytes 12296 | tf_op jit(solution)/shard_map/ppermute | solution.py:587
  3.0 3.9 %collective-permute-start.1 = (f32[8,128]{1,0:T(8,128)S(1)}, f32[8,128]{1,0:T(8,128)S(1)}, u32[]{:S(2)}, u32[]{:S(2)}) collective-permute-start(f32[8,128]{1,0:T(8,128)S(1)} %get-tuple-element.53), channel_id=1, source_target_pairs={{1,0},{2,1},{3,2},{0,3},{5,4},{6,5},{7,6},{4,7},{9,8},{10,9},{11,1... | collective-permute-start | bytes 12296 | tf_op jit(solution)/shard_map/ppermute | solution.py:588
  7.0 1.3 %collective-permute-start.2 = (f32[7,16,128]{2,1,0:T(8,128)S(1)}, f32[7,16,128]{2,1,0:T(8,128)S(1)}, u32[]{:S(2)}, u32[]{:S(2)}) collective-permute-start(f32[7,16,128]{2,1,0:T(8,128)S(1)} %get-tuple-element.57.own), channel_id=1, source_target_pairs={{0,4},{4,0},{8,12},{12,8},{16,20},{20,16},{24,28},{28,24},{32,36},... | collective-permute-start | bytes 172040 | tf_op jit(solution)/shard_map/ppermute | solution.py:634
  8.4 6.3 %collective-permute-start.3 = (f32[7,16,128]{2,1,0:T(8,128)S(1)}, f32[7,16,128]{2,1,0:T(8,128)S(1)}, u32[]{:S(2)}, u32[]{:S(2)}) collective-permute-start(f32[7,16,128]{2,1,0:T(8,128)S(1)} %pair.1.own.own_z), channel_id=1, source_target_pairs={{0,16},{4,20},{8,24},{12,28},{16,0},{20,4},{24,8},{28,12},{32,48},... | collective-permute-start | bytes 172040 | tf_op jit(solution)/shard_map/ppermute | solution.py:572
  12.4 5.4 %collective-permute-start.4 = (f32[7,16,128]{2,1,0:T(8,128)S(1)}, f32[7,16,128]{2,1,0:T(8,128)S(1)}, u32[]{:S(2)}, u32[]{:S(2)}) collective-permute-start(f32[7,16,128]{2,1,0:T(8,128)S(1)} %pair.1.own.own_z), channel_id=1, source_target_pairs={{0,24},{4,28},{8,16},{12,20},{16,8},{20,12},{24,0},{28,4},{32,56},... | collective-permute-start | bytes 172040 | tf_op jit(solution)/shard_map/ppermute | solution.py:572
  13.1 4.7 %collective-permute-start.5 = (f32[7,16,128]{2,1,0:T(8,128)S(1)}, f32[7,16,128]{2,1,0:T(8,128)S(1)}, u32[]{:S(2)}, u32[]{:S(2)}) collective-permute-start(f32[7,16,128]{2,1,0:T(8,128)S(1)} %pair.1.own.own_z), channel_id=1, source_target_pairs={{0,8},{4,12},{8,0},{12,4},{16,24},{20,28},{24,16},{28,20},{32,40},... | collective-permute-start | bytes 172040 | tf_op jit(solution)/shard_map/ppermute | solution.py:572
  17.9 5.8 %collective-permute-start.6 = (f32[7,16,128]{2,1,0:T(8,128)S(1)}, f32[7,16,128]{2,1,0:T(8,128)S(1)}, u32[]{:S(2)}, u32[]{:S(2)}) collective-permute-start(f32[7,16,128]{2,1,0:T(8,128)S(1)} %four.1.own_y), channel_id=1, source_target_pairs={{0,64},{4,68},{8,72},{12,76},{16,80},{20,84},{24,88},{28,92},{32,9... | collective-permute-start | bytes 172040 | tf_op jit(solution)/shard_map/ppermute | solution.py:572
  21.2 5.4 %collective-permute-start.7 = (f32[7,16,128]{2,1,0:T(8,128)S(1)}, f32[7,16,128]{2,1,0:T(8,128)S(1)}, u32[]{:S(2)}, u32[]{:S(2)}) collective-permute-start(f32[7,16,128]{2,1,0:T(8,128)S(1)} %four.1.own_y), channel_id=1, source_target_pairs={{0,96},{4,100},{8,104},{12,108},{16,112},{20,116},{24,120},{28,124... | collective-permute-start | bytes 172040 | tf_op jit(solution)/shard_map/ppermute | solution.py:572
  22.2 4.3 %collective-permute-start.8 = (f32[7,16,128]{2,1,0:T(8,128)S(1)}, f32[7,16,128]{2,1,0:T(8,128)S(1)}, u32[]{:S(2)}, u32[]{:S(2)}) collective-permute-start(f32[7,16,128]{2,1,0:T(8,128)S(1)} %four.1.own_y), channel_id=1, source_target_pairs={{0,32},{4,36},{8,40},{12,44},{16,48},{20,52},{24,56},{28,60},{32,0... | collective-permute-start | bytes 172040 | tf_op jit(solution)/shard_map/ppermute | solution.py:572
  27.0 5.3 %collective-permute-start.10 = (f32[8,128]{1,0:T(8,128)S(1)}, f32[8,128]{1,0:T(8,128)S(1)}, u32[]{:S(2)}, u32[]{:S(2)}) collective-permute-start(f32[8,128]{1,0:T(8,128)S(1)} %get-tuple-element.78.own), channel_id=1, source_target_pairs={{0,2},{1,3},{2,0},{3,1},{4,6},{5,7},{6,4},{7,5},{8,10},{9,11},{10,... | collective-permute-start | bytes 12296 | tf_op jit(solution)/shard_map/ppermute | solution.py:572
  29.3 4.8 %collective-permute-start.11 = (f32[8,128]{1,0:T(8,128)S(1)}, f32[8,128]{1,0:T(8,128)S(1)}, u32[]{:S(2)}, u32[]{:S(2)}) collective-permute-start(f32[8,128]{1,0:T(8,128)S(1)} %get-tuple-element.78.own), channel_id=1, source_target_pairs={{0,3},{1,2},{2,1},{3,0},{4,7},{5,6},{6,5},{7,4},{8,11},{9,10},{10,... | collective-permute-start | bytes 12296 | tf_op jit(solution)/shard_map/ppermute | solution.py:572
  30.7 3.6 %collective-permute-start.9 = (f32[8,128]{1,0:T(8,128)S(1)}, f32[8,128]{1,0:T(8,128)S(1)}, u32[]{:S(2)}, u32[]{:S(2)}) collective-permute-start(f32[8,128]{1,0:T(8,128)S(1)} %get-tuple-element.78.own), channel_id=1, source_target_pairs={{0,1},{1,0},{2,3},{3,2},{4,5},{5,4},{6,7},{7,6},{8,9},{9,8},{10,11... | collective-permute-start | bytes 12296 | tf_op jit(solution)/shard_map/ppermute | solution.py:572
